TPU v7x, 128 devices: a whole 4x4x4 slice. The times are simulated.
128 devices in a mesh: space: 8 (over z, x_hi), ens: 16 (over y, x_lo, core).
Axes of the slice: x: 4 (x_hi: 2, x_lo: 2; x = x_hi * 2 + x_lo), y: 4, z: 4, core: 2. Of those that a mesh axis runs over, the one named last changes fastest.
Arguments:
- log_perm: float32 [128, 16, 64, 512], P('ens', 'space'), may hold values from -4 to 4
- storage: float32 [16, 64, 512], P('space'), may hold values from 0.5 to 2
- head_init: float32 [16, 64, 512], P('space'), may hold values from -6 to 6
- well_cells: int32 [16], replicated, may hold values from 0 to 524287
- well_rates: float32 [16], replicated, may hold values from -12 to 12
- obs_cells: int32 [32], replicated, may hold values from 0 to 524287
- obs_values: float32 [32], replicated, may hold values from -6 to 6
- noise_var: float32 [32], replicated, may hold values from 0.05 to 0.5
- step_size: float32 [1], replicated, may hold values from 0.5 to 2
- perturb: float32 [128, 32], P('ens'), may hold values from -2 to 2
Outputs:
- head_field: float32 [128, 16, 64, 512], P('ens', 'space')
- updated: float32 [128, 16, 64, 512], P('ens', 'space')
All inputs are finite; a program needn't handle non-finite values.
Results may differ from a plain program's by a relative error of at most 0.00025.
Values sent between devices are 32-bit elements; how exact they have to be, the bound alone decides.
A program may use at most 192 MiB of HBM per device.

v0:
```python
import jax
import jax.numpy as jnp
from jax import lax
from jax.sharding import PartitionSpec as P

SWEEPS = 3


OMEGA = 0.8
HIGHEST = lax.Precision.HIGHEST
DIRECTIONS = [
    (a, b, c) for a in (-1, 0, 1) for b in (-1, 0, 1) for c in (-1, 0, 1) if (a, b, c) != (0, 0, 0)
]


def padded_2(block, sides, width):
    for axis, dim in sides:
        count = lax.axis_size(axis)
        forward = [(i, i + 1) for i in range(count - 1)]
        backward = [(target, source) for source, target in forward]
        low = lax.ppermute(
            lax.slice_in_dim(block, block.shape[dim] - width, None, axis=dim), axis, forward
        )
        high = lax.ppermute(lax.slice_in_dim(block, 0, width, axis=dim), axis, backward)
        block = jnp.concatenate([low, block, high], axis=dim)
    return block


def shifted(padded, a, b, c, planes, depth, across):
    return padded[..., 1 + a : 1 + a + planes, 1 + b : 1 + b + depth, 1 + c : 1 + c + across]


def solve_pair(factor, residual):
    first = lax.linalg.triangular_solve(factor, residual.T, left_side=True, lower=True)
    second = lax.linalg.triangular_solve(
        factor, first, left_side=True, lower=True, transpose_a=True
    )
    return second.T


def shards(
    log_perm,
    storage,
    head_init,
    well_cells,
    well_rates,
    obs_cells,
    obs_values,
    noise_var,
    step_size,
    perturb,
):
    members, planes, depth, across = log_perm.shape
    cell_count = planes * depth * across
    total_members = members * lax.axis_size("ens")
    offset = lax.axis_index("space") * cell_count
    cell_ids = lax.broadcasted_iota(jnp.int32, (1, cell_count), 1)
    hits = (cell_ids == (well_cells - offset)[:, None]).astype(jnp.float32)
    source = jnp.dot(well_rates, hits, precision=HIGHEST).reshape(planes, depth, across)
    permeability = jnp.exp(log_perm)
    rimmed = padded_2(permeability, (("space", 1),), 1)
    padded = jnp.pad(rimmed, ((0, 0), (0, 0), (1, 1), (1, 1)))
    transmit = []
    for a, b, c in DIRECTIONS:
        factor = 2.0 ** (1 - abs(a) - abs(b) - abs(c))
        neighbour = shifted(padded, a, b, c, planes, depth, across)
        transmit.append(factor * 2.0 * permeability * neighbour / (permeability + neighbour))
    diagonal = storage + sum(transmit)
    forcing = storage * head_init + source
    head_field = jnp.broadcast_to(head_init, log_perm.shape)
    for sweep_index in range(SWEEPS):
        rimmed_head = padded_2(head_field, (("space", 1),), 1)
        padded_head = jnp.pad(rimmed_head, ((0, 0), (0, 0), (1, 1), (1, 1)))
        gathered = sum(
            (
                transmit[i] * shifted(padded_head, a, b, c, planes, depth, across)
                for i, (a, b, c) in enumerate(DIRECTIONS)
            )
        )
        head_field = (1.0 - OMEGA) * head_field + OMEGA * (forcing + gathered) / diagonal
    local_obs = obs_cells - offset
    inside = ((local_obs >= 0) & (local_obs < cell_count)).astype(jnp.float32)
    picked = (
        jnp.take(
            head_field.reshape(members, cell_count), jnp.clip(local_obs, 0, cell_count - 1), axis=1
        )
        * inside
    )
    observed = lax.psum(picked, "space")
    every_obs = lax.all_gather(observed, "ens", axis=0, tiled=True)
    mean_obs = jnp.mean(every_obs, axis=0)
    spread = every_obs - mean_obs
    covariance = jnp.dot(spread.T, spread, precision=HIGHEST) / (total_members - 1)
    deviation = observed - mean_obs
    system = covariance + jnp.diag(noise_var / step_size[0])
    factor_lower = jnp.linalg.cholesky(system)
    gain_rows = solve_pair(factor_lower, obs_values[None, :] + perturb - observed)
    flat = log_perm.reshape(members, cell_count)
    piece_field = lax.all_gather(flat, "ens", axis=0, tiled=True)
    piece_dev = lax.all_gather(deviation, "ens", axis=0, tiled=True)
    mixing = jnp.dot(piece_dev, gain_rows.T, precision=HIGHEST)
    change = lax.dot_general(mixing, piece_field, (((0,), (0,)), ((), ())), precision=HIGHEST)
    updated = (flat + change / (total_members - 1)).reshape(log_perm.shape)
    return (head_field, updated)


def solution(mesh):
    return jax.shard_map(
        shards,
        mesh=mesh,
        in_specs=(
            P("ens", "space", None, None),
            P("space", None, None),
            P("space", None, None),
            P(),
            P(),
            P(),
            P(),
            P(),
            P(),
            P("ens", None),
        ),
        out_specs=(P("ens", "space", None, None), P("ens", "space", None, None)),
        check_vma=False,
    )
```

profile of v0, /device:TPU:25, one launch (start us, length us, event | category | flops | bytes accessed | tf_op | source)
XLA Modules:
  0.0 540.9 jit_solution(13911891176995488092)
XLA Ops:
  7.2 4.2 copy.30
  11.4 1.9 exp.3
  13.4 1.5 fusion.120
  14.9 4.8 collective-permute-start
  19.8 1.4 collective-permute-start.1
  21.2 1.1 broadcast_in_dim.53
  22.3 6.5 %collective-permute-start.2 = (f32[8,1,64,512]{3,2,1,0:T(8,128)}, f32[8,1,64,512]{3,2,1,0:T(8,128)}, u32[]{:S(2)}, u32[]{:S(2)}) collective-permute-start(f32[8,1,64,512]{3,2,1,0:T(8,128)} %broadcast_in_dim.53), channel_id=1, source_target_pairs={{0,16},{16,32},{32,48},{48,64},{64,80},{80,96},{96,112},{1,17},{17... | collective-permute-start | bytes 3145736 | tf_op jit(solution)/shard_map/ppermute | solution.py:21
  28.8 1.1 broadcast_in_dim.55
  29.9 1.3 collective-permute-start.3
  31.2 2.1 fusion.4
  33.3 1.7 reshape.43
  35.0 1.8 broadcast_multiply_fusion
  36.8 23.5 %collective-permute-done = f32[8,1,64,512]{3,2,1,0:T(8,128)S(1)} collective-permute-done((f32[8,1,64,512]{3,2,1,0:T(8,128)}, f32[8,1,64,512]{3,2,1,0:T(8,128)S(1)}, u32[]{:S(2)}, u32[]{:S(2)}) %collective-permute-start) | collective-permute-done | bytes 1048608 | tf_op jit(solution)/shard_map/ppermute | solution.py:21
  60.3 46.1 %collective-permute-done.1 = f32[8,1,64,512]{3,2,1,0:T(8,128)} collective-permute-done((f32[8,1,64,512]{3,2,1,0:T(8,128)}, f32[8,1,64,512]{3,2,1,0:T(8,128)}, u32[]{:S(2)}, u32[]{:S(2)}) %collective-permute-start.1) | collective-permute-done | bytes 1048608 | tf_op jit(solution)/shard_map/ppermute | solution.py:24
  106.4 3.7 select_maximum_fusion.6
  110.2 86.2 %collective-permute-done.3 = f32[8,1,64,512]{3,2,1,0:T(8,128)} collective-permute-done((f32[8,1,64,512]{3,2,1,0:T(8,128)}, f32[8,1,64,512]{3,2,1,0:T(8,128)}, u32[]{:S(2)}, u32[]{:S(2)}) %collective-permute-start.3) | collective-permute-done | bytes 1048608 | tf_op jit(solution)/shard_map/ppermute | solution.py:24
  196.3 0.3 broadcast_in_dim.54
  196.6 4.7 select_maximum_fusion.4
  201.3 23.9 %fusion.71 = f32[8,2,64,512]{3,2,1,0:T(8,128)} fusion(f32[8,4,66,514]{3,2,1,0:T(8,128)S(1)} %select_maximum_fusion.4, f32[8,1,64,512]{3,2,1,0:T(8,128)} %collective-permute-done.3, f32[8,2,64,512]{3,2,1,0:T(8,128)} %copy-done.5, f32[8,1,64,512]{3,2,1,0:T(8,128)} %collective-permute-done.2, f32[2,64,512]{2,1,0:T(8,128)S(1)} %copy-done.7, ...), kind=kLoop, calls=%fused_computation.139 | loop fusion | flops 87031808 | bytes 114032640 | tf_op jit(solution)/shard_map/add | solution.py:80
  225.3 1.9 fusion.119
  227.2 6.3 %collective-permute-start.4 = (f32[8,1,64,512]{3,2,1,0:T(8,128)S(1)}, f32[8,1,64,512]{3,2,1,0:T(8,128)S(1)}, u32[]{:S(2)}, u32[]{:S(2)}) collective-permute-start(f32[8,1,64,512]{3,2,1,0:T(8,128)S(1)} %get-tuple-element.12), channel_id=1, source_target_pairs={{0,16},{16,32},{32,48},{48,64},{64,80},{80,96},{96,112},{1,17},{17... | collective-permute-start | bytes 3145736 | tf_op jit(solution)/shard_map/ppermute | solution.py:21
  233.5 1.5 collective-permute-start.5
  234.9 17.0 %collective-permute-done.4 = f32[8,1,64,512]{3,2,1,0:T(8,128)S(1)} collective-permute-done((f32[8,1,64,512]{3,2,1,0:T(8,128)S(1)}, f32[8,1,64,512]{3,2,1,0:T(8,128)S(1)}, u32[]{:S(2)}, u32[]{:S(2)}) %collective-permute-start.4) | collective-permute-done | bytes 1048608 | tf_op jit(solution)/shard_map/ppermute | solution.py:21
  251.9 61.5 %collective-permute-done.5 = f32[8,1,64,512]{3,2,1,0:T(8,128)S(1)} collective-permute-done((f32[8,1,64,512]{3,2,1,0:T(8,128)S(1)}, f32[8,1,64,512]{3,2,1,0:T(8,128)S(1)}, u32[]{:S(2)}, u32[]{:S(2)}) %collective-permute-start.5) | collective-permute-done | bytes 1048608 | tf_op jit(solution)/shard_map/ppermute | solution.py:24
  313.4 1.0 copy-done.9
  314.4 2.7 select_maximum_fusion.2
  317.0 22.7 %fusion.40 = f32[8,2,64,512]{3,2,1,0:T(8,128)} fusion(f32[8,4,66,514]{3,2,1,0:T(8,128)S(1)} %select_maximum_fusion.2, f32[8,1,64,512]{3,2,1,0:T(8,128)} %copy-done.9, f32[8,2,64,512]{3,2,1,0:T(8,128)} %fusion.71, f32[8,1,64,512]{3,2,1,0:T(8,128)S(1)} %collective-permute-done.4, f32[2,64,512]{2,1,0:T(8,128)S(1)} %copy-done.7, ...), kind=kLoop, calls=%fused_computation.82 | loop fusion | flops 87556096 | bytes 113770496 | tf_op jit(solution)/shard_map/add | solution.py:80
  339.8 1.9 fusion.118
  341.7 4.7 collective-permute-start.6
  346.3 1.3 collective-permute-start.7
  348.4 18.5 %collective-permute-done.6 = f32[8,1,64,512]{3,2,1,0:T(8,128)S(1)} collective-permute-done((f32[8,1,64,512]{3,2,1,0:T(8,128)S(1)}, f32[8,1,64,512]{3,2,1,0:T(8,128)S(1)}, u32[]{:S(2)}, u32[]{:S(2)}) %collective-permute-start.6) | collective-permute-done | bytes 1048608 | tf_op jit(solution)/shard_map/ppermute | solution.py:21
  366.9 25.0 %collective-permute-done.7 = f32[8,1,64,512]{3,2,1,0:T(8,128)S(1)} collective-permute-done((f32[8,1,64,512]{3,2,1,0:T(8,128)S(1)}, f32[8,1,64,512]{3,2,1,0:T(8,128)S(1)}, u32[]{:S(2)}, u32[]{:S(2)}) %collective-permute-start.7) | collective-permute-done | bytes 1048608 | tf_op jit(solution)/shard_map/ppermute | solution.py:24
  391.8 1.0 copy-done.8
  392.8 2.7 select_maximum_fusion
  395.5 22.7 %fusion.9 = f32[8,2,64,512]{3,2,1,0:T(8,128)} fusion(f32[8,4,66,514]{3,2,1,0:T(8,128)S(1)} %select_maximum_fusion, f32[8,1,64,512]{3,2,1,0:T(8,128)} %copy-done.8, f32[8,2,64,512]{3,2,1,0:T(8,128)} %fusion.40, f32[8,1,64,512]{3,2,1,0:T(8,128)S(1)} %collective-permute-done.6, f32[2,64,512]{2,1,0:T(8,128)S(1)} %copy-done.7, ...), kind=kLoop, calls=%fused_computation.25 | loop fusion | flops 87556096 | bytes 113770496 | tf_op jit(solution)/shard_map/add | solution.py:80
  418.1 18.0 %copy.24 = f32[8,2,64,512]{0,3,2,1:T(8,128)} copy(f32[8,2,64,512]{3,2,1,0:T(8,128)} %fusion.9) | data formatting | bytes 4194304 | tf_op jit(solution)/shard_map/add | solution.py:80
  436.2 11.1 %gather_fusion = f32[32,8]{1,0:T(8,128)S(1)} fusion(f32[8,65536]{0,1:T(8,128)} %bitcast.36, s32[1024]{0:T(1024)S(1)} %pad_clamp_fusion), kind=kCustom, calls=%fused_computation | custom fusion | bytes 2176 | tf_op jit(solution)/shard_map/jit(_take)/gather | solution.py:84
  447.4 18.1 %psum.7 = f32[8,32]{1,0:T(8,128)S(1)} all-reduce(f32[8,32]{1,0:T(8,128)S(1)} %multiply_bitcast_fusion), channel_id=1, replica_groups=mesh['space'=8,'ens'=16] {'space'}, use_global_device_ids=true, to_apply=%region_0.1 | all-reduce | flops 256 | bytes 2048 | tf_op jit(solution)/shard_map/psum | solution.py:89
  465.5 21.9 %all_gather.9 = f32[128,32]{1,0:T(8,128)S(1)} all-gather(f32[8,32]{1,0:T(8,128)S(1)} %psum.7), channel_id=1, replica_groups=mesh['space'=8,'ens'=16] {'ens'}, dimensions={0}, use_global_device_ids=true | all-gather | bytes 17408 | tf_op jit(solution)/shard_map/all_gather | solution.py:90
  487.5 0.3 convolution_multiply_fusion.1
  487.9 2.9 cholesky.16
  490.8 0.6 compare_reduce_fusion
  491.5 0.7 fusion.107
  492.1 2.4 custom-call.8
  494.6 16.8 %all_gather.10 = f32[128,32]{1,0:T(8,128)S(1)} all-gather(f32[8,32]{1,0:T(8,128)S(1)} %broadcast_subtract_fusion), channel_id=1, replica_groups=mesh['space'=8,'ens'=16] {'ens'}, dimensions={0}, use_global_device_ids=true | all-gather | bytes 17408 | tf_op jit(solution)/shard_map/all_gather | solution.py:100
  511.7 0.2 fusion.121
  511.9 19.6 %fusion = f32[8,65536]{1,0:T(8,128)S(1)} fusion(f32[8,65536]{1,0:T(8,128)S(1)} %bitcast.38, f32[128,8]{0,1:T(8,128)S(1)} %fusion.121, f32[128,65536]{1,0:T(8,128)} %all-gather.2.cloned.1.call-done), kind=kOutput, calls=%fused_computation.2 | convolution fusion | flops 806354944 | bytes 37752832 | tf_op jit(solution)/shard_map/dot_general | solution.py:102
  531.5 2.5 copy.28
  (51 shorter events, 0.8 us)
Async XLA Ops:
  7.2 24.1 %copy-start = (f32[16]{0:T(128)S(1)}, f32[16]{0:T(128)}, u32[]{:S(2)}) copy-start(f32[16]{0:T(128)} %param.14) | copy-start | bytes 196
  7.2 504.7 %all-gather.2.cloned.1.call-start = ((), (), s32[]{:S(2)}) async-start(), calls=%async_computation | async-start | bytes 35651584 | tf_op jit(solution)/shard_map/all_gather | solution.py:99
  13.4 7.8 %copy-start.10 = (f32[2,64,512]{2,1,0:T(8,128)S(1)}, f32[2,64,512]{2,1,0:T(8,128)}, u32[]{:S(2)}) copy-start(f32[2,64,512]{2,1,0:T(8,128)} %param.12) | copy-start | bytes 786436
  14.9 16.3 %copy-start.15 = (s32[16]{0:T(128)S(1)}, s32[16]{0:T(128)}, u32[]{:S(2)}) copy-start(s32[16]{0:T(128)} %param.13) | copy-start | bytes 196
  14.9 45.4 %collective-permute-start = (f32[8,1,64,512]{3,2,1,0:T(8,128)}, f32[8,1,64,512]{3,2,1,0:T(8,128)S(1)}, u32[]{:S(2)}, u32[]{:S(2)}) collective-permute-start(f32[8,1,64,512]{3,2,1,0:T(8,128)} %get-tuple-element.14), channel_id=1, source_target_pairs={{0,16},{16,32},{32,48},{48,64},{64,80},{80,96},{96,112},{1,17},{17... | collective-permute-start | bytes 3145736 | tf_op jit(solution)/shard_map/ppermute | solution.py:21
  19.7 15.3 %copy-start.7 = (f32[2,64,512]{2,1,0:T(8,128)S(1)}, f32[2,64,512]{2,1,0:T(8,128)}, u32[]{:S(2)}) copy-start(f32[2,64,512]{2,1,0:T(8,128)} %param.11) | copy-start | bytes 786436
  19.8 86.7 %collective-permute-start.1 = (f32[8,1,64,512]{3,2,1,0:T(8,128)}, f32[8,1,64,512]{3,2,1,0:T(8,128)}, u32[]{:S(2)}, u32[]{:S(2)}) collective-permute-start(f32[8,1,64,512]{3,2,1,0:T(8,128)} %get-tuple-element.15), channel_id=1, source_target_pairs={{16,0},{32,16},{48,32},{64,48},{80,64},{96,80},{112,96},{17,1},{33... | collective-permute-start | bytes 3145736 | tf_op jit(solution)/shard_map/ppermute | solution.py:24
  22.3 87.8 %collective-permute-start.2 = (f32[8,1,64,512]{3,2,1,0:T(8,128)}, f32[8,1,64,512]{3,2,1,0:T(8,128)}, u32[]{:S(2)}, u32[]{:S(2)}) collective-permute-start(f32[8,1,64,512]{3,2,1,0:T(8,128)} %broadcast_in_dim.53), channel_id=1, source_target_pairs={{0,16},{16,32},{32,48},{48,64},{64,80},{80,96},{96,112},{1,17},{17... | collective-permute-start | bytes 3145736 | tf_op jit(solution)/shard_map/ppermute | solution.py:21
  29.9 166.4 %collective-permute-start.3 = (f32[8,1,64,512]{3,2,1,0:T(8,128)}, f32[8,1,64,512]{3,2,1,0:T(8,128)}, u32[]{:S(2)}, u32[]{:S(2)}) collective-permute-start(f32[8,1,64,512]{3,2,1,0:T(8,128)} %broadcast_in_dim.55), channel_id=1, source_target_pairs={{16,0},{32,16},{48,32},{64,48},{80,64},{96,80},{112,96},{17,1},{33... | collective-permute-start | bytes 3145736 | tf_op jit(solution)/shard_map/ppermute | solution.py:24
  36.8 159.5 %copy-start.11 = (f32[2,64,512]{2,1,0:T(8,128)S(1)}, f32[2,64,512]{2,1,0:T(8,128)}, u32[]{:S(2)}) copy-start(f32[2,64,512]{2,1,0:T(8,128)} %param.12) | copy-start | bytes 786436
  196.6 4.7 copy-start.5
  196.6 4.7 copy-start.2
  225.3 89.1 %copy-start.4 = (f32[8,2,64,512]{3,2,1,0:T(8,128)S(1)}, f32[8,2,64,512]{3,2,1,0:T(8,128)}, u32[]{:S(2)}) copy-start(f32[8,2,64,512]{3,2,1,0:T(8,128)} %fusion.71) | copy-start | bytes 6291460
  227.2 24.7 %collective-permute-start.4 = (f32[8,1,64,512]{3,2,1,0:T(8,128)S(1)}, f32[8,1,64,512]{3,2,1,0:T(8,128)S(1)}, u32[]{:S(2)}, u32[]{:S(2)}) collective-permute-start(f32[8,1,64,512]{3,2,1,0:T(8,128)S(1)} %get-tuple-element.12), channel_id=1, source_target_pairs={{0,16},{16,32},{32,48},{48,64},{64,80},{80,96},{96,112},{1,17},{17... | collective-permute-start | bytes 3145736 | tf_op jit(solution)/shard_map/ppermute | solution.py:21
  233.5 79.9 %collective-permute-start.5 = (f32[8,1,64,512]{3,2,1,0:T(8,128)S(1)}, f32[8,1,64,512]{3,2,1,0:T(8,128)S(1)}, u32[]{:S(2)}, u32[]{:S(2)}) collective-permute-start(f32[8,1,64,512]{3,2,1,0:T(8,128)S(1)} %get-tuple-element.13), channel_id=1, source_target_pairs={{16,0},{32,16},{48,32},{64,48},{80,64},{96,80},{112,96},{17,1},{33... | collective-permute-start | bytes 3145736 | tf_op jit(solution)/shard_map/ppermute | solution.py:24
  313.4 1.0 copy-start.9
  339.7 8.6 %copy-start.14 = (s32[32]{0:T(128)S(1)}, s32[32]{0:T(128)}, u32[]{:S(2)}) copy-start(s32[32]{0:T(128)} %param.15) | copy-start | bytes 388
  339.7 8.6 %copy-start.16 = (f32[32]{0:T(128)S(1)}, f32[32]{0:T(128)}, u32[]{:S(2)}) copy-start(f32[32]{0:T(128)} %param.17) | copy-start | bytes 388
  339.7 53.1 %copy-start.3 = (f32[8,2,64,512]{3,2,1,0:T(8,128)S(1)}, f32[8,2,64,512]{3,2,1,0:T(8,128)}, u32[]{:S(2)}) copy-start(f32[8,2,64,512]{3,2,1,0:T(8,128)} %fusion.40) | copy-start | bytes 6291460
  341.7 25.2 %collective-permute-start.6 = (f32[8,1,64,512]{3,2,1,0:T(8,128)S(1)}, f32[8,1,64,512]{3,2,1,0:T(8,128)S(1)}, u32[]{:S(2)}, u32[]{:S(2)}) collective-permute-start(f32[8,1,64,512]{3,2,1,0:T(8,128)S(1)} %get-tuple-element.10), channel_id=1, source_target_pairs={{0,16},{16,32},{32,48},{48,64},{64,80},{80,96},{96,112},{1,17},{17... | collective-permute-start | bytes 3145736 | tf_op jit(solution)/shard_map/ppermute | solution.py:21
  346.3 45.5 %collective-permute-start.7 = (f32[8,1,64,512]{3,2,1,0:T(8,128)S(1)}, f32[8,1,64,512]{3,2,1,0:T(8,128)S(1)}, u32[]{:S(2)}, u32[]{:S(2)}) collective-permute-start(f32[8,1,64,512]{3,2,1,0:T(8,128)S(1)} %get-tuple-element.11), channel_id=1, source_target_pairs={{16,0},{32,16},{48,32},{64,48},{80,64},{96,80},{112,96},{17,1},{33... | collective-permute-start | bytes 3145736 | tf_op jit(solution)/shard_map/ppermute | solution.py:24
  391.8 1.0 copy-start.8
  418.1 93.3 %copy-start.12 = (f32[8,32]{1,0:T(8,128)S(1)}, f32[8,32]{1,0:T(8,128)}, u32[]{:S(2)}) copy-start(f32[8,32]{1,0:T(8,128)} %param.19) | copy-start | bytes 3076
  418.1 93.3 %copy-start.13 = (f32[32]{0:T(128)S(1)}, f32[32]{0:T(128)}, u32[]{:S(2)}) copy-start(f32[32]{0:T(128)} %param.16) | copy-start | bytes 388
  418.1 93.7 %copy-start.6 = (f32[1,8,128,512]{3,1,2,0:T(8,128)S(1)}, f32[1,8,128,512]{3,1,2,0:T(8,128)}, u32[]{:S(2)}) copy-start(f32[1,8,128,512]{3,1,2,0:T(8,128)} %copy.30) | copy-start | bytes 6291460
  531.5 2.6 copy-start.1
Sparse Core Ops, SparseCore 0:
  11.5 214.5 all-gather.1
where the time goes:
time: 546 us; the launch traced here: 541 us
  waiting for transfers between devices  278 us (51%)
  other arithmetic  91.6 us (17%)
  blocking collectives  56.9 us (10%)
  local copies, waits for them, and re-layouts  49.4 us (9%)
  starting transfers between devices  27.8 us (5%)
  matrix products  22.4 us (4%)
  between operations  15 us (3%)
    ppermute x4, waiting for transfers between devices, padded_2(): lax.ppermute(lax.slice_in_dim(block, 0, width, axis=dim), axis, backward)  219 us
    add x3, other arithmetic, shards(): (1.0 - OMEGA) * head_field + OMEGA * (forcing + gathered) / diagonal  69.3 us
    ppermute x4, waiting for transfers between devices, padded_2(): lax.ppermute(lax.slice_in_dim(block, block.shape[dim] - width, None, axis...  59 us
    ppermute x4, starting transfers between devices, padded_2(): lax.ppermute(lax.slice_in_dim(block, block.shape[dim] - width, None, axis...  22.3 us
    all_gather x1, blocking collectives, shards(): every_obs = lax.all_gather(observed, 'ens', axis=0, tiled=True)  21.9 us
    dot_general x1, matrix products, shards(): lax.dot_general(mixing, piece_field, (((0,), (0,)), ((), ())), precision=...  19.6 us
    psum x1, blocking collectives, shards(): observed = lax.psum(picked, 'space')  18.1 us
    add x1, local copies, waits for them, and re-layouts, shards(): (1.0 - OMEGA) * head_field + OMEGA * (forcing + gathered) / diagonal  18 us
  transfers between devices with their start and end apart: 9, of which 7 were waited for; matrix products, arithmetic and copies ran while one was open for 25% of the time, Pallas kernels for 0%

commit v1 on v0

v1 whole, which is shorter than its diff:
```python
import jax
import jax.numpy as jnp
from jax import lax
from jax.sharding import PartitionSpec as P

SWEEPS = 3


OMEGA = 0.8
HIGHEST = lax.Precision.HIGHEST
DIRECTIONS = [
    (a, b, c) for a in (-1, 0, 1) for b in (-1, 0, 1) for c in (-1, 0, 1) if (a, b, c) != (0, 0, 0)
]


def shifted(padded, a, b, c, planes, depth, across):
    return padded[..., 1 + a : 1 + a + planes, 1 + b : 1 + b + depth, 1 + c : 1 + c + across]


def solve_pair(factor, residual):
    first = lax.linalg.triangular_solve(factor, residual.T, left_side=True, lower=True)
    second = lax.linalg.triangular_solve(
        factor, first, left_side=True, lower=True, transpose_a=True
    )
    return second.T


def forward(log_row, storage, head_init, source):
    planes, depth, across = log_row.shape
    permeability = jnp.exp(log_row)
    padded = jnp.pad(permeability, 1)
    transmit = []
    for a, b, c in DIRECTIONS:
        factor = 2.0 ** (1 - abs(a) - abs(b) - abs(c))
        neighbour = shifted(padded, a, b, c, planes, depth, across)
        transmit.append(factor * 2.0 * permeability * neighbour / (permeability + neighbour))
    diagonal = storage + sum(transmit)
    forcing = storage * head_init + source
    head_field = head_init
    for sweep_index in range(SWEEPS):
        padded_head = jnp.pad(head_field, 1)
        gathered = sum(
            (
                transmit[i] * shifted(padded_head, a, b, c, planes, depth, across)
                for i, (a, b, c) in enumerate(DIRECTIONS)
            )
        )
        head_field = (1.0 - OMEGA) * head_field + OMEGA * (forcing + gathered) / diagonal
    return head_field


def shards(
    log_perm,
    storage,
    head_init,
    well_cells,
    well_rates,
    obs_cells,
    obs_values,
    noise_var,
    step_size,
    perturb,
):
    members, planes, depth, across = log_perm.shape
    n_space = lax.axis_size("space")
    n_ens = lax.axis_size("ens")
    cell_count = planes * depth * across
    total_members = members * n_ens
    grid_planes = planes * n_space

    whole_log = lax.all_to_all(log_perm, "space", 0, 1, tiled=True)
    whole_storage = lax.all_gather(storage, "space", axis=0, tiled=True)
    whole_head = lax.all_gather(head_init, "space", axis=0, tiled=True)
    source = (
        jnp.zeros((grid_planes * depth * across,), jnp.float32)
        .at[well_cells]
        .add(well_rates)
        .reshape(grid_planes, depth, across)
    )
    field = forward(whole_log[0], whole_storage, whole_head, source)
    picked = field.reshape(-1)[obs_cells]
    head_field = lax.all_to_all(field[None], "space", 1, 0, tiled=True)

    every_obs = lax.all_gather(picked[None], ("ens", "space"), axis=0, tiled=True)
    every_perturb = lax.all_gather(perturb, "ens", axis=0, tiled=True)
    mean_obs = jnp.mean(every_obs, axis=0)
    spread = every_obs - mean_obs
    covariance = jnp.dot(spread.T, spread, precision=HIGHEST) / (total_members - 1)
    system = covariance + jnp.diag(noise_var / step_size[0])
    factor_lower = jnp.linalg.cholesky(system)
    gain_rows = solve_pair(factor_lower, obs_values[None, :] + every_perturb - every_obs)
    mixing = jnp.dot(gain_rows, spread.T, precision=HIGHEST)

    flat = log_perm.reshape(members, cell_count)
    column = lax.all_to_all(flat, "ens", 1, 0, tiled=True)
    change = jnp.dot(mixing, column, precision=HIGHEST)
    new_column = column + change / (total_members - 1)
    updated = lax.all_to_all(new_column, "ens", 0, 1, tiled=True).reshape(log_perm.shape)
    return (head_field, updated)


def solution(mesh):
    return jax.shard_map(
        shards,
        mesh=mesh,
        in_specs=(
            P("ens", "space", None, None),
            P("space", None, None),
            P("space", None, None),
            P(),
            P(),
            P(),
            P(),
            P(),
            P(),
            P("ens", None),
        ),
        out_specs=(P("ens", "space", None, None), P("ens", "space", None, None)),
        check_vma=False,
    )
```

time: 546 us -> 448 us (0.82)
  waiting for transfers between devices: 278 us -> 111 us
  other arithmetic: 91.6 us -> 174 us
  blocking collectives: 56.9 us -> 89.9 us
  local copies, waits for them, and re-layouts: 49.4 us -> 22 us
  matrix products: 22.4 us -> 6.47 us
    ppermute x8 -> x0, waiting for transfers between devices: 278 us -> none  [the longest x4 219 us: padded_2(): lax.ppermute(lax.slice_in_dim(block, 0, width, axis=dim), axis, backward)]
    add x3, other arithmetic: 69.3 us -> 165 us  [forward(): (1.0 - OMEGA) * head_field + OMEGA * (forcing + gathered) / diagonal]
    all_gather x1 -> x2, waiting for transfers between devices: 0.01 us -> 69.5 us  [the longest x1 54.8 us: shards(): whole_storage = lax.all_gather(storage, 'space', axis=0, tiled=True)]
    unnamed x0 -> x1, blocking collectives: none -> 63 us
    all_to_all x0 -> x4, waiting for transfers between devices: none -> 40.1 us  [the longest x1 25.9 us: shards(): lax.all_to_all(new_column, 'ens', 0, 1, tiled=True).reshape(log_perm.shape)]
    ppermute x8 -> x0, starting transfers between devices: 27.7 us -> none  [the longest x4 22.3 us: padded_2(): lax.ppermute(lax.slice_in_dim(block, block.shape[dim] - width, None, axis...]
    all_to_all x0 -> x4, starting transfers between devices: none -> 26.2 us  [the longest x1 7.99 us: shards(): lax.all_to_all(new_column, 'ens', 0, 1, tiled=True).reshape(log_perm.shape)]
    psum x1 -> x0, blocking collectives: 18.1 us -> none  [shards(): observed = lax.psum(picked, 'space')]
  transfers between devices with their start and end apart: 9 -> 6, of which waited for: 7 -> 4; matrix products, arithmetic and copies ran while one was open for 25% -> 43% of each run, Pallas kernels for 0% -> 0%
where the time goes in v1:
time: 448 us; the launch traced here: 445 us
  other arithmetic  174 us (39%)
  waiting for transfers between devices  111 us (25%)
  blocking collectives  89.9 us (20%)
  starting transfers between devices  26.3 us (6%)
  local copies, waits for them, and re-layouts  22 us (5%)
  between operations  15.6 us (3%)
  matrix products  6.47 us (1%)
    add x3, other arithmetic, forward(): (1.0 - OMEGA) * head_field + OMEGA * (forcing + gathered) / diagonal  165 us
    unnamed x1, blocking collectives  63 us
    all_gather x1, waiting for transfers between devices, shards(): whole_storage = lax.all_gather(storage, 'space', axis=0, tiled=True)  54.8 us
    all_gather x1, blocking collectives, shards(): every_perturb = lax.all_gather(perturb, 'ens', axis=0, tiled=True)  26.9 us
    all_to_all x1, waiting for transfers between devices, shards(): lax.all_to_all(new_column, 'ens', 0, 1, tiled=True).reshape(log_perm.shape)  25.9 us
    all_gather x1, waiting for transfers between devices, shards(): whole_head = lax.all_gather(head_init, 'space', axis=0, tiled=True)  14.7 us
    all_to_all x1, waiting for transfers between devices, shards(): head_field = lax.all_to_all(field[None], 'space', 1, 0, tiled=True)  14.2 us
  transfers between devices with their start and end apart: 6, of which 4 were waited for; matrix products, arithmetic and copies ran while one was open for 43% of the time, Pallas kernels for 0%

profile of v1, /device:TPU:25, one launch (start us, length us, event | category | flops | bytes accessed | tf_op | source)
XLA Modules:
  0.0 445.1 jit_solution(13774725080699963734)
XLA Ops:
  7.2 0.0 all-gather.4.cloned.1.call-start
  7.2 0.7 all-gather.4.cloned.1.call-update
  7.9 0.0 all-gather.6.cloned.1.call-start
  7.9 0.7 all-gather.6.cloned.1.call-update
  8.7 7.6 %all-to-all-start = ((f32[8,2,64,512]{3,2,1,0:T(8,128)}), f32[8,2,64,512]{3,2,1,0:T(8,128)}, u32[]{:S(2)}, u32[]{:S(2)}) async-start(f32[8,2,64,512]{3,2,1,0:T(8,128)} %param.10), calls=%async_computation | async-start | bytes 4194304 | tf_op jit(solution)/shard_map/all_to_all | solution.py:71
  16.3 0.0 copy-start.10
  16.3 1.5 all_to_all.45
  17.8 2.2 scatter_custom_fusion
  20.0 1.7 reshape.46
  22.4 0.0 copy-start.13
  22.5 0.0 copy-start.8
  22.5 0.0 copy-start.11
  22.5 4.2 copy.21
  26.7 0.6 dynamic-slice
  28.0 26.9 %all_gather.15 = f32[128,32]{1,0:T(8,128)S(1)} all-gather(f32[8,32]{1,0:T(8,128)S(1)} %copy-done.8), channel_id=1, replica_groups=mesh['space'=8,'ens'=16] {'ens'}, dimensions={0}, use_global_device_ids=true | all-gather | bytes 17408 | tf_op jit(solution)/shard_map/all_gather | solution.py:85
  54.9 7.0 %all-to-all-start.2 = ((f32[8,16,4096]{2,0,1:T(8,128)}), f32[8,16,4096]{2,0,1:T(8,128)}, u32[]{:S(2)}, u32[]{:S(2)}) async-start(f32[8,16,4096]{2,0,1:T(8,128)} %copy.21), calls=%async_computation.2 | async-start | bytes 4194304 | tf_op jit(solution)/shard_map/all_to_all | solution.py:95
  61.9 3.3 exp.6
  65.2 14.7 %all-gather.4.cloned.1.call-done = f32[16,64,512]{2,1,0:T(8,128)} async-done(((f32[2,64,512]{2,1,0:T(8,128)}), f32[16,64,512]{2,1,0:T(8,128)}) %all-gather.4.cloned.1.call-update) | async-done | bytes 2097168 | tf_op jit(solution)/shard_map/all_gather | solution.py:73
  79.9 54.8 %all-gather.6.cloned.1.call-done = f32[16,64,512]{2,1,0:T(8,128)} async-done(((f32[2,64,512]{2,1,0:T(8,128)}), f32[16,64,512]{2,1,0:T(8,128)}) %all-gather.6.cloned.1.call-update) | async-done | bytes 2097168 | tf_op jit(solution)/shard_map/all_gather | solution.py:72
  134.7 65.7 %fusion.54 = (f32[16,64,512]{2,1,0:T(8,128)}, f32[16,64,512]{2,1,0:T(8,128)}, f32[16,64,512]{2,1,0:T(8,128)}, f32[16,64,512]{2,1,0:T(8,128)}, f32[16,64,512]{2,1...) fusion(f32[16,64,512]{2,1,0:T(8,128)} %all-gather.4.cloned.1.ca, ...), kind=kLoop, calls=%fused_computation.161 | loop fusion | flops 85983232 | bytes 60817408 | tf_op jit(solution)/shard_map/add | solution.py:48
  200.4 52.4 %fusion.109 = f32[16,64,512]{2,1,0:T(8,128)} fusion(f32[16,64,512]{2,1,0:T(8,128)} %get-tuple-element.2, f32[16,64,512]{2,1,0:T(8,128)} %all-gather.6.cloned.1.call-done, f32[16,64,512]{2,1,0:T(8,128)} %get-tuple-element.3, f32[16,64,512]{2,1,0:T(8,128)} %get-tuple-element.26, f32[16,64,512]{2,1,0:T(8,128)} %get-tuple-element.25, ...), kind=kLoop, calls=%fused_computation.216 | loop fusion | flops 37748736 | bytes 62914560 | tf_op jit(solution)/shard_map/add | solution.py:48
  252.8 46.8 %fusion.164 = f32[16,64,512]{2,1,0:T(8,128)S(1)} fusion(f32[16,64,512]{2,1,0:T(8,128)} %fusion.109, f32[16,64,512]{2,1,0:T(8,128)S(1)} %copy-done.3, f32[16,64,512]{2,1,0:T(8,128)S(1)} %copy-done.4, f32[16,64,512]{2,1,0:T(8,128)} %get-tuple-element.26, f32[16,64,512]{2,1,0:T(8,128)} %get-tuple-element.25, f32[16,64,512]{2,1,0:T(8,128)} %get-tuple-element.24, ...), kind=kLoop, calls=%fused_computation.271 | loop fusion | flops 37748736 | bytes 62914560 | tf_op jit(solution)/shard_map/add | solution.py:48
  299.6 0.0 copy-start.1
  299.6 0.6 copy.26
  300.2 0.8 copy-done.1
  300.9 0.7 gather_fusion
  301.6 0.2 dynamic-update-slice.3
  301.9 63.0 %all-reduce.4 = f32[4096]{0:T(1024)S(1)} all-reduce(f32[4096]{0:T(1024)S(1)} %dynamic-update-slice.3), channel_id=2, replica_groups=mesh['space'=8,'ens'=16] {'ens','space'}, use_global_device_ids=true, to_apply=%add.4 | all-reduce | flops 4096 | bytes 32768
  364.9 0.1 reshape.65
  365.0 0.0 copy-start.9
  365.0 3.6 all-to-all-start.1
  368.7 0.3 convolution_multiply_fusion.1
  368.9 0.1 copy.23
  369.0 0.1 fusion.184
  369.1 2.9 cholesky.16
  372.0 0.6 compare_reduce_fusion
  372.7 0.7 fusion.179
  373.3 2.4 custom-call.8
  375.8 0.3 fusion.170
  376.0 0.2 fusion.180
  376.2 0.3 fusion.173
  376.5 5.5 %fusion.1 = f32[16,8,4096]{2,1,0:T(8,128)} fusion(f32[128,128]{1,0:T(8,128)S(1)} %fusion.173, f32[8,16,4096]{2,0,1:T(8,128)} %all-to-all-done.2), kind=kOutput, calls=%fused_computation.108 | convolution fusion | flops 806354944 | bytes 4259840 | tf_op jit(solution)/shard_map/dot_general | solution.py:96
  382.0 14.2 %all-to-all-done.1 = f32[1,16,64,512]{3,2,0,1:T(8,128)S(1)} async-done(((f32[1,16,64,512]{3,2,0,1:T(8,128)}), f32[1,16,64,512]{3,2,0,1:T(8,128)S(1)}, u32[]{:S(2)}, u32[]{:S(2)}) %all-to-all-start.1) | async-done | bytes 2097184 | tf_op jit(solution)/shard_map/all_to_all | solution.py:82
  396.2 8.0 %all-to-all-start.3 = ((f32[16,8,4096]{2,1,0:T(8,128)}), f32[16,8,4096]{2,1,0:T(8,128)}, u32[]{:S(2)}, u32[]{:S(2)}) async-start(f32[16,8,4096]{2,1,0:T(8,128)} %fusion.1), calls=%async_computation.3 | async-start | bytes 4194304 | tf_op jit(solution)/shard_map/all_to_all | solution.py:98
  404.2 25.9 %all-to-all-done.3 = f32[16,8,4096]{2,1,0:T(8,128)} async-done(((f32[16,8,4096]{2,1,0:T(8,128)}), f32[16,8,4096]{2,1,0:T(8,128)}, u32[]{:S(2)}, u32[]{:S(2)}) %all-to-all-start.3) | async-done | bytes 2097184 | tf_op jit(solution)/shard_map/all_to_all | solution.py:98
  430.0 4.1 copy.24
  434.2 2.7 reshape.48
  436.9 1.3 copy.30
  (31 shorter events, 0.1 us)
Async XLA Ops:
  7.2 72.7 %all-gather.4.cloned.1.call-start = ((), (), s32[]{:S(2)}) async-start(), calls=%async_computation.4 | async-start | bytes 2359296 | tf_op jit(solution)/shard_map/all_gather | solution.py:73
  7.9 126.8 %all-gather.6.cloned.1.call-start = ((), (), s32[]{:S(2)}) async-start(), calls=%async_computation.5 | async-start | bytes 2359296 | tf_op jit(solution)/shard_map/all_gather | solution.py:72
  8.6 7.7 %copy-start.7 = (f32[8,2,64,512]{3,2,1,0:T(8,128)S(1)}, f32[8,2,64,512]{3,2,1,0:T(8,128)}, u32[]{:S(2)}) copy-start(f32[8,2,64,512]{3,2,1,0:T(8,128)} %param.10) | copy-start | bytes 6291460
  8.7 46.2 %all-to-all-start = ((f32[8,2,64,512]{3,2,1,0:T(8,128)}), f32[8,2,64,512]{3,2,1,0:T(8,128)}, u32[]{:S(2)}, u32[]{:S(2)}) async-start(f32[8,2,64,512]{3,2,1,0:T(8,128)} %param.10), calls=%async_computation | async-start | bytes 4194304 | tf_op jit(solution)/shard_map/all_to_all | solution.py:71
  16.3 1.5 copy-start.10
  22.4 4.3 copy-start.13
  22.5 5.5 %copy-start.8 = (f32[8,32]{1,0:T(8,128)S(1)}, f32[8,32]{1,0:T(8,128)}, u32[]{:S(2)}) copy-start(f32[8,32]{1,0:T(8,128)} %param.19) | copy-start | bytes 3076
  22.5 32.4 %copy-start.11 = (s32[32]{0:T(128)S(1)}, s32[32]{0:T(128)}, u32[]{:S(2)}) copy-start(s32[32]{0:T(128)} %param.15) | copy-start | bytes 388
  22.5 32.4 %copy-start.12 = (f32[32]{0:T(128)S(1)}, f32[32]{0:T(128)}, u32[]{:S(2)}) copy-start(f32[32]{0:T(128)} %param.17) | copy-start | bytes 388
  54.9 310.1 %all-to-all-start.2 = ((f32[8,16,4096]{2,0,1:T(8,128)}), f32[8,16,4096]{2,0,1:T(8,128)}, u32[]{:S(2)}, u32[]{:S(2)}) async-start(f32[8,16,4096]{2,0,1:T(8,128)} %copy.21), calls=%async_computation.2 | async-start | bytes 4194304 | tf_op jit(solution)/shard_map/all_to_all | solution.py:95
  200.3 52.4 %copy-start = (f32[8,2,64,512]{3,2,1,0:T(8,128)S(1)}, f32[8,2,64,512]{3,2,1,0:T(8,128)}, u32[]{:S(2)}) copy-start(f32[8,2,64,512]{3,2,1,0:T(8,128)} %exp.6) | copy-start | bytes 6291460
  200.3 52.4 %copy-start.2 = (f32[16,64,512]{2,1,0:T(8,128)S(1)}, f32[16,64,512]{2,1,0:T(8,128)}, u32[]{:S(2)}) copy-start(f32[16,64,512]{2,1,0:T(8,128)} %all-gather.4.cloned.1.call-done) | copy-start | bytes 6291460
  200.4 52.4 %copy-start.3 = (f32[16,64,512]{2,1,0:T(8,128)S(1)}, f32[16,64,512]{2,1,0:T(8,128)}, u32[]{:S(2)}) copy-start(f32[16,64,512]{2,1,0:T(8,128)} %all-gather.6.cloned.1.call-done) | copy-start | bytes 6291460
  200.4 52.4 %copy-start.4 = (f32[16,64,512]{2,1,0:T(8,128)S(1)}, f32[16,64,512]{2,1,0:T(8,128)}, u32[]{:S(2)}) copy-start(f32[16,64,512]{2,1,0:T(8,128)} %get-tuple-element.3) | copy-start | bytes 6291460
  200.4 52.4 %copy-start.5 = (f32[16,64,512]{2,1,0:T(8,128)S(1)}, f32[16,64,512]{2,1,0:T(8,128)}, u32[]{:S(2)}) copy-start(f32[16,64,512]{2,1,0:T(8,128)} %get-tuple-element.4) | copy-start | bytes 6291460
  200.4 52.4 %copy-start.6 = (f32[16,64,512]{2,1,0:T(8,128)S(1)}, f32[16,64,512]{2,1,0:T(8,128)}, u32[]{:S(2)}) copy-start(f32[16,64,512]{2,1,0:T(8,128)} %get-tuple-element.5) | copy-start | bytes 6291460
  299.6 1.3 copy-start.1
  365.0 10.8 %copy-start.9 = (f32[32]{0:T(128)S(1)}, f32[32]{0:T(128)}, u32[]{:S(2)}) copy-start(f32[32]{0:T(128)} %param.16) | copy-start | bytes 388
  365.0 31.1 %all-to-all-start.1 = ((f32[1,16,64,512]{3,2,0,1:T(8,128)}), f32[1,16,64,512]{3,2,0,1:T(8,128)S(1)}, u32[]{:S(2)}, u32[]{:S(2)}) async-start(f32[1,16,64,512]{3,2,0,1:T(8,128)} %bitcast.40), calls=%async_computation.1 | async-start | bytes 4194304 | tf_op jit(solution)/shard_map/all_to_all | solution.py:82
  396.2 33.9 %all-to-all-start.3 = ((f32[16,8,4096]{2,1,0:T(8,128)}), f32[16,8,4096]{2,1,0:T(8,128)}, u32[]{:S(2)}, u32[]{:S(2)}) async-start(f32[16,8,4096]{2,1,0:T(8,128)} %fusion.1), calls=%async_computation.3 | async-start | bytes 4194304 | tf_op jit(solution)/shard_map/all_to_all | solution.py:98
Sparse Core Ops, SparseCore 0:
  10.3 69.5 all-gather.3
  82.2 52.3 all-gather.5

commit v2 on v1

--- a/solution.py
+++ b/solution.py
@@ -25,26 +25,36 @@
     return second.T
 
 
+HALF = [(a, b, c) for a, b, c in DIRECTIONS if (a, b, c) > (0, 0, 0)]
+
+
+def shift_to(padded, a, b, c, planes, depth, across):
+    return padded[1 + a : 1 + a + planes, 1 + b : 1 + b + depth, 1 + c : 1 + c + across]
+
+
 def forward(log_row, storage, head_init, source):
     planes, depth, across = log_row.shape
     permeability = jnp.exp(log_row)
     padded = jnp.pad(permeability, 1)
     transmit = []
-    for a, b, c in DIRECTIONS:
+    for a, b, c in HALF:
         factor = 2.0 ** (1 - abs(a) - abs(b) - abs(c))
-        neighbour = shifted(padded, a, b, c, planes, depth, across)
+        neighbour = shift_to(padded, a, b, c, planes, depth, across)
         transmit.append(factor * 2.0 * permeability * neighbour / (permeability + neighbour))
-    diagonal = storage + sum(transmit)
+    total = storage
+    for i, (a, b, c) in enumerate(HALF):
+        back = shift_to(jnp.pad(transmit[i], 1), -a, -b, -c, planes, depth, across)
+        total = total + transmit[i] + back
+    diagonal = total
     forcing = storage * head_init + source
     head_field = head_init
     for sweep_index in range(SWEEPS):
         padded_head = jnp.pad(head_field, 1)
-        gathered = sum(
-            (
-                transmit[i] * shifted(padded_head, a, b, c, planes, depth, across)
-                for i, (a, b, c) in enumerate(DIRECTIONS)
-            )
-        )
+        gathered = 0.0
+        for i, (a, b, c) in enumerate(HALF):
+            ahead = transmit[i] * shift_to(padded_head, a, b, c, planes, depth, across)
+            flow = jnp.pad(transmit[i] * head_field, 1)
+            gathered = gathered + ahead + shift_to(flow, -a, -b, -c, planes, depth, across)
         head_field = (1.0 - OMEGA) * head_field + OMEGA * (forcing + gathered) / diagonal
     return head_field
 
@@ -81,8 +91,10 @@
     picked = field.reshape(-1)[obs_cells]
     head_field = lax.all_to_all(field[None], "space", 1, 0, tiled=True)
 
-    every_obs = lax.all_gather(picked[None], ("ens", "space"), axis=0, tiled=True)
-    every_perturb = lax.all_gather(perturb, "ens", axis=0, tiled=True)
+    observed = lax.all_gather(picked[None], "space", axis=0, tiled=True)
+    both = lax.all_gather(jnp.concatenate([observed, perturb], axis=1), "ens", axis=0, tiled=True)
+    obs_count = observed.shape[1]
+    every_obs, every_perturb = both[:, :obs_count], both[:, obs_count:]
     mean_obs = jnp.mean(every_obs, axis=0)
     spread = every_obs - mean_obs
     covariance = jnp.dot(spread.T, spread, precision=HIGHEST) / (total_members - 1)

time: 448 us -> 428 us (0.955)
  blocking collectives: 89.9 us -> 37.5 us
  other arithmetic: 174 us -> 203 us
    mul x0 -> x5, other arithmetic: none -> 159 us  [forward(): flow = jnp.pad(transmit[i] * head_field, 1)]
    add x3 -> x1, other arithmetic: 165 us -> 35.1 us  [forward(): (1.0 - OMEGA) * head_field + OMEGA * (forcing + gathered) / diagonal]
    unnamed x1, blocking collectives: 63 us -> 16.3 us
    all_gather x1, waiting for transfers between devices: 54.8 us -> 20.5 us  [shards(): whole_storage = lax.all_gather(storage, 'space', axis=0, tiled=True)]
    all_to_all x1, waiting for transfers between devices: 0.01 us -> 18.5 us  [shards(): whole_log = lax.all_to_all(log_perm, 'space', 0, 1, tiled=True)]
    all_gather x1, waiting for transfers between devices: 14.7 us -> 32.3 us  [shards(): whole_head = lax.all_gather(head_init, 'space', axis=0, tiled=True)]
    all_gather x1, blocking collectives: 26.9 us -> 21.2 us  [shards(): lax.all_gather(jnp.concatenate([observed, perturb], axis=1), 'ens', axis=...]
  transfers between devices with their start and end apart: 6 -> 6, of which waited for: 4 -> 5; matrix products, arithmetic and copies ran while one was open for 43% -> 52% of each run, Pallas kernels for 0% -> 0%
where the time goes in v2:
time: 428 us; the launch traced here: 425 us
  other arithmetic  203 us (47%)
  waiting for transfers between devices  114 us (27%)
  blocking collectives  37.5 us (9%)
  starting transfers between devices  26.4 us (6%)
  local copies, waits for them, and re-layouts  22.2 us (5%)
  between operations  15.6 us (4%)
  matrix products  6.5 us (2%)
    mul x5, other arithmetic, forward(): flow = jnp.pad(transmit[i] * head_field, 1)  159 us
    add x1, other arithmetic, forward(): (1.0 - OMEGA) * head_field + OMEGA * (forcing + gathered) / diagonal  35.1 us
    all_gather x1, waiting for transfers between devices, shards(): whole_head = lax.all_gather(head_init, 'space', axis=0, tiled=True)  32.3 us
    all_to_all x1, waiting for transfers between devices, shards(): lax.all_to_all(new_column, 'ens', 0, 1, tiled=True).reshape(log_perm.shape)  25.9 us
    all_gather x1, blocking collectives, shards(): lax.all_gather(jnp.concatenate([observed, perturb], axis=1), 'ens', axis=...  21.2 us
    all_gather x1, waiting for transfers between devices, shards(): whole_storage = lax.all_gather(storage, 'space', axis=0, tiled=True)  20.5 us
    all_to_all x1, waiting for transfers between devices, shards(): whole_log = lax.all_to_all(log_perm, 'space', 0, 1, tiled=True)  18.5 us
    unnamed x1, blocking collectives  16.3 us
  transfers between devices with their start and end apart: 6, of which 5 were waited for; matrix products, arithmetic and copies ran while one was open for 52% of the time, Pallas kernels for 0%

profile of v2, /device:TPU:25, one launch (start us, length us, event | category | flops | bytes accessed | tf_op | source)
XLA Modules:
  0.0 424.8 jit_solution(2437369419998581295)
XLA Ops:
  7.2 0.0 all-gather.4.cloned.1.call-start
  7.2 0.7 all-gather.4.cloned.1.call-update
  7.9 7.6 %all-to-all-start = ((f32[8,2,64,512]{3,2,1,0:T(8,128)}), f32[8,2,64,512]{3,2,1,0:T(8,128)}, u32[]{:S(2)}, u32[]{:S(2)}) async-start(f32[8,2,64,512]{3,2,1,0:T(8,128)} %param.10), calls=%async_computation | async-start | bytes 4194304 | tf_op jit(solution)/shard_map/all_to_all | solution.py:81
  15.5 0.0 all-gather.6.cloned.1.call-start
  15.6 0.7 all-gather.6.cloned.1.call-update
  16.3 1.5 all_to_all.45
  17.9 2.2 scatter_custom_fusion
  20.1 2.9 reshape.46
  23.6 0.0 copy-start.7
  23.6 0.0 copy-start.5
  23.6 2.5 copy.21
  26.2 0.6 dynamic-slice
  27.5 18.5 %all-to-all-done = f32[8,2,64,512]{3,2,1,0:T(8,128)} async-done(((f32[8,2,64,512]{3,2,1,0:T(8,128)}), f32[8,2,64,512]{3,2,1,0:T(8,128)}, u32[]{:S(2)}, u32[]{:S(2)}) %all-to-all-start) | async-done | bytes 2097184 | tf_op jit(solution)/shard_map/all_to_all | solution.py:81
  46.0 6.3 %all-to-all-start.2 = ((f32[8,16,4096]{2,0,1:T(8,128)}), f32[8,16,4096]{2,0,1:T(8,128)}, u32[]{:S(2)}, u32[]{:S(2)}) async-start(f32[8,16,4096]{2,0,1:T(8,128)} %copy.21), calls=%async_computation.2 | async-start | bytes 4194304 | tf_op jit(solution)/shard_map/all_to_all | solution.py:107
  52.3 3.3 exp.6
  55.6 32.3 %all-gather.4.cloned.1.call-done = f32[16,64,512]{2,1,0:T(8,128)} async-done(((f32[2,64,512]{2,1,0:T(8,128)}), f32[16,64,512]{2,1,0:T(8,128)}) %all-gather.4.cloned.1.call-update) | async-done | bytes 2097168 | tf_op jit(solution)/shard_map/all_gather | solution.py:83
  87.9 33.5 %fusion.179 = (f32[16,64,512]{2,1,0:T(8,128)}, f32[16,64,512]{2,1,0:T(8,128)S(1)}, f32[16,64,512]{2,1,0:T(8,128)}, f32[16,64,512]{2,1,0:T(8,128)}, f32[16,64,512...) fusion(f32[16,64,512]{2,1,0:T(8,128)} %all-gather.4.cloned.1.ca, ...), kind=kLoop, calls=%fused_computation.312 | loop fusion | flops 28311552 | bytes 58720256 | tf_op jit(solution)/shard_map/mul | solution.py:56
  121.4 20.5 %all-gather.6.cloned.1.call-done = f32[16,64,512]{2,1,0:T(8,128)} async-done(((f32[2,64,512]{2,1,0:T(8,128)}), f32[16,64,512]{2,1,0:T(8,128)}) %all-gather.6.cloned.1.call-update) | async-done | bytes 2097168 | tf_op jit(solution)/shard_map/all_gather | solution.py:82
  141.9 49.9 %fusion.175 = (f32[16,64,512]{2,1,0:T(8,128)}, f32[16,64,512]{2,1,0:T(8,128)}, f32[16,64,512]{2,1,0:T(8,128)}, f32[16,64,512]{2,1,0:T(8,128)}) fusion(f32[16,64,512]{2,1,0:T(8,128)} %get-tuple-element.53, f32[16,64,512]{2,1,0:T(8,128)} %get-tuple-element.54, f32[16,64,512]{2,1,0:T(8,128)} %get-tuple-element.55, f32[16,64,512]{2,1,0:T(8,128)} %get-tuple-element.56, ...), kind=kLoop, calls=%fused_computation.310 | loop fusion | flops 37748736 | bytes 69206016 | tf_op jit(solution)/shard_map/mul | solution.py:56
  191.8 18.3 %fusion.192 = (f32[16,64,512]{2,1,0:T(8,128)}, f32[16,64,512]{2,1,0:T(8,128)}, f32[16,64,512]{2,1,0:T(8,128)}, f32[16,64,512]{2,1,0:T(8,128)}, f32[16,64,512]{2,...) fusion(f32[16,64,512]{2,1,0:T(8,128)S(1)} %get-tuple-element.11, ...), kind=kLoop, calls=%fused_computation.325 | loop fusion | flops 6291456 | bytes 52428800 | tf_op jit(solution)/shard_map/mul | solution.py:56
  210.1 38.7 %fusion.173 = (f32[16,64,512]{2,1,0:T(8,128)}, f32[16,64,512]{2,1,0:T(8,128)}) fusion(f32[16,64,512]{2,1,0:T(8,128)} %get-tuple-element.53, f32[16,64,512]{2,1,0:T(8,128)} %get-tuple-element.7, f32[16,64,512]{2,1,0:T(8,128)} %get-tuple-element.6, f32[16,64,512]{2,1,0:T(8,128)} %get-tuple-element.81, f32[16,64,512]{2,1,0:T(8,128)} %get-tuple-element.55, ...), kind=kLoop, calls=%fused_computation.309 | loop fusion | flops 23068672 | bytes 65011712 | tf_op jit(solution)/shard_map/mul | solution.py:56
  248.8 18.5 %fusion.191 = (f32[16,64,512]{2,1,0:T(8,128)}, f32[16,64,512]{2,1,0:T(8,128)}, f32[16,64,512]{2,1,0:T(8,128)}, f32[16,64,512]{2,1,0:T(8,128)}, f32[16,64,512]{2,...) fusion(f32[16,64,512]{2,1,0:T(8,128)S(1)} %get-tuple-element.11, ...), kind=kLoop, calls=%fused_computation.324 | loop fusion | flops 6291456 | bytes 52428800 | tf_op jit(solution)/shard_map/mul | solution.py:56
  267.3 35.1 %fusion.109 = f32[16,64,512]{2,1,0:T(8,128)} fusion(f32[16,64,512]{2,1,0:T(8,128)} %get-tuple-element.7, f32[16,64,512]{2,1,0:T(8,128)} %get-tuple-element.6, f32[16,64,512]{2,1,0:T(8,128)} %get-tuple-element.69, f32[16,64,512]{2,1,0:T(8,128)} %get-tuple-element.55, f32[16,64,512]{2,1,0:T(8,128)} %get-tuple-element.3, f32[16,64,512]{2,1,0:T(8,128)} %get-tuple-element.68, ...), kind=kLoop, calls=%fused_computation.216 | loop fusion | flops 22544384 | bytes 62914560 | tf_op jit(solution)/shard_map/add | solution.py:58
  302.4 2.1 copy.26
  304.5 0.7 gather_fusion
  305.2 0.2 dynamic-update-slice.3
  305.5 16.3 %all-reduce.56 = f32[256]{0:T(256)S(1)} all-reduce(f32[256]{0:T(256)S(1)} %dynamic-update-slice.3), channel_id=2, replica_groups=mesh['space'=8,'ens'=16] {'space'}, use_global_device_ids=true, to_apply=%add.56 | all-reduce | flops 256 | bytes 2048
  321.8 0.1 reshape.65
  321.9 0.1 pad_maximum_fusion
  322.0 21.2 %all_gather.15 = f32[128,64]{1,0:T(8,128)S(1)} all-gather(f32[8,64]{1,0:T(8,128)S(1)} %pad_maximum_fusion), channel_id=1, replica_groups=mesh['space'=8,'ens'=16] {'ens'}, dimensions={0}, use_global_device_ids=true | all-gather | bytes 34816 | tf_op jit(solution)/shard_map/all_gather | solution.py:95
  343.2 3.6 all-to-all-start.1
  346.8 0.3 convolution_multiply_fusion.1
  347.1 0.1 copy.23
  347.2 0.1 fusion.172
  347.2 2.9 cholesky.16
  350.2 0.6 compare_reduce_fusion
  350.8 0.7 fusion.167
  351.5 2.4 custom-call.8
  353.9 0.3 fusion.156
  354.2 0.2 fusion.168
  354.4 0.3 fusion.158
  354.7 5.5 %fusion.1 = f32[16,8,4096]{2,1,0:T(8,128)} fusion(f32[128,128]{1,0:T(8,128)S(1)} %fusion.158, f32[8,16,4096]{2,0,1:T(8,128)} %all-to-all-done.2), kind=kOutput, calls=%fused_computation.56 | convolution fusion | flops 806354944 | bytes 4259840 | tf_op jit(solution)/shard_map/dot_general | solution.py:108
  360.2 15.0 %all-to-all-done.1 = f32[1,16,64,512]{3,2,0,1:T(8,128)S(1)} async-done(((f32[1,16,64,512]{3,2,0,1:T(8,128)}), f32[1,16,64,512]{3,2,0,1:T(8,128)S(1)}, u32[]{:S(2)}, u32[]{:S(2)}) %all-to-all-start.1) | async-done | bytes 2097184 | tf_op jit(solution)/shard_map/all_to_all | solution.py:92
  375.2 8.7 %all-to-all-start.3 = ((f32[16,8,4096]{2,1,0:T(8,128)}), f32[16,8,4096]{2,1,0:T(8,128)}, u32[]{:S(2)}, u32[]{:S(2)}) async-start(f32[16,8,4096]{2,1,0:T(8,128)} %fusion.1), calls=%async_computation.3 | async-start | bytes 4194304 | tf_op jit(solution)/shard_map/all_to_all | solution.py:110
  383.9 25.9 %all-to-all-done.3 = f32[16,8,4096]{2,1,0:T(8,128)} async-done(((f32[16,8,4096]{2,1,0:T(8,128)}), f32[16,8,4096]{2,1,0:T(8,128)}, u32[]{:S(2)}, u32[]{:S(2)}) %all-to-all-start.3) | async-done | bytes 2097184 | tf_op jit(solution)/shard_map/all_to_all | solution.py:110
  409.8 4.1 copy.24
  413.9 2.7 reshape.48
  416.6 1.3 copy.30
  (23 shorter events, 0.1 us)
Async XLA Ops:
  7.2 80.7 %all-gather.4.cloned.1.call-start = ((), (), s32[]{:S(2)}) async-start(), calls=%async_computation.4 | async-start | bytes 2359296 | tf_op jit(solution)/shard_map/all_gather | solution.py:83
  7.9 8.4 %copy-start = (f32[8,2,64,512]{3,2,1,0:T(8,128)S(1)}, f32[8,2,64,512]{3,2,1,0:T(8,128)}, u32[]{:S(2)}) copy-start(f32[8,2,64,512]{3,2,1,0:T(8,128)} %param.10) | copy-start | bytes 6291460
  7.9 38.1 %all-to-all-start = ((f32[8,2,64,512]{3,2,1,0:T(8,128)}), f32[8,2,64,512]{3,2,1,0:T(8,128)}, u32[]{:S(2)}, u32[]{:S(2)}) async-start(f32[8,2,64,512]{3,2,1,0:T(8,128)} %param.10), calls=%async_computation | async-start | bytes 4194304 | tf_op jit(solution)/shard_map/all_to_all | solution.py:81
  15.5 126.4 %all-gather.6.cloned.1.call-start = ((), (), s32[]{:S(2)}) async-start(), calls=%async_computation.5 | async-start | bytes 2359296 | tf_op jit(solution)/shard_map/all_gather | solution.py:82
  16.3 1.5 copy-start.4
  20.1 3.5 copy-start.1
  23.6 2.6 copy-start.7
  23.6 3.8 copy-start.5
  23.6 3.8 copy-start.6
  46.0 297.2 %all-to-all-start.2 = ((f32[8,16,4096]{2,0,1:T(8,128)}), f32[8,16,4096]{2,0,1:T(8,128)}, u32[]{:S(2)}, u32[]{:S(2)}) async-start(f32[8,16,4096]{2,0,1:T(8,128)} %copy.21), calls=%async_computation.2 | async-start | bytes 4194304 | tf_op jit(solution)/shard_map/all_to_all | solution.py:107
  302.4 19.5 %copy-start.2 = (f32[8,32]{1,0:T(8,128)S(1)}, f32[8,32]{1,0:T(8,128)}, u32[]{:S(2)}) copy-start(f32[8,32]{1,0:T(8,128)} %param.19) | copy-start | bytes 3076
  343.2 10.8 %copy-start.3 = (f32[32]{0:T(128)S(1)}, f32[32]{0:T(128)}, u32[]{:S(2)}) copy-start(f32[32]{0:T(128)} %param.16) | copy-start | bytes 388
  343.2 32.0 %all-to-all-start.1 = ((f32[1,16,64,512]{3,2,0,1:T(8,128)}), f32[1,16,64,512]{3,2,0,1:T(8,128)S(1)}, u32[]{:S(2)}, u32[]{:S(2)}) async-start(f32[1,16,64,512]{3,2,0,1:T(8,128)} %bitcast.2), calls=%async_computation.1 | async-start | bytes 4194304 | tf_op jit(solution)/shard_map/all_to_all | solution.py:92
  375.2 34.6 %all-to-all-start.3 = ((f32[16,8,4096]{2,1,0:T(8,128)}), f32[16,8,4096]{2,1,0:T(8,128)}, u32[]{:S(2)}, u32[]{:S(2)}) async-start(f32[16,8,4096]{2,1,0:T(8,128)} %fusion.1), calls=%async_computation.3 | async-start | bytes 4194304 | tf_op jit(solution)/shard_map/all_to_all | solution.py:110
Sparse Core Ops, SparseCore 0:
  10.3 77.4 all-gather.3
  90.2 51.6 all-gather.5

commit v3 on v2

--- a/solution.py
+++ b/solution.py
@@ -1,4 +1,6 @@
 import jax
+from jax.experimental import pallas as pl
+from jax.experimental.pallas import tpu as pltpu
 import jax.numpy as jnp
 from jax import lax
 from jax.sharding import PartitionSpec as P
@@ -28,35 +30,99 @@
 HALF = [(a, b, c) for a, b, c in DIRECTIONS if (a, b, c) > (0, 0, 0)]
 
 
-def shift_to(padded, a, b, c, planes, depth, across):
-    return padded[1 + a : 1 + a + planes, 1 + b : 1 + b + depth, 1 + c : 1 + c + across]
+def shift_plane(x, b, c):
+    depth, across = x.shape
+    valid = None
+    if b != 0:
+        x = pltpu.roll(x, (-b) % depth, 0)
+        rows = lax.broadcasted_iota(jnp.int32, x.shape, 0) + b
+        valid = (rows >= 0) & (rows < depth)
+    if c != 0:
+        x = pltpu.roll(x, (-c) % across, 1)
+        cols = lax.broadcasted_iota(jnp.int32, x.shape, 1) + c
+        ok = (cols >= 0) & (cols < across)
+        valid = ok if valid is None else valid & ok
+    if valid is None:
+        return x
+    return jnp.where(valid, x, 0.0)
 
 
-def forward(log_row, storage, head_init, source):
+def forward_kernel(log_ref, sto_ref, init_ref, forc_ref, out_ref, perm, trans, diag, head_a, head_b):
+    planes, depth, across = log_ref.shape
+    zero = jnp.zeros((depth, across), jnp.float32)
+    for buf in (perm, head_a, head_b):
+        buf[0] = zero
+        buf[planes + 1] = zero
+
+    def fill(p, carry):
+        perm[p + 1] = jnp.exp(log_ref[p])
+        head_a[p + 1] = init_ref[p]
+        return carry
+
+    lax.fori_loop(0, planes, fill, 0)
+
+    def transmissibility(p, carry):
+        own = perm[p + 1]
+        for k, (a, b, c) in enumerate(HALF):
+            factor = 2.0 ** (1 - abs(a) - abs(b) - abs(c))
+            other = shift_plane(perm[p + 1 + a], b, c)
+            trans[k, p] = factor * 2.0 * own * other / (own + other)
+        return carry
+
+    lax.fori_loop(0, planes, transmissibility, 0)
+
+    def diagonal(p, carry):
+        total = sto_ref[p]
+        for k, (a, b, c) in enumerate(HALF):
+            back = p - a
+            inside = (back >= 0) & (back < planes)
+            behind = shift_plane(trans[k, jnp.clip(back, 0, planes - 1)], -b, -c)
+            total = total + trans[k, p] + jnp.where(inside, behind, 0.0)
+        diag[p] = total
+        return carry
+
+    lax.fori_loop(0, planes, diagonal, 0)
+
+    def sweep(source, target, padded_target):
+        def body(p, carry):
+            gathered = None
+            for k, (a, b, c) in enumerate(HALF):
+                ahead = trans[k, p] * shift_plane(source[p + 1 + a], b, c)
+                back = jnp.clip(p - a, 0, planes - 1)
+                flow = shift_plane(trans[k, back] * source[p + 1 - a], -b, -c)
+                term = ahead + flow
+                gathered = term if gathered is None else gathered + term
+            value = (1.0 - OMEGA) * source[p + 1] + OMEGA * (forc_ref[p] + gathered) / diag[p]
+            if padded_target:
+                target[p + 1] = value
+            else:
+                target[p] = value
+            return carry
+
+        lax.fori_loop(0, planes, body, 0)
+
+    sweep(head_a, head_b, True)
+    sweep(head_b, head_a, True)
+    sweep(head_a, out_ref, False)
+
+
+def forward_pallas(log_row, storage, head_init, forcing):
     planes, depth, across = log_row.shape
-    permeability = jnp.exp(log_row)
-    padded = jnp.pad(permeability, 1)
-    transmit = []
-    for a, b, c in HALF:
-        factor = 2.0 ** (1 - abs(a) - abs(b) - abs(c))
-        neighbour = shift_to(padded, a, b, c, planes, depth, across)
-        transmit.append(factor * 2.0 * permeability * neighbour / (permeability + neighbour))
-    total = storage
-    for i, (a, b, c) in enumerate(HALF):
-        back = shift_to(jnp.pad(transmit[i], 1), -a, -b, -c, planes, depth, across)
-        total = total + transmit[i] + back
-    diagonal = total
-    forcing = storage * head_init + source
-    head_field = head_init
-    for sweep_index in range(SWEEPS):
-        padded_head = jnp.pad(head_field, 1)
-        gathered = 0.0
-        for i, (a, b, c) in enumerate(HALF):
-            ahead = transmit[i] * shift_to(padded_head, a, b, c, planes, depth, across)
-            flow = jnp.pad(transmit[i] * head_field, 1)
-            gathered = gathered + ahead + shift_to(flow, -a, -b, -c, planes, depth, across)
-        head_field = (1.0 - OMEGA) * head_field + OMEGA * (forcing + gathered) / diagonal
-    return head_field
+    vmem = pl.BlockSpec(memory_space=pltpu.VMEM)
+    return pl.pallas_call(
+        forward_kernel,
+        out_shape=jax.ShapeDtypeStruct((planes, depth, across), jnp.float32),
+        in_specs=[vmem] * 4,
+        out_specs=vmem,
+        scratch_shapes=[
+            pltpu.VMEM((planes + 2, depth, across), jnp.float32),
+            pltpu.VMEM((len(HALF), planes, depth, across), jnp.float32),
+            pltpu.VMEM((planes, depth, across), jnp.float32),
+            pltpu.VMEM((planes + 2, depth, across), jnp.float32),
+            pltpu.VMEM((planes + 2, depth, across), jnp.float32),
+        ],
+        compiler_params=pltpu.CompilerParams(vmem_limit_bytes=66 * 1024 * 1024),
+    )(log_row, storage, head_init, forcing)
 
 
 def shards(
@@ -87,7 +153,8 @@
         .add(well_rates)
         .reshape(grid_planes, depth, across)
     )
-    field = forward(whole_log[0], whole_storage, whole_head, source)
+    forcing = whole_storage * whole_head + source
+    field = forward_pallas(whole_log[0], whole_storage, whole_head, forcing)
     picked = field.reshape(-1)[obs_cells]
     head_field = lax.all_to_all(field[None], "space", 1, 0, tiled=True)
 

time: 428 us -> 332 us (0.78)
  other arithmetic: 203 us -> 14.3 us
  Pallas kernels: 0 us -> 58.8 us
  waiting for transfers between devices: 114 us -> 149 us
    mul x5 -> x0, other arithmetic: 159 us -> none  [forward(): flow = jnp.pad(transmit[i] * head_field, 1)]
    pallas_call x0 -> x1, Pallas kernels: none -> 58.8 us  [forward_pallas(): pl.pallas_call(forward_kernel, out_shape=jax.ShapeDtypeStruct((planes, de...]
    add x1, other arithmetic: 35.1 us -> 5.02 us  [shards(): forcing = whole_storage * whole_head + source]
    all_gather x1, waiting for transfers between devices: 32.3 us -> 54 us  [shards(): whole_head = lax.all_gather(head_init, 'space', axis=0, tiled=True)]
    all_gather x1, waiting for transfers between devices: 20.5 us -> 29.8 us  [shards(): whole_storage = lax.all_gather(storage, 'space', axis=0, tiled=True)]
    all_to_all x1, waiting for transfers between devices: 18.5 us -> 23.5 us  [shards(): whole_log = lax.all_to_all(log_perm, 'space', 0, 1, tiled=True)]
  transfers between devices with their start and end apart: 6 -> 6, of which waited for: 5 -> 5; matrix products, arithmetic and copies ran while one was open for 52% -> 9% of each run, Pallas kernels for 0% -> 18%
where the time goes in v3:
time: 332 us; the launch traced here: 329 us
  waiting for transfers between devices  149 us (45%)
  Pallas kernels  58.8 us (18%)
  blocking collectives  37.5 us (11%)
  starting transfers between devices  26.2 us (8%)
  local copies, waits for them, and re-layouts  20.5 us (6%)
  between operations  15.4 us (5%)
  other arithmetic  14.3 us (4%)
  matrix products  6.5 us (2%)
    pallas_call x1, Pallas kernels, forward_pallas(): pl.pallas_call(forward_kernel, out_shape=jax.ShapeDtypeStruct((planes, de...  58.8 us
    all_gather x1, waiting for transfers between devices, shards(): whole_head = lax.all_gather(head_init, 'space', axis=0, tiled=True)  54 us
    all_gather x1, waiting for transfers between devices, shards(): whole_storage = lax.all_gather(storage, 'space', axis=0, tiled=True)  29.8 us
    all_to_all x1, waiting for transfers between devices, shards(): lax.all_to_all(new_column, 'ens', 0, 1, tiled=True).reshape(log_perm.shape)  25.9 us
    all_to_all x1, waiting for transfers between devices, shards(): whole_log = lax.all_to_all(log_perm, 'space', 0, 1, tiled=True)  23.5 us
    all_gather x1, blocking collectives, shards(): lax.all_gather(jnp.concatenate([observed, perturb], axis=1), 'ens', axis=...  21.2 us
    unnamed x1, blocking collectives  16.3 us
    all_to_all x1, waiting for transfers between devices, shards(): head_field = lax.all_to_all(field[None], 'space', 1, 0, tiled=True)  15 us
  transfers between devices with their start and end apart: 6, of which 5 were waited for; matrix products, arithmetic and copies ran while one was open for 9% of the time, Pallas kernels for 18%

profile of v3, /device:TPU:25, one launch (start us, length us, event | category | flops | bytes accessed | tf_op | source)
XLA Modules:
  0.0 328.8 jit_solution(14675795948080348748)
XLA Ops:
  7.2 0.0 all-gather.4.cloned.1.call-start
  7.2 0.7 all-gather.4.cloned.1.call-update
  7.9 0.0 all-gather.6.cloned.1.call-start
  7.9 0.7 all-gather.6.cloned.1.call-update
  8.6 7.5 %all-to-all-start = ((f32[8,2,64,512]{3,2,1,0:T(8,128)}), f32[8,2,64,512]{3,2,1,0:T(8,128)S(1)}, u32[]{:S(2)}, u32[]{:S(2)}) async-start(f32[8,2,64,512]{3,2,1,0:T(8,128)} %param.10), calls=%async_computation | async-start | bytes 4194304 | tf_op jit(solution)/shard_map/all_to_all | solution.py:147
  16.2 2.8 all_to_all.45
  18.9 4.1 %copy.21 = f32[8,16,4096]{2,0,1:T(8,128)} copy(f32[8,16,4096]{2,1,0:T(8,128)} %all_to_all.45) | data formatting | bytes 4194304 | tf_op jit(solution)/shard_map/all_to_all | solution.py:174
  23.0 23.5 %all-to-all-done = f32[8,2,64,512]{3,2,1,0:T(8,128)S(1)} async-done(((f32[8,2,64,512]{3,2,1,0:T(8,128)}), f32[8,2,64,512]{3,2,1,0:T(8,128)S(1)}, u32[]{:S(2)}, u32[]{:S(2)}) %all-to-all-start) | async-done | bytes 2097184 | tf_op jit(solution)/shard_map/all_to_all | solution.py:147
  46.5 6.3 %all-to-all-start.2 = ((f32[8,16,4096]{2,0,1:T(8,128)}), f32[8,16,4096]{2,0,1:T(8,128)}, u32[]{:S(2)}, u32[]{:S(2)}) async-start(f32[8,16,4096]{2,0,1:T(8,128)} %copy.21), calls=%async_computation.2 | async-start | bytes 4194304 | tf_op jit(solution)/shard_map/all_to_all | solution.py:174
  52.8 1.3 scatter_custom_fusion
  54.1 0.0 copy-start.7
  54.2 0.0 copy-start.5
  54.2 0.0 copy-start.6
  54.2 1.5 reshape.45
  56.3 0.6 dynamic-slice
  57.5 0.6 pad_clamp_fusion
  58.1 0.5 broadcast_divide_fusion
  58.6 29.8 %all-gather.4.cloned.1.call-done.sto_ref = f32[16,64,512]{2,1,0:T(8,128)} async-done(((f32[2,64,512]{2,1,0:T(8,128)}), f32[16,64,512]{2,1,0:T(8,128)}) %all-gather.4.cloned.1.call-update) | async-done | bytes 2097168 | tf_op jit(solution)/shard_map/all_gather | solution.py:148
  88.4 54.0 %all-gather.6.cloned.1.call-done.init_ref = f32[16,64,512]{2,1,0:T(8,128)} async-done(((f32[2,64,512]{2,1,0:T(8,128)}), f32[16,64,512]{2,1,0:T(8,128)}) %all-gather.6.cloned.1.call-update) | async-done | bytes 2097168 | tf_op jit(solution)/shard_map/all_gather | solution.py:149
  142.4 5.0 %multiply_add_fusion.forc_ref = f32[16,64,512]{2,1,0:T(8,128)} fusion(f32[16,64,512]{2,1,0:T(8,128)} %reshape.45, f32[16,64,512]{2,1,0:T(8,128)} %all-gather.4.cloned.1.call-done.sto_ref, f32[16,64,512]{2,1,0:T(8,128)} %all-gather.6.cloned.1.call-done.init_ref), kind=kLoop, calls=%fused_computation.6 | loop fusion | flops 1048576 | bytes 8388608 | tf_op jit(solution)/shard_map/add | solution.py:156
  147.4 58.8 %shard_map.113 = f32[16,64,512]{2,1,0:T(8,128)} custom-call(f32[16,64,512]{2,1,0:T(8,128)} %bitcast.36, f32[16,64,512]{2,1,0:T(8,128)} %all-gather.4.cloned.1.call-done.sto_ref, f32[16,64,512]{2,1,0:T(8,128)} %all-gather.6.cloned.1.call-done.init_ref, f32[16,64,512]{2,1,0:T(8,128)} %multiply_add_fusion.forc_ref), custom_call_target="tpu_custom_call" | custom-call | tf_op jit(solution)/shard_map/pallas_call | solution.py:112
  206.2 2.1 copy.26
  208.4 0.8 gather_fusion
  209.2 0.2 dynamic-update-slice.3
  209.5 16.3 %all-reduce = f32[256]{0:T(256)S(1)} all-reduce(f32[256]{0:T(256)S(1)} %dynamic-update-slice.3), channel_id=2, replica_groups=mesh['space'=8,'ens'=16] {'space'}, use_global_device_ids=true, to_apply=%add | all-reduce | flops 256 | bytes 2048
  225.8 0.1 reshape.64
  225.9 0.1 pad_maximum_fusion
  225.9 21.2 %all_gather.15 = f32[128,64]{1,0:T(8,128)S(1)} all-gather(f32[8,64]{1,0:T(8,128)S(1)} %pad_maximum_fusion), channel_id=1, replica_groups=mesh['space'=8,'ens'=16] {'ens'}, dimensions={0}, use_global_device_ids=true | all-gather | bytes 34816 | tf_op jit(solution)/shard_map/all_gather | solution.py:162
  247.2 0.0 all-to-all-done.2
  247.2 0.0 copy-start.3
  247.2 3.6 %all-to-all-start.1 = ((f32[1,16,64,512]{3,2,0,1:T(8,128)}), f32[1,16,64,512]{3,2,0,1:T(8,128)S(1)}, u32[]{:S(2)}, u32[]{:S(2)}) async-start(f32[1,16,64,512]{3,2,0,1:T(8,128)} %bitcast.2), calls=%async_computation.1 | async-start | bytes 4194304 | tf_op jit(solution)/shard_map/all_to_all | solution.py:159
  250.8 0.3 convolution_multiply_fusion.1
  251.1 0.1 copy.23
  251.2 0.1 fusion.22
  251.2 2.9 cholesky.16
  254.2 0.6 compare_reduce_fusion
  254.8 0.7 fusion.17
  255.5 2.4 custom-call.8
  257.9 0.3 fusion.6
  258.2 0.2 fusion.18
  258.4 0.3 fusion.8
  258.7 5.5 %fusion.1 = f32[16,8,4096]{2,1,0:T(8,128)} fusion(f32[128,128]{1,0:T(8,128)S(1)} %fusion.8, f32[8,16,4096]{2,0,1:T(8,128)} %all-to-all-done.2), kind=kOutput, calls=%fused_computation.4 | convolution fusion | flops 806354944 | bytes 4259840 | tf_op jit(solution)/shard_map/dot_general | solution.py:175
  264.2 15.0 %all-to-all-done.1 = f32[1,16,64,512]{3,2,0,1:T(8,128)S(1)} async-done(((f32[1,16,64,512]{3,2,0,1:T(8,128)}), f32[1,16,64,512]{3,2,0,1:T(8,128)S(1)}, u32[]{:S(2)}, u32[]{:S(2)}) %all-to-all-start.1) | async-done | bytes 2097184 | tf_op jit(solution)/shard_map/all_to_all | solution.py:159
  279.2 8.7 %all-to-all-start.3 = ((f32[16,8,4096]{2,1,0:T(8,128)}), f32[16,8,4096]{2,1,0:T(8,128)}, u32[]{:S(2)}, u32[]{:S(2)}) async-start(f32[16,8,4096]{2,1,0:T(8,128)} %fusion.1), calls=%async_computation.3 | async-start | bytes 4194304 | tf_op jit(solution)/shard_map/all_to_all | solution.py:177
  287.9 25.9 %all-to-all-done.3 = f32[16,8,4096]{2,1,0:T(8,128)} async-done(((f32[16,8,4096]{2,1,0:T(8,128)}), f32[16,8,4096]{2,1,0:T(8,128)}, u32[]{:S(2)}, u32[]{:S(2)}) %all-to-all-start.3) | async-done | bytes 2097184 | tf_op jit(solution)/shard_map/all_to_all | solution.py:177
  313.8 4.1 %copy.24 = f32[8,16,4096]{2,1,0:T(8,128)} copy(f32[8,16,4096]{2,0,1:T(8,128)} %bitcast.13) | data formatting | bytes 4194304 | tf_op jit(solution)/shard_map/all_to_all | solution.py:177
  317.9 2.7 reshape.47
  320.6 1.3 copy.30
  (18 shorter events, 0.1 us)
Async XLA Ops:
  7.2 81.2 %all-gather.4.cloned.1.call-start = ((), (), s32[]{:S(2)}) async-start(), calls=%async_computation.4 | async-start | bytes 2359296 | tf_op jit(solution)/shard_map/all_gather | solution.py:148
  7.9 134.5 %all-gather.6.cloned.1.call-start = ((), (), s32[]{:S(2)}) async-start(), calls=%async_computation.5 | async-start | bytes 2359296 | tf_op jit(solution)/shard_map/all_gather | solution.py:149
  8.6 37.8 %all-to-all-start = ((f32[8,2,64,512]{3,2,1,0:T(8,128)}), f32[8,2,64,512]{3,2,1,0:T(8,128)S(1)}, u32[]{:S(2)}, u32[]{:S(2)}) async-start(f32[8,2,64,512]{3,2,1,0:T(8,128)} %param.10), calls=%async_computation | async-start | bytes 4194304 | tf_op jit(solution)/shard_map/all_to_all | solution.py:147
  23.0 29.8 %copy-start.4 = (s32[16]{0:T(128)S(1)}, s32[16]{0:T(128)}, u32[]{:S(2)}) copy-start(s32[16]{0:T(128)} %param.13) | copy-start | bytes 196
  46.5 6.3 %copy-start = (f32[8,2,64,512]{3,2,1,0:T(8,128)}, f32[8,2,64,512]{3,2,1,0:T(8,128)S(1)}, u32[]{:S(2)}) copy-start(f32[8,2,64,512]{3,2,1,0:T(8,128)S(1)} %all-to-all-done) | copy-start | bytes 6291460
  46.5 200.7 %all-to-all-start.2 = ((f32[8,16,4096]{2,0,1:T(8,128)}), f32[8,16,4096]{2,0,1:T(8,128)}, u32[]{:S(2)}, u32[]{:S(2)}) async-start(f32[8,16,4096]{2,0,1:T(8,128)} %copy.21), calls=%async_computation.2 | async-start | bytes 4194304 | tf_op jit(solution)/shard_map/all_to_all | solution.py:174
  54.1 2.2 copy-start.7
  54.2 3.3 %copy-start.5 = (s32[32]{0:T(128)S(1)}, s32[32]{0:T(128)}, u32[]{:S(2)}) copy-start(s32[32]{0:T(128)} %param.15) | copy-start | bytes 388
  54.2 3.9 %copy-start.6 = (f32[32]{0:T(128)S(1)}, f32[32]{0:T(128)}, u32[]{:S(2)}) copy-start(f32[32]{0:T(128)} %param.17) | copy-start | bytes 388
  206.2 19.6 %copy-start.1 = (f32[8,32]{1,0:T(8,128)S(1)}, f32[8,32]{1,0:T(8,128)}, u32[]{:S(2)}) copy-start(f32[8,32]{1,0:T(8,128)} %param.19) | copy-start | bytes 3076
  247.2 4.0 %copy-start.2 = (f32[32]{0:T(128)S(1)}, f32[32]{0:T(128)}, u32[]{:S(2)}) copy-start(f32[32]{0:T(128)} %broadcast_divide_fusion) | copy-start | bytes 388
  247.2 10.8 %copy-start.3 = (f32[32]{0:T(128)S(1)}, f32[32]{0:T(128)}, u32[]{:S(2)}) copy-start(f32[32]{0:T(128)} %param.16) | copy-start | bytes 388
  247.2 32.0 %all-to-all-start.1 = ((f32[1,16,64,512]{3,2,0,1:T(8,128)}), f32[1,16,64,512]{3,2,0,1:T(8,128)S(1)}, u32[]{:S(2)}, u32[]{:S(2)}) async-start(f32[1,16,64,512]{3,2,0,1:T(8,128)} %bitcast.2), calls=%async_computation.1 | async-start | bytes 4194304 | tf_op jit(solution)/shard_map/all_to_all | solution.py:159
  279.2 34.6 %all-to-all-start.3 = ((f32[16,8,4096]{2,1,0:T(8,128)}), f32[16,8,4096]{2,1,0:T(8,128)}, u32[]{:S(2)}, u32[]{:S(2)}) async-start(f32[16,8,4096]{2,1,0:T(8,128)} %fusion.1), calls=%async_computation.3 | async-start | bytes 4194304 | tf_op jit(solution)/shard_map/all_to_all | solution.py:177
Sparse Core Ops, SparseCore 0:
  10.3 77.9 all-gather.3
  90.7 51.6 all-gather.5

commit v4 on v3

--- a/solution.py
+++ b/solution.py
@@ -145,8 +145,12 @@
     grid_planes = planes * n_space
 
     whole_log = lax.all_to_all(log_perm, "space", 0, 1, tiled=True)
-    whole_storage = lax.all_gather(storage, "space", axis=0, tiled=True)
-    whole_head = lax.all_gather(head_init, "space", axis=0, tiled=True)
+    core = lax.axis_index("ens") % 2
+    mine = lax.all_gather(jnp.where(core == 0, storage, head_init), "space", axis=0, tiled=True)
+    pairs = [(e, e ^ 1) for e in range(n_ens)]
+    other = lax.ppermute(mine, "ens", pairs)
+    whole_storage = jnp.where(core == 0, mine, other)
+    whole_head = jnp.where(core == 0, other, mine)
     source = (
         jnp.zeros((grid_planes * depth * across,), jnp.float32)
         .at[well_cells]

time: 332 us -> 287 us (0.86)
  waiting for transfers between devices: 149 us -> 101 us
    all_to_all x1, waiting for transfers between devices: 23.5 us -> 0.01 us  [shards(): whole_log = lax.all_to_all(log_perm, 'space', 0, 1, tiled=True)]
    all_gather x2 -> x1, waiting for transfers between devices: 83.8 us -> 60.4 us  [shards(): lax.all_gather(jnp.where(core == 0, storage, head_init), 'space', axis=0,...]
  transfers between devices with their start and end apart: 6 -> 6, of which waited for: 5 -> 3; matrix products, arithmetic and copies ran while one was open for 9% -> 11% of each run, Pallas kernels for 18% -> 21%
where the time goes in v4:
time: 287 us; the launch traced here: 284 us
  waiting for transfers between devices  101 us (35%)
  Pallas kernels  58.8 us (20%)
  blocking collectives  37.7 us (13%)
  starting transfers between devices  25.9 us (9%)
  local copies, waits for them, and re-layouts  20.8 us (7%)
  other arithmetic  17.6 us (6%)
  between operations  15.5 us (5%)
  matrix products  6.5 us (2%)
    all_gather x1, waiting for transfers between devices, shards(): lax.all_gather(jnp.where(core == 0, storage, head_init), 'space', axis=0,...  60.4 us
    pallas_call x1, Pallas kernels, forward_pallas(): pl.pallas_call(forward_kernel, out_shape=jax.ShapeDtypeStruct((planes, de...  58.8 us
    all_to_all x1, waiting for transfers between devices, shards(): lax.all_to_all(new_column, 'ens', 0, 1, tiled=True).reshape(log_perm.shape)  25.9 us
    all_gather x1, blocking collectives, shards(): lax.all_gather(jnp.concatenate([observed, perturb], axis=1), 'ens', axis=...  19.8 us
    unnamed x1, blocking collectives  17.9 us
    all_to_all x1, waiting for transfers between devices, shards(): head_field = lax.all_to_all(field[None], 'space', 1, 0, tiled=True)  14.8 us
    all_to_all x1, starting transfers between devices, shards(): lax.all_to_all(new_column, 'ens', 0, 1, tiled=True).reshape(log_perm.shape)  8.74 us
    all_to_all x1, starting transfers between devices, shards(): whole_log = lax.all_to_all(log_perm, 'space', 0, 1, tiled=True)  7.51 us
  transfers between devices with their start and end apart: 6, of which 3 were waited for; matrix products, arithmetic and copies ran while one was open for 11% of the time, Pallas kernels for 21%

profile of v4, /device:TPU:25, one launch (start us, length us, event | category | flops | bytes accessed | tf_op | source)
XLA Modules:
  0.0 283.7 jit_solution(9683882408878268860)
XLA Ops:
  7.2 0.0 all-gather.3.cloned.1.call-start
  7.2 1.7 broadcast_select_fusion.2
  8.9 0.0 all-gather.3.cloned.1.call-update
  8.9 7.5 %all-to-all-start = ((f32[8,2,64,512]{3,2,1,0:T(8,128)}), f32[8,2,64,512]{3,2,1,0:T(8,128)S(1)}, u32[]{:S(2)}, u32[]{:S(2)}) async-start(f32[8,2,64,512]{3,2,1,0:T(8,128)} %param.10), calls=%async_computation | async-start | bytes 4194304 | tf_op jit(solution)/shard_map/all_to_all | solution.py:147
  16.5 60.4 %all-gather.3.cloned.1.call-done = f32[16,64,512]{2,1,0:T(8,128)} async-done(((f32[2,64,512]{2,1,0:T(8,128)}), f32[16,64,512]{2,1,0:T(8,128)}) %all-gather.3.cloned.1.call-update) | async-done | bytes 2097168 | tf_op jit(solution)/shard_map/all_gather | solution.py:149
  76.9 1.1 collective-permute-start
  78.0 2.7 all_to_all.45
  80.7 4.1 %copy.21 = f32[8,16,4096]{2,0,1:T(8,128)} copy(f32[8,16,4096]{2,1,0:T(8,128)} %all_to_all.45) | data formatting | bytes 4194304 | tf_op jit(solution)/shard_map/all_to_all | solution.py:178
  84.8 0.0 all-to-all-done
  84.8 4.7 %all-to-all-start.2 = ((f32[8,16,4096]{2,0,1:T(8,128)}), f32[8,16,4096]{2,0,1:T(8,128)}, u32[]{:S(2)}, u32[]{:S(2)}) async-start(f32[8,16,4096]{2,0,1:T(8,128)} %copy.21), calls=%async_computation.2 | async-start | bytes 4194304 | tf_op jit(solution)/shard_map/all_to_all | solution.py:178
  89.5 0.0 copy-done
  89.5 2.2 scatter_custom_fusion
  91.8 1.8 reshape.45
  94.2 0.6 dynamic-slice
  95.5 0.6 pad_clamp_fusion
  96.1 0.0 copy-done.6
  96.1 0.5 broadcast_divide_fusion
  96.6 0.0 collective-permute-done
  96.6 5.7 %multiply_add_fusion = (f32[16,64,512]{2,1,0:T(8,128)}, f32[16,64,512]{2,1,0:T(8,128)}, f32[16,64,512]{2,1,0:T(8,128)}) fusion(f32[16,64,512]{2,1,0:T(8,128)S(1)} %reshape.45, f32[16,64,512]{2,1,0:T(8,128)} %collective-permute-done, f32[16,64,512]{2,1,0:T(8,128)} %all-gather.3.cloned.1.call-done, pred[]{:T(512)S(6)} %eq.12), kind=kLoop, calls=%fused_computation.6 | loop fusion | flops 2097152 | bytes 12582913 | tf_op jit(solution)/shard_map/add | solution.py:160
  102.3 58.8 %shard_map.113 = f32[16,64,512]{2,1,0:T(8,128)} custom-call(f32[16,64,512]{2,1,0:T(8,128)} %bitcast.36, f32[16,64,512]{2,1,0:T(8,128)} %get-tuple-element.4.sto_ref, f32[16,64,512]{2,1,0:T(8,128)} %get-tuple-element.3.init_ref, f32[16,64,512]{2,1,0:T(8,128)} %get-tuple-element.2.forc_ref), custom_call_target="tpu_custom_call" | custom-call | tf_op jit(solution)/shard_map/pallas_call | solution.py:112
  161.0 2.1 copy.26
  163.2 0.8 gather_fusion
  164.0 0.2 dynamic-update-slice.3
  164.2 17.9 %all-reduce = f32[256]{0:T(256)S(1)} all-reduce(f32[256]{0:T(256)S(1)} %dynamic-update-slice.3), channel_id=2, replica_groups=mesh['space'=8,'ens'=16] {'space'}, use_global_device_ids=true, to_apply=%add | all-reduce | flops 256 | bytes 2048
  182.1 0.1 reshape.64
  182.2 0.1 pad_maximum_fusion
  182.3 19.8 %all_gather.11 = f32[128,64]{1,0:T(8,128)S(1)} all-gather(f32[8,64]{1,0:T(8,128)S(1)} %pad_maximum_fusion), channel_id=1, replica_groups=mesh['space'=8,'ens'=16] {'ens'}, dimensions={0}, use_global_device_ids=true | all-gather | bytes 34816 | tf_op jit(solution)/shard_map/all_gather | solution.py:166
  202.1 0.0 all-to-all-done.2
  202.1 0.0 copy-start.3
  202.1 3.8 %all-to-all-start.1 = ((f32[1,16,64,512]{3,2,0,1:T(8,128)}), f32[1,16,64,512]{3,2,0,1:T(8,128)S(1)}, u32[]{:S(2)}, u32[]{:S(2)}) async-start(f32[1,16,64,512]{3,2,0,1:T(8,128)} %bitcast.2), calls=%async_computation.1 | async-start | bytes 4194304 | tf_op jit(solution)/shard_map/all_to_all | solution.py:163
  205.9 0.3 convolution_multiply_fusion.1
  206.2 0.1 copy.23
  206.3 0.0 copy-done.2
  206.3 0.1 fusion.22
  206.4 2.9 %cholesky.16 = f32[32,32]{1,0:T(8,128)S(1)} custom-call(f32[32,32]{1,0:T(8,128)S(1)} %fusion.22), custom_call_target="Cholesky" | custom-call | tf_op jit(solution)/shard_map/jit(cholesky)/cholesky | solution.py:173
  209.3 0.6 compare_reduce_fusion
  210.0 0.7 fusion.17
  210.6 2.4 custom-call.8
  213.1 0.3 fusion.6
  213.3 0.2 fusion.18
  213.5 0.3 fusion.8
  213.8 5.5 %fusion.1 = f32[16,8,4096]{2,1,0:T(8,128)} fusion(f32[128,128]{1,0:T(8,128)S(1)} %fusion.8, f32[8,16,4096]{2,0,1:T(8,128)} %all-to-all-done.2), kind=kOutput, calls=%fused_computation.4 | convolution fusion | flops 806354944 | bytes 4259840 | tf_op jit(solution)/shard_map/dot_general | solution.py:179
  219.3 14.8 %all-to-all-done.1 = f32[1,16,64,512]{3,2,0,1:T(8,128)S(1)} async-done(((f32[1,16,64,512]{3,2,0,1:T(8,128)}), f32[1,16,64,512]{3,2,0,1:T(8,128)S(1)}, u32[]{:S(2)}, u32[]{:S(2)}) %all-to-all-start.1) | async-done | bytes 2097184 | tf_op jit(solution)/shard_map/all_to_all | solution.py:163
  234.1 8.7 %all-to-all-start.3 = ((f32[16,8,4096]{2,1,0:T(8,128)}), f32[16,8,4096]{2,1,0:T(8,128)}, u32[]{:S(2)}, u32[]{:S(2)}) async-start(f32[16,8,4096]{2,1,0:T(8,128)} %fusion.1), calls=%async_computation.3 | async-start | bytes 4194304 | tf_op jit(solution)/shard_map/all_to_all | solution.py:181
  242.8 25.9 %all-to-all-done.3 = f32[16,8,4096]{2,1,0:T(8,128)} async-done(((f32[16,8,4096]{2,1,0:T(8,128)}), f32[16,8,4096]{2,1,0:T(8,128)}, u32[]{:S(2)}, u32[]{:S(2)}) %all-to-all-start.3) | async-done | bytes 2097184 | tf_op jit(solution)/shard_map/all_to_all | solution.py:181
  268.7 4.1 %copy.24 = f32[8,16,4096]{2,1,0:T(8,128)} copy(f32[8,16,4096]{2,0,1:T(8,128)} %bitcast.13) | data formatting | bytes 4194304 | tf_op jit(solution)/shard_map/all_to_all | solution.py:181
  272.9 2.7 reshape.47
  275.6 1.3 copy.30
  (18 shorter events, 0.1 us)
Async XLA Ops:
  7.2 69.7 %all-gather.3.cloned.1.call-start = ((), (), s32[]{:S(2)}) async-start(), calls=%async_computation.4 | async-start | bytes 2359296 | tf_op jit(solution)/shard_map/all_gather | solution.py:149
  8.9 75.9 %all-to-all-start = ((f32[8,2,64,512]{3,2,1,0:T(8,128)}), f32[8,2,64,512]{3,2,1,0:T(8,128)S(1)}, u32[]{:S(2)}, u32[]{:S(2)}) async-start(f32[8,2,64,512]{3,2,1,0:T(8,128)} %param.10), calls=%async_computation | async-start | bytes 4194304 | tf_op jit(solution)/shard_map/all_to_all | solution.py:147
  76.9 19.7 %collective-permute-start = (f32[16,64,512]{2,1,0:T(8,128)}, f32[16,64,512]{2,1,0:T(8,128)}, u32[]{:S(2)}, u32[]{:S(2)}) collective-permute-start(f32[16,64,512]{2,1,0:T(8,128)} %all-gather.3.cloned.1.call-done), channel_id=1, source_target_pairs={{0,1},{1,0},{2,3},{3,2},{4,5},{5,4},{6,7},{7,6},{8,9},{9,8},{10,11... | collective-permute-start | bytes 6291464 | tf_op jit(solution)/shard_map/ppermute | solution.py:151
  84.8 4.7 %copy-start.4 = (s32[16]{0:T(128)S(1)}, s32[16]{0:T(128)}, u32[]{:S(2)}) copy-start(s32[16]{0:T(128)} %param.13) | copy-start | bytes 196
  84.8 4.7 %copy-start = (f32[8,2,64,512]{3,2,1,0:T(8,128)}, f32[8,2,64,512]{3,2,1,0:T(8,128)S(1)}, u32[]{:S(2)}) copy-start(f32[8,2,64,512]{3,2,1,0:T(8,128)S(1)} %all-to-all-done) | copy-start | bytes 6291460
  84.8 117.3 %all-to-all-start.2 = ((f32[8,16,4096]{2,0,1:T(8,128)}), f32[8,16,4096]{2,0,1:T(8,128)}, u32[]{:S(2)}, u32[]{:S(2)}) async-start(f32[8,16,4096]{2,0,1:T(8,128)} %copy.21), calls=%async_computation.2 | async-start | bytes 4194304 | tf_op jit(solution)/shard_map/all_to_all | solution.py:178
  91.8 2.4 copy-start.7
  91.8 3.7 %copy-start.5 = (s32[32]{0:T(128)S(1)}, s32[32]{0:T(128)}, u32[]{:S(2)}) copy-start(s32[32]{0:T(128)} %param.15) | copy-start | bytes 388
  91.8 4.3 %copy-start.6 = (f32[32]{0:T(128)S(1)}, f32[32]{0:T(128)}, u32[]{:S(2)}) copy-start(f32[32]{0:T(128)} %param.17) | copy-start | bytes 388
  161.0 21.2 %copy-start.1 = (f32[8,32]{1,0:T(8,128)S(1)}, f32[8,32]{1,0:T(8,128)}, u32[]{:S(2)}) copy-start(f32[8,32]{1,0:T(8,128)} %param.19) | copy-start | bytes 3076
  202.1 4.2 %copy-start.2 = (f32[32]{0:T(128)S(1)}, f32[32]{0:T(128)}, u32[]{:S(2)}) copy-start(f32[32]{0:T(128)} %broadcast_divide_fusion) | copy-start | bytes 388
  202.1 10.9 %copy-start.3 = (f32[32]{0:T(128)S(1)}, f32[32]{0:T(128)}, u32[]{:S(2)}) copy-start(f32[32]{0:T(128)} %param.16) | copy-start | bytes 388
  202.1 32.0 %all-to-all-start.1 = ((f32[1,16,64,512]{3,2,0,1:T(8,128)}), f32[1,16,64,512]{3,2,0,1:T(8,128)S(1)}, u32[]{:S(2)}, u32[]{:S(2)}) async-start(f32[1,16,64,512]{3,2,0,1:T(8,128)} %bitcast.2), calls=%async_computation.1 | async-start | bytes 4194304 | tf_op jit(solution)/shard_map/all_to_all | solution.py:163
  234.1 34.6 %all-to-all-start.3 = ((f32[16,8,4096]{2,1,0:T(8,128)}), f32[16,8,4096]{2,1,0:T(8,128)}, u32[]{:S(2)}, u32[]{:S(2)}) async-start(f32[16,8,4096]{2,1,0:T(8,128)} %fusion.1), calls=%async_computation.3 | async-start | bytes 4194304 | tf_op jit(solution)/shard_map/all_to_all | solution.py:181
Sparse Core Ops, SparseCore 0:
  10.9 65.9 all-gather.2

commit v5 on v4

--- a/solution.py
+++ b/solution.py
@@ -47,8 +47,23 @@
     return jnp.where(valid, x, 0.0)
 
 
-def forward_kernel(log_ref, sto_ref, init_ref, forc_ref, out_ref, perm, trans, diag, head_a, head_b):
+def forward_kernel(
+    log_ref, sto_ref, init_ref, forc_ref, field_ref, out_ref,
+    perm, trans, diag, head_a, head_b, send_sems, recv_sems, local_sem,
+):
     planes, depth, across = log_ref.shape
+    slabs = out_ref.shape[0]
+    thick = planes // slabs
+    me = lax.axis_index("space")
+    ens = lax.axis_index("ens")
+    mesh_id = pl.DeviceIdType.MESH
+
+    barrier = pltpu.get_barrier_semaphore()
+    for s in range(slabs):
+        @pl.when(me != s)
+        def _():
+            pl.semaphore_signal(barrier, 1, device_id=(s, ens), device_id_type=mesh_id)
+
     zero = jnp.zeros((depth, across), jnp.float32)
     for buf in (perm, head_a, head_b):
         buf[0] = zero
@@ -83,45 +98,97 @@
 
     lax.fori_loop(0, planes, diagonal, 0)
 
-    def sweep(source, target, padded_target):
+    def relax(source, p):
+        gathered = None
+        for k, (a, b, c) in enumerate(HALF):
+            ahead = trans[k, p] * shift_plane(source[p + 1 + a], b, c)
+            back = jnp.clip(p - a, 0, planes - 1)
+            flow = shift_plane(trans[k, back] * source[p + 1 - a], -b, -c)
+            term = ahead + flow
+            gathered = term if gathered is None else gathered + term
+        return (1.0 - OMEGA) * source[p + 1] + OMEGA * (forc_ref[p] + gathered) / diag[p]
+
+    def sweep(source, target):
         def body(p, carry):
-            gathered = None
-            for k, (a, b, c) in enumerate(HALF):
-                ahead = trans[k, p] * shift_plane(source[p + 1 + a], b, c)
-                back = jnp.clip(p - a, 0, planes - 1)
-                flow = shift_plane(trans[k, back] * source[p + 1 - a], -b, -c)
-                term = ahead + flow
-                gathered = term if gathered is None else gathered + term
-            value = (1.0 - OMEGA) * source[p + 1] + OMEGA * (forc_ref[p] + gathered) / diag[p]
-            if padded_target:
-                target[p + 1] = value
-            else:
-                target[p] = value
+            target[p + 1] = relax(source, p)
             return carry
 
         lax.fori_loop(0, planes, body, 0)
 
-    sweep(head_a, head_b, True)
-    sweep(head_b, head_a, True)
-    sweep(head_a, out_ref, False)
-
-
-def forward_pallas(log_row, storage, head_init, forcing):
+    sweep(head_a, head_b)
+    sweep(head_b, head_a)
+    pl.semaphore_wait(barrier, slabs - 1)
+
+    def send(s):
+        return pltpu.make_async_remote_copy(
+            src_ref=field_ref.at[pl.ds(s * thick, thick)],
+            dst_ref=out_ref.at[me],
+            send_sem=send_sems.at[s],
+            recv_sem=recv_sems.at[me],
+            device_id=(s, ens),
+            device_id_type=mesh_id,
+        )
+
+    def keep():
+        return pltpu.make_async_copy(
+            field_ref.at[pl.ds(me * thick, thick)], out_ref.at[me], local_sem
+        )
+
+    def last(s, carry):
+        for j in range(thick):
+            p = s * thick + j
+            field_ref[p] = relax(head_a, p)
+
+        @pl.when(s != me)
+        def _():
+            send(s).start()
+
+        @pl.when(s == me)
+        def _():
+            keep().start()
+
+        return carry
+
+    lax.fori_loop(0, slabs, last, 0)
+    keep().wait()
+    for s in range(slabs):
+        @pl.when(me != s)
+        def _():
+            send(s).wait_send()
+            pltpu.make_async_remote_copy(
+                src_ref=field_ref.at[pl.ds(s * thick, thick)],
+                dst_ref=out_ref.at[s],
+                send_sem=send_sems.at[s],
+                recv_sem=recv_sems.at[s],
+                device_id=(s, ens),
+                device_id_type=mesh_id,
+            ).wait_recv()
+
+
+def forward_pallas(log_row, storage, head_init, forcing, slabs):
     planes, depth, across = log_row.shape
     vmem = pl.BlockSpec(memory_space=pltpu.VMEM)
     return pl.pallas_call(
         forward_kernel,
-        out_shape=jax.ShapeDtypeStruct((planes, depth, across), jnp.float32),
+        out_shape=(
+            jax.ShapeDtypeStruct((planes, depth, across), jnp.float32),
+            jax.ShapeDtypeStruct((slabs, planes // slabs, depth, across), jnp.float32),
+        ),
         in_specs=[vmem] * 4,
-        out_specs=vmem,
+        out_specs=(vmem, pl.BlockSpec(memory_space=pl.ANY)),
         scratch_shapes=[
             pltpu.VMEM((planes + 2, depth, across), jnp.float32),
             pltpu.VMEM((len(HALF), planes, depth, across), jnp.float32),
             pltpu.VMEM((planes, depth, across), jnp.float32),
             pltpu.VMEM((planes + 2, depth, across), jnp.float32),
             pltpu.VMEM((planes + 2, depth, across), jnp.float32),
+            pltpu.SemaphoreType.DMA((slabs,)),
+            pltpu.SemaphoreType.DMA((slabs,)),
+            pltpu.SemaphoreType.DMA,
         ],
-        compiler_params=pltpu.CompilerParams(vmem_limit_bytes=66 * 1024 * 1024),
+        compiler_params=pltpu.CompilerParams(
+            vmem_limit_bytes=66 * 1024 * 1024, collective_id=0, has_side_effects=True
+        ),
     )(log_row, storage, head_init, forcing)
 
 
@@ -158,9 +225,8 @@
         .reshape(grid_planes, depth, across)
     )
     forcing = whole_storage * whole_head + source
-    field = forward_pallas(whole_log[0], whole_storage, whole_head, forcing)
+    field, head_field = forward_pallas(whole_log[0], whole_storage, whole_head, forcing, n_space)
     picked = field.reshape(-1)[obs_cells]
-    head_field = lax.all_to_all(field[None], "space", 1, 0, tiled=True)
 
     observed = lax.all_gather(picked[None], "space", axis=0, tiled=True)
     both = lax.all_gather(jnp.concatenate([observed, perturb], axis=1), "ens", axis=0, tiled=True)

time: 287 us -> 294 us (1.024)
  Pallas kernels: 58.8 us -> 79.2 us
  starting transfers between devices: 25.9 us -> 18 us
  waiting for transfers between devices: 101 us -> 94.4 us
  blocking collectives: 37.7 us -> 42.1 us
    pallas_call x1, Pallas kernels: 58.8 us -> 79.2 us  [forward_pallas(): pl.pallas_call(forward_kernel, out_shape=(jax.ShapeDtypeStruct((planes, d...]
    all_to_all x1 -> x0, waiting for transfers between devices: 14.8 us -> none  [shards(): head_field = lax.all_to_all(field[None], 'space', 1, 0, tiled=True)]
    all_to_all x1, waiting for transfers between devices: 0.01 us -> 10.8 us  [shards(): whole_log = lax.all_to_all(log_perm, 'space', 0, 1, tiled=True)]
    all_to_all x1 -> x0, starting transfers between devices: 3.79 us -> none  [shards(): head_field = lax.all_to_all(field[None], 'space', 1, 0, tiled=True)]
    unnamed x1, blocking collectives: 17.9 us -> 21.2 us
    all_to_all x1, starting transfers between devices: 7.51 us -> 4.34 us  [shards(): whole_log = lax.all_to_all(log_perm, 'space', 0, 1, tiled=True)]
  transfers between devices with their start and end apart: 6 -> 5, of which waited for: 3 -> 3; matrix products, arithmetic and copies ran while one was open for 11% -> 9% of each run, Pallas kernels for 21% -> 27%
where the time goes in v5:
time: 294 us; the launch traced here: 291 us
  waiting for transfers between devices  94.4 us (32%)
  Pallas kernels  79.2 us (27%)
  blocking collectives  42.1 us (14%)
  local copies, waits for them, and re-layouts  18.3 us (6%)
  starting transfers between devices  18 us (6%)
  other arithmetic  16.8 us (6%)
  between operations  15.5 us (5%)
  matrix products  6.5 us (2%)
    pallas_call x1, Pallas kernels, forward_pallas(): pl.pallas_call(forward_kernel, out_shape=(jax.ShapeDtypeStruct((planes, d...  79.2 us
    all_gather x1, waiting for transfers between devices, shards(): lax.all_gather(jnp.where(core == 0, storage, head_init), 'space', axis=0,...  57.8 us
    all_to_all x1, waiting for transfers between devices, shards(): lax.all_to_all(new_column, 'ens', 0, 1, tiled=True).reshape(log_perm.shape)  25.8 us
    unnamed x1, blocking collectives  21.2 us
    all_gather x1, blocking collectives, shards(): lax.all_gather(jnp.concatenate([observed, perturb], axis=1), 'ens', axis=...  21 us
    all_to_all x1, waiting for transfers between devices, shards(): whole_log = lax.all_to_all(log_perm, 'space', 0, 1, tiled=True)  10.8 us
    all_to_all x1, starting transfers between devices, shards(): lax.all_to_all(new_column, 'ens', 0, 1, tiled=True).reshape(log_perm.shape)  7.23 us
  transfers between devices with their start and end apart: 5, of which 3 were waited for; matrix products, arithmetic and copies ran while one was open for 9% of the time, Pallas kernels for 27%

profile of v5, /device:TPU:25, one launch (start us, length us, event | category | flops | bytes accessed | tf_op | source)
XLA Modules:
  0.0 290.9 jit_solution(4579586653385886708)
XLA Ops:
  7.2 0.0 all-gather.3.cloned.1.call-start
  7.2 1.7 broadcast_select_fusion.2
  8.9 0.0 all-gather.3.cloned.1.call-update
  8.9 0.0 copy-start
  9.0 57.8 %all-gather.3.cloned.1.call-done = f32[16,64,512]{2,1,0:T(8,128)} async-done(((f32[2,64,512]{2,1,0:T(8,128)}), f32[16,64,512]{2,1,0:T(8,128)}) %all-gather.3.cloned.1.call-update) | async-done | bytes 2097168 | tf_op jit(solution)/shard_map/all_gather | solution.py:216
  66.8 1.1 collective-permute-start
  67.9 4.3 %all-to-all-start = ((f32[8,2,64,512]{3,2,1,0:T(8,128)}), f32[8,2,64,512]{3,2,1,0:T(8,128)}, u32[]{:S(2)}, u32[]{:S(2)}) async-start(f32[8,2,64,512]{3,2,1,0:T(8,128)} %param.10), calls=%async_computation | async-start | bytes 4194304 | tf_op jit(solution)/shard_map/all_to_all | solution.py:214
  72.3 0.0 copy-start.6
  72.3 1.5 all_to_all.34
  73.8 2.2 scatter_custom_fusion
  76.0 1.7 reshape.42
  78.4 0.0 copy-start.9
  78.4 0.0 copy-start.7
  78.4 0.0 copy-start.8
  78.4 4.3 %copy.20 = f32[8,16,4096]{2,0,1:T(8,128)} copy(f32[8,16,4096]{2,1,0:T(8,128)} %all_to_all.34) | data formatting | bytes 4194304 | tf_op jit(solution)/shard_map/all_to_all | solution.py:244
  82.8 0.6 dynamic-slice
  84.0 0.6 pad_clamp_fusion
  84.6 0.5 broadcast_divide_fusion
  85.2 0.0 collective-permute-done
  85.2 4.9 %multiply_add_fusion = (f32[16,64,512]{2,1,0:T(8,128)}, f32[16,64,512]{2,1,0:T(8,128)}, f32[16,64,512]{2,1,0:T(8,128)}) fusion(f32[16,64,512]{2,1,0:T(8,128)S(1)} %reshape.42, f32[16,64,512]{2,1,0:T(8,128)} %collective-permute-done, f32[16,64,512]{2,1,0:T(8,128)S(1)} %copy-done.1, pred[]{:T(512)S(6)} %eq.12), kind=kLoop, calls=%fused_computation.6 | loop fusion | flops 2097152 | bytes 12582913 | tf_op jit(solution)/shard_map/add | solution.py:227
  90.1 10.8 %all-to-all-done = f32[8,2,64,512]{3,2,1,0:T(8,128)} async-done(((f32[8,2,64,512]{3,2,1,0:T(8,128)}), f32[8,2,64,512]{3,2,1,0:T(8,128)}, u32[]{:S(2)}, u32[]{:S(2)}) %all-to-all-start) | async-done | bytes 2097184 | tf_op jit(solution)/shard_map/all_to_all | solution.py:214
  100.9 5.3 %all-to-all-start.1 = ((f32[8,16,4096]{2,0,1:T(8,128)}), f32[8,16,4096]{2,0,1:T(8,128)}, u32[]{:S(2)}, u32[]{:S(2)}) async-start(f32[8,16,4096]{2,0,1:T(8,128)} %copy.20), calls=%async_computation.1 | async-start | bytes 4194304 | tf_op jit(solution)/shard_map/all_to_all | solution.py:244
  106.1 79.2 %shard_map.113 = (f32[16,64,512]{2,1,0:T(8,128)}, f32[8,2,64,512]{3,2,1,0:T(8,128)}) custom-call(f32[16,64,512]{2,1,0:T(8,128)} %bitcast.log_ref, f32[16,64,512]{2,1,0:T(8,128)} %get-tuple-element.8.sto_ref, f32[16,64,512]{2,1,0:T(8,128)} %get-tuple-element.7.init_ref, f32[16,64,512]{2,1,0:T(8,128)} %get-tuple-element.6.forc_ref), custom_call_target="tpu_custom_call" | custom-call | tf_op jit(solution)/shard_map/pallas_call | solution.py:171
  185.4 0.0 copy-start.3
  185.4 0.0 copy-start.5
  185.4 2.1 copy.25
  187.5 0.8 gather_fusion
  188.4 0.2 dynamic-update-slice.3
  188.6 21.2 %all-reduce = f32[256]{0:T(256)S(1)} all-reduce(f32[256]{0:T(256)S(1)} %dynamic-update-slice.3), channel_id=2, replica_groups=mesh['space'=8,'ens'=16] {'space'}, use_global_device_ids=true, to_apply=%add | all-reduce | flops 256 | bytes 2048
  209.8 0.1 reshape.61
  209.8 0.1 pad_maximum_fusion
  209.9 21.0 %all_gather.11 = f32[128,64]{1,0:T(8,128)S(1)} all-gather(f32[8,64]{1,0:T(8,128)S(1)} %pad_maximum_fusion), channel_id=1, replica_groups=mesh['space'=8,'ens'=16] {'ens'}, dimensions={0}, use_global_device_ids=true | all-gather | bytes 34816 | tf_op jit(solution)/shard_map/all_gather | solution.py:232
  230.9 0.3 convolution_multiply_fusion.1
  231.2 0.1 copy.22
  231.3 0.1 fusion.22
  231.4 2.9 %cholesky.16 = f32[32,32]{1,0:T(8,128)S(1)} custom-call(f32[32,32]{1,0:T(8,128)S(1)} %fusion.22), custom_call_target="Cholesky" | custom-call | tf_op jit(solution)/shard_map/jit(cholesky)/cholesky | solution.py:239
  234.3 0.6 compare_reduce_fusion
  235.0 0.7 fusion.17
  235.6 2.4 custom-call.8
  238.0 0.3 fusion.6
  238.3 0.2 fusion.18
  238.5 0.3 fusion.8
  238.8 5.5 %fusion.1 = f32[16,8,4096]{2,1,0:T(8,128)} fusion(f32[128,128]{1,0:T(8,128)S(1)} %fusion.8, f32[8,16,4096]{2,0,1:T(8,128)} %all-to-all-done.1), kind=kOutput, calls=%fused_computation.4 | convolution fusion | flops 806354944 | bytes 4259840 | tf_op jit(solution)/shard_map/dot_general | solution.py:245
  244.3 7.2 %all-to-all-start.2 = ((f32[16,8,4096]{2,1,0:T(8,128)}), f32[16,8,4096]{2,1,0:T(8,128)S(1)}, u32[]{:S(2)}, u32[]{:S(2)}) async-start(f32[16,8,4096]{2,1,0:T(8,128)} %fusion.1), calls=%async_computation.2 | async-start | bytes 4194304 | tf_op jit(solution)/shard_map/all_to_all | solution.py:247
  251.5 25.8 %all-to-all-done.2 = f32[16,8,4096]{2,1,0:T(8,128)S(1)} async-done(((f32[16,8,4096]{2,1,0:T(8,128)}), f32[16,8,4096]{2,1,0:T(8,128)S(1)}, u32[]{:S(2)}, u32[]{:S(2)}) %all-to-all-start.2) | async-done | bytes 2097184 | tf_op jit(solution)/shard_map/all_to_all | solution.py:247
  277.3 2.5 copy.23
  279.9 2.9 reshape.44
  282.7 1.3 copy.29
  (20 shorter events, 0.1 us)
Async XLA Ops:
  7.2 59.6 %all-gather.3.cloned.1.call-start = ((), (), s32[]{:S(2)}) async-start(), calls=%async_computation.3 | async-start | bytes 2359296 | tf_op jit(solution)/shard_map/all_gather | solution.py:216
  8.9 63.3 %copy-start = (f32[8,2,64,512]{3,2,1,0:T(8,128)S(1)}, f32[8,2,64,512]{3,2,1,0:T(8,128)}, u32[]{:S(2)}) copy-start(f32[8,2,64,512]{3,2,1,0:T(8,128)} %param.10) | copy-start | bytes 6291460
  66.8 18.4 %collective-permute-start = (f32[16,64,512]{2,1,0:T(8,128)}, f32[16,64,512]{2,1,0:T(8,128)}, u32[]{:S(2)}, u32[]{:S(2)}) collective-permute-start(f32[16,64,512]{2,1,0:T(8,128)} %all-gather.3.cloned.1.call-done), channel_id=1, source_target_pairs={{0,1},{1,0},{2,3},{3,2},{4,5},{5,4},{6,7},{7,6},{8,9},{9,8},{10,11... | collective-permute-start | bytes 6291464 | tf_op jit(solution)/shard_map/ppermute | solution.py:218
  67.9 33.0 %all-to-all-start = ((f32[8,2,64,512]{3,2,1,0:T(8,128)}), f32[8,2,64,512]{3,2,1,0:T(8,128)}, u32[]{:S(2)}, u32[]{:S(2)}) async-start(f32[8,2,64,512]{3,2,1,0:T(8,128)} %param.10), calls=%async_computation | async-start | bytes 4194304 | tf_op jit(solution)/shard_map/all_to_all | solution.py:214
  72.3 1.5 copy-start.6
  78.4 4.4 %copy-start.9 = (u32[128]{0:T(128)S(1)}, u32[128]{0:T(128)}, u32[]{:S(2)}) copy-start(u32[128]{0:T(128)} %constant.86) | copy-start | bytes 1540
  78.4 5.6 %copy-start.7 = (s32[32]{0:T(128)S(1)}, s32[32]{0:T(128)}, u32[]{:S(2)}) copy-start(s32[32]{0:T(128)} %param.15) | copy-start | bytes 388
  78.4 6.2 %copy-start.8 = (f32[32]{0:T(128)S(1)}, f32[32]{0:T(128)}, u32[]{:S(2)}) copy-start(f32[32]{0:T(128)} %param.17) | copy-start | bytes 388
  78.4 6.7 %copy-start.1 = (f32[16,64,512]{2,1,0:T(8,128)S(1)}, f32[16,64,512]{2,1,0:T(8,128)}, u32[]{:S(2)}) copy-start(f32[16,64,512]{2,1,0:T(8,128)} %all-gather.3.cloned.1.call-done) | copy-start | bytes 6291460
  100.9 138.0 %all-to-all-start.1 = ((f32[8,16,4096]{2,0,1:T(8,128)}), f32[8,16,4096]{2,0,1:T(8,128)}, u32[]{:S(2)}, u32[]{:S(2)}) async-start(f32[8,16,4096]{2,0,1:T(8,128)} %copy.20), calls=%async_computation.1 | async-start | bytes 4194304 | tf_op jit(solution)/shard_map/all_to_all | solution.py:244
  185.4 24.5 %copy-start.3 = (f32[8,32]{1,0:T(8,128)S(1)}, f32[8,32]{1,0:T(8,128)}, u32[]{:S(2)}) copy-start(f32[8,32]{1,0:T(8,128)} %param.19) | copy-start | bytes 3076
  185.4 45.9 %copy-start.4 = (f32[32]{0:T(128)S(1)}, f32[32]{0:T(128)}, u32[]{:S(2)}) copy-start(f32[32]{0:T(128)} %broadcast_divide_fusion) | copy-start | bytes 388
  185.4 52.7 %copy-start.5 = (f32[32]{0:T(128)S(1)}, f32[32]{0:T(128)}, u32[]{:S(2)}) copy-start(f32[32]{0:T(128)} %param.16) | copy-start | bytes 388
  244.3 33.0 %all-to-all-start.2 = ((f32[16,8,4096]{2,1,0:T(8,128)}), f32[16,8,4096]{2,1,0:T(8,128)S(1)}, u32[]{:S(2)}, u32[]{:S(2)}) async-start(f32[16,8,4096]{2,1,0:T(8,128)} %fusion.1), calls=%async_computation.2 | async-start | bytes 4194304 | tf_op jit(solution)/shard_map/all_to_all | solution.py:247
  279.9 2.9 copy-start.2
Sparse Core Ops, SparseCore 0:
  10.9 55.8 all-gather.2

commit v6 on v4

--- a/solution.py
+++ b/solution.py
@@ -123,6 +123,74 @@
         ],
         compiler_params=pltpu.CompilerParams(vmem_limit_bytes=66 * 1024 * 1024),
     )(log_row, storage, head_init, forcing)
+
+
+def gather_kernel(row_ref, out_ref, landing, send_sem, recv_sem):
+    total = landing.shape[0]
+    n_space = lax.axis_size("space")
+    me_s = lax.axis_index("space")
+    me_e = lax.axis_index("ens")
+    mine = me_e * n_space + me_s
+    mesh_id = pl.DeviceIdType.MESH
+
+    barrier = pltpu.get_barrier_semaphore()
+
+    def greet(i, carry):
+        @pl.when(i != mine)
+        def _():
+            pl.semaphore_signal(
+                barrier, 1, device_id=(i % n_space, i // n_space), device_id_type=mesh_id
+            )
+
+        return carry
+
+    lax.fori_loop(0, total, greet, 0)
+    pl.semaphore_wait(barrier, total - 1)
+
+    def send(i, carry):
+        @pl.when(i != mine)
+        def _():
+            pltpu.make_async_remote_copy(
+                src_ref=row_ref,
+                dst_ref=landing.at[pl.ds(mine, 1)],
+                send_sem=send_sem,
+                recv_sem=recv_sem,
+                device_id=(i % n_space, i // n_space),
+                device_id_type=mesh_id,
+            ).start()
+
+        return carry
+
+    lax.fori_loop(0, total, send, 0)
+    landing[pl.ds(mine, 1)] = row_ref[...]
+    partner = (mine + 1) % total
+    everything = pltpu.make_async_remote_copy(
+        src_ref=landing.at[pl.ds(0, total - 1)],
+        dst_ref=landing.at[pl.ds(1, total - 1)],
+        send_sem=send_sem,
+        recv_sem=recv_sem,
+        device_id=(partner % n_space, partner // n_space),
+        device_id_type=mesh_id,
+    )
+    everything.wait_send()
+    everything.wait_recv()
+    out_ref[...] = landing[...]
+
+
+def gather_rows(row, total):
+    vmem = pl.BlockSpec(memory_space=pltpu.VMEM)
+    return pl.pallas_call(
+        gather_kernel,
+        out_shape=jax.ShapeDtypeStruct((total,) + row.shape[1:], jnp.float32),
+        in_specs=[vmem],
+        out_specs=vmem,
+        scratch_shapes=[
+            pltpu.VMEM((total,) + row.shape[1:], jnp.float32),
+            pltpu.SemaphoreType.DMA,
+            pltpu.SemaphoreType.DMA,
+        ],
+        compiler_params=pltpu.CompilerParams(collective_id=1, has_side_effects=True),
+    )(row)
 
 
 def shards(
@@ -162,10 +230,13 @@
     picked = field.reshape(-1)[obs_cells]
     head_field = lax.all_to_all(field[None], "space", 1, 0, tiled=True)
 
-    observed = lax.all_gather(picked[None], "space", axis=0, tiled=True)
-    both = lax.all_gather(jnp.concatenate([observed, perturb], axis=1), "ens", axis=0, tiled=True)
-    obs_count = observed.shape[1]
-    every_obs, every_perturb = both[:, :obs_count], both[:, obs_count:]
+    obs_count = picked.shape[0]
+    own_perturb = lax.dynamic_index_in_dim(perturb, lax.axis_index("space"), 0, keepdims=False)
+    row = jnp.zeros((1, 8, 128), jnp.float32)
+    row = row.at[0, 0, :obs_count].set(picked).at[0, 0, obs_count : 2 * obs_count].set(own_perturb)
+    rows = gather_rows(row, total_members)
+    every_obs = rows[:, 0, :obs_count]
+    every_perturb = rows[:, 0, obs_count : 2 * obs_count]
     mean_obs = jnp.mean(every_obs, axis=0)
     spread = every_obs - mean_obs
     covariance = jnp.dot(spread.T, spread, precision=HIGHEST) / (total_members - 1)

time: 287 us -> 266 us (0.927)
  blocking collectives: 37.7 us -> 0 us
  Pallas kernels: 58.8 us -> 77.1 us
    all_gather x1 -> x0, blocking collectives: 19.8 us -> none  [shards(): lax.all_gather(jnp.concatenate([observed, perturb], axis=1), 'ens', axis=...]
    pallas_call x0 -> x1, Pallas kernels: none -> 18.3 us  [gather_rows(): pl.pallas_call(gather_kernel, out_shape=jax.ShapeDtypeStruct((total,) + r...]
    unnamed x1 -> x0, blocking collectives: 17.9 us -> none
  transfers between devices with their start and end apart: 6 -> 6, of which waited for: 3 -> 3; matrix products, arithmetic and copies ran while one was open for 11% -> 13% of each run, Pallas kernels for 21% -> 29%
where the time goes in v6:
time: 266 us; the launch traced here: 263 us
  waiting for transfers between devices  99.6 us (37%)
  Pallas kernels  77.1 us (29%)
  starting transfers between devices  23.3 us (9%)
  local copies, waits for them, and re-layouts  22 us (8%)
  other arithmetic  20 us (8%)
  between operations  14.8 us (6%)
  matrix products  6.47 us (2%)
    all_gather x1, waiting for transfers between devices, shards(): lax.all_gather(jnp.where(core == 0, storage, head_init), 'space', axis=0,...  60.4 us
    pallas_call x1, Pallas kernels, forward_pallas(): pl.pallas_call(forward_kernel, out_shape=jax.ShapeDtypeStruct((planes, de...  58.8 us
    all_to_all x1, waiting for transfers between devices, shards(): lax.all_to_all(new_column, 'ens', 0, 1, tiled=True).reshape(log_perm.shape)  25.9 us
    pallas_call x1, Pallas kernels, gather_rows(): pl.pallas_call(gather_kernel, out_shape=jax.ShapeDtypeStruct((total,) + r...  18.3 us
    all_to_all x1, waiting for transfers between devices, shards(): head_field = lax.all_to_all(field[None], 'space', 1, 0, tiled=True)  13.3 us
    all_to_all x1, starting transfers between devices, shards(): whole_log = lax.all_to_all(log_perm, 'space', 0, 1, tiled=True)  7.51 us
    all_to_all x2, local copies, waits for them, and re-layouts, shards(): column = lax.all_to_all(flat, 'ens', 1, 0, tiled=True)  6.86 us
    all_to_all x1, starting transfers between devices, shards(): lax.all_to_all(new_column, 'ens', 0, 1, tiled=True).reshape(log_perm.shape)  5.93 us
  transfers between devices with their start and end apart: 6, of which 3 were waited for; matrix products, arithmetic and copies ran while one was open for 13% of the time, Pallas kernels for 29%

profile of v6, /device:TPU:25, one launch (start us, length us, event | category | flops | bytes accessed | tf_op | source)
XLA Modules:
  0.0 263.2 jit_solution(15005451520419757441)
XLA Ops:
  7.2 0.0 all-gather.2.cloned.1.call-start
  7.2 1.7 broadcast_select_fusion.2
  8.9 0.0 all-gather.2.cloned.1.call-update
  8.9 7.5 %all-to-all-start = ((f32[8,2,64,512]{3,2,1,0:T(8,128)}), f32[8,2,64,512]{3,2,1,0:T(8,128)S(1)}, u32[]{:S(2)}, u32[]{:S(2)}) async-start(f32[8,2,64,512]{3,2,1,0:T(8,128)} %param.14), calls=%async_computation | async-start | bytes 4194304 | tf_op jit(solution)/shard_map/all_to_all | solution.py:215
  16.5 60.4 %all-gather.2.cloned.1.call-done = f32[16,64,512]{2,1,0:T(8,128)} async-done(((f32[2,64,512]{2,1,0:T(8,128)}), f32[16,64,512]{2,1,0:T(8,128)}) %all-gather.2.cloned.1.call-update) | async-done | bytes 2097168 | tf_op jit(solution)/shard_map/all_gather | solution.py:217
  76.9 1.1 collective-permute-start
  78.0 2.7 %all_to_all.45 = f32[8,16,4096]{2,1,0:T(8,128)} reshape(f32[8,2,64,512]{3,2,1,0:T(8,128)} %param.14) | data formatting | bytes 4194304 | tf_op jit(solution)/shard_map/all_to_all | solution.py:249
  80.7 4.1 %copy.21 = f32[8,16,4096]{2,0,1:T(8,128)} copy(f32[8,16,4096]{2,1,0:T(8,128)} %all_to_all.45) | data formatting | bytes 4194304 | tf_op jit(solution)/shard_map/all_to_all | solution.py:249
  84.8 0.0 all-to-all-done
  84.8 4.7 %all-to-all-start.2 = ((f32[8,16,4096]{2,0,1:T(8,128)}), f32[8,16,4096]{2,0,1:T(8,128)}, u32[]{:S(2)}, u32[]{:S(2)}) async-start(f32[8,16,4096]{2,0,1:T(8,128)} %copy.21), calls=%async_computation.2 | async-start | bytes 4194304 | tf_op jit(solution)/shard_map/all_to_all | solution.py:249
  89.5 0.0 copy-done.5
  89.5 0.0 copy-done
  89.6 2.2 scatter_custom_fusion
  91.8 1.8 reshape.130
  94.2 1.2 dynamic-slice_bitcast_fusion
  95.4 0.0 copy-done.6
  95.4 0.6 pad_clamp_fusion
  96.0 0.0 copy-done.7
  96.0 0.5 broadcast_divide_fusion
  96.5 0.0 collective-permute-done
  96.5 5.7 %multiply_add_fusion = (f32[16,64,512]{2,1,0:T(8,128)}, f32[16,64,512]{2,1,0:T(8,128)}, f32[16,64,512]{2,1,0:T(8,128)}) fusion(f32[16,64,512]{2,1,0:T(8,128)S(1)} %reshape.130, f32[16,64,512]{2,1,0:T(8,128)} %collective-permute-done, f32[16,64,512]{2,1,0:T(8,128)} %all-gather.2.cloned.1.call-done, pred[]{:T(512)S(6)} %eq.12), kind=kLoop, calls=%fused_computation.6 | loop fusion | flops 2097152 | bytes 12582913 | tf_op jit(solution)/shard_map/add | solution.py:228
  102.2 58.8 %shard_map.113 = f32[16,64,512]{2,1,0:T(8,128)} custom-call(f32[16,64,512]{2,1,0:T(8,128)} %bitcast.44, f32[16,64,512]{2,1,0:T(8,128)} %get-tuple-element.28.sto_ref, f32[16,64,512]{2,1,0:T(8,128)} %get-tuple-element.27.init_ref, f32[16,64,512]{2,1,0:T(8,128)} %get-tuple-element.26.forc_ref), custom_call_target="tpu_custom_call" | custom-call | tf_op jit(solution)/shard_map/pallas_call | solution.py:112
  161.0 2.1 copy.26
  163.2 0.8 gather_fusion
  164.0 0.3 scatter.9.row_ref
  164.3 0.6 copy-done.1
  164.9 18.3 %shard_map.114 = f32[128,8,128]{2,1,0:T(8,128)} custom-call(f32[1,8,128]{2,1,0:T(8,128)} %copy-done.1), custom_call_target="tpu_custom_call" | custom-call | tf_op jit(solution)/shard_map/pallas_call | solution.py:182
  183.2 1.4 fusion.15
  184.6 0.0 all-to-all-done.2
  184.6 4.1 %all-to-all-start.1 = ((f32[1,16,64,512]{3,2,0,1:T(8,128)}), f32[1,16,64,512]{3,2,0,1:T(8,128)S(1)}, u32[]{:S(2)}, u32[]{:S(2)}) async-start(f32[1,16,64,512]{3,2,0,1:T(8,128)} %bitcast.2), calls=%async_computation.1 | async-start | bytes 4194304 | tf_op jit(solution)/shard_map/all_to_all | solution.py:231
  188.7 1.1 broadcast_subtract_fusion
  189.8 0.3 convolution_multiply_fusion.1
  190.1 0.1 copy.23
  190.1 0.1 fusion.14
  190.2 2.9 %cholesky.16 = f32[32,32]{1,0:T(8,128)S(1)} custom-call(f32[32,32]{1,0:T(8,128)S(1)} %fusion.14), custom_call_target="Cholesky" | custom-call | tf_op jit(solution)/shard_map/jit(cholesky)/cholesky | solution.py:244
  193.2 0.6 compare_reduce_fusion
  193.8 0.7 fusion.8
  194.5 2.4 custom-call.8
  196.9 0.3 fusion.11
  197.2 0.2 fusion.9
  197.3 0.3 fusion.5
  197.6 5.5 %fusion.1 = f32[16,8,4096]{2,1,0:T(8,128)} fusion(f32[128,128]{1,0:T(8,128)S(1)} %fusion.5, f32[8,16,4096]{2,0,1:T(8,128)} %all-to-all-done.2), kind=kOutput, calls=%fused_computation.4 | convolution fusion | flops 806354944 | bytes 4259840 | tf_op jit(solution)/shard_map/dot_general | solution.py:250
  203.1 13.3 %all-to-all-done.1 = f32[1,16,64,512]{3,2,0,1:T(8,128)S(1)} async-done(((f32[1,16,64,512]{3,2,0,1:T(8,128)}), f32[1,16,64,512]{3,2,0,1:T(8,128)S(1)}, u32[]{:S(2)}, u32[]{:S(2)}) %all-to-all-start.1) | async-done | bytes 2097184 | tf_op jit(solution)/shard_map/all_to_all | solution.py:231
  216.4 5.9 %all-to-all-start.3 = ((f32[16,8,4096]{2,1,0:T(8,128)}), f32[16,8,4096]{2,1,0:T(8,128)}, u32[]{:S(2)}, u32[]{:S(2)}) async-start(f32[16,8,4096]{2,1,0:T(8,128)} %fusion.1), calls=%async_computation.3 | async-start | bytes 4194304 | tf_op jit(solution)/shard_map/all_to_all | solution.py:252
  222.3 25.9 %all-to-all-done.3 = f32[16,8,4096]{2,1,0:T(8,128)} async-done(((f32[16,8,4096]{2,1,0:T(8,128)}), f32[16,8,4096]{2,1,0:T(8,128)}, u32[]{:S(2)}, u32[]{:S(2)}) %all-to-all-start.3) | async-done | bytes 2097184 | tf_op jit(solution)/shard_map/all_to_all | solution.py:252
  248.2 4.1 %copy.24 = f32[8,16,4096]{2,1,0:T(8,128)} copy(f32[8,16,4096]{2,0,1:T(8,128)} %bitcast.17) | data formatting | bytes 4194304 | tf_op jit(solution)/shard_map/all_to_all | solution.py:252
  252.3 2.7 %reshape.134 = f32[8,2,64,512]{3,2,1,0:T(8,128)} reshape(f32[8,16,4096]{2,1,0:T(8,128)} %copy.24) | data formatting | bytes 4194304 | tf_op jit(solution)/shard_map/reshape | solution.py:252
  255.1 1.3 copy.30
  (16 shorter events, 0.1 us)
Async XLA Ops:
  7.2 69.7 %all-gather.2.cloned.1.call-start = ((), (), s32[]{:S(2)}) async-start(), calls=%async_computation.4 | async-start | bytes 2359296 | tf_op jit(solution)/shard_map/all_gather | solution.py:217
  8.9 75.9 %all-to-all-start = ((f32[8,2,64,512]{3,2,1,0:T(8,128)}), f32[8,2,64,512]{3,2,1,0:T(8,128)S(1)}, u32[]{:S(2)}, u32[]{:S(2)}) async-start(f32[8,2,64,512]{3,2,1,0:T(8,128)} %param.14), calls=%async_computation | async-start | bytes 4194304 | tf_op jit(solution)/shard_map/all_to_all | solution.py:215
  76.9 19.7 %collective-permute-start = (f32[16,64,512]{2,1,0:T(8,128)}, f32[16,64,512]{2,1,0:T(8,128)}, u32[]{:S(2)}, u32[]{:S(2)}) collective-permute-start(f32[16,64,512]{2,1,0:T(8,128)} %all-gather.2.cloned.1.call-done), channel_id=1, source_target_pairs={{0,1},{1,0},{2,3},{3,2},{4,5},{5,4},{6,7},{7,6},{8,9},{9,8},{10,11... | collective-permute-start | bytes 6291464 | tf_op jit(solution)/shard_map/ppermute | solution.py:219
  84.8 4.7 %copy-start.5 = (s32[16]{0:T(128)S(1)}, s32[16]{0:T(128)}, u32[]{:S(2)}) copy-start(s32[16]{0:T(128)} %param.17) | copy-start | bytes 196
  84.8 4.7 %copy-start = (f32[8,2,64,512]{3,2,1,0:T(8,128)}, f32[8,2,64,512]{3,2,1,0:T(8,128)S(1)}, u32[]{:S(2)}) copy-start(f32[8,2,64,512]{3,2,1,0:T(8,128)S(1)} %all-to-all-done) | copy-start | bytes 6291460
  84.8 99.8 %all-to-all-start.2 = ((f32[8,16,4096]{2,0,1:T(8,128)}), f32[8,16,4096]{2,0,1:T(8,128)}, u32[]{:S(2)}, u32[]{:S(2)}) async-start(f32[8,16,4096]{2,0,1:T(8,128)} %copy.21), calls=%async_computation.2 | async-start | bytes 4194304 | tf_op jit(solution)/shard_map/all_to_all | solution.py:249
  91.8 3.7 %copy-start.6 = (s32[32]{0:T(128)S(1)}, s32[32]{0:T(128)}, u32[]{:S(2)}) copy-start(s32[32]{0:T(128)} %param.19) | copy-start | bytes 388
  91.8 4.2 %copy-start.7 = (f32[32]{0:T(128)S(1)}, f32[32]{0:T(128)}, u32[]{:S(2)}) copy-start(f32[32]{0:T(128)} %param.21) | copy-start | bytes 388
  161.0 3.0 %copy-start.4 = (f32[1,1,32]{2,1,0:T(1,128)S(1)}, f32[1,1,32]{2,1,0:T(1,128)}, u32[]{:S(2)}) copy-start(f32[1,1,32]{2,1,0:T(1,128)} %dynamic-slice_bitcast_fusion) | copy-start | bytes 388
  161.0 22.2 %copy-start.3 = (f32[32]{0:T(128)S(1)}, f32[32]{0:T(128)}, u32[]{:S(2)}) copy-start(f32[32]{0:T(128)} %param.20) | copy-start | bytes 388
  164.3 0.6 copy-start.1
  184.6 5.5 %copy-start.2 = (f32[32]{0:T(128)S(1)}, f32[32]{0:T(128)}, u32[]{:S(2)}) copy-start(f32[32]{0:T(128)} %broadcast_divide_fusion) | copy-start | bytes 388
  184.6 31.8 %all-to-all-start.1 = ((f32[1,16,64,512]{3,2,0,1:T(8,128)}), f32[1,16,64,512]{3,2,0,1:T(8,128)S(1)}, u32[]{:S(2)}, u32[]{:S(2)}) async-start(f32[1,16,64,512]{3,2,0,1:T(8,128)} %bitcast.2), calls=%async_computation.1 | async-start | bytes 4194304 | tf_op jit(solution)/shard_map/all_to_all | solution.py:231
  216.4 31.8 %all-to-all-start.3 = ((f32[16,8,4096]{2,1,0:T(8,128)}), f32[16,8,4096]{2,1,0:T(8,128)}, u32[]{:S(2)}, u32[]{:S(2)}) async-start(f32[16,8,4096]{2,1,0:T(8,128)} %fusion.1), calls=%async_computation.3 | async-start | bytes 4194304 | tf_op jit(solution)/shard_map/all_to_all | solution.py:252
Sparse Core Ops, SparseCore 0:
  10.9 65.9 all-gather.1

commit v7 on v6

--- a/solution.py
+++ b/solution.py
@@ -191,6 +191,104 @@
         ],
         compiler_params=pltpu.CompilerParams(collective_id=1, has_side_effects=True),
     )(row)
+
+
+def return_kernel(field_ref, column_ref, head_out, update_out,
+                  head_send, head_recv, upd_send, upd_recv, local_sems):
+    slabs, thick = head_out.shape[0], head_out.shape[1]
+    groups = update_out.shape[1] // column_ref.shape[1]
+    rows = column_ref.shape[1]
+    members = update_out.shape[0]
+    me_s = lax.axis_index("space")
+    me_e = lax.axis_index("ens")
+    mesh_id = pl.DeviceIdType.MESH
+
+    barrier = pltpu.get_barrier_semaphore()
+    for s in range(slabs):
+        @pl.when(me_s != s)
+        def _():
+            pl.semaphore_signal(barrier, 1, device_id=(s, me_e), device_id_type=mesh_id)
+    for e in range(groups):
+        @pl.when(me_e != e)
+        def _():
+            pl.semaphore_signal(barrier, 1, device_id=(me_s, e), device_id_type=mesh_id)
+    pl.semaphore_wait(barrier, slabs - 1 + groups - 1)
+
+    def upd_copy(e, source_e):
+        return pltpu.make_async_remote_copy(
+            src_ref=column_ref.at[pl.ds(e * members, members)],
+            dst_ref=update_out.at[:, pl.ds(source_e * rows, rows)],
+            send_sem=upd_send.at[e],
+            recv_sem=upd_recv.at[source_e],
+            device_id=(me_s, e),
+            device_id_type=mesh_id,
+        )
+
+    def head_copy(s, source_s):
+        return pltpu.make_async_remote_copy(
+            src_ref=field_ref.at[pl.ds(s * thick, thick)],
+            dst_ref=head_out.at[source_s],
+            send_sem=head_send.at[s],
+            recv_sem=head_recv.at[source_s],
+            device_id=(s, me_e),
+            device_id_type=mesh_id,
+        )
+
+    keep_upd = pltpu.make_async_copy(
+        column_ref.at[pl.ds(me_e * members, members)],
+        update_out.at[:, pl.ds(me_e * rows, rows)],
+        local_sems.at[0],
+    )
+    keep_head = pltpu.make_async_copy(
+        field_ref.at[pl.ds(me_s * thick, thick)], head_out.at[me_s], local_sems.at[1]
+    )
+    for e in range(groups):
+        @pl.when(me_e != e)
+        def _():
+            upd_copy(e, me_e).start()
+    for s in range(slabs):
+        @pl.when(me_s != s)
+        def _():
+            head_copy(s, me_s).start()
+    keep_upd.start()
+    keep_head.start()
+    keep_upd.wait()
+    keep_head.wait()
+    for e in range(groups):
+        @pl.when(me_e != e)
+        def _():
+            upd_copy(e, me_e).wait_send()
+            upd_copy(e, e).wait_recv()
+    for s in range(slabs):
+        @pl.when(me_s != s)
+        def _():
+            head_copy(s, me_s).wait_send()
+            head_copy(s, s).wait_recv()
+
+
+def send_back(field, column, slabs):
+    planes, depth, across = field.shape
+    total, rows, _ = column.shape
+    groups = planes * depth // rows // slabs
+    members = total // groups
+    anywhere = pl.BlockSpec(memory_space=pl.ANY)
+    return pl.pallas_call(
+        return_kernel,
+        out_shape=(
+            jax.ShapeDtypeStruct((slabs, planes // slabs, depth, across), jnp.float32),
+            jax.ShapeDtypeStruct((members, groups * rows, across), jnp.float32),
+        ),
+        in_specs=[anywhere, anywhere],
+        out_specs=(anywhere, anywhere),
+        scratch_shapes=[
+            pltpu.SemaphoreType.DMA((slabs,)),
+            pltpu.SemaphoreType.DMA((slabs,)),
+            pltpu.SemaphoreType.DMA((groups,)),
+            pltpu.SemaphoreType.DMA((groups,)),
+            pltpu.SemaphoreType.DMA((2,)),
+        ],
+        compiler_params=pltpu.CompilerParams(collective_id=2, has_side_effects=True),
+    )(field, column)
 
 
 def shards(
@@ -228,7 +326,6 @@
     forcing = whole_storage * whole_head + source
     field = forward_pallas(whole_log[0], whole_storage, whole_head, forcing)
     picked = field.reshape(-1)[obs_cells]
-    head_field = lax.all_to_all(field[None], "space", 1, 0, tiled=True)
 
     obs_count = picked.shape[0]
     own_perturb = lax.dynamic_index_in_dim(perturb, lax.axis_index("space"), 0, keepdims=False)
@@ -245,11 +342,12 @@
     gain_rows = solve_pair(factor_lower, obs_values[None, :] + every_perturb - every_obs)
     mixing = jnp.dot(gain_rows, spread.T, precision=HIGHEST)
 
-    flat = log_perm.reshape(members, cell_count)
-    column = lax.all_to_all(flat, "ens", 1, 0, tiled=True)
-    change = jnp.dot(mixing, column, precision=HIGHEST)
-    new_column = column + change / (total_members - 1)
-    updated = lax.all_to_all(new_column, "ens", 0, 1, tiled=True).reshape(log_perm.shape)
+    slab_rows = planes * depth
+    band = lax.all_to_all(log_perm.reshape(members, slab_rows, across), "ens", 1, 0, tiled=True)
+    change = jnp.einsum("jk,kry->jry", mixing, band, precision=HIGHEST)
+    new_band = band + change / (total_members - 1)
+    head_field, updated = send_back(field, new_band, n_space)
+    updated = updated.reshape(log_perm.shape)
     return (head_field, updated)
 
 

time: 266 us -> 280 us (1.053)
  the two profiles are of different devices: /device:TPU:25 before, /device:TPU:104 now
where the time goes in v7:
time: 280 us; the launch traced here: 279 us
  Pallas kernels  143 us (51%)
  waiting for transfers between devices  59.4 us (21%)
  local copies, waits for them, and re-layouts  24.1 us (9%)
  other arithmetic  22 us (8%)
  between operations  14.8 us (5%)
  starting transfers between devices  12.3 us (4%)
  matrix products  3.99 us (1%)
    pallas_call x1, Pallas kernels, send_back(): pl.pallas_call(return_kernel, out_shape=(jax.ShapeDtypeStruct((slabs, pla...  68.3 us
    pallas_call x1, Pallas kernels, forward_pallas(): pl.pallas_call(forward_kernel, out_shape=jax.ShapeDtypeStruct((planes, de...  58.8 us
    all_gather x1, waiting for transfers between devices, shards(): lax.all_gather(jnp.where(core == 0, storage, head_init), 'space', axis=0,...  48.3 us
    pallas_call x1, Pallas kernels, gather_rows(): pl.pallas_call(gather_kernel, out_shape=jax.ShapeDtypeStruct((total,) + r...  15.7 us
    unnamed x26, local copies, waits for them, and re-layouts  14.3 us
    all_to_all x1, waiting for transfers between devices, shards(): whole_log = lax.all_to_all(log_perm, 'space', 0, 1, tiled=True)  11.1 us
    all_to_all x1, starting transfers between devices, shards(): whole_log = lax.all_to_all(log_perm, 'space', 0, 1, tiled=True)  6.36 us
    all_to_all x1, starting transfers between devices, shards(): lax.all_to_all(log_perm.reshape(members, slab_rows, across), 'ens', 1, 0,...  5.86 us
  transfers between devices with their start and end apart: 4, of which 2 were waited for; matrix products, arithmetic and copies ran while one was open for 7% of the time, Pallas kernels for 0%

profile of v7, /device:TPU:104, one launch (start us, length us, event | category | flops | bytes accessed | tf_op | source)
XLA Modules:
  0.0 279.4 jit_solution(5659178590443852780)
XLA Ops:
  7.2 0.0 all-gather.2.cloned.1.call-start
  7.2 1.7 broadcast_select_fusion.2
  8.9 0.0 all-gather.2.cloned.1.call-update
  8.9 4.1 %copy.21 = f32[8,2,64,512]{3,0,2,1:T(8,128)} copy(f32[8,2,64,512]{3,2,1,0:T(8,128)} %param.14) | data formatting | bytes 4194304 | tf_op args[0]
  13.1 5.9 %all-to-all-start.1 = ((f32[8,128,512]{2,0,1:T(8,128)}), f32[8,128,512]{2,0,1:T(8,128)S(1)}, u32[]{:S(2)}, u32[]{:S(2)}) async-start(f32[8,128,512]{2,0,1:T(8,128)} %bitcast.42), calls=%async_computation.1 | async-start | bytes 4194304 | tf_op jit(solution)/shard_map/all_to_all | solution.py:346
  18.9 48.3 %all-gather.2.cloned.1.call-done = f32[16,64,512]{2,1,0:T(8,128)} async-done(((f32[2,64,512]{2,1,0:T(8,128)}), f32[16,64,512]{2,1,0:T(8,128)}) %all-gather.2.cloned.1.call-update) | async-done | bytes 2097168 | tf_op jit(solution)/shard_map/all_gather | solution.py:315
  67.2 0.0 collective-permute-start
  67.2 0.0 all-to-all-done.1
  67.3 1.3 copy-done.1
  68.6 6.4 %all-to-all-start = ((f32[8,2,64,512]{3,2,1,0:T(8,128)}), f32[8,2,64,512]{3,2,1,0:T(8,128)}, u32[]{:S(2)}, u32[]{:S(2)}) async-start(f32[8,2,64,512]{3,2,1,0:T(8,128)} %param.14), calls=%async_computation | async-start | bytes 4194304 | tf_op jit(solution)/shard_map/all_to_all | solution.py:313
  74.9 0.0 copy-done.8
  74.9 2.2 scatter_custom_fusion
  77.2 1.8 reshape.121
  79.6 1.3 dynamic-slice_bitcast_fusion
  80.9 0.0 copy-done.9
  80.9 0.6 pad_clamp_fusion
  81.5 0.0 copy-done.10
  81.5 0.5 broadcast_divide_fusion
  82.0 4.7 %copy.23 = f32[16,8,8,512]{3,2,1,0:T(8,128)} copy(f32[16,8,8,512]{3,1,2,0:T(8,128)} %bitcast.41) | data formatting | bytes 4194304 | tf_op jit(solution)/shard_map/all_to_all | solution.py:346
  86.7 0.0 collective-permute-done
  86.7 4.9 %multiply_add_fusion = (f32[16,64,512]{2,1,0:T(8,128)}, f32[16,64,512]{2,1,0:T(8,128)}, f32[16,64,512]{2,1,0:T(8,128)}) fusion(f32[16,64,512]{2,1,0:T(8,128)S(1)} %reshape.121, f32[16,64,512]{2,1,0:T(8,128)} %collective-permute-done, f32[16,64,512]{2,1,0:T(8,128)S(1)} %copy-done.2, pred[]{:T(512)S(6)} %eq.12), kind=kLoop, calls=%fused_computation.6 | loop fusion | flops 2097152 | bytes 12582913 | tf_op jit(solution)/shard_map/add | solution.py:326
  91.6 11.1 %all-to-all-done = f32[8,2,64,512]{3,2,1,0:T(8,128)} async-done(((f32[8,2,64,512]{3,2,1,0:T(8,128)}), f32[8,2,64,512]{3,2,1,0:T(8,128)}, u32[]{:S(2)}, u32[]{:S(2)}) %all-to-all-start) | async-done | bytes 2097184 | tf_op jit(solution)/shard_map/all_to_all | solution.py:313
  102.7 58.8 %shard_map.113.field_ref = f32[16,64,512]{2,1,0:T(8,128)} custom-call(f32[16,64,512]{2,1,0:T(8,128)} %bitcast.log_ref, f32[16,64,512]{2,1,0:T(8,128)} %get-tuple-element.32.sto_ref, f32[16,64,512]{2,1,0:T(8,128)} %get-tuple-element.31.init_ref, f32[16,64,512]{2,1,0:T(8,128)} %get-tuple-element.30.forc_ref), custom_call_target="tpu_custom_call" | custom-call | tf_op jit(solution)/shard_map/pallas_call | solution.py:112
  161.5 3.6 %copy.30 = f32[128,4,8,128]{3,1,2,0:T(4,128)} copy(f32[128,4,8,128]{3,2,1,0:T(8,128)} %bitcast.40) | data formatting | bytes 4194304
  165.1 1.7 gather_fusion
  166.8 0.3 scatter.9.row_ref
  167.1 0.6 copy-done.4
  167.7 15.7 %shard_map.114 = f32[128,8,128]{2,1,0:T(8,128)} custom-call(f32[1,8,128]{2,1,0:T(8,128)} %copy-done.4), custom_call_target="tpu_custom_call" | custom-call | tf_op jit(solution)/shard_map/pallas_call | solution.py:182
  183.4 0.0 copy-done.6
  183.4 1.4 fusion.14
  184.8 1.1 broadcast_subtract_fusion
  185.9 0.3 convolution_multiply_fusion
  186.2 0.1 copy.25
  186.3 0.1 fusion.13
  186.3 2.9 %cholesky.16 = f32[32,32]{1,0:T(8,128)S(1)} custom-call(f32[32,32]{1,0:T(8,128)S(1)} %fusion.13), custom_call_target="Cholesky" | custom-call | tf_op jit(solution)/shard_map/jit(cholesky)/cholesky | solution.py:341
  189.3 0.6 compare_reduce_fusion
  189.9 0.7 fusion.7
  190.6 2.4 custom-call.8
  193.0 0.3 fusion.10
  193.3 0.2 fusion.8
  193.5 0.3 convolution_bitcast_fusion
  193.8 0.0 copy-done
  193.8 3.0 %fusion.1 = f32[128,8,512]{2,0,1:T(8,128)S(1)} fusion(f32[128,128,1]{1,0,2:T(8,128)S(1)} %convolution_bitcast_fusion, f32[128,8,512]{2,1,0:T(8,128)S(1)} %bitcast.39), kind=kOutput, calls=%fused_computation.4 | convolution fusion | flops 805306368 | bytes 4259840 | tf_op jit(solution)/shard_map/jk,kry->jry/dot_general | solution.py:347
  196.8 2.8 %fusion.column_ref = f32[128,8,512]{2,1,0:T(8,128)} fusion(f32[128,8,512]{2,0,1:T(8,128)S(1)} %fusion.1, f32[16,8,8,512]{3,2,1,0:T(8,128)S(1)} %copy-done), kind=kLoop, calls=%fused_computation.3 | loop fusion | flops 1048576 | bytes 6291456 | tf_op jit(solution)/shard_map/add | solution.py:348
  199.6 68.3 %shard_map.115 = (f32[8,2,64,512]{3,2,1,0:T(8,128)}, f32[8,128,512]{2,1,0:T(8,128)}) custom-call(f32[16,64,512]{2,1,0:T(8,128)} %shard_map.113.field_ref, f32[128,8,512]{2,1,0:T(8,128)} %fusion.column_ref), custom_call_target="tpu_custom_call" | custom-call | tf_op jit(solution)/shard_map/pallas_call | solution.py:275
  268.0 3.3 %copy.40 = f32[8,2,64,512]{3,2,1,0:T(8,128)} copy(f32[8,2,64,512]{3,2,1,0:T(8,128)} %get-tuple-element.38) | data formatting | bytes 4194304
  271.2 0.0 copy-done.3
  271.2 1.3 copy.41
  (19 shorter events, 0.1 us)
Async XLA Ops:
  7.2 60.1 %all-gather.2.cloned.1.call-start = ((), (), s32[]{:S(2)}) async-start(), calls=%async_computation.2 | async-start | bytes 2359296 | tf_op jit(solution)/shard_map/all_gather | solution.py:315
  13.1 54.2 %all-to-all-start.1 = ((f32[8,128,512]{2,0,1:T(8,128)}), f32[8,128,512]{2,0,1:T(8,128)S(1)}, u32[]{:S(2)}, u32[]{:S(2)}) async-start(f32[8,128,512]{2,0,1:T(8,128)} %bitcast.42), calls=%async_computation.1 | async-start | bytes 4194304 | tf_op jit(solution)/shard_map/all_to_all | solution.py:346
  18.9 56.0 %copy-start.8 = (s32[16]{0:T(128)S(1)}, s32[16]{0:T(128)}, u32[]{:S(2)}) copy-start(s32[16]{0:T(128)} %param.17) | copy-start | bytes 196
  67.2 19.5 %collective-permute-start = (f32[16,64,512]{2,1,0:T(8,128)}, f32[16,64,512]{2,1,0:T(8,128)}, u32[]{:S(2)}, u32[]{:S(2)}) collective-permute-start(f32[16,64,512]{2,1,0:T(8,128)} %all-gather.2.cloned.1.call-done), channel_id=1, source_target_pairs={{0,1},{1,0},{2,3},{3,2},{4,5},{5,4},{6,7},{7,6},{8,9},{9,8},{10,11... | collective-permute-start | bytes 6291464 | tf_op jit(solution)/shard_map/ppermute | solution.py:317
  67.2 1.3 copy-start.1
  68.6 34.1 %all-to-all-start = ((f32[8,2,64,512]{3,2,1,0:T(8,128)}), f32[8,2,64,512]{3,2,1,0:T(8,128)}, u32[]{:S(2)}, u32[]{:S(2)}) async-start(f32[8,2,64,512]{3,2,1,0:T(8,128)} %param.14), calls=%async_computation | async-start | bytes 4194304 | tf_op jit(solution)/shard_map/all_to_all | solution.py:313
  77.1 3.7 %copy-start.9 = (s32[32]{0:T(128)S(1)}, s32[32]{0:T(128)}, u32[]{:S(2)}) copy-start(s32[32]{0:T(128)} %param.19) | copy-start | bytes 388
  77.1 4.3 %copy-start.10 = (f32[32]{0:T(128)S(1)}, f32[32]{0:T(128)}, u32[]{:S(2)}) copy-start(f32[32]{0:T(128)} %param.21) | copy-start | bytes 388
  82.0 4.7 %copy-start.2 = (f32[16,64,512]{2,1,0:T(8,128)S(1)}, f32[16,64,512]{2,1,0:T(8,128)}, u32[]{:S(2)}) copy-start(f32[16,64,512]{2,1,0:T(8,128)} %all-gather.2.cloned.1.call-done) | copy-start | bytes 6291460
  161.5 5.3 %copy-start.7 = (f32[1,1,32]{2,1,0:T(1,128)S(1)}, f32[1,1,32]{2,1,0:T(1,128)}, u32[]{:S(2)}) copy-start(f32[1,1,32]{2,1,0:T(1,128)} %dynamic-slice_bitcast_fusion) | copy-start | bytes 388
  161.5 21.9 %copy-start.6 = (f32[32]{0:T(128)S(1)}, f32[32]{0:T(128)}, u32[]{:S(2)}) copy-start(f32[32]{0:T(128)} %param.20) | copy-start | bytes 388
  161.5 24.8 %copy-start.5 = (f32[32]{0:T(128)S(1)}, f32[32]{0:T(128)}, u32[]{:S(2)}) copy-start(f32[32]{0:T(128)} %broadcast_divide_fusion) | copy-start | bytes 388
  161.5 32.3 %copy-start = (f32[16,8,8,512]{3,2,1,0:T(8,128)S(1)}, f32[16,8,8,512]{3,2,1,0:T(8,128)}, u32[]{:S(2)}) copy-start(f32[16,8,8,512]{3,2,1,0:T(8,128)} %copy.23) | copy-start | bytes 6291460
  167.1 0.6 copy-start.4
  267.9 3.3 %copy-start.3 = (f32[8,128,512]{2,1,0:T(8,128)S(1)}, f32[8,128,512]{2,1,0:T(8,128)}, u32[]{:S(2)}) copy-start(f32[8,128,512]{2,1,0:T(8,128)} %get-tuple-element.29) | copy-start | bytes 6291460
Sparse Core Ops, SparseCore 0:
  10.9 56.2 all-gather.1

commit v8 on v7

--- a/solution.py
+++ b/solution.py
@@ -193,9 +193,7 @@
     )(row)
 
 
-def return_kernel(field_ref, column_ref, head_out, update_out,
-                  head_send, head_recv, upd_send, upd_recv, local_sems):
-    slabs, thick = head_out.shape[0], head_out.shape[1]
+def return_kernel(column_ref, update_out, upd_send, upd_recv, local_sem):
     groups = update_out.shape[1] // column_ref.shape[1]
     rows = column_ref.shape[1]
     members = update_out.shape[0]
@@ -204,15 +202,11 @@
     mesh_id = pl.DeviceIdType.MESH
 
     barrier = pltpu.get_barrier_semaphore()
-    for s in range(slabs):
-        @pl.when(me_s != s)
-        def _():
-            pl.semaphore_signal(barrier, 1, device_id=(s, me_e), device_id_type=mesh_id)
     for e in range(groups):
         @pl.when(me_e != e)
         def _():
             pl.semaphore_signal(barrier, 1, device_id=(me_s, e), device_id_type=mesh_id)
-    pl.semaphore_wait(barrier, slabs - 1 + groups - 1)
+    pl.semaphore_wait(barrier, groups - 1)
 
     def upd_copy(e, source_e):
         return pltpu.make_async_remote_copy(
@@ -224,71 +218,41 @@
             device_id_type=mesh_id,
         )
 
-    def head_copy(s, source_s):
-        return pltpu.make_async_remote_copy(
-            src_ref=field_ref.at[pl.ds(s * thick, thick)],
-            dst_ref=head_out.at[source_s],
-            send_sem=head_send.at[s],
-            recv_sem=head_recv.at[source_s],
-            device_id=(s, me_e),
-            device_id_type=mesh_id,
-        )
-
     keep_upd = pltpu.make_async_copy(
         column_ref.at[pl.ds(me_e * members, members)],
         update_out.at[:, pl.ds(me_e * rows, rows)],
-        local_sems.at[0],
-    )
-    keep_head = pltpu.make_async_copy(
-        field_ref.at[pl.ds(me_s * thick, thick)], head_out.at[me_s], local_sems.at[1]
+        local_sem,
     )
     for e in range(groups):
         @pl.when(me_e != e)
         def _():
             upd_copy(e, me_e).start()
-    for s in range(slabs):
-        @pl.when(me_s != s)
-        def _():
-            head_copy(s, me_s).start()
     keep_upd.start()
-    keep_head.start()
     keep_upd.wait()
-    keep_head.wait()
     for e in range(groups):
         @pl.when(me_e != e)
         def _():
             upd_copy(e, me_e).wait_send()
             upd_copy(e, e).wait_recv()
-    for s in range(slabs):
-        @pl.when(me_s != s)
-        def _():
-            head_copy(s, me_s).wait_send()
-            head_copy(s, s).wait_recv()
-
-
-def send_back(field, column, slabs):
-    planes, depth, across = field.shape
-    total, rows, _ = column.shape
-    groups = planes * depth // rows // slabs
+
+
+def send_back(column, slab_rows):
+    total, rows, across = column.shape
+    groups = slab_rows // rows
     members = total // groups
     anywhere = pl.BlockSpec(memory_space=pl.ANY)
     return pl.pallas_call(
         return_kernel,
-        out_shape=(
-            jax.ShapeDtypeStruct((slabs, planes // slabs, depth, across), jnp.float32),
-            jax.ShapeDtypeStruct((members, groups * rows, across), jnp.float32),
-        ),
-        in_specs=[anywhere, anywhere],
-        out_specs=(anywhere, anywhere),
+        out_shape=jax.ShapeDtypeStruct((members, slab_rows, across), jnp.float32),
+        in_specs=[anywhere],
+        out_specs=anywhere,
         scratch_shapes=[
-            pltpu.SemaphoreType.DMA((slabs,)),
-            pltpu.SemaphoreType.DMA((slabs,)),
             pltpu.SemaphoreType.DMA((groups,)),
             pltpu.SemaphoreType.DMA((groups,)),
-            pltpu.SemaphoreType.DMA((2,)),
+            pltpu.SemaphoreType.DMA,
         ],
         compiler_params=pltpu.CompilerParams(collective_id=2, has_side_effects=True),
-    )(field, column)
+    )(column)
 
 
 def shards(
@@ -326,6 +290,7 @@
     forcing = whole_storage * whole_head + source
     field = forward_pallas(whole_log[0], whole_storage, whole_head, forcing)
     picked = field.reshape(-1)[obs_cells]
+    head_field = lax.all_to_all(field[None], "space", 1, 0, tiled=True)
 
     obs_count = picked.shape[0]
     own_perturb = lax.dynamic_index_in_dim(perturb, lax.axis_index("space"), 0, keepdims=False)
@@ -346,7 +311,7 @@
     band = lax.all_to_all(log_perm.reshape(members, slab_rows, across), "ens", 1, 0, tiled=True)
     change = jnp.einsum("jk,kry->jry", mixing, band, precision=HIGHEST)
     new_band = band + change / (total_members - 1)
-    head_field, updated = send_back(field, new_band, n_space)
+    updated = send_back(new_band, slab_rows)
     updated = updated.reshape(log_perm.shape)
     return (head_field, updated)
 

time: 280 us -> 260 us (0.929)
  the two profiles are of different devices: /device:TPU:104 before, /device:TPU:25 now
where the time goes in v8:
time: 260 us; the launch traced here: 259 us
  Pallas kernels  117 us (45%)
  waiting for transfers between devices  62.4 us (24%)
  other arithmetic  22.1 us (8%)
  local copies, waits for them, and re-layouts  21.7 us (8%)
  starting transfers between devices  16.1 us (6%)
  between operations  14.9 us (6%)
  matrix products  3.99 us (2%)
    pallas_call x1, Pallas kernels, forward_pallas(): pl.pallas_call(forward_kernel, out_shape=jax.ShapeDtypeStruct((planes, de...  58.8 us
    all_gather x1, waiting for transfers between devices, shards(): lax.all_gather(jnp.where(core == 0, storage, head_init), 'space', axis=0,...  50.5 us
    pallas_call x1, Pallas kernels, send_back(): pl.pallas_call(return_kernel, out_shape=jax.ShapeDtypeStruct((members, sl...  40.6 us
    pallas_call x1, Pallas kernels, gather_rows(): pl.pallas_call(gather_kernel, out_shape=jax.ShapeDtypeStruct((total,) + r...  17.9 us
    unnamed x26, local copies, waits for them, and re-layouts  12.8 us
    all_to_all x1, waiting for transfers between devices, shards(): whole_log = lax.all_to_all(log_perm, 'space', 0, 1, tiled=True)  11.9 us
    all_to_all x1, starting transfers between devices, shards(): lax.all_to_all(log_perm.reshape(members, slab_rows, across), 'ens', 1, 0,...  5.95 us
  transfers between devices with their start and end apart: 5, of which 2 were waited for; matrix products, arithmetic and copies ran while one was open for 13% of the time, Pallas kernels for 16%

profile of v8, /device:TPU:25, one launch (start us, length us, event | category | flops | bytes accessed | tf_op | source)
XLA Modules:
  0.0 258.5 jit_solution(5076127371803962904)
XLA Ops:
  7.2 0.0 all-gather.2.cloned.1.call-start
  7.2 1.7 broadcast_select_fusion.2
  8.9 0.0 all-gather.2.cloned.1.call-update
  8.9 4.1 %copy.22 = f32[8,2,64,512]{3,0,2,1:T(8,128)} copy(f32[8,2,64,512]{3,2,1,0:T(8,128)} %param.14) | data formatting | bytes 4194304 | tf_op args[0]
  13.1 5.9 %all-to-all-start.2 = ((f32[8,128,512]{2,0,1:T(8,128)}), f32[8,128,512]{2,0,1:T(8,128)S(1)}, u32[]{:S(2)}, u32[]{:S(2)}) async-start(f32[8,128,512]{2,0,1:T(8,128)} %bitcast.47), calls=%async_computation.2 | async-start | bytes 4194304 | tf_op jit(solution)/shard_map/all_to_all | solution.py:311
  19.0 50.5 %all-gather.2.cloned.1.call-done = f32[16,64,512]{2,1,0:T(8,128)} async-done(((f32[2,64,512]{2,1,0:T(8,128)}), f32[16,64,512]{2,1,0:T(8,128)}) %all-gather.2.cloned.1.call-update) | async-done | bytes 2097168 | tf_op jit(solution)/shard_map/all_gather | solution.py:279
  69.6 1.1 collective-permute-start
  70.6 0.0 all-to-all-done.2
  70.7 1.3 copy-done.1
  72.0 4.4 %all-to-all-start = ((f32[8,2,64,512]{3,2,1,0:T(8,128)}), f32[8,2,64,512]{3,2,1,0:T(8,128)}, u32[]{:S(2)}, u32[]{:S(2)}) async-start(f32[8,2,64,512]{3,2,1,0:T(8,128)} %param.14), calls=%async_computation | async-start | bytes 4194304 | tf_op jit(solution)/shard_map/all_to_all | solution.py:277
  76.3 0.0 copy-done.8
  76.4 2.2 scatter_custom_fusion
  78.6 1.8 reshape.124
  81.0 1.3 dynamic-slice_bitcast_fusion
  82.2 0.0 copy-done.9
  82.3 0.6 pad_clamp_fusion
  82.9 0.0 copy-done.10
  82.9 0.6 broadcast_divide_fusion
  83.5 4.7 %copy.24 = f32[16,8,8,512]{3,2,1,0:T(8,128)} copy(f32[16,8,8,512]{3,1,2,0:T(8,128)} %bitcast.46) | data formatting | bytes 4194304 | tf_op jit(solution)/shard_map/all_to_all | solution.py:311
  88.2 0.0 collective-permute-done
  88.2 4.9 %multiply_add_fusion = (f32[16,64,512]{2,1,0:T(8,128)}, f32[16,64,512]{2,1,0:T(8,128)}, f32[16,64,512]{2,1,0:T(8,128)}) fusion(f32[16,64,512]{2,1,0:T(8,128)S(1)} %reshape.124, f32[16,64,512]{2,1,0:T(8,128)} %collective-permute-done, f32[16,64,512]{2,1,0:T(8,128)S(1)} %copy-done.3, pred[]{:T(512)S(6)} %eq.12), kind=kLoop, calls=%fused_computation.6 | loop fusion | flops 2097152 | bytes 12582913 | tf_op jit(solution)/shard_map/add | solution.py:290
  93.1 11.9 %all-to-all-done = f32[8,2,64,512]{3,2,1,0:T(8,128)} async-done(((f32[8,2,64,512]{3,2,1,0:T(8,128)}), f32[8,2,64,512]{3,2,1,0:T(8,128)}, u32[]{:S(2)}, u32[]{:S(2)}) %all-to-all-start) | async-done | bytes 2097184 | tf_op jit(solution)/shard_map/all_to_all | solution.py:277
  105.0 58.8 %shard_map.113 = f32[16,64,512]{2,1,0:T(8,128)} custom-call(f32[16,64,512]{2,1,0:T(8,128)} %bitcast.log_ref, f32[16,64,512]{2,1,0:T(8,128)} %get-tuple-element.28.sto_ref, f32[16,64,512]{2,1,0:T(8,128)} %get-tuple-element.27.init_ref, f32[16,64,512]{2,1,0:T(8,128)} %get-tuple-element.26.forc_ref), custom_call_target="tpu_custom_call" | custom-call | tf_op jit(solution)/shard_map/pallas_call | solution.py:112
  163.7 2.1 copy.31
  165.9 0.8 gather_fusion
  166.7 0.3 scatter.9.row_ref
  167.0 0.6 copy-done.4
  167.6 17.9 %shard_map.114 = f32[128,8,128]{2,1,0:T(8,128)} custom-call(f32[1,8,128]{2,1,0:T(8,128)} %copy-done.4), custom_call_target="tpu_custom_call" | custom-call | tf_op jit(solution)/shard_map/pallas_call | solution.py:182
  185.6 1.4 fusion.14
  187.0 1.1 broadcast_subtract_fusion
  188.1 0.3 convolution_multiply_fusion
  188.3 0.1 copy.26
  188.4 4.7 %all-to-all-start.1 = ((f32[1,16,64,512]{3,2,0,1:T(8,128)}), f32[1,16,64,512]{3,2,0,1:T(8,128)}, u32[]{:S(2)}, u32[]{:S(2)}) async-start(f32[1,16,64,512]{3,2,0,1:T(8,128)} %bitcast.45), calls=%async_computation.1 | async-start | bytes 4194304 | tf_op jit(solution)/shard_map/all_to_all | solution.py:293
  193.1 0.1 fusion.13
  193.2 2.9 %cholesky.16 = f32[32,32]{1,0:T(8,128)S(1)} custom-call(f32[32,32]{1,0:T(8,128)S(1)} %fusion.13), custom_call_target="Cholesky" | custom-call | tf_op jit(solution)/shard_map/jit(cholesky)/cholesky | solution.py:306
  196.1 0.6 compare_reduce_fusion
  196.8 0.7 fusion.7
  197.4 2.4 custom-call.8
  199.9 0.3 fusion.10
  200.1 0.2 fusion.8
  200.3 0.3 convolution_bitcast_fusion
  200.6 3.0 %fusion.1 = f32[128,8,512]{2,0,1:T(8,128)S(1)} fusion(f32[128,128,1]{1,0,2:T(8,128)S(1)} %convolution_bitcast_fusion, f32[128,8,512]{2,1,0:T(8,128)S(1)} %bitcast.43), kind=kOutput, calls=%fused_computation.4 | convolution fusion | flops 805306368 | bytes 4259840 | tf_op jit(solution)/shard_map/jk,kry->jry/dot_general | solution.py:312
  203.6 2.8 %fusion.column_ref = f32[128,8,512]{2,1,0:T(8,128)} fusion(f32[128,8,512]{2,0,1:T(8,128)S(1)} %fusion.1, f32[16,8,8,512]{3,2,1,0:T(8,128)S(1)} %copy-done), kind=kLoop, calls=%fused_computation.3 | loop fusion | flops 1048576 | bytes 6291456 | tf_op jit(solution)/shard_map/add | solution.py:313
  206.4 40.6 %shard_map.115 = f32[8,128,512]{2,1,0:T(8,128)} custom-call(f32[128,8,512]{2,1,0:T(8,128)} %fusion.column_ref), custom_call_target="tpu_custom_call" | custom-call | tf_op jit(solution)/shard_map/pallas_call | solution.py:244
  247.0 0.0 all-to-all-done.1
  247.0 3.3 %copy.41 = f32[8,2,64,512]{3,2,1,0:T(8,128)} copy(f32[8,2,64,512]{3,2,1,0:T(8,128)} %bitcast.3) | data formatting | bytes 4194304
  250.3 0.0 copy-done.2
  250.3 1.3 copy.42
  (21 shorter events, 0.1 us)
Async XLA Ops:
  7.2 62.4 %all-gather.2.cloned.1.call-start = ((), (), s32[]{:S(2)}) async-start(), calls=%async_computation.3 | async-start | bytes 2359296 | tf_op jit(solution)/shard_map/all_gather | solution.py:279
  13.1 57.6 %all-to-all-start.2 = ((f32[8,128,512]{2,0,1:T(8,128)}), f32[8,128,512]{2,0,1:T(8,128)S(1)}, u32[]{:S(2)}, u32[]{:S(2)}) async-start(f32[8,128,512]{2,0,1:T(8,128)} %bitcast.47), calls=%async_computation.2 | async-start | bytes 4194304 | tf_op jit(solution)/shard_map/all_to_all | solution.py:311
  19.0 57.3 %copy-start.8 = (s32[16]{0:T(128)S(1)}, s32[16]{0:T(128)}, u32[]{:S(2)}) copy-start(s32[16]{0:T(128)} %param.17) | copy-start | bytes 196
  69.6 18.6 %collective-permute-start = (f32[16,64,512]{2,1,0:T(8,128)}, f32[16,64,512]{2,1,0:T(8,128)}, u32[]{:S(2)}, u32[]{:S(2)}) collective-permute-start(f32[16,64,512]{2,1,0:T(8,128)} %all-gather.2.cloned.1.call-done), channel_id=1, source_target_pairs={{0,1},{1,0},{2,3},{3,2},{4,5},{5,4},{6,7},{7,6},{8,9},{9,8},{10,11... | collective-permute-start | bytes 6291464 | tf_op jit(solution)/shard_map/ppermute | solution.py:281
  70.6 1.3 copy-start.1
  72.0 33.0 %all-to-all-start = ((f32[8,2,64,512]{3,2,1,0:T(8,128)}), f32[8,2,64,512]{3,2,1,0:T(8,128)}, u32[]{:S(2)}, u32[]{:S(2)}) async-start(f32[8,2,64,512]{3,2,1,0:T(8,128)} %param.14), calls=%async_computation | async-start | bytes 4194304 | tf_op jit(solution)/shard_map/all_to_all | solution.py:277
  78.6 3.7 %copy-start.9 = (s32[32]{0:T(128)S(1)}, s32[32]{0:T(128)}, u32[]{:S(2)}) copy-start(s32[32]{0:T(128)} %param.19) | copy-start | bytes 388
  78.6 4.3 %copy-start.10 = (f32[32]{0:T(128)S(1)}, f32[32]{0:T(128)}, u32[]{:S(2)}) copy-start(f32[32]{0:T(128)} %param.21) | copy-start | bytes 388
  83.5 4.7 %copy-start.3 = (f32[16,64,512]{2,1,0:T(8,128)S(1)}, f32[16,64,512]{2,1,0:T(8,128)}, u32[]{:S(2)}) copy-start(f32[16,64,512]{2,1,0:T(8,128)} %all-gather.2.cloned.1.call-done) | copy-start | bytes 6291460
  163.7 3.0 %copy-start.7 = (f32[1,1,32]{2,1,0:T(1,128)S(1)}, f32[1,1,32]{2,1,0:T(1,128)}, u32[]{:S(2)}) copy-start(f32[1,1,32]{2,1,0:T(1,128)} %dynamic-slice_bitcast_fusion) | copy-start | bytes 388
  163.7 21.8 %copy-start.6 = (f32[32]{0:T(128)S(1)}, f32[32]{0:T(128)}, u32[]{:S(2)}) copy-start(f32[32]{0:T(128)} %param.20) | copy-start | bytes 388
  167.0 0.6 copy-start.4
  188.4 4.7 %copy-start.5 = (f32[32]{0:T(128)S(1)}, f32[32]{0:T(128)}, u32[]{:S(2)}) copy-start(f32[32]{0:T(128)} %broadcast_divide_fusion) | copy-start | bytes 388
  188.4 12.2 %copy-start = (f32[16,8,8,512]{3,2,1,0:T(8,128)S(1)}, f32[16,8,8,512]{3,2,1,0:T(8,128)}, u32[]{:S(2)}) copy-start(f32[16,8,8,512]{3,2,1,0:T(8,128)} %copy.24) | copy-start | bytes 6291460
  188.4 58.6 %all-to-all-start.1 = ((f32[1,16,64,512]{3,2,0,1:T(8,128)}), f32[1,16,64,512]{3,2,0,1:T(8,128)}, u32[]{:S(2)}, u32[]{:S(2)}) async-start(f32[1,16,64,512]{3,2,0,1:T(8,128)} %bitcast.45), calls=%async_computation.1 | async-start | bytes 4194304 | tf_op jit(solution)/shard_map/all_to_all | solution.py:293
  247.0 3.3 %copy-start.2 = (f32[8,128,512]{2,1,0:T(8,128)S(1)}, f32[8,128,512]{2,1,0:T(8,128)}, u32[]{:S(2)}) copy-start(f32[8,128,512]{2,1,0:T(8,128)} %shard_map.115) | copy-start | bytes 6291460
Sparse Core Ops, SparseCore 0:
  10.9 58.5 all-gather.1

commit v9 on v8

--- a/solution.py
+++ b/solution.py
@@ -275,6 +275,10 @@
     grid_planes = planes * n_space
 
     whole_log = lax.all_to_all(log_perm, "space", 0, 1, tiled=True)
+    slab_rows = planes * depth
+    by_rows, whole_log = lax.optimization_barrier(
+        (log_perm.reshape(members, slab_rows, across), whole_log)
+    )
     core = lax.axis_index("ens") % 2
     mine = lax.all_gather(jnp.where(core == 0, storage, head_init), "space", axis=0, tiled=True)
     pairs = [(e, e ^ 1) for e in range(n_ens)]
@@ -307,8 +311,7 @@
     gain_rows = solve_pair(factor_lower, obs_values[None, :] + every_perturb - every_obs)
     mixing = jnp.dot(gain_rows, spread.T, precision=HIGHEST)
 
-    slab_rows = planes * depth
-    band = lax.all_to_all(log_perm.reshape(members, slab_rows, across), "ens", 1, 0, tiled=True)
+    band = lax.all_to_all(by_rows, "ens", 1, 0, tiled=True)
     change = jnp.einsum("jk,kry->jry", mixing, band, precision=HIGHEST)
     new_band = band + change / (total_members - 1)
     updated = send_back(new_band, slab_rows)

time: 260 us -> 279 us (1.073)
  waiting for transfers between devices: 62.4 us -> 79.2 us
    all_to_all x1, waiting for transfers between devices: 0.01 us -> 18.7 us  [shards(): band = lax.all_to_all(by_rows, 'ens', 1, 0, tiled=True)]
    all_to_all x1, waiting for transfers between devices: 11.9 us -> 0.01 us  [shards(): whole_log = lax.all_to_all(log_perm, 'space', 0, 1, tiled=True)]
    all_gather x1, waiting for transfers between devices: 50.5 us -> 60.4 us  [shards(): lax.all_gather(jnp.where(core == 0, storage, head_init), 'space', axis=0,...]
    all_to_all x1, starting transfers between devices: 4.35 us -> 7.51 us  [shards(): whole_log = lax.all_to_all(log_perm, 'space', 0, 1, tiled=True)]
  transfers between devices with their start and end apart: 5 -> 5, of which waited for: 2 -> 2; matrix products, arithmetic and copies ran while one was open for 13% -> 10% of each run, Pallas kernels for 16% -> 15%
where the time goes in v9:
time: 279 us; the launch traced here: 278 us
  Pallas kernels  118 us (42%)
  waiting for transfers between devices  79.2 us (28%)
  other arithmetic  22.1 us (8%)
  local copies, waits for them, and re-layouts  21.7 us (8%)
  starting transfers between devices  17.9 us (6%)
  between operations  14.9 us (5%)
  matrix products  4 us (1%)
    all_gather x1, waiting for transfers between devices, shards(): lax.all_gather(jnp.where(core == 0, storage, head_init), 'space', axis=0,...  60.4 us
    pallas_call x1, Pallas kernels, forward_pallas(): pl.pallas_call(forward_kernel, out_shape=jax.ShapeDtypeStruct((planes, de...  58.8 us
    pallas_call x1, Pallas kernels, send_back(): pl.pallas_call(return_kernel, out_shape=jax.ShapeDtypeStruct((members, sl...  41 us
    all_to_all x1, waiting for transfers between devices, shards(): band = lax.all_to_all(by_rows, 'ens', 1, 0, tiled=True)  18.7 us
    pallas_call x1, Pallas kernels, gather_rows(): pl.pallas_call(gather_kernel, out_shape=jax.ShapeDtypeStruct((total,) + r...  18.6 us
    unnamed x26, local copies, waits for them, and re-layouts  12.8 us
    all_to_all x1, starting transfers between devices, shards(): whole_log = lax.all_to_all(log_perm, 'space', 0, 1, tiled=True)  7.51 us
  transfers between devices with their start and end apart: 5, of which 2 were waited for; matrix products, arithmetic and copies ran while one was open for 10% of the time, Pallas kernels for 15%

profile of v9, /device:TPU:25, one launch (start us, length us, event | category | flops | bytes accessed | tf_op | source)
XLA Modules:
  0.0 278.0 jit_solution(5867465020590202332)
XLA Ops:
  7.2 0.0 all-gather.2.cloned.1.call-start
  7.2 1.7 broadcast_select_fusion.2
  8.9 0.0 all-gather.2.cloned.1.call-update
  8.9 7.5 %all-to-all-start = ((f32[8,2,64,512]{3,2,1,0:T(8,128)}), f32[8,2,64,512]{3,2,1,0:T(8,128)S(1)}, u32[]{:S(2)}, u32[]{:S(2)}) async-start(f32[8,2,64,512]{3,2,1,0:T(8,128)} %param.14), calls=%async_computation | async-start | bytes 4194304 | tf_op jit(solution)/shard_map/all_to_all | solution.py:277
  16.5 60.4 %all-gather.2.cloned.1.call-done = f32[16,64,512]{2,1,0:T(8,128)} async-done(((f32[2,64,512]{2,1,0:T(8,128)}), f32[16,64,512]{2,1,0:T(8,128)}) %all-gather.2.cloned.1.call-update) | async-done | bytes 2097168 | tf_op jit(solution)/shard_map/all_gather | solution.py:283
  76.9 1.1 collective-permute-start
  78.0 4.1 %copy.21 = f32[8,2,64,512]{3,0,2,1:T(8,128)} copy(f32[8,2,64,512]{3,2,1,0:T(8,128)} %param.14) | data formatting | bytes 4194304 | tf_op args[0]
  82.1 0.0 all-to-all-done
  82.1 1.3 copy-done.1
  83.4 4.6 %all-to-all-start.2 = ((f32[8,128,512]{2,0,1:T(8,128)}), f32[8,128,512]{2,0,1:T(8,128)}, u32[]{:S(2)}, u32[]{:S(2)}) async-start(f32[8,128,512]{2,0,1:T(8,128)} %bitcast.48), calls=%async_computation.2 | async-start | bytes 4194304 | tf_op jit(solution)/shard_map/all_to_all | solution.py:314
  88.0 0.0 copy-done.8
  88.0 2.2 scatter_custom_fusion
  90.2 1.8 reshape.124
  92.6 1.3 dynamic-slice_bitcast_fusion
  93.9 0.6 pad_clamp_fusion
  94.5 0.0 copy-done.10
  94.5 0.6 broadcast_divide_fusion
  95.1 18.7 %all-to-all-done.2 = f32[8,128,512]{2,0,1:T(8,128)} async-done(((f32[8,128,512]{2,0,1:T(8,128)}), f32[8,128,512]{2,0,1:T(8,128)}, u32[]{:S(2)}, u32[]{:S(2)}) %all-to-all-start.2) | async-done | bytes 2097184 | tf_op jit(solution)/shard_map/all_to_all | solution.py:314
  113.8 4.7 %copy.24 = f32[16,8,8,512]{3,2,1,0:T(8,128)} copy(f32[16,8,8,512]{3,1,2,0:T(8,128)} %bitcast.8) | data formatting | bytes 4194304 | tf_op jit(solution)/shard_map/all_to_all | solution.py:314
  118.5 0.0 collective-permute-done
  118.6 4.9 %multiply_add_fusion = (f32[16,64,512]{2,1,0:T(8,128)}, f32[16,64,512]{2,1,0:T(8,128)}, f32[16,64,512]{2,1,0:T(8,128)}) fusion(f32[16,64,512]{2,1,0:T(8,128)S(1)} %reshape.124, f32[16,64,512]{2,1,0:T(8,128)} %collective-permute-done, f32[16,64,512]{2,1,0:T(8,128)S(1)} %copy-done.3, pred[]{:T(512)S(6)} %eq.12), kind=kLoop, calls=%fused_computation.6 | loop fusion | flops 2097152 | bytes 12582913 | tf_op jit(solution)/shard_map/add | solution.py:294
  123.5 58.8 %shard_map.113 = f32[16,64,512]{2,1,0:T(8,128)} custom-call(f32[16,64,512]{2,1,0:T(8,128)} %bitcast.47, f32[16,64,512]{2,1,0:T(8,128)} %get-tuple-element.32.sto_ref, f32[16,64,512]{2,1,0:T(8,128)} %get-tuple-element.31.init_ref, f32[16,64,512]{2,1,0:T(8,128)} %get-tuple-element.30.forc_ref), custom_call_target="tpu_custom_call" | custom-call | tf_op jit(solution)/shard_map/pallas_call | solution.py:112
  182.2 2.1 copy.31
  184.4 0.8 gather_fusion
  185.2 0.0 copy-done.7
  185.2 0.3 scatter.9.row_ref
  185.5 0.6 copy-done.4
  186.1 18.6 %shard_map.114 = f32[128,8,128]{2,1,0:T(8,128)} custom-call(f32[1,8,128]{2,1,0:T(8,128)} %copy-done.4), custom_call_target="tpu_custom_call" | custom-call | tf_op jit(solution)/shard_map/pallas_call | solution.py:182
  204.7 1.4 fusion.14
  206.1 1.1 broadcast_subtract_fusion
  207.2 0.3 convolution_multiply_fusion
  207.4 0.1 copy.26
  207.5 4.7 %all-to-all-start.1 = ((f32[1,16,64,512]{3,2,0,1:T(8,128)}), f32[1,16,64,512]{3,2,0,1:T(8,128)}, u32[]{:S(2)}, u32[]{:S(2)}) async-start(f32[1,16,64,512]{3,2,0,1:T(8,128)} %bitcast.46), calls=%async_computation.1 | async-start | bytes 4194304 | tf_op jit(solution)/shard_map/all_to_all | solution.py:297
  212.2 0.0 copy-done.5
  212.2 0.1 fusion.13
  212.3 2.9 %cholesky.16 = f32[32,32]{1,0:T(8,128)S(1)} custom-call(f32[32,32]{1,0:T(8,128)S(1)} %fusion.13), custom_call_target="Cholesky" | custom-call | tf_op jit(solution)/shard_map/jit(cholesky)/cholesky | solution.py:310
  215.2 0.6 compare_reduce_fusion
  215.9 0.7 fusion.7
  216.5 2.4 custom-call.8
  219.0 0.3 fusion.10
  219.2 0.2 fusion.8
  219.4 0.3 convolution_bitcast_fusion
  219.7 3.0 %fusion.1 = f32[128,8,512]{2,0,1:T(8,128)S(1)} fusion(f32[128,128,1]{1,0,2:T(8,128)S(1)} %convolution_bitcast_fusion, f32[128,8,512]{2,1,0:T(8,128)S(1)} %bitcast.44), kind=kOutput, calls=%fused_computation.4 | convolution fusion | flops 805306368 | bytes 4259840 | tf_op jit(solution)/shard_map/jk,kry->jry/dot_general | solution.py:315
  222.7 2.8 %fusion.column_ref = f32[128,8,512]{2,1,0:T(8,128)} fusion(f32[128,8,512]{2,0,1:T(8,128)S(1)} %fusion.1, f32[16,8,8,512]{3,2,1,0:T(8,128)S(1)} %copy-done), kind=kLoop, calls=%fused_computation.3 | loop fusion | flops 1048576 | bytes 6291456 | tf_op jit(solution)/shard_map/add | solution.py:316
  225.5 41.0 %shard_map.115 = f32[8,128,512]{2,1,0:T(8,128)} custom-call(f32[128,8,512]{2,1,0:T(8,128)} %fusion.column_ref), custom_call_target="tpu_custom_call" | custom-call | tf_op jit(solution)/shard_map/pallas_call | solution.py:244
  266.5 0.0 all-to-all-done.1
  266.6 3.3 %copy.41 = f32[8,2,64,512]{3,2,1,0:T(8,128)} copy(f32[8,2,64,512]{3,2,1,0:T(8,128)} %bitcast.5) | data formatting | bytes 4194304
  269.9 1.3 copy.42
  (21 shorter events, 0.1 us)
Async XLA Ops:
  7.2 69.7 %all-gather.2.cloned.1.call-start = ((), (), s32[]{:S(2)}) async-start(), calls=%async_computation.3 | async-start | bytes 2359296 | tf_op jit(solution)/shard_map/all_gather | solution.py:283
  8.9 73.2 %all-to-all-start = ((f32[8,2,64,512]{3,2,1,0:T(8,128)}), f32[8,2,64,512]{3,2,1,0:T(8,128)S(1)}, u32[]{:S(2)}, u32[]{:S(2)}) async-start(f32[8,2,64,512]{3,2,1,0:T(8,128)} %param.14), calls=%async_computation | async-start | bytes 4194304 | tf_op jit(solution)/shard_map/all_to_all | solution.py:277
  76.9 41.7 %collective-permute-start = (f32[16,64,512]{2,1,0:T(8,128)}, f32[16,64,512]{2,1,0:T(8,128)}, u32[]{:S(2)}, u32[]{:S(2)}) collective-permute-start(f32[16,64,512]{2,1,0:T(8,128)} %all-gather.2.cloned.1.call-done), channel_id=1, source_target_pairs={{0,1},{1,0},{2,3},{3,2},{4,5},{5,4},{6,7},{7,6},{8,9},{9,8},{10,11... | collective-permute-start | bytes 6291464 | tf_op jit(solution)/shard_map/ppermute | solution.py:285
  82.1 1.3 copy-start.1
  82.1 5.9 %copy-start.8 = (s32[16]{0:T(128)S(1)}, s32[16]{0:T(128)}, u32[]{:S(2)}) copy-start(s32[16]{0:T(128)} %param.17) | copy-start | bytes 196
  83.4 30.4 %all-to-all-start.2 = ((f32[8,128,512]{2,0,1:T(8,128)}), f32[8,128,512]{2,0,1:T(8,128)}, u32[]{:S(2)}, u32[]{:S(2)}) async-start(f32[8,128,512]{2,0,1:T(8,128)} %bitcast.48), calls=%async_computation.2 | async-start | bytes 4194304 | tf_op jit(solution)/shard_map/all_to_all | solution.py:314
  90.2 3.7 %copy-start.9 = (s32[32]{0:T(128)S(1)}, s32[32]{0:T(128)}, u32[]{:S(2)}) copy-start(s32[32]{0:T(128)} %param.19) | copy-start | bytes 388
  90.2 4.3 %copy-start.10 = (f32[32]{0:T(128)S(1)}, f32[32]{0:T(128)}, u32[]{:S(2)}) copy-start(f32[32]{0:T(128)} %param.21) | copy-start | bytes 388
  113.8 4.7 %copy-start.3 = (f32[16,64,512]{2,1,0:T(8,128)S(1)}, f32[16,64,512]{2,1,0:T(8,128)}, u32[]{:S(2)}) copy-start(f32[16,64,512]{2,1,0:T(8,128)} %all-gather.2.cloned.1.call-done) | copy-start | bytes 6291460
  182.2 3.0 %copy-start.7 = (f32[1,1,32]{2,1,0:T(1,128)S(1)}, f32[1,1,32]{2,1,0:T(1,128)}, u32[]{:S(2)}) copy-start(f32[1,1,32]{2,1,0:T(1,128)} %dynamic-slice_bitcast_fusion) | copy-start | bytes 388
  182.2 22.4 %copy-start.6 = (f32[32]{0:T(128)S(1)}, f32[32]{0:T(128)}, u32[]{:S(2)}) copy-start(f32[32]{0:T(128)} %param.20) | copy-start | bytes 388
  185.5 0.6 copy-start.4
  207.5 4.7 %copy-start.5 = (f32[32]{0:T(128)S(1)}, f32[32]{0:T(128)}, u32[]{:S(2)}) copy-start(f32[32]{0:T(128)} %broadcast_divide_fusion) | copy-start | bytes 388
  207.5 12.2 %copy-start = (f32[16,8,8,512]{3,2,1,0:T(8,128)S(1)}, f32[16,8,8,512]{3,2,1,0:T(8,128)}, u32[]{:S(2)}) copy-start(f32[16,8,8,512]{3,2,1,0:T(8,128)} %copy.24) | copy-start | bytes 6291460
  207.5 59.0 %all-to-all-start.1 = ((f32[1,16,64,512]{3,2,0,1:T(8,128)}), f32[1,16,64,512]{3,2,0,1:T(8,128)}, u32[]{:S(2)}, u32[]{:S(2)}) async-start(f32[1,16,64,512]{3,2,0,1:T(8,128)} %bitcast.46), calls=%async_computation.1 | async-start | bytes 4194304 | tf_op jit(solution)/shard_map/all_to_all | solution.py:297
  266.6 3.3 %copy-start.2 = (f32[8,128,512]{2,1,0:T(8,128)S(1)}, f32[8,128,512]{2,1,0:T(8,128)}, u32[]{:S(2)}) copy-start(f32[8,128,512]{2,1,0:T(8,128)} %shard_map.115) | copy-start | bytes 6291460
Sparse Core Ops, SparseCore 0:
  10.9 65.9 all-gather.1

commit v10 on v8

--- a/solution.py
+++ b/solution.py
@@ -253,6 +253,28 @@
         ],
         compiler_params=pltpu.CompilerParams(collective_id=2, has_side_effects=True),
     )(column)
+
+
+def gather_grid(slab, n_space, n_ens):
+    rows = n_space // 2
+    me_s = lax.axis_index("space")
+    z, half = me_s // 2, me_s % 2
+    pieces = [(slab, me_s)]
+    for flip in (0, 1):
+        for dz in range(1 - flip, rows):
+            pairs = []
+            for s in range(n_space):
+                zs, hs = s // 2, s % 2
+                t = ((zs + dz) % rows) * 2 + (hs ^ flip)
+                for e in range(n_ens):
+                    pairs.append((s * n_ens + e, t * n_ens + (e ^ (2 * flip))))
+            got = lax.ppermute(slab, ("space", "ens"), pairs)
+            pieces.append((got, ((z - dz) % rows) * 2 + (half ^ flip)))
+    thick = slab.shape[0]
+    grid = jnp.zeros((n_space * thick,) + slab.shape[1:], slab.dtype)
+    for got, source in pieces:
+        grid = lax.dynamic_update_slice_in_dim(grid, got, source * thick, axis=0)
+    return grid
 
 
 def shards(
@@ -276,7 +298,7 @@
 
     whole_log = lax.all_to_all(log_perm, "space", 0, 1, tiled=True)
     core = lax.axis_index("ens") % 2
-    mine = lax.all_gather(jnp.where(core == 0, storage, head_init), "space", axis=0, tiled=True)
+    mine = gather_grid(jnp.where(core == 0, storage, head_init), n_space, n_ens)
     pairs = [(e, e ^ 1) for e in range(n_ens)]
     other = lax.ppermute(mine, "ens", pairs)
     whole_storage = jnp.where(core == 0, mine, other)

time: 260 us -> 233 us (0.90)
  waiting for transfers between devices: 62.4 us -> 25.9 us
  starting transfers between devices: 16.1 us -> 33 us
  between operations: 14.9 us -> 1.49 us
  local copies, waits for them, and re-layouts: 21.7 us -> 27.8 us
    all_gather x1 -> x0, waiting for transfers between devices: 50.5 us -> none  [shards(): lax.all_gather(jnp.where(core == 0, storage, head_init), 'space', axis=0,...]
    ppermute x0 -> x7, waiting for transfers between devices: none -> 14.8 us  [gather_grid(): got = lax.ppermute(slab, ('space', 'ens'), pairs)]
    ppermute x0 -> x7, starting transfers between devices: none -> 12.4 us  [gather_grid(): got = lax.ppermute(slab, ('space', 'ens'), pairs)]
    dynamic_update_slice x0 -> x7, local copies, waits for them, and re-layouts: none -> 5.99 us  [gather_grid(): grid = lax.dynamic_update_slice_in_dim(grid, got, source * thick, axis=0)]
    ppermute x1, starting transfers between devices: 1.08 us -> 5.2 us  [shards(): other = lax.ppermute(mine, 'ens', pairs)]
    unnamed x26 -> x28, local copies, waits for them, and re-layouts: 12.8 us -> 11.5 us
  transfers between devices with their start and end apart: 5 -> 11, of which waited for: 2 -> 4; matrix products, arithmetic and copies ran while one was open for 13% -> 16% of each run, Pallas kernels for 16% -> 18%
where the time goes in v10:
time: 233 us; the launch traced here: 232 us
  Pallas kernels  118 us (51%)
  starting transfers between devices  33 us (14%)
  local copies, waits for them, and re-layouts  27.8 us (12%)
  waiting for transfers between devices  25.9 us (11%)
  other arithmetic  21.8 us (9%)
  matrix products  4 us (2%)
    pallas_call x1, Pallas kernels, forward_pallas(): pl.pallas_call(forward_kernel, out_shape=jax.ShapeDtypeStruct((planes, de...  58.8 us
    pallas_call x1, Pallas kernels, send_back(): pl.pallas_call(return_kernel, out_shape=jax.ShapeDtypeStruct((members, sl...  40.6 us
    pallas_call x1, Pallas kernels, gather_rows(): pl.pallas_call(gather_kernel, out_shape=jax.ShapeDtypeStruct((total,) + r...  18.3 us
    ppermute x7, waiting for transfers between devices, gather_grid(): got = lax.ppermute(slab, ('space', 'ens'), pairs)  14.8 us
    ppermute x7, starting transfers between devices, gather_grid(): got = lax.ppermute(slab, ('space', 'ens'), pairs)  12.4 us
    unnamed x28, local copies, waits for them, and re-layouts  11.5 us
    all_to_all x1, waiting for transfers between devices, shards(): whole_log = lax.all_to_all(log_perm, 'space', 0, 1, tiled=True)  11.1 us
    dynamic_update_slice x7, local copies, waits for them, and re-layouts, gather_grid(): grid = lax.dynamic_update_slice_in_dim(grid, got, source * thick, axis=0)  5.99 us
  transfers between devices with their start and end apart: 11, of which 4 were waited for; matrix products, arithmetic and copies ran while one was open for 16% of the time, Pallas kernels for 18%

profile of v10, /device:TPU:25, one launch (start us, length us, event | category | flops | bytes accessed | tf_op | source)
XLA Modules:
  0.0 231.8 jit_solution(6691939582351045037)
XLA Ops:
  0.6 4.1 %copy.22 = f32[8,2,64,512]{3,0,2,1:T(8,128)} copy(f32[8,2,64,512]{3,2,1,0:T(8,128)} %param.14) | data formatting | bytes 4194304 | tf_op args[0]
  4.8 6.0 %all-to-all-start.2 = ((f32[8,128,512]{2,0,1:T(8,128)}), f32[8,128,512]{2,0,1:T(8,128)S(1)}, u32[]{:S(2)}, u32[]{:S(2)}) async-start(f32[8,128,512]{2,0,1:T(8,128)} %bitcast.47), calls=%async_computation.2 | async-start | bytes 4194304 | tf_op jit(solution)/shard_map/all_to_all | solution.py:333
  10.7 1.6 broadcast_in_dim.40
  12.3 0.8 constant_dynamic-update-slice_fusion.7
  13.1 1.6 collective-permute-start
  14.7 3.3 %collective-permute-start.1 = (f32[2,64,512]{2,1,0:T(8,128)S(1)}, f32[2,64,512]{2,1,0:T(8,128)S(1)}, u32[]{:S(2)}, u32[]{:S(2)}) collective-permute-start(f32[2,64,512]{2,1,0:T(8,128)S(1)} %get-tuple-element.30), channel_id=1, source_target_pairs={{0,64},{1,65},{2,66},{3,67},{4,68},{5,69},{6,70},{7,71},{8,72},{9,... | collective-permute-start | bytes 786440 | tf_op jit(solution)/shard_map/ppermute | solution.py:271
  18.0 0.7 collective-permute-start.2
  18.8 2.5 %collective-permute-start.3 = (f32[2,64,512]{2,1,0:T(8,128)S(1)}, f32[2,64,512]{2,1,0:T(8,128)S(1)}, u32[]{:S(2)}, u32[]{:S(2)}) collective-permute-start(f32[2,64,512]{2,1,0:T(8,128)S(1)} %get-tuple-element.30), channel_id=1, source_target_pairs={{0,18},{1,19},{2,16},{3,17},{4,22},{5,23},{6,20},{7,21},{8,26},{9,... | collective-permute-start | bytes 786440 | tf_op jit(solution)/shard_map/ppermute | solution.py:271
  21.2 0.7 collective-permute-start.4
  21.9 1.4 collective-permute-done
  23.3 3.6 %collective-permute-start.5 = (f32[2,64,512]{2,1,0:T(8,128)S(1)}, f32[2,64,512]{2,1,0:T(8,128)S(1)}, u32[]{:S(2)}, u32[]{:S(2)}) collective-permute-start(f32[2,64,512]{2,1,0:T(8,128)S(1)} %get-tuple-element.30), channel_id=1, source_target_pairs={{0,82},{1,83},{2,80},{3,81},{4,86},{5,87},{6,84},{7,85},{8,90},{9,... | collective-permute-start | bytes 786440 | tf_op jit(solution)/shard_map/ppermute | solution.py:271
  26.9 1.7 constant_dynamic-update-slice_fusion.6
  28.6 9.6 %collective-permute-done.1 = f32[2,64,512]{2,1,0:T(8,128)S(1)} collective-permute-done((f32[2,64,512]{2,1,0:T(8,128)S(1)}, f32[2,64,512]{2,1,0:T(8,128)S(1)}, u32[]{:S(2)}, u32[]{:S(2)}) %collective-permute-start.1) | collective-permute-done | bytes 262176 | tf_op jit(solution)/shard_map/ppermute | solution.py:271
  38.2 0.7 constant_dynamic-update-slice_fusion.5
  38.9 0.7 constant_dynamic-update-slice_fusion.4
  39.7 0.7 constant_dynamic-update-slice_fusion.3
  40.4 0.7 constant_dynamic-update-slice_fusion.2
  41.1 0.7 constant_dynamic-update-slice_fusion.1
  41.8 3.7 %collective-permute-done.6 = f32[2,64,512]{2,1,0:T(8,128)S(1)} collective-permute-done((f32[2,64,512]{2,1,0:T(8,128)S(1)}, f32[2,64,512]{2,1,0:T(8,128)S(1)}, u32[]{:S(2)}, u32[]{:S(2)}) %collective-permute-start.6) | collective-permute-done | bytes 262176 | tf_op jit(solution)/shard_map/ppermute | solution.py:271
  45.5 0.7 constant_dynamic-update-slice_fusion
  46.3 5.2 %collective-permute-start.7 = (f32[16,64,512]{2,1,0:T(8,128)}, f32[16,64,512]{2,1,0:T(8,128)}, u32[]{:S(2)}, u32[]{:S(2)}) collective-permute-start(f32[16,64,512]{2,1,0:T(8,128)} %constant_dynamic-update-slice_fusion), channel_id=1, source_target_pairs={{0,1},{1,0},{2,3},{3,2},{4,5},{5,4},{6,7},{7,6},{8,9},{9,8},{10,11... | collective-permute-start | bytes 6291464 | tf_op jit(solution)/shard_map/ppermute | solution.py:303
  51.5 4.8 %all-to-all-start = ((f32[8,2,64,512]{3,2,1,0:T(8,128)}), f32[8,2,64,512]{3,2,1,0:T(8,128)}, u32[]{:S(2)}, u32[]{:S(2)}) async-start(f32[8,2,64,512]{3,2,1,0:T(8,128)} %param.14), calls=%async_computation | async-start | bytes 4194304 | tf_op jit(solution)/shard_map/all_to_all | solution.py:299
  56.3 2.2 scatter_custom_fusion
  58.5 1.8 reshape.124
  60.9 1.2 fusion.14
  62.1 0.6 pad_clamp_fusion
  62.7 0.5 broadcast_divide_fusion
  63.2 4.6 %copy.24 = f32[16,8,8,512]{3,2,1,0:T(8,128)} copy(f32[16,8,8,512]{3,1,2,0:T(8,128)} %bitcast.46) | data formatting | bytes 4194304 | tf_op jit(solution)/shard_map/all_to_all | solution.py:333
  67.8 5.7 %multiply_add_fusion = (f32[16,64,512]{2,1,0:T(8,128)}, f32[16,64,512]{2,1,0:T(8,128)}, f32[16,64,512]{2,1,0:T(8,128)}) fusion(f32[16,64,512]{2,1,0:T(8,128)S(1)} %reshape.124, f32[16,64,512]{2,1,0:T(8,128)} %collective-permute-done.7, f32[16,64,512]{2,1,0:T(8,128)} %constant_dynamic-update-slice_fusion, pred[]{:T(512)S(6)} %eq.20), kind=kLoop, calls=%fused_computation.6 | loop fusion | flops 2097152 | bytes 12582913 | tf_op jit(solution)/shard_map/add | solution.py:312
  73.5 11.1 %all-to-all-done = f32[8,2,64,512]{3,2,1,0:T(8,128)} async-done(((f32[8,2,64,512]{3,2,1,0:T(8,128)}), f32[8,2,64,512]{3,2,1,0:T(8,128)}, u32[]{:S(2)}, u32[]{:S(2)}) %all-to-all-start) | async-done | bytes 2097184 | tf_op jit(solution)/shard_map/all_to_all | solution.py:299
  84.6 58.8 %shard_map.113 = f32[16,64,512]{2,1,0:T(8,128)} custom-call(f32[16,64,512]{2,1,0:T(8,128)} %bitcast.log_ref, f32[16,64,512]{2,1,0:T(8,128)} %get-tuple-element.28.sto_ref, f32[16,64,512]{2,1,0:T(8,128)} %get-tuple-element.27.init_ref, f32[16,64,512]{2,1,0:T(8,128)} %get-tuple-element.26.forc_ref), custom_call_target="tpu_custom_call" | custom-call | tf_op jit(solution)/shard_map/pallas_call | solution.py:112
  143.4 2.1 copy.31
  145.5 0.8 gather_fusion
  146.7 0.6 copy-done.5
  147.3 18.3 %shard_map.114 = f32[128,8,128]{2,1,0:T(8,128)} custom-call(f32[1,8,128]{2,1,0:T(8,128)} %copy-done.5), custom_call_target="tpu_custom_call" | custom-call | tf_op jit(solution)/shard_map/pallas_call | solution.py:182
  165.6 1.4 fusion.15
  167.0 1.1 broadcast_subtract_fusion
  168.5 4.7 %all-to-all-start.1 = ((f32[1,16,64,512]{3,2,0,1:T(8,128)}), f32[1,16,64,512]{3,2,0,1:T(8,128)}, u32[]{:S(2)}, u32[]{:S(2)}) async-start(f32[1,16,64,512]{3,2,0,1:T(8,128)} %bitcast.45), calls=%async_computation.1 | async-start | bytes 4194304 | tf_op jit(solution)/shard_map/all_to_all | solution.py:315
  173.3 2.9 %cholesky.16 = f32[32,32]{1,0:T(8,128)S(1)} custom-call(f32[32,32]{1,0:T(8,128)S(1)} %fusion.13), custom_call_target="Cholesky" | custom-call | tf_op jit(solution)/shard_map/jit(cholesky)/cholesky | solution.py:328
  176.2 0.6 compare_reduce_fusion
  176.9 0.7 fusion.7
  177.5 2.4 %custom-call.8 = f32[1,32,32]{1,2,0:T(8,128)S(1)} custom-call(f32[1,32,32]{2,1,0:T(8,128)S(1)} %fusion.7), custom_call_target="InvertDiagBlocksLowerTriangular" | custom-call | tf_op jit(solution)/shard_map/triangular_solve | solution.py:24
  180.4 0.3 convolution_bitcast_fusion
  180.7 3.0 %fusion.1 = f32[128,8,512]{2,0,1:T(8,128)S(1)} fusion(f32[128,128,1]{1,0,2:T(8,128)S(1)} %convolution_bitcast_fusion, f32[128,8,512]{2,1,0:T(8,128)S(1)} %bitcast.43), kind=kOutput, calls=%fused_computation.4 | convolution fusion | flops 805306368 | bytes 4259840 | tf_op jit(solution)/shard_map/jk,kry->jry/dot_general | solution.py:334
  183.7 2.8 %fusion.column_ref = f32[128,8,512]{2,1,0:T(8,128)} fusion(f32[128,8,512]{2,0,1:T(8,128)S(1)} %fusion.1, f32[16,8,8,512]{3,2,1,0:T(8,128)S(1)} %copy-done), kind=kLoop, calls=%fused_computation.3 | loop fusion | flops 1048576 | bytes 6291456 | tf_op jit(solution)/shard_map/add | solution.py:335
  186.5 40.6 %shard_map.115 = f32[8,128,512]{2,1,0:T(8,128)} custom-call(f32[128,8,512]{2,1,0:T(8,128)} %fusion.column_ref), custom_call_target="tpu_custom_call" | custom-call | tf_op jit(solution)/shard_map/pallas_call | solution.py:244
  227.2 3.3 %copy.49 = f32[8,2,64,512]{3,2,1,0:T(8,128)} copy(f32[8,2,64,512]{3,2,1,0:T(8,128)} %bitcast.3) | data formatting | bytes 4194304
  230.4 1.3 copy.50
  (42 shorter events, 1.2 us)
Async XLA Ops:
  4.8 46.7 %all-to-all-start.2 = ((f32[8,128,512]{2,0,1:T(8,128)}), f32[8,128,512]{2,0,1:T(8,128)S(1)}, u32[]{:S(2)}, u32[]{:S(2)}) async-start(f32[8,128,512]{2,0,1:T(8,128)} %bitcast.47), calls=%async_computation.2 | async-start | bytes 4194304 | tf_op jit(solution)/shard_map/all_to_all | solution.py:333
  10.7 1.6 copy-start.3
  10.7 1.6 copy-start.4
  13.1 10.2 %collective-permute-start = (f32[2,64,512]{2,1,0:T(8,128)S(1)}, f32[2,64,512]{2,1,0:T(8,128)}, u32[]{:S(2)}, u32[]{:S(2)}) collective-permute-start(f32[2,64,512]{2,1,0:T(8,128)S(1)} %get-tuple-element.30), channel_id=1, source_target_pairs={{0,32},{1,33},{2,34},{3,35},{4,36},{5,37},{6,38},{7,39},{8,40},{9,... | collective-permute-start | bytes 786440 | tf_op jit(solution)/shard_map/ppermute | solution.py:271
  14.7 23.5 %collective-permute-start.1 = (f32[2,64,512]{2,1,0:T(8,128)S(1)}, f32[2,64,512]{2,1,0:T(8,128)S(1)}, u32[]{:S(2)}, u32[]{:S(2)}) collective-permute-start(f32[2,64,512]{2,1,0:T(8,128)S(1)} %get-tuple-element.30), channel_id=1, source_target_pairs={{0,64},{1,65},{2,66},{3,67},{4,68},{5,69},{6,70},{7,71},{8,72},{9,... | collective-permute-start | bytes 786440 | tf_op jit(solution)/shard_map/ppermute | solution.py:271
  18.0 20.9 %collective-permute-start.2 = (f32[2,64,512]{2,1,0:T(8,128)S(1)}, f32[2,64,512]{2,1,0:T(8,128)S(1)}, u32[]{:S(2)}, u32[]{:S(2)}) collective-permute-start(f32[2,64,512]{2,1,0:T(8,128)S(1)} %get-tuple-element.30), channel_id=1, source_target_pairs={{0,96},{1,97},{2,98},{3,99},{4,100},{5,101},{6,102},{7,103},{8,104... | collective-permute-start | bytes 786440 | tf_op jit(solution)/shard_map/ppermute | solution.py:271
  18.8 20.9 %collective-permute-start.3 = (f32[2,64,512]{2,1,0:T(8,128)S(1)}, f32[2,64,512]{2,1,0:T(8,128)S(1)}, u32[]{:S(2)}, u32[]{:S(2)}) collective-permute-start(f32[2,64,512]{2,1,0:T(8,128)S(1)} %get-tuple-element.30), channel_id=1, source_target_pairs={{0,18},{1,19},{2,16},{3,17},{4,22},{5,23},{6,20},{7,21},{8,26},{9,... | collective-permute-start | bytes 786440 | tf_op jit(solution)/shard_map/ppermute | solution.py:271
  21.2 19.2 %collective-permute-start.4 = (f32[2,64,512]{2,1,0:T(8,128)S(1)}, f32[2,64,512]{2,1,0:T(8,128)S(1)}, u32[]{:S(2)}, u32[]{:S(2)}) collective-permute-start(f32[2,64,512]{2,1,0:T(8,128)S(1)} %get-tuple-element.30), channel_id=1, source_target_pairs={{0,50},{1,51},{2,48},{3,49},{4,54},{5,55},{6,52},{7,53},{8,58},{9,... | collective-permute-start | bytes 786440 | tf_op jit(solution)/shard_map/ppermute | solution.py:271
  23.3 17.8 %collective-permute-start.5 = (f32[2,64,512]{2,1,0:T(8,128)S(1)}, f32[2,64,512]{2,1,0:T(8,128)S(1)}, u32[]{:S(2)}, u32[]{:S(2)}) collective-permute-start(f32[2,64,512]{2,1,0:T(8,128)S(1)} %get-tuple-element.30), channel_id=1, source_target_pairs={{0,82},{1,83},{2,80},{3,81},{4,86},{5,87},{6,84},{7,85},{8,90},{9,... | collective-permute-start | bytes 786440 | tf_op jit(solution)/shard_map/ppermute | solution.py:271
  38.2 7.3 %collective-permute-start.6 = (f32[2,64,512]{2,1,0:T(8,128)S(1)}, f32[2,64,512]{2,1,0:T(8,128)S(1)}, u32[]{:S(2)}, u32[]{:S(2)}) collective-permute-start(f32[2,64,512]{2,1,0:T(8,128)S(1)} %get-tuple-element.30), channel_id=1, source_target_pairs={{0,114},{1,115},{2,112},{3,113},{4,118},{5,119},{6,116},{7,117},{8... | collective-permute-start | bytes 786440 | tf_op jit(solution)/shard_map/ppermute | solution.py:271
  46.3 10.0 %copy-start.9 = (s32[16]{0:T(128)S(1)}, s32[16]{0:T(128)}, u32[]{:S(2)}) copy-start(s32[16]{0:T(128)} %param.17) | copy-start | bytes 196
  46.3 21.5 %collective-permute-start.7 = (f32[16,64,512]{2,1,0:T(8,128)}, f32[16,64,512]{2,1,0:T(8,128)}, u32[]{:S(2)}, u32[]{:S(2)}) collective-permute-start(f32[16,64,512]{2,1,0:T(8,128)} %constant_dynamic-update-slice_fusion), channel_id=1, source_target_pairs={{0,1},{1,0},{2,3},{3,2},{4,5},{5,4},{6,7},{7,6},{8,9},{9,8},{10,11... | collective-permute-start | bytes 6291464 | tf_op jit(solution)/shard_map/ppermute | solution.py:303
  51.5 4.8 %copy-start.1 = (f32[8,128,512]{2,0,1:T(8,128)}, f32[8,128,512]{2,0,1:T(8,128)S(1)}, u32[]{:S(2)}) copy-start(f32[8,128,512]{2,0,1:T(8,128)S(1)} %all-to-all-done.2) | copy-start | bytes 6291460
  51.5 33.1 %all-to-all-start = ((f32[8,2,64,512]{3,2,1,0:T(8,128)}), f32[8,2,64,512]{3,2,1,0:T(8,128)}, u32[]{:S(2)}, u32[]{:S(2)}) async-start(f32[8,2,64,512]{3,2,1,0:T(8,128)} %param.14), calls=%async_computation | async-start | bytes 4194304 | tf_op jit(solution)/shard_map/all_to_all | solution.py:299
  58.5 3.7 %copy-start.10 = (s32[32]{0:T(128)S(1)}, s32[32]{0:T(128)}, u32[]{:S(2)}) copy-start(s32[32]{0:T(128)} %param.19) | copy-start | bytes 388
  58.5 4.3 %copy-start.11 = (f32[32]{0:T(128)S(1)}, f32[32]{0:T(128)}, u32[]{:S(2)}) copy-start(f32[32]{0:T(128)} %param.21) | copy-start | bytes 388
  143.4 3.0 %copy-start.8 = (f32[1,1,32]{2,1,0:T(1,128)S(1)}, f32[1,1,32]{2,1,0:T(1,128)}, u32[]{:S(2)}) copy-start(f32[1,1,32]{2,1,0:T(1,128)} %fusion.14) | copy-start | bytes 388
  143.4 22.2 %copy-start.7 = (f32[32]{0:T(128)S(1)}, f32[32]{0:T(128)}, u32[]{:S(2)}) copy-start(f32[32]{0:T(128)} %param.20) | copy-start | bytes 388
  146.7 0.6 copy-start.5
  168.5 4.7 %copy-start.6 = (f32[32]{0:T(128)S(1)}, f32[32]{0:T(128)}, u32[]{:S(2)}) copy-start(f32[32]{0:T(128)} %broadcast_divide_fusion) | copy-start | bytes 388
  168.5 12.2 %copy-start = (f32[16,8,8,512]{3,2,1,0:T(8,128)S(1)}, f32[16,8,8,512]{3,2,1,0:T(8,128)}, u32[]{:S(2)}) copy-start(f32[16,8,8,512]{3,2,1,0:T(8,128)} %copy.24) | copy-start | bytes 6291460
  168.5 58.7 %all-to-all-start.1 = ((f32[1,16,64,512]{3,2,0,1:T(8,128)}), f32[1,16,64,512]{3,2,0,1:T(8,128)}, u32[]{:S(2)}, u32[]{:S(2)}) async-start(f32[1,16,64,512]{3,2,0,1:T(8,128)} %bitcast.45), calls=%async_computation.1 | async-start | bytes 4194304 | tf_op jit(solution)/shard_map/all_to_all | solution.py:315
  227.1 3.3 %copy-start.2 = (f32[8,128,512]{2,1,0:T(8,128)S(1)}, f32[8,128,512]{2,1,0:T(8,128)}, u32[]{:S(2)}) copy-start(f32[8,128,512]{2,1,0:T(8,128)} %shard_map.115) | copy-start | bytes 6291460

commit v11 on v10

--- a/solution.py
+++ b/solution.py
@@ -47,8 +47,38 @@
     return jnp.where(valid, x, 0.0)
 
 
-def forward_kernel(log_ref, sto_ref, init_ref, forc_ref, out_ref, perm, trans, diag, head_a, head_b):
+def forward_kernel(
+    log_ref, sto_ref, init_ref, forc_ref, rows_ref, out_ref, band_ref,
+    perm, trans, diag, head_a, head_b, band_send, band_recv, local_sem,
+):
     planes, depth, across = log_ref.shape
+    members, slab_rows, _ = rows_ref.shape
+    groups = band_ref.shape[0] // members
+    rows = slab_rows // groups
+    me_s = lax.axis_index("space")
+    me_e = lax.axis_index("ens")
+    mesh_id = pl.DeviceIdType.MESH
+    barrier = pltpu.get_barrier_semaphore()
+    for e in range(groups):
+        @pl.when(me_e != e)
+        def _():
+            pl.semaphore_signal(barrier, 1, device_id=(me_s, e), device_id_type=mesh_id)
+
+    def band_copy(e, source_e):
+        return pltpu.make_async_remote_copy(
+            src_ref=rows_ref.at[:, pl.ds(e * rows, rows)],
+            dst_ref=band_ref.at[pl.ds(source_e * members, members)],
+            send_sem=band_send.at[e],
+            recv_sem=band_recv.at[source_e],
+            device_id=(me_s, e),
+            device_id_type=mesh_id,
+        )
+
+    keep_band = pltpu.make_async_copy(
+        rows_ref.at[:, pl.ds(me_e * rows, rows)],
+        band_ref.at[pl.ds(me_e * members, members)],
+        local_sem,
+    )
     zero = jnp.zeros((depth, across), jnp.float32)
     for buf in (perm, head_a, head_b):
         buf[0] = zero
@@ -70,6 +100,13 @@
         return carry
 
     lax.fori_loop(0, planes, transmissibility, 0)
+
+    pl.semaphore_wait(barrier, groups - 1)
+    for e in range(groups):
+        @pl.when(me_e != e)
+        def _():
+            band_copy(e, me_e).start()
+    keep_band.start()
 
     def diagonal(p, carry):
         total = sto_ref[p]
@@ -104,25 +141,41 @@
     sweep(head_a, head_b, True)
     sweep(head_b, head_a, True)
     sweep(head_a, out_ref, False)
-
-
-def forward_pallas(log_row, storage, head_init, forcing):
+    keep_band.wait()
+    for e in range(groups):
+        @pl.when(me_e != e)
+        def _():
+            band_copy(e, me_e).wait_send()
+            band_copy(e, e).wait_recv()
+
+
+def forward_pallas(log_row, storage, head_init, forcing, by_rows, groups):
     planes, depth, across = log_row.shape
+    members, slab_rows, _ = by_rows.shape
     vmem = pl.BlockSpec(memory_space=pltpu.VMEM)
+    anywhere = pl.BlockSpec(memory_space=pl.ANY)
     return pl.pallas_call(
         forward_kernel,
-        out_shape=jax.ShapeDtypeStruct((planes, depth, across), jnp.float32),
-        in_specs=[vmem] * 4,
-        out_specs=vmem,
+        out_shape=(
+            jax.ShapeDtypeStruct((planes, depth, across), jnp.float32),
+            jax.ShapeDtypeStruct((members * groups, slab_rows // groups, across), jnp.float32),
+        ),
+        in_specs=[vmem] * 4 + [anywhere],
+        out_specs=(vmem, anywhere),
         scratch_shapes=[
             pltpu.VMEM((planes + 2, depth, across), jnp.float32),
             pltpu.VMEM((len(HALF), planes, depth, across), jnp.float32),
             pltpu.VMEM((planes, depth, across), jnp.float32),
             pltpu.VMEM((planes + 2, depth, across), jnp.float32),
             pltpu.VMEM((planes + 2, depth, across), jnp.float32),
+            pltpu.SemaphoreType.DMA((groups,)),
+            pltpu.SemaphoreType.DMA((groups,)),
+            pltpu.SemaphoreType.DMA,
         ],
-        compiler_params=pltpu.CompilerParams(vmem_limit_bytes=66 * 1024 * 1024),
-    )(log_row, storage, head_init, forcing)
+        compiler_params=pltpu.CompilerParams(
+            vmem_limit_bytes=66 * 1024 * 1024, collective_id=3, has_side_effects=True
+        ),
+    )(log_row, storage, head_init, forcing, by_rows)
 
 
 def gather_kernel(row_ref, out_ref, landing, send_sem, recv_sem):
@@ -310,7 +363,11 @@
         .reshape(grid_planes, depth, across)
     )
     forcing = whole_storage * whole_head + source
-    field = forward_pallas(whole_log[0], whole_storage, whole_head, forcing)
+    slab_rows = planes * depth
+    by_rows = log_perm.reshape(members, slab_rows, across)
+    field, band = forward_pallas(
+        whole_log[0], whole_storage, whole_head, forcing, by_rows, n_ens
+    )
     picked = field.reshape(-1)[obs_cells]
     head_field = lax.all_to_all(field[None], "space", 1, 0, tiled=True)
 
@@ -329,8 +386,6 @@
     gain_rows = solve_pair(factor_lower, obs_values[None, :] + every_perturb - every_obs)
     mixing = jnp.dot(gain_rows, spread.T, precision=HIGHEST)
 
-    slab_rows = planes * depth
-    band = lax.all_to_all(log_perm.reshape(members, slab_rows, across), "ens", 1, 0, tiled=True)
     change = jnp.einsum("jk,kry->jry", mixing, band, precision=HIGHEST)
     new_band = band + change / (total_members - 1)
     updated = send_back(new_band, slab_rows)

time: 233 us -> 224 us (0.961)
  local copies, waits for them, and re-layouts: 27.8 us -> 18.2 us
  starting transfers between devices: 33 us -> 27.2 us
  waiting for transfers between devices: 25.9 us -> 31.1 us
    all_to_all x1 -> x0, starting transfers between devices: 5.95 us -> none  [shards(): lax.all_to_all(log_perm.reshape(members, slab_rows, across), 'ens', 1, 0,...]
    all_to_all x1 -> x0, local copies, waits for them, and re-layouts: 4.57 us -> none  [shards(): lax.all_to_all(log_perm.reshape(members, slab_rows, across), 'ens', 1, 0,...]
    all_to_all x1, waiting for transfers between devices: 11.1 us -> 15.5 us  [shards(): whole_log = lax.all_to_all(log_perm, 'space', 0, 1, tiled=True)]
    unnamed x28 -> x25, local copies, waits for them, and re-layouts: 11.5 us -> 7.38 us
  transfers between devices with their start and end apart: 11 -> 10, of which waited for: 4 -> 4; matrix products, arithmetic and copies ran while one was open for 16% -> 13% of each run, Pallas kernels for 18% -> 18%
where the time goes in v11:
time: 224 us; the launch traced here: 222 us
  Pallas kernels  118 us (53%)
  waiting for transfers between devices  31.1 us (14%)
  starting transfers between devices  27.2 us (12%)
  other arithmetic  21.8 us (10%)
  local copies, waits for them, and re-layouts  18.2 us (8%)
  matrix products  3.99 us (2%)
    pallas_call x1, Pallas kernels, forward_pallas(): pl.pallas_call(forward_kernel, out_shape=(jax.ShapeDtypeStruct((planes, d...  59.3 us
    pallas_call x1, Pallas kernels, send_back(): pl.pallas_call(return_kernel, out_shape=jax.ShapeDtypeStruct((members, sl...  40.7 us
    pallas_call x1, Pallas kernels, gather_rows(): pl.pallas_call(gather_kernel, out_shape=jax.ShapeDtypeStruct((total,) + r...  18.4 us
    all_to_all x1, waiting for transfers between devices, shards(): whole_log = lax.all_to_all(log_perm, 'space', 0, 1, tiled=True)  15.5 us
    ppermute x7, waiting for transfers between devices, gather_grid(): got = lax.ppermute(slab, ('space', 'ens'), pairs)  15.5 us
    ppermute x7, starting transfers between devices, gather_grid(): got = lax.ppermute(slab, ('space', 'ens'), pairs)  12.4 us
    unnamed x25, local copies, waits for them, and re-layouts  7.38 us
    add x1, other arithmetic, shards(): forcing = whole_storage * whole_head + source  5.7 us
  transfers between devices with their start and end apart: 10, of which 4 were waited for; matrix products, arithmetic and copies ran while one was open for 13% of the time, Pallas kernels for 18%

profile of v11, /device:TPU:25, one launch (start us, length us, event | category | flops | bytes accessed | tf_op | source)
XLA Modules:
  0.0 222.2 jit_solution(950134565758637484)
XLA Ops:
  0.7 1.6 broadcast_in_dim.40
  2.3 0.8 constant_dynamic-update-slice_fusion.7
  3.0 1.6 collective-permute-start
  4.6 3.3 %collective-permute-start.1 = (f32[2,64,512]{2,1,0:T(8,128)S(1)}, f32[2,64,512]{2,1,0:T(8,128)S(1)}, u32[]{:S(2)}, u32[]{:S(2)}) collective-permute-start(f32[2,64,512]{2,1,0:T(8,128)S(1)} %get-tuple-element.34), channel_id=1, source_target_pairs={{0,64},{1,65},{2,66},{3,67},{4,68},{5,69},{6,70},{7,71},{8,72},{9,... | collective-permute-start | bytes 786440 | tf_op jit(solution)/shard_map/ppermute | solution.py:324
  7.9 0.7 collective-permute-start.2
  8.7 2.5 %collective-permute-start.3 = (f32[2,64,512]{2,1,0:T(8,128)S(1)}, f32[2,64,512]{2,1,0:T(8,128)S(1)}, u32[]{:S(2)}, u32[]{:S(2)}) collective-permute-start(f32[2,64,512]{2,1,0:T(8,128)S(1)} %get-tuple-element.34), channel_id=1, source_target_pairs={{0,18},{1,19},{2,16},{3,17},{4,22},{5,23},{6,20},{7,21},{8,26},{9,... | collective-permute-start | bytes 786440 | tf_op jit(solution)/shard_map/ppermute | solution.py:324
  11.2 0.7 collective-permute-start.4
  11.8 1.0 collective-permute-done
  12.8 3.6 %collective-permute-start.5 = (f32[2,64,512]{2,1,0:T(8,128)S(1)}, f32[2,64,512]{2,1,0:T(8,128)S(1)}, u32[]{:S(2)}, u32[]{:S(2)}) collective-permute-start(f32[2,64,512]{2,1,0:T(8,128)S(1)} %get-tuple-element.34), channel_id=1, source_target_pairs={{0,82},{1,83},{2,80},{3,81},{4,86},{5,87},{6,84},{7,85},{8,90},{9,... | collective-permute-start | bytes 786440 | tf_op jit(solution)/shard_map/ppermute | solution.py:324
  16.4 0.7 constant_dynamic-update-slice_fusion.6
  17.1 10.8 %collective-permute-done.1 = f32[2,64,512]{2,1,0:T(8,128)S(1)} collective-permute-done((f32[2,64,512]{2,1,0:T(8,128)S(1)}, f32[2,64,512]{2,1,0:T(8,128)S(1)}, u32[]{:S(2)}, u32[]{:S(2)}) %collective-permute-start.1) | collective-permute-done | bytes 262176 | tf_op jit(solution)/shard_map/ppermute | solution.py:324
  28.0 0.7 constant_dynamic-update-slice_fusion.5
  28.7 0.7 constant_dynamic-update-slice_fusion.4
  29.4 0.7 constant_dynamic-update-slice_fusion.3
  30.1 0.7 constant_dynamic-update-slice_fusion.2
  30.9 0.7 constant_dynamic-update-slice_fusion.1
  31.6 3.7 %collective-permute-done.6 = f32[2,64,512]{2,1,0:T(8,128)S(1)} collective-permute-done((f32[2,64,512]{2,1,0:T(8,128)S(1)}, f32[2,64,512]{2,1,0:T(8,128)S(1)}, u32[]{:S(2)}, u32[]{:S(2)}) %collective-permute-start.6) | collective-permute-done | bytes 262176 | tf_op jit(solution)/shard_map/ppermute | solution.py:324
  35.3 0.7 constant_dynamic-update-slice_fusion
  36.0 5.6 %collective-permute-start.7 = (f32[16,64,512]{2,1,0:T(8,128)}, f32[16,64,512]{2,1,0:T(8,128)}, u32[]{:S(2)}, u32[]{:S(2)}) collective-permute-start(f32[16,64,512]{2,1,0:T(8,128)} %constant_dynamic-update-slice_fusion), channel_id=1, source_target_pairs={{0,1},{1,0},{2,3},{3,2},{4,5},{5,4},{6,7},{7,6},{8,9},{9,8},{10,11... | collective-permute-start | bytes 6291464 | tf_op jit(solution)/shard_map/ppermute | solution.py:356
  41.6 4.6 %all-to-all-start = ((f32[8,2,64,512]{3,2,1,0:T(8,128)}), f32[8,2,64,512]{3,2,1,0:T(8,128)}, u32[]{:S(2)}, u32[]{:S(2)}) async-start(f32[8,2,64,512]{3,2,1,0:T(8,128)} %param.14), calls=%async_computation | async-start | bytes 4194304 | tf_op jit(solution)/shard_map/all_to_all | solution.py:352
  46.2 2.2 scatter_custom_fusion
  48.4 1.8 reshape.124
  50.8 1.2 fusion.14
  52.0 0.6 pad_clamp_fusion
  52.6 0.5 broadcast_divide_fusion
  53.2 5.7 %multiply_add_fusion = (f32[16,64,512]{2,1,0:T(8,128)}, f32[16,64,512]{2,1,0:T(8,128)}, f32[16,64,512]{2,1,0:T(8,128)}) fusion(f32[16,64,512]{2,1,0:T(8,128)S(1)} %reshape.124, f32[16,64,512]{2,1,0:T(8,128)} %collective-permute-done.7, f32[16,64,512]{2,1,0:T(8,128)} %constant_dynamic-update-slice_fusion, pred[]{:T(512)S(6)} %eq.20), kind=kLoop, calls=%fused_computation.6 | loop fusion | flops 2097152 | bytes 12582913 | tf_op jit(solution)/shard_map/add | solution.py:365
  58.9 15.5 %all-to-all-done = f32[8,2,64,512]{3,2,1,0:T(8,128)} async-done(((f32[8,2,64,512]{3,2,1,0:T(8,128)}), f32[8,2,64,512]{3,2,1,0:T(8,128)}, u32[]{:S(2)}, u32[]{:S(2)}) %all-to-all-start) | async-done | bytes 2097184 | tf_op jit(solution)/shard_map/all_to_all | solution.py:352
  74.4 59.3 %shard_map.113 = (f32[16,64,512]{2,1,0:T(8,128)}, f32[128,8,512]{2,1,0:T(8,128)}) custom-call(f32[16,64,512]{2,1,0:T(8,128)} %bitcast.log_ref, f32[16,64,512]{2,1,0:T(8,128)} %get-tuple-element.32.sto_ref, f32[16,64,512]{2,1,0:T(8,128)} %get-tuple-element.31.init_ref, f32[16,64,512]{2,1,0:T(8,128)} %get-tuple-element.30.forc_ref, f32[8,128,512]{2,1,0:T(8,128)} %bitcast.1.rows_ref), custom_call_target="tpu_custom_call" | custom-call | tf_op jit(solution)/shard_map/pallas_call | solution.py:157
  133.7 2.1 copy.26
  135.9 0.8 gather_fusion
  136.7 0.3 scatter.9.row_ref
  137.0 0.6 copy-done.4
  137.6 18.4 %shard_map.114 = f32[128,8,128]{2,1,0:T(8,128)} custom-call(f32[1,8,128]{2,1,0:T(8,128)} %copy-done.4), custom_call_target="tpu_custom_call" | custom-call | tf_op jit(solution)/shard_map/pallas_call | solution.py:235
  156.0 1.4 fusion.15
  157.4 1.1 broadcast_subtract_fusion
  158.5 0.3 convolution_multiply_fusion
  158.8 4.7 %all-to-all-start.1 = ((f32[1,16,64,512]{3,2,0,1:T(8,128)}), f32[1,16,64,512]{3,2,0,1:T(8,128)}, u32[]{:S(2)}, u32[]{:S(2)}) async-start(f32[1,16,64,512]{3,2,0,1:T(8,128)} %bitcast.39), calls=%async_computation.1 | async-start | bytes 4194304 | tf_op jit(solution)/shard_map/all_to_all | solution.py:372
  163.6 2.9 %cholesky.16 = f32[32,32]{1,0:T(8,128)S(1)} custom-call(f32[32,32]{1,0:T(8,128)S(1)} %fusion.13), custom_call_target="Cholesky" | custom-call | tf_op jit(solution)/shard_map/jit(cholesky)/cholesky | solution.py:385
  166.5 0.6 compare_reduce_fusion
  167.2 0.7 fusion.7
  167.8 2.4 %custom-call.8 = f32[1,32,32]{1,2,0:T(8,128)S(1)} custom-call(f32[1,32,32]{2,1,0:T(8,128)S(1)} %fusion.7), custom_call_target="InvertDiagBlocksLowerTriangular" | custom-call | tf_op jit(solution)/shard_map/triangular_solve | solution.py:24
  170.3 0.3 fusion.10
  170.7 0.3 convolution_bitcast_fusion
  171.0 3.0 %fusion.1 = f32[128,8,512]{2,0,1:T(8,128)S(1)} fusion(f32[128,128,1]{1,0,2:T(8,128)S(1)} %convolution_bitcast_fusion, f32[128,8,512]{2,1,0:T(8,128)S(1)} %copy-done), kind=kOutput, calls=%fused_computation.4 | convolution fusion | flops 805306368 | bytes 4259840 | tf_op jit(solution)/shard_map/jk,kry->jry/dot_general | solution.py:389
  174.0 2.8 %fusion.column_ref = f32[128,8,512]{2,1,0:T(8,128)} fusion(f32[128,8,512]{2,1,0:T(8,128)S(1)} %copy-done, f32[128,8,512]{2,0,1:T(8,128)S(1)} %fusion.1), kind=kLoop, calls=%fused_computation.3 | loop fusion | flops 1048576 | bytes 6291456 | tf_op jit(solution)/shard_map/add | solution.py:390
  176.8 40.7 %shard_map.115 = f32[8,128,512]{2,1,0:T(8,128)} custom-call(f32[128,8,512]{2,1,0:T(8,128)} %fusion.column_ref), custom_call_target="tpu_custom_call" | custom-call | tf_op jit(solution)/shard_map/pallas_call | solution.py:297
  217.6 3.3 %copy.44 = f32[8,2,64,512]{3,2,1,0:T(8,128)} copy(f32[8,2,64,512]{3,2,1,0:T(8,128)} %bitcast.4) | data formatting | bytes 4194304
  220.9 1.3 copy.45
  (36 shorter events, 0.4 us)
Async XLA Ops:
  0.6 1.6 copy-start.2
  0.6 1.6 copy-start.3
  3.0 9.8 %collective-permute-start = (f32[2,64,512]{2,1,0:T(8,128)S(1)}, f32[2,64,512]{2,1,0:T(8,128)S(1)}, u32[]{:S(2)}, u32[]{:S(2)}) collective-permute-start(f32[2,64,512]{2,1,0:T(8,128)S(1)} %get-tuple-element.34), channel_id=1, source_target_pairs={{0,32},{1,33},{2,34},{3,35},{4,36},{5,37},{6,38},{7,39},{8,40},{9,... | collective-permute-start | bytes 786440 | tf_op jit(solution)/shard_map/ppermute | solution.py:324
  4.6 23.3 %collective-permute-start.1 = (f32[2,64,512]{2,1,0:T(8,128)S(1)}, f32[2,64,512]{2,1,0:T(8,128)S(1)}, u32[]{:S(2)}, u32[]{:S(2)}) collective-permute-start(f32[2,64,512]{2,1,0:T(8,128)S(1)} %get-tuple-element.34), channel_id=1, source_target_pairs={{0,64},{1,65},{2,66},{3,67},{4,68},{5,69},{6,70},{7,71},{8,72},{9,... | collective-permute-start | bytes 786440 | tf_op jit(solution)/shard_map/ppermute | solution.py:324
  7.9 20.7 %collective-permute-start.2 = (f32[2,64,512]{2,1,0:T(8,128)S(1)}, f32[2,64,512]{2,1,0:T(8,128)S(1)}, u32[]{:S(2)}, u32[]{:S(2)}) collective-permute-start(f32[2,64,512]{2,1,0:T(8,128)S(1)} %get-tuple-element.34), channel_id=1, source_target_pairs={{0,96},{1,97},{2,98},{3,99},{4,100},{5,101},{6,102},{7,103},{8,104... | collective-permute-start | bytes 786440 | tf_op jit(solution)/shard_map/ppermute | solution.py:324
  8.7 20.7 %collective-permute-start.3 = (f32[2,64,512]{2,1,0:T(8,128)S(1)}, f32[2,64,512]{2,1,0:T(8,128)S(1)}, u32[]{:S(2)}, u32[]{:S(2)}) collective-permute-start(f32[2,64,512]{2,1,0:T(8,128)S(1)} %get-tuple-element.34), channel_id=1, source_target_pairs={{0,18},{1,19},{2,16},{3,17},{4,22},{5,23},{6,20},{7,21},{8,26},{9,... | collective-permute-start | bytes 786440 | tf_op jit(solution)/shard_map/ppermute | solution.py:324
  11.2 19.0 %collective-permute-start.4 = (f32[2,64,512]{2,1,0:T(8,128)S(1)}, f32[2,64,512]{2,1,0:T(8,128)S(1)}, u32[]{:S(2)}, u32[]{:S(2)}) collective-permute-start(f32[2,64,512]{2,1,0:T(8,128)S(1)} %get-tuple-element.34), channel_id=1, source_target_pairs={{0,50},{1,51},{2,48},{3,49},{4,54},{5,55},{6,52},{7,53},{8,58},{9,... | collective-permute-start | bytes 786440 | tf_op jit(solution)/shard_map/ppermute | solution.py:324
  12.8 18.1 %collective-permute-start.5 = (f32[2,64,512]{2,1,0:T(8,128)S(1)}, f32[2,64,512]{2,1,0:T(8,128)S(1)}, u32[]{:S(2)}, u32[]{:S(2)}) collective-permute-start(f32[2,64,512]{2,1,0:T(8,128)S(1)} %get-tuple-element.34), channel_id=1, source_target_pairs={{0,82},{1,83},{2,80},{3,81},{4,86},{5,87},{6,84},{7,85},{8,90},{9,... | collective-permute-start | bytes 786440 | tf_op jit(solution)/shard_map/ppermute | solution.py:324
  28.0 7.3 %collective-permute-start.6 = (f32[2,64,512]{2,1,0:T(8,128)S(1)}, f32[2,64,512]{2,1,0:T(8,128)S(1)}, u32[]{:S(2)}, u32[]{:S(2)}) collective-permute-start(f32[2,64,512]{2,1,0:T(8,128)S(1)} %get-tuple-element.34), channel_id=1, source_target_pairs={{0,114},{1,115},{2,112},{3,113},{4,118},{5,119},{6,116},{7,117},{8... | collective-permute-start | bytes 786440 | tf_op jit(solution)/shard_map/ppermute | solution.py:324
  36.0 10.2 %copy-start.8 = (s32[16]{0:T(128)S(1)}, s32[16]{0:T(128)}, u32[]{:S(2)}) copy-start(s32[16]{0:T(128)} %param.17) | copy-start | bytes 196
  36.0 17.1 %collective-permute-start.7 = (f32[16,64,512]{2,1,0:T(8,128)}, f32[16,64,512]{2,1,0:T(8,128)}, u32[]{:S(2)}, u32[]{:S(2)}) collective-permute-start(f32[16,64,512]{2,1,0:T(8,128)} %constant_dynamic-update-slice_fusion), channel_id=1, source_target_pairs={{0,1},{1,0},{2,3},{3,2},{4,5},{5,4},{6,7},{7,6},{8,9},{9,8},{10,11... | collective-permute-start | bytes 6291464 | tf_op jit(solution)/shard_map/ppermute | solution.py:356
  41.6 32.8 %all-to-all-start = ((f32[8,2,64,512]{3,2,1,0:T(8,128)}), f32[8,2,64,512]{3,2,1,0:T(8,128)}, u32[]{:S(2)}, u32[]{:S(2)}) async-start(f32[8,2,64,512]{3,2,1,0:T(8,128)} %param.14), calls=%async_computation | async-start | bytes 4194304 | tf_op jit(solution)/shard_map/all_to_all | solution.py:352
  48.4 3.6 %copy-start.9 = (s32[32]{0:T(128)S(1)}, s32[32]{0:T(128)}, u32[]{:S(2)}) copy-start(s32[32]{0:T(128)} %param.19) | copy-start | bytes 388
  48.4 4.2 %copy-start.10 = (f32[32]{0:T(128)S(1)}, f32[32]{0:T(128)}, u32[]{:S(2)}) copy-start(f32[32]{0:T(128)} %param.21) | copy-start | bytes 388
  133.7 3.0 %copy-start.7 = (f32[1,1,32]{2,1,0:T(1,128)S(1)}, f32[1,1,32]{2,1,0:T(1,128)}, u32[]{:S(2)}) copy-start(f32[1,1,32]{2,1,0:T(1,128)} %fusion.14) | copy-start | bytes 388
  133.7 22.2 %copy-start.6 = (f32[32]{0:T(128)S(1)}, f32[32]{0:T(128)}, u32[]{:S(2)}) copy-start(f32[32]{0:T(128)} %param.20) | copy-start | bytes 388
  137.0 0.6 copy-start.4
  158.8 4.7 %copy-start.5 = (f32[32]{0:T(128)S(1)}, f32[32]{0:T(128)}, u32[]{:S(2)}) copy-start(f32[32]{0:T(128)} %broadcast_divide_fusion) | copy-start | bytes 388
  158.8 12.2 %copy-start = (f32[128,8,512]{2,1,0:T(8,128)S(1)}, f32[128,8,512]{2,1,0:T(8,128)}, u32[]{:S(2)}) copy-start(f32[128,8,512]{2,1,0:T(8,128)} %get-tuple-element.29) | copy-start | bytes 6291460
  158.8 58.7 %all-to-all-start.1 = ((f32[1,16,64,512]{3,2,0,1:T(8,128)}), f32[1,16,64,512]{3,2,0,1:T(8,128)}, u32[]{:S(2)}, u32[]{:S(2)}) async-start(f32[1,16,64,512]{3,2,0,1:T(8,128)} %bitcast.39), calls=%async_computation.1 | async-start | bytes 4194304 | tf_op jit(solution)/shard_map/all_to_all | solution.py:372
  217.6 3.3 %copy-start.1 = (f32[8,128,512]{2,1,0:T(8,128)S(1)}, f32[8,128,512]{2,1,0:T(8,128)}, u32[]{:S(2)}) copy-start(f32[8,128,512]{2,1,0:T(8,128)} %shard_map.115) | copy-start | bytes 6291460

commit v12 on v11

--- a/solution.py
+++ b/solution.py
@@ -330,6 +330,30 @@
     return grid
 
 
+def gather_particle(log_perm, n_space, n_ens):
+    rows = n_space // 2
+    me_s = lax.axis_index("space")
+    z, half = me_s // 2, me_s % 2
+    pieces = [(lax.dynamic_index_in_dim(log_perm, me_s, 0, keepdims=False), me_s)]
+    for flip in (0, 1):
+        for dz in range(1 - flip, rows):
+            pairs = []
+            for s in range(n_space):
+                zs, hs = s // 2, s % 2
+                t = ((zs + dz) % rows) * 2 + (hs ^ flip)
+                for e in range(n_ens):
+                    pairs.append((s * n_ens + e, t * n_ens + e))
+            target = ((z + dz) % rows) * 2 + (half ^ flip)
+            outgoing = lax.dynamic_index_in_dim(log_perm, target, 0, keepdims=False)
+            got = lax.ppermute(outgoing, ("space", "ens"), pairs)
+            pieces.append((got, ((z - dz) % rows) * 2 + (half ^ flip)))
+    thick = log_perm.shape[1]
+    whole = jnp.zeros((n_space * thick,) + log_perm.shape[2:], log_perm.dtype)
+    for got, source in pieces:
+        whole = lax.dynamic_update_slice_in_dim(whole, got, source * thick, axis=0)
+    return whole
+
+
 def shards(
     log_perm,
     storage,
@@ -349,7 +373,7 @@
     total_members = members * n_ens
     grid_planes = planes * n_space
 
-    whole_log = lax.all_to_all(log_perm, "space", 0, 1, tiled=True)
+    whole_log = gather_particle(log_perm, n_space, n_ens)
     core = lax.axis_index("ens") % 2
     mine = gather_grid(jnp.where(core == 0, storage, head_init), n_space, n_ens)
     pairs = [(e, e ^ 1) for e in range(n_ens)]
@@ -366,7 +390,7 @@
     slab_rows = planes * depth
     by_rows = log_perm.reshape(members, slab_rows, across)
     field, band = forward_pallas(
-        whole_log[0], whole_storage, whole_head, forcing, by_rows, n_ens
+        whole_log, whole_storage, whole_head, forcing, by_rows, n_ens
     )
     picked = field.reshape(-1)[obs_cells]
     head_field = lax.all_to_all(field[None], "space", 1, 0, tiled=True)

time: 224 us -> 237 us (1.058)
  local copies, waits for them, and re-layouts: 18.2 us -> 27.6 us
  waiting for transfers between devices: 31.1 us -> 23.1 us
  starting transfers between devices: 27.2 us -> 34.8 us
  Pallas kernels: 118 us -> 123 us
    all_to_all x1 -> x0, waiting for transfers between devices: 15.5 us -> none  [shards(): whole_log = lax.all_to_all(log_perm, 'space', 0, 1, tiled=True)]
    ppermute x0 -> x7, starting transfers between devices: none -> 12.3 us  [gather_particle(): got = lax.ppermute(outgoing, ('space', 'ens'), pairs)]
    ppermute x0 -> x7, waiting for transfers between devices: none -> 8.54 us  [gather_particle(): got = lax.ppermute(outgoing, ('space', 'ens'), pairs)]
    dynamic_update_slice x0 -> x8, local copies, waits for them, and re-layouts: none -> 5.76 us  [gather_particle(): whole = lax.dynamic_update_slice_in_dim(whole, got, source * thick, axis=0)]
    all_to_all x1 -> x0, starting transfers between devices: 4.6 us -> none  [shards(): whole_log = lax.all_to_all(log_perm, 'space', 0, 1, tiled=True)]
    pallas_call x1, Pallas kernels: 18.4 us -> 22.4 us  [gather_rows(): pl.pallas_call(gather_kernel, out_shape=jax.ShapeDtypeStruct((total,) + r...]
    another operation x1 -> x3, local copies, waits for them, and re-layouts: 1.22 us -> 4.34 us
    unnamed x25 -> x27, local copies, waits for them, and re-layouts: 7.38 us -> 7.38 us
  transfers between devices with their start and end apart: 10 -> 16, of which waited for: 4 -> 5; matrix products, arithmetic and copies ran while one was open for 13% -> 14% of each run, Pallas kernels for 18% -> 17%
where the time goes in v12:
time: 237 us; the launch traced here: 236 us
  Pallas kernels  123 us (52%)
  starting transfers between devices  34.8 us (15%)
  local copies, waits for them, and re-layouts  27.6 us (12%)
  waiting for transfers between devices  23.1 us (10%)
  other arithmetic  21.9 us (9%)
  matrix products  4 us (2%)
    pallas_call x1, Pallas kernels, forward_pallas(): pl.pallas_call(forward_kernel, out_shape=(jax.ShapeDtypeStruct((planes, d...  59.3 us
    pallas_call x1, Pallas kernels, send_back(): pl.pallas_call(return_kernel, out_shape=jax.ShapeDtypeStruct((members, sl...  41.2 us
    pallas_call x1, Pallas kernels, gather_rows(): pl.pallas_call(gather_kernel, out_shape=jax.ShapeDtypeStruct((total,) + r...  22.4 us
    ppermute x7, waiting for transfers between devices, gather_grid(): got = lax.ppermute(slab, ('space', 'ens'), pairs)  14.6 us
    ppermute x7, starting transfers between devices, gather_grid(): got = lax.ppermute(slab, ('space', 'ens'), pairs)  12.4 us
    ppermute x7, starting transfers between devices, gather_particle(): got = lax.ppermute(outgoing, ('space', 'ens'), pairs)  12.3 us
    ppermute x7, waiting for transfers between devices, gather_particle(): got = lax.ppermute(outgoing, ('space', 'ens'), pairs)  8.54 us
    unnamed x27, local copies, waits for them, and re-layouts  7.38 us
  transfers between devices with their start and end apart: 16, of which 5 were waited for; matrix products, arithmetic and copies ran while one was open for 14% of the time, Pallas kernels for 17%

profile of v12, /device:TPU:25, one launch (start us, length us, event | category | flops | bytes accessed | tf_op | source)
XLA Modules:
  0.0 235.8 jit_solution(2115320929790823006)
XLA Ops:
  0.7 1.6 broadcast.142.clone.1
  2.2 0.8 constant_dynamic-update-slice_fusion.7
  3.0 1.7 collective-permute-start.7
  4.6 3.3 %collective-permute-start.8 = (f32[2,64,512]{2,1,0:T(8,128)S(1)}, f32[2,64,512]{2,1,0:T(8,128)S(1)}, u32[]{:S(2)}, u32[]{:S(2)}) collective-permute-start(f32[2,64,512]{2,1,0:T(8,128)S(1)} %get-tuple-element.34), channel_id=1, source_target_pairs={{0,64},{1,65},{2,66},{3,67},{4,68},{5,69},{6,70},{7,71},{8,72},{9,... | collective-permute-start | bytes 786440 | tf_op jit(solution)/shard_map/ppermute | solution.py:324
  7.9 0.7 collective-permute-start.9
  8.6 2.5 %collective-permute-start.10 = (f32[2,64,512]{2,1,0:T(8,128)S(1)}, f32[2,64,512]{2,1,0:T(8,128)S(1)}, u32[]{:S(2)}, u32[]{:S(2)}) collective-permute-start(f32[2,64,512]{2,1,0:T(8,128)S(1)} %get-tuple-element.34), channel_id=1, source_target_pairs={{0,18},{1,19},{2,16},{3,17},{4,22},{5,23},{6,20},{7,21},{8,26},{9,... | collective-permute-start | bytes 786440 | tf_op jit(solution)/shard_map/ppermute | solution.py:324
  11.8 1.1 collective-permute-done.7
  12.9 3.6 %collective-permute-start.12 = (f32[2,64,512]{2,1,0:T(8,128)S(1)}, f32[2,64,512]{2,1,0:T(8,128)S(1)}, u32[]{:S(2)}, u32[]{:S(2)}) collective-permute-start(f32[2,64,512]{2,1,0:T(8,128)S(1)} %get-tuple-element.34), channel_id=1, source_target_pairs={{0,82},{1,83},{2,80},{3,81},{4,86},{5,87},{6,84},{7,85},{8,90},{9,... | collective-permute-start | bytes 786440 | tf_op jit(solution)/shard_map/ppermute | solution.py:324
  16.5 1.7 constant_dynamic-update-slice_fusion.6
  18.2 9.8 %collective-permute-done.8 = f32[2,64,512]{2,1,0:T(8,128)S(1)} collective-permute-done((f32[2,64,512]{2,1,0:T(8,128)S(1)}, f32[2,64,512]{2,1,0:T(8,128)S(1)}, u32[]{:S(2)}, u32[]{:S(2)}) %collective-permute-start.8) | collective-permute-done | bytes 262176 | tf_op jit(solution)/shard_map/ppermute | solution.py:324
  28.6 0.7 constant_dynamic-update-slice_fusion.4
  30.1 0.7 constant_dynamic-update-slice_fusion.2
  30.8 0.7 constant_dynamic-update-slice_fusion.1
  31.6 3.7 %collective-permute-done.13 = f32[2,64,512]{2,1,0:T(8,128)S(1)} collective-permute-done((f32[2,64,512]{2,1,0:T(8,128)S(1)}, f32[2,64,512]{2,1,0:T(8,128)S(1)}, u32[]{:S(2)}, u32[]{:S(2)}) %collective-permute-start.13) | collective-permute-done | bytes 262176 | tf_op jit(solution)/shard_map/ppermute | solution.py:324
  36.0 5.6 %collective-permute-start.14 = (f32[16,64,512]{2,1,0:T(8,128)}, f32[16,64,512]{2,1,0:T(8,128)}, u32[]{:S(2)}, u32[]{:S(2)}) collective-permute-start(f32[16,64,512]{2,1,0:T(8,128)} %constant_dynamic-update-slice_fusion), channel_id=1, source_target_pairs={{0,1},{1,0},{2,3},{3,2},{4,5},{5,4},{6,7},{7,6},{8,9},{9,8},{10,11... | collective-permute-start | bytes 6291464 | tf_op jit(solution)/shard_map/ppermute | solution.py:380
  41.5 1.2 dynamic-slice_bitcast_fusion
  42.7 2.4 %collective-permute-start.1 = (f32[2,64,512]{2,1,0:T(8,128)}, f32[2,64,512]{2,1,0:T(8,128)S(1)}, u32[]{:S(2)}, u32[]{:S(2)}) collective-permute-start(f32[2,64,512]{2,1,0:T(8,128)} %get-tuple-element.40), channel_id=1, source_target_pairs={{0,64},{1,65},{2,66},{3,67},{4,68},{5,69},{6,70},{7,71},{8,72},{9,... | collective-permute-start | bytes 786440 | tf_op jit(solution)/shard_map/ppermute | solution.py:348
  45.4 2.2 collective-permute-start.3
  48.8 1.6 broadcast.142.clone
  50.4 0.7 bitcast_dynamic-update-slice_fusion
  51.7 1.2 fusion.14
  52.9 2.2 scatter_custom_fusion
  55.1 1.7 reshape.120
  56.9 1.8 collective-permute-start.4
  58.7 0.7 constant_dynamic-update-slice_fusion.14
  59.4 2.1 collective-permute-start.5
  62.3 3.5 %collective-permute-start.6 = (f32[2,64,512]{2,1,0:T(8,128)S(1)}, f32[2,64,512]{2,1,0:T(8,128)S(1)}, u32[]{:S(2)}, u32[]{:S(2)}) collective-permute-start(f32[2,64,512]{2,1,0:T(8,128)S(1)} %get-tuple-element.35), channel_id=1, source_target_pairs={{0,112},{1,113},{2,114},{3,115},{4,116},{5,117},{6,118},{7,119},{8... | collective-permute-start | bytes 786440 | tf_op jit(solution)/shard_map/ppermute | solution.py:348
  66.5 0.7 constant_dynamic-update-slice_fusion.11
  67.2 0.7 constant_dynamic-update-slice_fusion.10
  67.9 5.2 %collective-permute-done.5 = f32[2,64,512]{2,1,0:T(8,128)S(1)} collective-permute-done((f32[2,64,512]{2,1,0:T(8,128)}, f32[2,64,512]{2,1,0:T(8,128)S(1)}, u32[]{:S(2)}, u32[]{:S(2)}) %collective-permute-start.5) | collective-permute-done | bytes 262176 | tf_op jit(solution)/shard_map/ppermute | solution.py:348
  73.1 0.7 constant_dynamic-update-slice_fusion.9
  73.8 3.4 %collective-permute-done.6 = f32[2,64,512]{2,1,0:T(8,128)S(1)} collective-permute-done((f32[2,64,512]{2,1,0:T(8,128)S(1)}, f32[2,64,512]{2,1,0:T(8,128)S(1)}, u32[]{:S(2)}, u32[]{:S(2)}) %collective-permute-start.6) | collective-permute-done | bytes 262176 | tf_op jit(solution)/shard_map/ppermute | solution.py:348
  77.2 0.7 constant_dynamic-update-slice_fusion.8.log_ref
  77.9 5.7 %multiply_add_fusion = (f32[16,64,512]{2,1,0:T(8,128)}, f32[16,64,512]{2,1,0:T(8,128)}, f32[16,64,512]{2,1,0:T(8,128)}) fusion(f32[16,64,512]{2,1,0:T(8,128)S(1)} %reshape.120, f32[16,64,512]{2,1,0:T(8,128)} %collective-permute-done.14, f32[16,64,512]{2,1,0:T(8,128)} %constant_dynamic-update-slice_fusion, pred[]{:T(512)S(6)} %eq.35), kind=kLoop, calls=%fused_computation.6 | loop fusion | flops 2097152 | bytes 12582913 | tf_op jit(solution)/shard_map/add | solution.py:389
  83.6 59.3 %shard_map.113 = (f32[16,64,512]{2,1,0:T(8,128)}, f32[128,8,512]{2,1,0:T(8,128)}) custom-call(f32[16,64,512]{2,1,0:T(8,128)} %constant_dynamic-update-slice_fusion.8.log_ref, f32[16,64,512]{2,1,0:T(8,128)} %get-tuple-element.32.sto_ref, f32[16,64,512]{2,1,0:T(8,128)} %get-tuple-element.31.init_ref, f32[16,64,512]{2,1,0:T(8,128)} %get-tuple-element.30.forc_ref, ...), custom_call_target="tpu_custom_call" | custom-call | tf_op jit(solution)/shard_map/pallas_call | solution.py:157
  142.9 2.1 copy.26
  145.1 0.8 gather_fusion
  146.8 22.4 %shard_map.114 = f32[128,8,128]{2,1,0:T(8,128)} custom-call(f32[1,8,128]{2,1,0:T(8,128)} %copy-done.5), custom_call_target="tpu_custom_call" | custom-call | tf_op jit(solution)/shard_map/pallas_call | solution.py:235
  169.2 1.4 fusion.15
  170.7 1.1 broadcast_subtract_fusion
  172.1 4.5 %all-to-all-start = ((f32[1,16,64,512]{3,2,0,1:T(8,128)}), f32[1,16,64,512]{3,2,0,1:T(8,128)}, u32[]{:S(2)}, u32[]{:S(2)}) async-start(f32[1,16,64,512]{3,2,0,1:T(8,128)} %bitcast.55), calls=%async_computation | async-start | bytes 4194304 | tf_op jit(solution)/shard_map/all_to_all | solution.py:396
  176.7 2.9 %cholesky.16 = f32[32,32]{1,0:T(8,128)S(1)} custom-call(f32[32,32]{1,0:T(8,128)S(1)} %fusion.13), custom_call_target="Cholesky" | custom-call | tf_op jit(solution)/shard_map/jit(cholesky)/cholesky | solution.py:409
  180.9 2.4 %custom-call.8 = f32[1,32,32]{1,2,0:T(8,128)S(1)} custom-call(f32[1,32,32]{2,1,0:T(8,128)S(1)} %fusion.7), custom_call_target="InvertDiagBlocksLowerTriangular" | custom-call | tf_op jit(solution)/shard_map/triangular_solve | solution.py:24
  184.1 3.0 %fusion.1 = f32[128,8,512]{2,0,1:T(8,128)S(1)} fusion(f32[128,128,1]{1,0,2:T(8,128)S(1)} %convolution_bitcast_fusion, f32[128,8,512]{2,1,0:T(8,128)S(1)} %copy-done.1), kind=kOutput, calls=%fused_computation.4 | convolution fusion | flops 805306368 | bytes 4259840 | tf_op jit(solution)/shard_map/jk,kry->jry/dot_general | solution.py:413
  187.1 2.8 %fusion.column_ref = f32[128,8,512]{2,1,0:T(8,128)} fusion(f32[128,8,512]{2,1,0:T(8,128)S(1)} %copy-done.1, f32[128,8,512]{2,0,1:T(8,128)S(1)} %fusion.1), kind=kLoop, calls=%fused_computation.3 | loop fusion | flops 1048576 | bytes 6291456 | tf_op jit(solution)/shard_map/add | solution.py:414
  189.9 41.2 %shard_map.115 = f32[8,128,512]{2,1,0:T(8,128)} custom-call(f32[128,8,512]{2,1,0:T(8,128)} %fusion.column_ref), custom_call_target="tpu_custom_call" | custom-call | tf_op jit(solution)/shard_map/pallas_call | solution.py:297
  231.1 3.3 %copy.54 = f32[8,2,64,512]{3,2,1,0:T(8,128)} copy(f32[8,2,64,512]{3,2,1,0:T(8,128)} %bitcast.11) | data formatting | bytes 4194304
  234.4 1.3 copy.55
  (60 shorter events, 9.0 us)
Async XLA Ops:
  0.6 1.6 copy-start.3
  0.6 1.6 copy-start.4
  3.0 38.6 %copy-start = (f32[8,2,64,512]{3,2,1,0:T(8,128)S(1)}, f32[8,2,64,512]{3,2,1,0:T(8,128)}, u32[]{:S(2)}) copy-start(f32[8,2,64,512]{3,2,1,0:T(8,128)} %param.14) | copy-start | bytes 6291460
  3.0 9.9 %collective-permute-start.7 = (f32[2,64,512]{2,1,0:T(8,128)S(1)}, f32[2,64,512]{2,1,0:T(8,128)}, u32[]{:S(2)}, u32[]{:S(2)}) collective-permute-start(f32[2,64,512]{2,1,0:T(8,128)S(1)} %get-tuple-element.34), channel_id=1, source_target_pairs={{0,32},{1,33},{2,34},{3,35},{4,36},{5,37},{6,38},{7,39},{8,40},{9,... | collective-permute-start | bytes 786440 | tf_op jit(solution)/shard_map/ppermute | solution.py:324
  4.6 23.3 %collective-permute-start.8 = (f32[2,64,512]{2,1,0:T(8,128)S(1)}, f32[2,64,512]{2,1,0:T(8,128)S(1)}, u32[]{:S(2)}, u32[]{:S(2)}) collective-permute-start(f32[2,64,512]{2,1,0:T(8,128)S(1)} %get-tuple-element.34), channel_id=1, source_target_pairs={{0,64},{1,65},{2,66},{3,67},{4,68},{5,69},{6,70},{7,71},{8,72},{9,... | collective-permute-start | bytes 786440 | tf_op jit(solution)/shard_map/ppermute | solution.py:324
  7.9 20.7 %collective-permute-start.9 = (f32[2,64,512]{2,1,0:T(8,128)S(1)}, f32[2,64,512]{2,1,0:T(8,128)S(1)}, u32[]{:S(2)}, u32[]{:S(2)}) collective-permute-start(f32[2,64,512]{2,1,0:T(8,128)S(1)} %get-tuple-element.34), channel_id=1, source_target_pairs={{0,96},{1,97},{2,98},{3,99},{4,100},{5,101},{6,102},{7,103},{8,104... | collective-permute-start | bytes 786440 | tf_op jit(solution)/shard_map/ppermute | solution.py:324
  8.6 20.7 %collective-permute-start.10 = (f32[2,64,512]{2,1,0:T(8,128)S(1)}, f32[2,64,512]{2,1,0:T(8,128)S(1)}, u32[]{:S(2)}, u32[]{:S(2)}) collective-permute-start(f32[2,64,512]{2,1,0:T(8,128)S(1)} %get-tuple-element.34), channel_id=1, source_target_pairs={{0,18},{1,19},{2,16},{3,17},{4,22},{5,23},{6,20},{7,21},{8,26},{9,... | collective-permute-start | bytes 786440 | tf_op jit(solution)/shard_map/ppermute | solution.py:324
  11.1 19.0 %collective-permute-start.11 = (f32[2,64,512]{2,1,0:T(8,128)S(1)}, f32[2,64,512]{2,1,0:T(8,128)S(1)}, u32[]{:S(2)}, u32[]{:S(2)}) collective-permute-start(f32[2,64,512]{2,1,0:T(8,128)S(1)} %get-tuple-element.34), channel_id=1, source_target_pairs={{0,50},{1,51},{2,48},{3,49},{4,54},{5,55},{6,52},{7,53},{8,58},{9,... | collective-permute-start | bytes 786440 | tf_op jit(solution)/shard_map/ppermute | solution.py:324
  12.9 18.0 %collective-permute-start.12 = (f32[2,64,512]{2,1,0:T(8,128)S(1)}, f32[2,64,512]{2,1,0:T(8,128)S(1)}, u32[]{:S(2)}, u32[]{:S(2)}) collective-permute-start(f32[2,64,512]{2,1,0:T(8,128)S(1)} %get-tuple-element.34), channel_id=1, source_target_pairs={{0,82},{1,83},{2,80},{3,81},{4,86},{5,87},{6,84},{7,85},{8,90},{9,... | collective-permute-start | bytes 786440 | tf_op jit(solution)/shard_map/ppermute | solution.py:324
  27.9 7.3 %collective-permute-start.13 = (f32[2,64,512]{2,1,0:T(8,128)S(1)}, f32[2,64,512]{2,1,0:T(8,128)S(1)}, u32[]{:S(2)}, u32[]{:S(2)}) collective-permute-start(f32[2,64,512]{2,1,0:T(8,128)S(1)} %get-tuple-element.34), channel_id=1, source_target_pairs={{0,114},{1,115},{2,112},{3,113},{4,118},{5,119},{6,116},{7,117},{8... | collective-permute-start | bytes 786440 | tf_op jit(solution)/shard_map/ppermute | solution.py:324
  31.6 16.7 %copy-start.9 = (s32[16]{0:T(128)S(1)}, s32[16]{0:T(128)}, u32[]{:S(2)}) copy-start(s32[16]{0:T(128)} %param.17) | copy-start | bytes 196
  31.6 16.7 %copy-start.10 = (s32[32]{0:T(128)S(1)}, s32[32]{0:T(128)}, u32[]{:S(2)}) copy-start(s32[32]{0:T(128)} %param.19) | copy-start | bytes 388
  31.6 16.7 %copy-start.11 = (f32[32]{0:T(128)S(1)}, f32[32]{0:T(128)}, u32[]{:S(2)}) copy-start(f32[32]{0:T(128)} %param.21) | copy-start | bytes 388
  36.0 41.9 %collective-permute-start.14 = (f32[16,64,512]{2,1,0:T(8,128)}, f32[16,64,512]{2,1,0:T(8,128)}, u32[]{:S(2)}, u32[]{:S(2)}) collective-permute-start(f32[16,64,512]{2,1,0:T(8,128)} %constant_dynamic-update-slice_fusion), channel_id=1, source_target_pairs={{0,1},{1,0},{2,3},{3,2},{4,5},{5,4},{6,7},{7,6},{8,9},{9,8},{10,11... | collective-permute-start | bytes 6291464 | tf_op jit(solution)/shard_map/ppermute | solution.py:380
  42.7 14.1 %collective-permute-start = (f32[2,64,512]{2,1,0:T(8,128)}, f32[2,64,512]{2,1,0:T(8,128)S(1)}, u32[]{:S(2)}, u32[]{:S(2)}) collective-permute-start(f32[2,64,512]{2,1,0:T(8,128)} %get-tuple-element.41), channel_id=1, source_target_pairs={{0,32},{1,33},{2,34},{3,35},{4,36},{5,37},{6,38},{7,39},{8,40},{9,... | collective-permute-start | bytes 786440 | tf_op jit(solution)/shard_map/ppermute | solution.py:348
  42.7 16.7 %collective-permute-start.1 = (f32[2,64,512]{2,1,0:T(8,128)}, f32[2,64,512]{2,1,0:T(8,128)S(1)}, u32[]{:S(2)}, u32[]{:S(2)}) collective-permute-start(f32[2,64,512]{2,1,0:T(8,128)} %get-tuple-element.40), channel_id=1, source_target_pairs={{0,64},{1,65},{2,66},{3,67},{4,68},{5,69},{6,70},{7,71},{8,72},{9,... | collective-permute-start | bytes 786440 | tf_op jit(solution)/shard_map/ppermute | solution.py:348
  45.2 17.1 %collective-permute-start.2 = (f32[2,64,512]{2,1,0:T(8,128)}, f32[2,64,512]{2,1,0:T(8,128)S(1)}, u32[]{:S(2)}, u32[]{:S(2)}) collective-permute-start(f32[2,64,512]{2,1,0:T(8,128)} %get-tuple-element.39), channel_id=1, source_target_pairs={{0,96},{1,97},{2,98},{3,99},{4,100},{5,101},{6,102},{7,103},{8,104... | collective-permute-start | bytes 786440 | tf_op jit(solution)/shard_map/ppermute | solution.py:348
  45.4 21.1 %collective-permute-start.3 = (f32[2,64,512]{2,1,0:T(8,128)}, f32[2,64,512]{2,1,0:T(8,128)S(1)}, u32[]{:S(2)}, u32[]{:S(2)}) collective-permute-start(f32[2,64,512]{2,1,0:T(8,128)} %get-tuple-element.38), channel_id=1, source_target_pairs={{0,16},{1,17},{2,18},{3,19},{4,20},{5,21},{6,22},{7,23},{8,24},{9,... | collective-permute-start | bytes 786440 | tf_op jit(solution)/shard_map/ppermute | solution.py:348
  56.9 10.3 %collective-permute-start.4 = (f32[2,64,512]{2,1,0:T(8,128)}, f32[2,64,512]{2,1,0:T(8,128)S(1)}, u32[]{:S(2)}, u32[]{:S(2)}) collective-permute-start(f32[2,64,512]{2,1,0:T(8,128)} %get-tuple-element.37), channel_id=1, source_target_pairs={{0,48},{1,49},{2,50},{3,51},{4,52},{5,53},{6,54},{7,55},{8,56},{9,... | collective-permute-start | bytes 786440 | tf_op jit(solution)/shard_map/ppermute | solution.py:348
  59.4 13.6 %collective-permute-start.5 = (f32[2,64,512]{2,1,0:T(8,128)}, f32[2,64,512]{2,1,0:T(8,128)S(1)}, u32[]{:S(2)}, u32[]{:S(2)}) collective-permute-start(f32[2,64,512]{2,1,0:T(8,128)} %get-tuple-element.36), channel_id=1, source_target_pairs={{0,80},{1,81},{2,82},{3,83},{4,84},{5,85},{6,86},{7,87},{8,88},{9,... | collective-permute-start | bytes 786440 | tf_op jit(solution)/shard_map/ppermute | solution.py:348
  62.3 14.9 %collective-permute-start.6 = (f32[2,64,512]{2,1,0:T(8,128)S(1)}, f32[2,64,512]{2,1,0:T(8,128)S(1)}, u32[]{:S(2)}, u32[]{:S(2)}) collective-permute-start(f32[2,64,512]{2,1,0:T(8,128)S(1)} %get-tuple-element.35), channel_id=1, source_target_pairs={{0,112},{1,113},{2,114},{3,115},{4,116},{5,117},{6,118},{7,119},{8... | collective-permute-start | bytes 786440 | tf_op jit(solution)/shard_map/ppermute | solution.py:348
  142.9 3.0 %copy-start.8 = (f32[1,1,32]{2,1,0:T(1,128)S(1)}, f32[1,1,32]{2,1,0:T(1,128)}, u32[]{:S(2)}) copy-start(f32[1,1,32]{2,1,0:T(1,128)} %fusion.14) | copy-start | bytes 388
  142.9 26.3 %copy-start.7 = (f32[32]{0:T(128)S(1)}, f32[32]{0:T(128)}, u32[]{:S(2)}) copy-start(f32[32]{0:T(128)} %param.20) | copy-start | bytes 388
  146.2 0.6 copy-start.5
  172.1 4.5 %copy-start.6 = (f32[32]{0:T(128)S(1)}, f32[32]{0:T(128)}, u32[]{:S(2)}) copy-start(f32[32]{0:T(128)} %broadcast_divide_fusion) | copy-start | bytes 388
  172.1 12.0 %copy-start.1 = (f32[128,8,512]{2,1,0:T(8,128)S(1)}, f32[128,8,512]{2,1,0:T(8,128)}, u32[]{:S(2)}) copy-start(f32[128,8,512]{2,1,0:T(8,128)} %get-tuple-element.29) | copy-start | bytes 6291460
  172.1 59.0 %all-to-all-start = ((f32[1,16,64,512]{3,2,0,1:T(8,128)}), f32[1,16,64,512]{3,2,0,1:T(8,128)}, u32[]{:S(2)}, u32[]{:S(2)}) async-start(f32[1,16,64,512]{3,2,0,1:T(8,128)} %bitcast.55), calls=%async_computation | async-start | bytes 4194304 | tf_op jit(solution)/shard_map/all_to_all | solution.py:396
  231.1 3.3 %copy-start.2 = (f32[8,128,512]{2,1,0:T(8,128)S(1)}, f32[8,128,512]{2,1,0:T(8,128)}, u32[]{:S(2)}) copy-start(f32[8,128,512]{2,1,0:T(8,128)} %shard_map.115) | copy-start | bytes 6291460

commit v13 on v11

--- a/solution.py
+++ b/solution.py
@@ -350,12 +350,8 @@
     grid_planes = planes * n_space
 
     whole_log = lax.all_to_all(log_perm, "space", 0, 1, tiled=True)
-    core = lax.axis_index("ens") % 2
-    mine = gather_grid(jnp.where(core == 0, storage, head_init), n_space, n_ens)
-    pairs = [(e, e ^ 1) for e in range(n_ens)]
-    other = lax.ppermute(mine, "ens", pairs)
-    whole_storage = jnp.where(core == 0, mine, other)
-    whole_head = jnp.where(core == 0, other, mine)
+    both_grids = gather_grid(jnp.stack([storage, head_init], axis=1), n_space, n_ens)
+    whole_storage, whole_head = both_grids[:, 0], both_grids[:, 1]
     source = (
         jnp.zeros((grid_planes * depth * across,), jnp.float32)
         .at[well_cells]

time: 224 us -> 242 us (1.080)
  local copies, waits for them, and re-layouts: 18.2 us -> 29 us
  waiting for transfers between devices: 31.1 us -> 40.8 us
  Pallas kernels: 118 us -> 121 us
  starting transfers between devices: 27.2 us -> 24.2 us
    ppermute x7, waiting for transfers between devices: 15.5 us -> 40.8 us  [gather_grid(): got = lax.ppermute(slab, ('space', 'ens'), pairs)]
    all_to_all x1, waiting for transfers between devices: 15.5 us -> 0.01 us  [shards(): whole_log = lax.all_to_all(log_perm, 'space', 0, 1, tiled=True)]
    ppermute x1 -> x0, starting transfers between devices: 5.56 us -> none  [shards(): other = lax.ppermute(mine, 'ens', pairs)]
    squeeze x0 -> x1, local copies, waits for them, and re-layouts: none -> 5.09 us  [shards(): whole_storage, whole_head = (both_grids[:, 0], both_grids[:, 1])]
    dynamic_update_slice x7, local copies, waits for them, and re-layouts: 5.04 us -> 10.1 us  [gather_grid(): grid = lax.dynamic_update_slice_in_dim(grid, got, source * thick, axis=0)]
    pallas_call x1, Pallas kernels: 18.4 us -> 21.2 us  [gather_rows(): pl.pallas_call(gather_kernel, out_shape=jax.ShapeDtypeStruct((total,) + r...]
    ppermute x7, starting transfers between devices: 12.4 us -> 15.1 us  [gather_grid(): got = lax.ppermute(slab, ('space', 'ens'), pairs)]
    unnamed x25 -> x27, local copies, waits for them, and re-layouts: 7.38 us -> 7.38 us
  transfers between devices with their start and end apart: 10 -> 9, of which waited for: 4 -> 6; matrix products, arithmetic and copies ran while one was open for 13% -> 16% of each run, Pallas kernels for 18% -> 17%
where the time goes in v13:
time: 242 us; the launch traced here: 241 us
  Pallas kernels  121 us (50%)
  waiting for transfers between devices  40.8 us (17%)
  local copies, waits for them, and re-layouts  29 us (12%)
  starting transfers between devices  24.2 us (10%)
  other arithmetic  19.8 us (8%)
  matrix products  3.99 us (2%)
    pallas_call x1, Pallas kernels, forward_pallas(): pl.pallas_call(forward_kernel, out_shape=(jax.ShapeDtypeStruct((planes, d...  59.3 us
    pallas_call x1, Pallas kernels, send_back(): pl.pallas_call(return_kernel, out_shape=jax.ShapeDtypeStruct((members, sl...  40.9 us
    ppermute x7, waiting for transfers between devices, gather_grid(): got = lax.ppermute(slab, ('space', 'ens'), pairs)  40.8 us
    pallas_call x1, Pallas kernels, gather_rows(): pl.pallas_call(gather_kernel, out_shape=jax.ShapeDtypeStruct((total,) + r...  21.2 us
    ppermute x7, starting transfers between devices, gather_grid(): got = lax.ppermute(slab, ('space', 'ens'), pairs)  15.1 us
    dynamic_update_slice x7, local copies, waits for them, and re-layouts, gather_grid(): grid = lax.dynamic_update_slice_in_dim(grid, got, source * thick, axis=0)  10.1 us
    unnamed x27, local copies, waits for them, and re-layouts  7.38 us
    squeeze x1, local copies, waits for them, and re-layouts, shards(): whole_storage, whole_head = (both_grids[:, 0], both_grids[:, 1])  5.09 us
  transfers between devices with their start and end apart: 9, of which 6 were waited for; matrix products, arithmetic and copies ran while one was open for 16% of the time, Pallas kernels for 17%

profile of v13, /device:TPU:25, one launch (start us, length us, event | category | flops | bytes accessed | tf_op | source)
XLA Modules:
  0.0 240.7 jit_solution(13970144095276448865)
XLA Ops:
  0.7 2.5 %broadcast_in_dim.40 = f32[16,2,64,512]{3,2,0,1:T(8,128)} broadcast(f32[]{:T(128)} %constant.175.clone.1), dimensions={} | broadcast | bytes 4194308 | tf_op jit(solution)/shard_map/broadcast_in_dim | solution.py:327
  3.1 0.9 pad_maximum_fusion
  4.1 1.6 collective-permute-start
  5.7 3.3 %collective-permute-start.1 = (f32[2,2,64,512]{3,2,0,1:T(8,128)S(1)}, f32[2,2,64,512]{3,2,0,1:T(8,128)}, u32[]{:S(2)}, u32[]{:S(2)}) collective-permute-start(f32[2,2,64,512]{3,2,0,1:T(8,128)S(1)} %get-tuple-element.35), channel_id=1, source_target_pairs={{0,64},{1,65},{2,66},{3,67},{4,68},{5,69},{6,70},{7,71},{8,72},{9,... | collective-permute-start | bytes 1572872 | tf_op jit(solution)/shard_map/ppermute | solution.py:324
  9.1 0.7 collective-permute-start.2
  9.8 2.5 %collective-permute-start.3 = (f32[2,2,64,512]{3,2,0,1:T(8,128)S(1)}, f32[2,2,64,512]{3,2,0,1:T(8,128)}, u32[]{:S(2)}, u32[]{:S(2)}) collective-permute-start(f32[2,2,64,512]{3,2,0,1:T(8,128)S(1)} %get-tuple-element.35), channel_id=1, source_target_pairs={{0,18},{1,19},{2,16},{3,17},{4,22},{5,23},{6,20},{7,21},{8,26},{9,... | collective-permute-start | bytes 1572872 | tf_op jit(solution)/shard_map/ppermute | solution.py:324
  12.2 0.7 collective-permute-start.4
  12.9 4.4 %all-to-all-start = ((f32[8,2,64,512]{3,2,1,0:T(8,128)}), f32[8,2,64,512]{3,2,1,0:T(8,128)}, u32[]{:S(2)}, u32[]{:S(2)}) async-start(f32[8,2,64,512]{3,2,1,0:T(8,128)} %param.14), calls=%async_computation | async-start | bytes 4194304 | tf_op jit(solution)/shard_map/all_to_all | solution.py:352
  18.1 0.6 broadcast_divide_fusion
  18.6 0.6 pad_clamp_fusion
  19.2 1.2 fusion.14
  20.5 1.3 scatter_custom_fusion
  21.8 1.5 reshape.124
  23.3 6.3 %collective-permute-start.5 = (f32[2,2,64,512]{3,2,0,1:T(8,128)S(1)}, f32[2,2,64,512]{3,2,0,1:T(8,128)S(1)}, u32[]{:S(2)}, u32[]{:S(2)}) collective-permute-start(f32[2,2,64,512]{3,2,0,1:T(8,128)S(1)} %get-tuple-element.35), channel_id=1, source_target_pairs={{0,82},{1,83},{2,80},{3,81},{4,86},{5,87},{6,84},{7,85},{8,90},{9,... | collective-permute-start | bytes 1572872 | tf_op jit(solution)/shard_map/ppermute | solution.py:324
  29.6 1.9 constant_dynamic-update-slice_fusion.6
  31.5 5.9 %collective-permute-done.1 = f32[2,2,64,512]{3,2,0,1:T(8,128)} collective-permute-done((f32[2,2,64,512]{3,2,0,1:T(8,128)S(1)}, f32[2,2,64,512]{3,2,0,1:T(8,128)}, u32[]{:S(2)}, u32[]{:S(2)}) %collective-permute-start.1) | collective-permute-done | bytes 524320 | tf_op jit(solution)/shard_map/ppermute | solution.py:324
  37.4 1.9 constant_dynamic-update-slice_fusion.5
  39.3 3.1 %collective-permute-done.2 = f32[2,2,64,512]{3,2,0,1:T(8,128)} collective-permute-done((f32[2,2,64,512]{3,2,0,1:T(8,128)S(1)}, f32[2,2,64,512]{3,2,0,1:T(8,128)}, u32[]{:S(2)}, u32[]{:S(2)}) %collective-permute-start.2) | collective-permute-done | bytes 524320 | tf_op jit(solution)/shard_map/ppermute | solution.py:324
  42.4 1.9 constant_dynamic-update-slice_fusion.4
  44.3 1.1 collective-permute-done.3
  45.5 1.9 constant_dynamic-update-slice_fusion.3
  47.3 9.2 %collective-permute-done.4 = f32[2,2,64,512]{3,2,0,1:T(8,128)S(1)} collective-permute-done((f32[2,2,64,512]{3,2,0,1:T(8,128)S(1)}, f32[2,2,64,512]{3,2,0,1:T(8,128)S(1)}, u32[]{:S(2)}, u32[]{:S(2)}) %collective-permute-start.4) | collective-permute-done | bytes 524320 | tf_op jit(solution)/shard_map/ppermute | solution.py:324
  56.6 0.8 constant_dynamic-update-slice_fusion.2
  57.4 11.0 %collective-permute-done.5 = f32[2,2,64,512]{3,2,0,1:T(8,128)S(1)} collective-permute-done((f32[2,2,64,512]{3,2,0,1:T(8,128)S(1)}, f32[2,2,64,512]{3,2,0,1:T(8,128)S(1)}, u32[]{:S(2)}, u32[]{:S(2)}) %collective-permute-start.5) | collective-permute-done | bytes 524320 | tf_op jit(solution)/shard_map/ppermute | solution.py:324
  68.4 0.8 constant_dynamic-update-slice_fusion.1
  69.2 10.4 %collective-permute-done.6 = f32[2,2,64,512]{3,2,0,1:T(8,128)S(1)} collective-permute-done((f32[2,2,64,512]{3,2,0,1:T(8,128)S(1)}, f32[2,2,64,512]{3,2,0,1:T(8,128)S(1)}, u32[]{:S(2)}, u32[]{:S(2)}) %collective-permute-start.6) | collective-permute-done | bytes 524320 | tf_op jit(solution)/shard_map/ppermute | solution.py:324
  79.7 0.8 constant_dynamic-update-slice_fusion
  80.5 5.1 %slice_bitcast_fusion = (f32[16,64,512]{2,1,0:T(8,128)}, f32[16,64,512]{2,1,0:T(8,128)}) fusion(f32[16,2,64,512]{3,2,0,1:T(8,128)} %constant_dynamic-update-slice_fusion), kind=kLoop, calls=%fused_computation.2 | loop fusion | bytes 8388608 | tf_op jit(solution)/shard_map/squeeze | solution.py:354
  85.6 4.3 %multiply_add_fusion.forc_ref = f32[16,64,512]{2,1,0:T(8,128)} fusion(f32[16,64,512]{2,1,0:T(8,128)S(1)} %copy-done.2, f32[16,2,64,512]{3,2,0,1:T(8,128)} %constant_dynamic-update-slice_fusion), kind=kLoop, calls=%fused_computation.8 | loop fusion | flops 1048576 | bytes 8388608 | tf_op jit(solution)/shard_map/add | solution.py:361
  89.9 59.3 %shard_map.113 = (f32[16,64,512]{2,1,0:T(8,128)}, f32[128,8,512]{2,1,0:T(8,128)}) custom-call(f32[16,64,512]{2,1,0:T(8,128)} %bitcast.log_ref, f32[16,64,512]{2,1,0:T(8,128)} %get-tuple-element.31.sto_ref, f32[16,64,512]{2,1,0:T(8,128)} %get-tuple-element.30.init_ref, f32[16,64,512]{2,1,0:T(8,128)} %multiply_add_fusion.forc_ref, f32[8,128,512]{2,1,0:T(8,128)} %bitcast.5.rows_ref), custom_call_target="tpu_custom_call" | custom-call | tf_op jit(solution)/shard_map/pallas_call | solution.py:157
  149.2 2.1 copy.26
  151.4 0.8 gather_fusion
  152.2 0.3 scatter.9.row_ref
  152.5 0.6 copy-done.5
  153.1 21.2 %shard_map.114 = f32[128,8,128]{2,1,0:T(8,128)} custom-call(f32[1,8,128]{2,1,0:T(8,128)} %copy-done.5), custom_call_target="tpu_custom_call" | custom-call | tf_op jit(solution)/shard_map/pallas_call | solution.py:235
  174.3 1.4 fusion.15
  175.8 1.1 broadcast_subtract_fusion
  177.2 4.7 %all-to-all-start.1 = ((f32[1,16,64,512]{3,2,0,1:T(8,128)}), f32[1,16,64,512]{3,2,0,1:T(8,128)}, u32[]{:S(2)}, u32[]{:S(2)}) async-start(f32[1,16,64,512]{3,2,0,1:T(8,128)} %bitcast.49), calls=%async_computation.1 | async-start | bytes 4194304 | tf_op jit(solution)/shard_map/all_to_all | solution.py:368
  181.9 2.9 %cholesky.16 = f32[32,32]{1,0:T(8,128)S(1)} custom-call(f32[32,32]{1,0:T(8,128)S(1)} %fusion.13), custom_call_target="Cholesky" | custom-call | tf_op jit(solution)/shard_map/jit(cholesky)/cholesky | solution.py:381
  184.9 0.6 compare_reduce_fusion
  185.5 0.7 fusion.7
  186.2 2.4 %custom-call.8 = f32[1,32,32]{1,2,0:T(8,128)S(1)} custom-call(f32[1,32,32]{2,1,0:T(8,128)S(1)} %fusion.7), custom_call_target="InvertDiagBlocksLowerTriangular" | custom-call | tf_op jit(solution)/shard_map/triangular_solve | solution.py:24
  189.1 0.3 convolution_bitcast_fusion
  189.4 3.0 %fusion.1 = f32[128,8,512]{2,0,1:T(8,128)S(1)} fusion(f32[128,128,1]{1,0,2:T(8,128)S(1)} %convolution_bitcast_fusion, f32[128,8,512]{2,1,0:T(8,128)S(1)} %copy-done), kind=kOutput, calls=%fused_computation.6 | convolution fusion | flops 805306368 | bytes 4259840 | tf_op jit(solution)/shard_map/jk,kry->jry/dot_general | solution.py:385
  192.4 2.8 %fusion.column_ref = f32[128,8,512]{2,1,0:T(8,128)} fusion(f32[128,8,512]{2,1,0:T(8,128)S(1)} %copy-done, f32[128,8,512]{2,0,1:T(8,128)S(1)} %fusion.1), kind=kLoop, calls=%fused_computation.5 | loop fusion | flops 1048576 | bytes 6291456 | tf_op jit(solution)/shard_map/add | solution.py:386
  195.2 40.9 %shard_map.115 = f32[8,128,512]{2,1,0:T(8,128)} custom-call(f32[128,8,512]{2,1,0:T(8,128)} %fusion.column_ref), custom_call_target="tpu_custom_call" | custom-call | tf_op jit(solution)/shard_map/pallas_call | solution.py:297
  236.1 3.3 %copy.44 = f32[8,2,64,512]{3,2,1,0:T(8,128)} copy(f32[8,2,64,512]{3,2,1,0:T(8,128)} %bitcast.8) | data formatting | bytes 4194304
  239.4 1.3 copy.45
  (37 shorter events, 0.9 us)
Async XLA Ops:
  0.6 2.5 %copy-start.3 = (f32[2,64,512]{2,1,0:T(8,128)S(1)}, f32[2,64,512]{2,1,0:T(8,128)}, u32[]{:S(2)}) copy-start(f32[2,64,512]{2,1,0:T(8,128)} %param.16) | copy-start | bytes 786436
  0.6 2.5 %copy-start.4 = (f32[2,64,512]{2,1,0:T(8,128)S(1)}, f32[2,64,512]{2,1,0:T(8,128)}, u32[]{:S(2)}) copy-start(f32[2,64,512]{2,1,0:T(8,128)} %param.15) | copy-start | bytes 786436
  4.1 13.3 %copy-start.9 = (s32[16]{0:T(128)S(1)}, s32[16]{0:T(128)}, u32[]{:S(2)}) copy-start(s32[16]{0:T(128)} %param.17) | copy-start | bytes 196
  4.1 13.3 %copy-start.10 = (s32[32]{0:T(128)S(1)}, s32[32]{0:T(128)}, u32[]{:S(2)}) copy-start(s32[32]{0:T(128)} %param.19) | copy-start | bytes 388
  4.1 13.9 %copy-start.11 = (f32[32]{0:T(128)S(1)}, f32[32]{0:T(128)}, u32[]{:S(2)}) copy-start(f32[32]{0:T(128)} %param.21) | copy-start | bytes 388
  4.1 19.2 %collective-permute-start = (f32[2,2,64,512]{3,2,0,1:T(8,128)S(1)}, f32[2,2,64,512]{3,2,0,1:T(8,128)}, u32[]{:S(2)}, u32[]{:S(2)}) collective-permute-start(f32[2,2,64,512]{3,2,0,1:T(8,128)S(1)} %get-tuple-element.35), channel_id=1, source_target_pairs={{0,32},{1,33},{2,34},{3,35},{4,36},{5,37},{6,38},{7,39},{8,40},{9,... | collective-permute-start | bytes 1572872 | tf_op jit(solution)/shard_map/ppermute | solution.py:324
  5.7 31.7 %collective-permute-start.1 = (f32[2,2,64,512]{3,2,0,1:T(8,128)S(1)}, f32[2,2,64,512]{3,2,0,1:T(8,128)}, u32[]{:S(2)}, u32[]{:S(2)}) collective-permute-start(f32[2,2,64,512]{3,2,0,1:T(8,128)S(1)} %get-tuple-element.35), channel_id=1, source_target_pairs={{0,64},{1,65},{2,66},{3,67},{4,68},{5,69},{6,70},{7,71},{8,72},{9,... | collective-permute-start | bytes 1572872 | tf_op jit(solution)/shard_map/ppermute | solution.py:324
  9.1 33.4 %collective-permute-start.2 = (f32[2,2,64,512]{3,2,0,1:T(8,128)S(1)}, f32[2,2,64,512]{3,2,0,1:T(8,128)}, u32[]{:S(2)}, u32[]{:S(2)}) collective-permute-start(f32[2,2,64,512]{3,2,0,1:T(8,128)S(1)} %get-tuple-element.35), channel_id=1, source_target_pairs={{0,96},{1,97},{2,98},{3,99},{4,100},{5,101},{6,102},{7,103},{8,104... | collective-permute-start | bytes 1572872 | tf_op jit(solution)/shard_map/ppermute | solution.py:324
  9.8 35.7 %collective-permute-start.3 = (f32[2,2,64,512]{3,2,0,1:T(8,128)S(1)}, f32[2,2,64,512]{3,2,0,1:T(8,128)}, u32[]{:S(2)}, u32[]{:S(2)}) collective-permute-start(f32[2,2,64,512]{3,2,0,1:T(8,128)S(1)} %get-tuple-element.35), channel_id=1, source_target_pairs={{0,18},{1,19},{2,16},{3,17},{4,22},{5,23},{6,20},{7,21},{8,26},{9,... | collective-permute-start | bytes 1572872 | tf_op jit(solution)/shard_map/ppermute | solution.py:324
  12.2 44.3 %collective-permute-start.4 = (f32[2,2,64,512]{3,2,0,1:T(8,128)S(1)}, f32[2,2,64,512]{3,2,0,1:T(8,128)S(1)}, u32[]{:S(2)}, u32[]{:S(2)}) collective-permute-start(f32[2,2,64,512]{3,2,0,1:T(8,128)S(1)} %get-tuple-element.35), channel_id=1, source_target_pairs={{0,50},{1,51},{2,48},{3,49},{4,54},{5,55},{6,52},{7,53},{8,58},{9,... | collective-permute-start | bytes 1572872 | tf_op jit(solution)/shard_map/ppermute | solution.py:324
  12.9 77.0 %all-to-all-start = ((f32[8,2,64,512]{3,2,1,0:T(8,128)}), f32[8,2,64,512]{3,2,1,0:T(8,128)}, u32[]{:S(2)}, u32[]{:S(2)}) async-start(f32[8,2,64,512]{3,2,1,0:T(8,128)} %param.14), calls=%async_computation | async-start | bytes 4194304 | tf_op jit(solution)/shard_map/all_to_all | solution.py:352
  23.3 45.1 %collective-permute-start.5 = (f32[2,2,64,512]{3,2,0,1:T(8,128)S(1)}, f32[2,2,64,512]{3,2,0,1:T(8,128)S(1)}, u32[]{:S(2)}, u32[]{:S(2)}) collective-permute-start(f32[2,2,64,512]{3,2,0,1:T(8,128)S(1)} %get-tuple-element.35), channel_id=1, source_target_pairs={{0,82},{1,83},{2,80},{3,81},{4,86},{5,87},{6,84},{7,85},{8,90},{9,... | collective-permute-start | bytes 1572872 | tf_op jit(solution)/shard_map/ppermute | solution.py:324
  37.4 42.2 %collective-permute-start.6 = (f32[2,2,64,512]{3,2,0,1:T(8,128)S(1)}, f32[2,2,64,512]{3,2,0,1:T(8,128)S(1)}, u32[]{:S(2)}, u32[]{:S(2)}) collective-permute-start(f32[2,2,64,512]{3,2,0,1:T(8,128)S(1)} %get-tuple-element.35), channel_id=1, source_target_pairs={{0,114},{1,115},{2,112},{3,113},{4,118},{5,119},{6,116},{7,117},{8... | collective-permute-start | bytes 1572872 | tf_op jit(solution)/shard_map/ppermute | solution.py:324
  80.5 5.1 %copy-start.2 = (f32[16,64,512]{2,1,0:T(8,128)S(1)}, f32[16,64,512]{2,1,0:T(8,128)}, u32[]{:S(2)}) copy-start(f32[16,64,512]{2,1,0:T(8,128)} %reshape.124) | copy-start | bytes 6291460
  149.2 3.0 %copy-start.8 = (f32[1,1,32]{2,1,0:T(1,128)S(1)}, f32[1,1,32]{2,1,0:T(1,128)}, u32[]{:S(2)}) copy-start(f32[1,1,32]{2,1,0:T(1,128)} %fusion.14) | copy-start | bytes 388
  149.2 25.1 %copy-start.7 = (f32[32]{0:T(128)S(1)}, f32[32]{0:T(128)}, u32[]{:S(2)}) copy-start(f32[32]{0:T(128)} %param.20) | copy-start | bytes 388
  152.5 0.6 copy-start.5
  177.2 4.7 %copy-start.6 = (f32[32]{0:T(128)S(1)}, f32[32]{0:T(128)}, u32[]{:S(2)}) copy-start(f32[32]{0:T(128)} %broadcast_divide_fusion) | copy-start | bytes 388
  177.2 12.2 %copy-start = (f32[128,8,512]{2,1,0:T(8,128)S(1)}, f32[128,8,512]{2,1,0:T(8,128)}, u32[]{:S(2)}) copy-start(f32[128,8,512]{2,1,0:T(8,128)} %get-tuple-element.29) | copy-start | bytes 6291460
  177.2 58.9 %all-to-all-start.1 = ((f32[1,16,64,512]{3,2,0,1:T(8,128)}), f32[1,16,64,512]{3,2,0,1:T(8,128)}, u32[]{:S(2)}, u32[]{:S(2)}) async-start(f32[1,16,64,512]{3,2,0,1:T(8,128)} %bitcast.49), calls=%async_computation.1 | async-start | bytes 4194304 | tf_op jit(solution)/shard_map/all_to_all | solution.py:368
  236.1 3.3 %copy-start.1 = (f32[8,128,512]{2,1,0:T(8,128)S(1)}, f32[8,128,512]{2,1,0:T(8,128)}, u32[]{:S(2)}) copy-start(f32[8,128,512]{2,1,0:T(8,128)} %shard_map.115) | copy-start | bytes 6291460

commit v14 on v11

--- a/solution.py
+++ b/solution.py
@@ -330,6 +330,61 @@
     return grid
 
 
+def particle_kernel(log_ref, whole_ref, send_sems, recv_sems, local_sem):
+    slabs, thick = log_ref.shape[0], log_ref.shape[1]
+    me_s = lax.axis_index("space")
+    me_e = lax.axis_index("ens")
+    mesh_id = pl.DeviceIdType.MESH
+    barrier = pltpu.get_barrier_semaphore()
+    for s in range(slabs):
+        @pl.when(me_s != s)
+        def _():
+            pl.semaphore_signal(barrier, 1, device_id=(s, me_e), device_id_type=mesh_id)
+    pl.semaphore_wait(barrier, slabs - 1)
+
+    def send(t, source_s):
+        return pltpu.make_async_remote_copy(
+            src_ref=log_ref.at[t],
+            dst_ref=whole_ref.at[pl.ds(source_s * thick, thick)],
+            send_sem=send_sems.at[t],
+            recv_sem=recv_sems.at[source_s],
+            device_id=(t, me_e),
+            device_id_type=mesh_id,
+        )
+
+    keep = pltpu.make_async_copy(
+        log_ref.at[me_s], whole_ref.at[pl.ds(me_s * thick, thick)], local_sem
+    )
+    for t in range(slabs):
+        @pl.when(me_s != t)
+        def _():
+            send(t, me_s).start()
+    keep.start()
+    keep.wait()
+    for t in range(slabs):
+        @pl.when(me_s != t)
+        def _():
+            send(t, me_s).wait_send()
+            send(t, t).wait_recv()
+
+
+def gather_particle(log_perm):
+    slabs, thick, depth, across = log_perm.shape
+    anywhere = pl.BlockSpec(memory_space=pl.ANY)
+    return pl.pallas_call(
+        particle_kernel,
+        out_shape=jax.ShapeDtypeStruct((slabs * thick, depth, across), jnp.float32),
+        in_specs=[anywhere],
+        out_specs=anywhere,
+        scratch_shapes=[
+            pltpu.SemaphoreType.DMA((slabs,)),
+            pltpu.SemaphoreType.DMA((slabs,)),
+            pltpu.SemaphoreType.DMA,
+        ],
+        compiler_params=pltpu.CompilerParams(collective_id=4, has_side_effects=True),
+    )(log_perm)
+
+
 def shards(
     log_perm,
     storage,
@@ -349,7 +404,7 @@
     total_members = members * n_ens
     grid_planes = planes * n_space
 
-    whole_log = lax.all_to_all(log_perm, "space", 0, 1, tiled=True)
+    whole_log = gather_particle(log_perm)
     core = lax.axis_index("ens") % 2
     mine = gather_grid(jnp.where(core == 0, storage, head_init), n_space, n_ens)
     pairs = [(e, e ^ 1) for e in range(n_ens)]
@@ -366,7 +421,7 @@
     slab_rows = planes * depth
     by_rows = log_perm.reshape(members, slab_rows, across)
     field, band = forward_pallas(
-        whole_log[0], whole_storage, whole_head, forcing, by_rows, n_ens
+        whole_log, whole_storage, whole_head, forcing, by_rows, n_ens
     )
     picked = field.reshape(-1)[obs_cells]
     head_field = lax.all_to_all(field[None], "space", 1, 0, tiled=True)

time: 224 us -> 240 us (1.071)
  Pallas kernels: 118 us -> 155 us
  waiting for transfers between devices: 31.1 us -> 15.5 us
  starting transfers between devices: 27.2 us -> 22.6 us
    pallas_call x0 -> x1, Pallas kernels: none -> 31.3 us  [gather_particle(): pl.pallas_call(particle_kernel, out_shape=jax.ShapeDtypeStruct((slabs * t...]
    all_to_all x1 -> x0, waiting for transfers between devices: 15.5 us -> none  [shards(): whole_log = lax.all_to_all(log_perm, 'space', 0, 1, tiled=True)]
    pallas_call x1, Pallas kernels: 18.4 us -> 24.4 us  [gather_rows(): pl.pallas_call(gather_kernel, out_shape=jax.ShapeDtypeStruct((total,) + r...]
    all_to_all x1 -> x0, starting transfers between devices: 4.6 us -> none  [shards(): whole_log = lax.all_to_all(log_perm, 'space', 0, 1, tiled=True)]
  transfers between devices with their start and end apart: 10 -> 9, of which waited for: 4 -> 3; matrix products, arithmetic and copies ran while one was open for 13% -> 10% of each run, Pallas kernels for 18% -> 30%
where the time goes in v14:
time: 240 us; the launch traced here: 239 us
  Pallas kernels  155 us (65%)
  starting transfers between devices  22.6 us (9%)
  other arithmetic  21.8 us (9%)
  local copies, waits for them, and re-layouts  18.1 us (8%)
  waiting for transfers between devices  15.5 us (6%)
  matrix products  3.99 us (2%)
    pallas_call x1, Pallas kernels, forward_pallas(): pl.pallas_call(forward_kernel, out_shape=(jax.ShapeDtypeStruct((planes, d...  59.3 us
    pallas_call x1, Pallas kernels, send_back(): pl.pallas_call(return_kernel, out_shape=jax.ShapeDtypeStruct((members, sl...  40.2 us
    pallas_call x1, Pallas kernels, gather_particle(): pl.pallas_call(particle_kernel, out_shape=jax.ShapeDtypeStruct((slabs * t...  31.3 us
    pallas_call x1, Pallas kernels, gather_rows(): pl.pallas_call(gather_kernel, out_shape=jax.ShapeDtypeStruct((total,) + r...  24.4 us
    ppermute x7, waiting for transfers between devices, gather_grid(): got = lax.ppermute(slab, ('space', 'ens'), pairs)  15.5 us
    ppermute x7, starting transfers between devices, gather_grid(): got = lax.ppermute(slab, ('space', 'ens'), pairs)  12.4 us
    unnamed x25, local copies, waits for them, and re-layouts  7.38 us
    add x1, other arithmetic, shards(): forcing = whole_storage * whole_head + source  5.7 us
  transfers between devices with their start and end apart: 9, of which 3 were waited for; matrix products, arithmetic and copies ran while one was open for 10% of the time, Pallas kernels for 30%

profile of v14, /device:TPU:25, one launch (start us, length us, event | category | flops | bytes accessed | tf_op | source)
XLA Modules:
  0.0 238.8 jit_solution(3161077411622482762)
XLA Ops:
  0.7 1.6 broadcast_in_dim.40
  2.3 0.8 constant_dynamic-update-slice_fusion.7
  3.0 1.6 collective-permute-start
  4.6 3.3 %collective-permute-start.1 = (f32[2,64,512]{2,1,0:T(8,128)S(1)}, f32[2,64,512]{2,1,0:T(8,128)S(1)}, u32[]{:S(2)}, u32[]{:S(2)}) collective-permute-start(f32[2,64,512]{2,1,0:T(8,128)S(1)} %get-tuple-element.34), channel_id=1, source_target_pairs={{0,64},{1,65},{2,66},{3,67},{4,68},{5,69},{6,70},{7,71},{8,72},{9,... | collective-permute-start | bytes 786440 | tf_op jit(solution)/shard_map/ppermute | solution.py:324
  7.9 0.7 collective-permute-start.2
  8.7 2.5 %collective-permute-start.3 = (f32[2,64,512]{2,1,0:T(8,128)S(1)}, f32[2,64,512]{2,1,0:T(8,128)S(1)}, u32[]{:S(2)}, u32[]{:S(2)}) collective-permute-start(f32[2,64,512]{2,1,0:T(8,128)S(1)} %get-tuple-element.34), channel_id=1, source_target_pairs={{0,18},{1,19},{2,16},{3,17},{4,22},{5,23},{6,20},{7,21},{8,26},{9,... | collective-permute-start | bytes 786440 | tf_op jit(solution)/shard_map/ppermute | solution.py:324
  11.2 0.7 collective-permute-start.4
  11.8 1.0 collective-permute-done
  12.8 3.6 %collective-permute-start.5 = (f32[2,64,512]{2,1,0:T(8,128)S(1)}, f32[2,64,512]{2,1,0:T(8,128)S(1)}, u32[]{:S(2)}, u32[]{:S(2)}) collective-permute-start(f32[2,64,512]{2,1,0:T(8,128)S(1)} %get-tuple-element.34), channel_id=1, source_target_pairs={{0,82},{1,83},{2,80},{3,81},{4,86},{5,87},{6,84},{7,85},{8,90},{9,... | collective-permute-start | bytes 786440 | tf_op jit(solution)/shard_map/ppermute | solution.py:324
  16.4 0.7 constant_dynamic-update-slice_fusion.6
  17.1 10.8 %collective-permute-done.1 = f32[2,64,512]{2,1,0:T(8,128)S(1)} collective-permute-done((f32[2,64,512]{2,1,0:T(8,128)S(1)}, f32[2,64,512]{2,1,0:T(8,128)S(1)}, u32[]{:S(2)}, u32[]{:S(2)}) %collective-permute-start.1) | collective-permute-done | bytes 262176 | tf_op jit(solution)/shard_map/ppermute | solution.py:324
  28.0 0.7 constant_dynamic-update-slice_fusion.5
  28.7 0.7 constant_dynamic-update-slice_fusion.4
  29.4 0.7 constant_dynamic-update-slice_fusion.3
  30.1 0.7 constant_dynamic-update-slice_fusion.2
  30.9 0.7 constant_dynamic-update-slice_fusion.1
  31.6 3.7 %collective-permute-done.6 = f32[2,64,512]{2,1,0:T(8,128)S(1)} collective-permute-done((f32[2,64,512]{2,1,0:T(8,128)S(1)}, f32[2,64,512]{2,1,0:T(8,128)S(1)}, u32[]{:S(2)}, u32[]{:S(2)}) %collective-permute-start.6) | collective-permute-done | bytes 262176 | tf_op jit(solution)/shard_map/ppermute | solution.py:324
  35.3 0.7 constant_dynamic-update-slice_fusion
  36.0 5.6 %collective-permute-start.7 = (f32[16,64,512]{2,1,0:T(8,128)}, f32[16,64,512]{2,1,0:T(8,128)}, u32[]{:S(2)}, u32[]{:S(2)}) collective-permute-start(f32[16,64,512]{2,1,0:T(8,128)} %constant_dynamic-update-slice_fusion), channel_id=1, source_target_pairs={{0,1},{1,0},{2,3},{3,2},{4,5},{5,4},{6,7},{7,6},{8,9},{9,8},{10,11... | collective-permute-start | bytes 6291464 | tf_op jit(solution)/shard_map/ppermute | solution.py:411
  41.6 2.2 scatter_custom_fusion
  43.8 1.7 reshape.120
  45.5 31.3 %shard_map.113.log_ref = f32[16,64,512]{2,1,0:T(8,128)} custom-call(f32[8,2,64,512]{3,2,1,0:T(8,128)} %log_ref.1), custom_call_target="tpu_custom_call" | custom-call | tf_op jit(solution)/shard_map/pallas_call | solution.py:374
  77.5 1.2 fusion.14
  78.8 0.6 pad_clamp_fusion
  79.3 0.5 broadcast_divide_fusion
  79.9 5.7 %multiply_add_fusion = (f32[16,64,512]{2,1,0:T(8,128)}, f32[16,64,512]{2,1,0:T(8,128)}, f32[16,64,512]{2,1,0:T(8,128)}) fusion(f32[16,64,512]{2,1,0:T(8,128)S(1)} %reshape.120, f32[16,64,512]{2,1,0:T(8,128)} %collective-permute-done.7, f32[16,64,512]{2,1,0:T(8,128)} %constant_dynamic-update-slice_fusion, pred[]{:T(512)S(6)} %eq.20), kind=kLoop, calls=%fused_computation.6 | loop fusion | flops 2097152 | bytes 12582913 | tf_op jit(solution)/shard_map/add | solution.py:420
  85.6 59.3 %shard_map.114 = (f32[16,64,512]{2,1,0:T(8,128)}, f32[128,8,512]{2,1,0:T(8,128)}) custom-call(f32[16,64,512]{2,1,0:T(8,128)} %shard_map.113.log_ref, f32[16,64,512]{2,1,0:T(8,128)} %get-tuple-element.32.sto_ref, f32[16,64,512]{2,1,0:T(8,128)} %get-tuple-element.31.init_ref, f32[16,64,512]{2,1,0:T(8,128)} %get-tuple-element.30.forc_ref, f32[8,128,512]{2,1,0:T(8,128)} %bitcast.37), custom_call_target="tpu_custom_call" | custom-call | tf_op jit(solution)/shard_map/pallas_call | solution.py:157
  144.9 2.1 copy.26
  147.0 0.8 gather_fusion
  147.8 0.3 scatter.9.row_ref
  148.1 0.6 copy-done.4
  148.7 24.4 %shard_map.115 = f32[128,8,128]{2,1,0:T(8,128)} custom-call(f32[1,8,128]{2,1,0:T(8,128)} %copy-done.4), custom_call_target="tpu_custom_call" | custom-call | tf_op jit(solution)/shard_map/pallas_call | solution.py:235
  173.1 1.4 fusion.15
  174.6 1.1 broadcast_subtract_fusion
  175.6 0.3 convolution_multiply_fusion
  176.0 4.7 %all-to-all-start = ((f32[1,16,64,512]{3,2,0,1:T(8,128)}), f32[1,16,64,512]{3,2,0,1:T(8,128)}, u32[]{:S(2)}, u32[]{:S(2)}) async-start(f32[1,16,64,512]{3,2,0,1:T(8,128)} %bitcast.39), calls=%async_computation | async-start | bytes 4194304 | tf_op jit(solution)/shard_map/all_to_all | solution.py:427
  180.7 2.9 %cholesky.16 = f32[32,32]{1,0:T(8,128)S(1)} custom-call(f32[32,32]{1,0:T(8,128)S(1)} %fusion.13), custom_call_target="Cholesky" | custom-call | tf_op jit(solution)/shard_map/jit(cholesky)/cholesky | solution.py:440
  183.7 0.6 compare_reduce_fusion
  184.3 0.7 fusion.7
  185.0 2.4 %custom-call.8 = f32[1,32,32]{1,2,0:T(8,128)S(1)} custom-call(f32[1,32,32]{2,1,0:T(8,128)S(1)} %fusion.7), custom_call_target="InvertDiagBlocksLowerTriangular" | custom-call | tf_op jit(solution)/shard_map/triangular_solve | solution.py:24
  187.4 0.3 fusion.10
  187.7 0.2 fusion.8
  187.8 0.3 convolution_bitcast_fusion
  188.2 3.0 %fusion.1 = f32[128,8,512]{2,0,1:T(8,128)S(1)} fusion(f32[128,128,1]{1,0,2:T(8,128)S(1)} %convolution_bitcast_fusion, f32[128,8,512]{2,1,0:T(8,128)S(1)} %copy-done), kind=kOutput, calls=%fused_computation.4 | convolution fusion | flops 805306368 | bytes 4259840 | tf_op jit(solution)/shard_map/jk,kry->jry/dot_general | solution.py:444
  191.2 2.8 %fusion.column_ref = f32[128,8,512]{2,1,0:T(8,128)} fusion(f32[128,8,512]{2,1,0:T(8,128)S(1)} %copy-done, f32[128,8,512]{2,0,1:T(8,128)S(1)} %fusion.1), kind=kLoop, calls=%fused_computation.3 | loop fusion | flops 1048576 | bytes 6291456 | tf_op jit(solution)/shard_map/add | solution.py:445
  194.0 40.2 %shard_map.116 = f32[8,128,512]{2,1,0:T(8,128)} custom-call(f32[128,8,512]{2,1,0:T(8,128)} %fusion.column_ref), custom_call_target="tpu_custom_call" | custom-call | tf_op jit(solution)/shard_map/pallas_call | solution.py:297
  234.2 3.3 %copy.44 = f32[8,2,64,512]{3,2,1,0:T(8,128)} copy(f32[8,2,64,512]{3,2,1,0:T(8,128)} %bitcast.3) | data formatting | bytes 4194304
  237.5 1.3 copy.45
  (35 shorter events, 0.3 us)
Async XLA Ops:
  0.6 1.6 copy-start.2
  0.6 1.6 copy-start.3
  3.0 38.6 %copy-start.8 = (s32[16]{0:T(128)S(1)}, s32[16]{0:T(128)}, u32[]{:S(2)}) copy-start(s32[16]{0:T(128)} %param.17) | copy-start | bytes 196
  3.0 9.8 %collective-permute-start = (f32[2,64,512]{2,1,0:T(8,128)S(1)}, f32[2,64,512]{2,1,0:T(8,128)S(1)}, u32[]{:S(2)}, u32[]{:S(2)}) collective-permute-start(f32[2,64,512]{2,1,0:T(8,128)S(1)} %get-tuple-element.34), channel_id=1, source_target_pairs={{0,32},{1,33},{2,34},{3,35},{4,36},{5,37},{6,38},{7,39},{8,40},{9,... | collective-permute-start | bytes 786440 | tf_op jit(solution)/shard_map/ppermute | solution.py:324
  4.6 23.3 %collective-permute-start.1 = (f32[2,64,512]{2,1,0:T(8,128)S(1)}, f32[2,64,512]{2,1,0:T(8,128)S(1)}, u32[]{:S(2)}, u32[]{:S(2)}) collective-permute-start(f32[2,64,512]{2,1,0:T(8,128)S(1)} %get-tuple-element.34), channel_id=1, source_target_pairs={{0,64},{1,65},{2,66},{3,67},{4,68},{5,69},{6,70},{7,71},{8,72},{9,... | collective-permute-start | bytes 786440 | tf_op jit(solution)/shard_map/ppermute | solution.py:324
  7.9 20.7 %collective-permute-start.2 = (f32[2,64,512]{2,1,0:T(8,128)S(1)}, f32[2,64,512]{2,1,0:T(8,128)S(1)}, u32[]{:S(2)}, u32[]{:S(2)}) collective-permute-start(f32[2,64,512]{2,1,0:T(8,128)S(1)} %get-tuple-element.34), channel_id=1, source_target_pairs={{0,96},{1,97},{2,98},{3,99},{4,100},{5,101},{6,102},{7,103},{8,104... | collective-permute-start | bytes 786440 | tf_op jit(solution)/shard_map/ppermute | solution.py:324
  8.7 20.7 %collective-permute-start.3 = (f32[2,64,512]{2,1,0:T(8,128)S(1)}, f32[2,64,512]{2,1,0:T(8,128)S(1)}, u32[]{:S(2)}, u32[]{:S(2)}) collective-permute-start(f32[2,64,512]{2,1,0:T(8,128)S(1)} %get-tuple-element.34), channel_id=1, source_target_pairs={{0,18},{1,19},{2,16},{3,17},{4,22},{5,23},{6,20},{7,21},{8,26},{9,... | collective-permute-start | bytes 786440 | tf_op jit(solution)/shard_map/ppermute | solution.py:324
  11.2 19.0 %collective-permute-start.4 = (f32[2,64,512]{2,1,0:T(8,128)S(1)}, f32[2,64,512]{2,1,0:T(8,128)S(1)}, u32[]{:S(2)}, u32[]{:S(2)}) collective-permute-start(f32[2,64,512]{2,1,0:T(8,128)S(1)} %get-tuple-element.34), channel_id=1, source_target_pairs={{0,50},{1,51},{2,48},{3,49},{4,54},{5,55},{6,52},{7,53},{8,58},{9,... | collective-permute-start | bytes 786440 | tf_op jit(solution)/shard_map/ppermute | solution.py:324
  12.8 18.1 %collective-permute-start.5 = (f32[2,64,512]{2,1,0:T(8,128)S(1)}, f32[2,64,512]{2,1,0:T(8,128)S(1)}, u32[]{:S(2)}, u32[]{:S(2)}) collective-permute-start(f32[2,64,512]{2,1,0:T(8,128)S(1)} %get-tuple-element.34), channel_id=1, source_target_pairs={{0,82},{1,83},{2,80},{3,81},{4,86},{5,87},{6,84},{7,85},{8,90},{9,... | collective-permute-start | bytes 786440 | tf_op jit(solution)/shard_map/ppermute | solution.py:324
  28.0 7.3 %collective-permute-start.6 = (f32[2,64,512]{2,1,0:T(8,128)S(1)}, f32[2,64,512]{2,1,0:T(8,128)S(1)}, u32[]{:S(2)}, u32[]{:S(2)}) collective-permute-start(f32[2,64,512]{2,1,0:T(8,128)S(1)} %get-tuple-element.34), channel_id=1, source_target_pairs={{0,114},{1,115},{2,112},{3,113},{4,118},{5,119},{6,116},{7,117},{8... | collective-permute-start | bytes 786440 | tf_op jit(solution)/shard_map/ppermute | solution.py:324
  36.0 43.8 %collective-permute-start.7 = (f32[16,64,512]{2,1,0:T(8,128)}, f32[16,64,512]{2,1,0:T(8,128)}, u32[]{:S(2)}, u32[]{:S(2)}) collective-permute-start(f32[16,64,512]{2,1,0:T(8,128)} %constant_dynamic-update-slice_fusion), channel_id=1, source_target_pairs={{0,1},{1,0},{2,3},{3,2},{4,5},{5,4},{6,7},{7,6},{8,9},{9,8},{10,11... | collective-permute-start | bytes 6291464 | tf_op jit(solution)/shard_map/ppermute | solution.py:411
  45.5 33.2 %copy-start.9 = (s32[32]{0:T(128)S(1)}, s32[32]{0:T(128)}, u32[]{:S(2)}) copy-start(s32[32]{0:T(128)} %param.19) | copy-start | bytes 388
  45.5 33.8 %copy-start.10 = (f32[32]{0:T(128)S(1)}, f32[32]{0:T(128)}, u32[]{:S(2)}) copy-start(f32[32]{0:T(128)} %param.21) | copy-start | bytes 388
  144.9 3.0 %copy-start.7 = (f32[1,1,32]{2,1,0:T(1,128)S(1)}, f32[1,1,32]{2,1,0:T(1,128)}, u32[]{:S(2)}) copy-start(f32[1,1,32]{2,1,0:T(1,128)} %fusion.14) | copy-start | bytes 388
  144.9 28.3 %copy-start.6 = (f32[32]{0:T(128)S(1)}, f32[32]{0:T(128)}, u32[]{:S(2)}) copy-start(f32[32]{0:T(128)} %param.20) | copy-start | bytes 388
  148.1 0.6 copy-start.4
  176.0 4.7 %copy-start.5 = (f32[32]{0:T(128)S(1)}, f32[32]{0:T(128)}, u32[]{:S(2)}) copy-start(f32[32]{0:T(128)} %broadcast_divide_fusion) | copy-start | bytes 388
  176.0 12.2 %copy-start = (f32[128,8,512]{2,1,0:T(8,128)S(1)}, f32[128,8,512]{2,1,0:T(8,128)}, u32[]{:S(2)}) copy-start(f32[128,8,512]{2,1,0:T(8,128)} %get-tuple-element.29) | copy-start | bytes 6291460
  176.0 58.2 %all-to-all-start = ((f32[1,16,64,512]{3,2,0,1:T(8,128)}), f32[1,16,64,512]{3,2,0,1:T(8,128)}, u32[]{:S(2)}, u32[]{:S(2)}) async-start(f32[1,16,64,512]{3,2,0,1:T(8,128)} %bitcast.39), calls=%async_computation | async-start | bytes 4194304 | tf_op jit(solution)/shard_map/all_to_all | solution.py:427
  234.2 3.3 %copy-start.1 = (f32[8,128,512]{2,1,0:T(8,128)S(1)}, f32[8,128,512]{2,1,0:T(8,128)}, u32[]{:S(2)}) copy-start(f32[8,128,512]{2,1,0:T(8,128)} %shard_map.116) | copy-start | bytes 6291460

commit v15 on v11

--- a/solution.py
+++ b/solution.py
@@ -47,6 +47,15 @@
     return jnp.where(valid, x, 0.0)
 
 
+def roll_plane(x, b, c):
+    depth, across = x.shape
+    if b != 0:
+        x = pltpu.roll(x, (-b) % depth, 0)
+    if c != 0:
+        x = pltpu.roll(x, (-c) % across, 1)
+    return x
+
+
 def forward_kernel(
     log_ref, sto_ref, init_ref, forc_ref, rows_ref, out_ref, band_ref,
     perm, trans, diag, head_a, head_b, band_send, band_recv, local_sem,
@@ -113,7 +122,7 @@
         for k, (a, b, c) in enumerate(HALF):
             back = p - a
             inside = (back >= 0) & (back < planes)
-            behind = shift_plane(trans[k, jnp.clip(back, 0, planes - 1)], -b, -c)
+            behind = roll_plane(trans[k, jnp.clip(back, 0, planes - 1)], -b, -c)
             total = total + trans[k, p] + jnp.where(inside, behind, 0.0)
         diag[p] = total
         return carry
@@ -124,9 +133,9 @@
         def body(p, carry):
             gathered = None
             for k, (a, b, c) in enumerate(HALF):
-                ahead = trans[k, p] * shift_plane(source[p + 1 + a], b, c)
+                ahead = trans[k, p] * roll_plane(source[p + 1 + a], b, c)
                 back = jnp.clip(p - a, 0, planes - 1)
-                flow = shift_plane(trans[k, back] * source[p + 1 - a], -b, -c)
+                flow = roll_plane(trans[k, back] * source[p + 1 - a], -b, -c)
                 term = ahead + flow
                 gathered = term if gathered is None else gathered + term
             value = (1.0 - OMEGA) * source[p + 1] + OMEGA * (forc_ref[p] + gathered) / diag[p]

time: 224 us -> 222 us (level)
  no operation moved by 1% of the time
where the time goes in v15:
time: 222 us; the launch traced here: 221 us
  Pallas kernels  117 us (53%)
  waiting for transfers between devices  31.1 us (14%)
  starting transfers between devices  27.2 us (12%)
  other arithmetic  21.8 us (10%)
  local copies, waits for them, and re-layouts  18.2 us (8%)
  matrix products  3.99 us (2%)
    pallas_call x1, Pallas kernels, forward_pallas(): pl.pallas_call(forward_kernel, out_shape=(jax.ShapeDtypeStruct((planes, d...  57.7 us
    pallas_call x1, Pallas kernels, send_back(): pl.pallas_call(return_kernel, out_shape=jax.ShapeDtypeStruct((members, sl...  40.7 us
    pallas_call x1, Pallas kernels, gather_rows(): pl.pallas_call(gather_kernel, out_shape=jax.ShapeDtypeStruct((total,) + r...  18.4 us
    all_to_all x1, waiting for transfers between devices, shards(): whole_log = lax.all_to_all(log_perm, 'space', 0, 1, tiled=True)  15.5 us
    ppermute x7, waiting for transfers between devices, gather_grid(): got = lax.ppermute(slab, ('space', 'ens'), pairs)  15.5 us
    ppermute x7, starting transfers between devices, gather_grid(): got = lax.ppermute(slab, ('space', 'ens'), pairs)  12.4 us
    unnamed x25, local copies, waits for them, and re-layouts  7.38 us
    add x1, other arithmetic, shards(): forcing = whole_storage * whole_head + source  5.7 us
  transfers between devices with their start and end apart: 10, of which 4 were waited for; matrix products, arithmetic and copies ran while one was open for 13% of the time, Pallas kernels for 18%

profile of v15, /device:TPU:25, one launch (start us, length us, event | category | flops | bytes accessed | tf_op | source)
XLA Modules:
  0.0 220.6 jit_solution(6685159095877964856)
XLA Ops:
  0.7 1.6 broadcast_in_dim.40
  2.3 0.8 constant_dynamic-update-slice_fusion.7
  3.0 1.6 collective-permute-start
  4.6 3.3 %collective-permute-start.1 = (f32[2,64,512]{2,1,0:T(8,128)S(1)}, f32[2,64,512]{2,1,0:T(8,128)S(1)}, u32[]{:S(2)}, u32[]{:S(2)}) collective-permute-start(f32[2,64,512]{2,1,0:T(8,128)S(1)} %get-tuple-element.34), channel_id=1, source_target_pairs={{0,64},{1,65},{2,66},{3,67},{4,68},{5,69},{6,70},{7,71},{8,72},{9,... | collective-permute-start | bytes 786440 | tf_op jit(solution)/shard_map/ppermute | solution.py:333
  7.9 0.7 collective-permute-start.2
  8.7 2.5 %collective-permute-start.3 = (f32[2,64,512]{2,1,0:T(8,128)S(1)}, f32[2,64,512]{2,1,0:T(8,128)S(1)}, u32[]{:S(2)}, u32[]{:S(2)}) collective-permute-start(f32[2,64,512]{2,1,0:T(8,128)S(1)} %get-tuple-element.34), channel_id=1, source_target_pairs={{0,18},{1,19},{2,16},{3,17},{4,22},{5,23},{6,20},{7,21},{8,26},{9,... | collective-permute-start | bytes 786440 | tf_op jit(solution)/shard_map/ppermute | solution.py:333
  11.2 0.7 collective-permute-start.4
  11.8 1.0 collective-permute-done
  12.8 3.6 %collective-permute-start.5 = (f32[2,64,512]{2,1,0:T(8,128)S(1)}, f32[2,64,512]{2,1,0:T(8,128)S(1)}, u32[]{:S(2)}, u32[]{:S(2)}) collective-permute-start(f32[2,64,512]{2,1,0:T(8,128)S(1)} %get-tuple-element.34), channel_id=1, source_target_pairs={{0,82},{1,83},{2,80},{3,81},{4,86},{5,87},{6,84},{7,85},{8,90},{9,... | collective-permute-start | bytes 786440 | tf_op jit(solution)/shard_map/ppermute | solution.py:333
  16.4 0.7 constant_dynamic-update-slice_fusion.6
  17.1 10.8 %collective-permute-done.1 = f32[2,64,512]{2,1,0:T(8,128)S(1)} collective-permute-done((f32[2,64,512]{2,1,0:T(8,128)S(1)}, f32[2,64,512]{2,1,0:T(8,128)S(1)}, u32[]{:S(2)}, u32[]{:S(2)}) %collective-permute-start.1) | collective-permute-done | bytes 262176 | tf_op jit(solution)/shard_map/ppermute | solution.py:333
  28.0 0.7 constant_dynamic-update-slice_fusion.5
  28.7 0.7 constant_dynamic-update-slice_fusion.4
  29.4 0.7 constant_dynamic-update-slice_fusion.3
  30.1 0.7 constant_dynamic-update-slice_fusion.2
  30.9 0.7 constant_dynamic-update-slice_fusion.1
  31.6 3.7 %collective-permute-done.6 = f32[2,64,512]{2,1,0:T(8,128)S(1)} collective-permute-done((f32[2,64,512]{2,1,0:T(8,128)S(1)}, f32[2,64,512]{2,1,0:T(8,128)S(1)}, u32[]{:S(2)}, u32[]{:S(2)}) %collective-permute-start.6) | collective-permute-done | bytes 262176 | tf_op jit(solution)/shard_map/ppermute | solution.py:333
  35.3 0.7 constant_dynamic-update-slice_fusion
  36.0 5.6 %collective-permute-start.7 = (f32[16,64,512]{2,1,0:T(8,128)}, f32[16,64,512]{2,1,0:T(8,128)}, u32[]{:S(2)}, u32[]{:S(2)}) collective-permute-start(f32[16,64,512]{2,1,0:T(8,128)} %constant_dynamic-update-slice_fusion), channel_id=1, source_target_pairs={{0,1},{1,0},{2,3},{3,2},{4,5},{5,4},{6,7},{7,6},{8,9},{9,8},{10,11... | collective-permute-start | bytes 6291464 | tf_op jit(solution)/shard_map/ppermute | solution.py:365
  41.6 4.6 %all-to-all-start = ((f32[8,2,64,512]{3,2,1,0:T(8,128)}), f32[8,2,64,512]{3,2,1,0:T(8,128)}, u32[]{:S(2)}, u32[]{:S(2)}) async-start(f32[8,2,64,512]{3,2,1,0:T(8,128)} %param.14), calls=%async_computation | async-start | bytes 4194304 | tf_op jit(solution)/shard_map/all_to_all | solution.py:361
  46.2 2.2 scatter_custom_fusion
  48.4 1.8 reshape.124
  50.8 1.2 fusion.14
  52.0 0.6 pad_clamp_fusion
  52.6 0.5 broadcast_divide_fusion
  53.2 5.7 %multiply_add_fusion = (f32[16,64,512]{2,1,0:T(8,128)}, f32[16,64,512]{2,1,0:T(8,128)}, f32[16,64,512]{2,1,0:T(8,128)}) fusion(f32[16,64,512]{2,1,0:T(8,128)S(1)} %reshape.124, f32[16,64,512]{2,1,0:T(8,128)} %collective-permute-done.7, f32[16,64,512]{2,1,0:T(8,128)} %constant_dynamic-update-slice_fusion, pred[]{:T(512)S(6)} %eq.20), kind=kLoop, calls=%fused_computation.6 | loop fusion | flops 2097152 | bytes 12582913 | tf_op jit(solution)/shard_map/add | solution.py:374
  58.9 15.5 %all-to-all-done = f32[8,2,64,512]{3,2,1,0:T(8,128)} async-done(((f32[8,2,64,512]{3,2,1,0:T(8,128)}), f32[8,2,64,512]{3,2,1,0:T(8,128)}, u32[]{:S(2)}, u32[]{:S(2)}) %all-to-all-start) | async-done | bytes 2097184 | tf_op jit(solution)/shard_map/all_to_all | solution.py:361
  74.4 57.7 %shard_map.113 = (f32[16,64,512]{2,1,0:T(8,128)}, f32[128,8,512]{2,1,0:T(8,128)}) custom-call(f32[16,64,512]{2,1,0:T(8,128)} %bitcast.log_ref, f32[16,64,512]{2,1,0:T(8,128)} %get-tuple-element.32.sto_ref, f32[16,64,512]{2,1,0:T(8,128)} %get-tuple-element.31.init_ref, f32[16,64,512]{2,1,0:T(8,128)} %get-tuple-element.30.forc_ref, f32[8,128,512]{2,1,0:T(8,128)} %bitcast.1.rows_ref), custom_call_target="tpu_custom_call" | custom-call | tf_op jit(solution)/shard_map/pallas_call | solution.py:166
  132.1 2.1 copy.26
  134.3 0.8 gather_fusion
  135.1 0.3 scatter.9.row_ref
  135.4 0.6 copy-done.4
  136.0 18.4 %shard_map.114 = f32[128,8,128]{2,1,0:T(8,128)} custom-call(f32[1,8,128]{2,1,0:T(8,128)} %copy-done.4), custom_call_target="tpu_custom_call" | custom-call | tf_op jit(solution)/shard_map/pallas_call | solution.py:244
  154.4 1.4 fusion.15
  155.8 1.1 broadcast_subtract_fusion
  156.9 0.3 convolution_multiply_fusion
  157.2 4.7 %all-to-all-start.1 = ((f32[1,16,64,512]{3,2,0,1:T(8,128)}), f32[1,16,64,512]{3,2,0,1:T(8,128)}, u32[]{:S(2)}, u32[]{:S(2)}) async-start(f32[1,16,64,512]{3,2,0,1:T(8,128)} %bitcast.39), calls=%async_computation.1 | async-start | bytes 4194304 | tf_op jit(solution)/shard_map/all_to_all | solution.py:381
  162.0 2.9 %cholesky.16 = f32[32,32]{1,0:T(8,128)S(1)} custom-call(f32[32,32]{1,0:T(8,128)S(1)} %fusion.13), custom_call_target="Cholesky" | custom-call | tf_op jit(solution)/shard_map/jit(cholesky)/cholesky | solution.py:394
  164.9 0.6 compare_reduce_fusion
  165.6 0.7 fusion.7
  166.2 2.4 %custom-call.8 = f32[1,32,32]{1,2,0:T(8,128)S(1)} custom-call(f32[1,32,32]{2,1,0:T(8,128)S(1)} %fusion.7), custom_call_target="InvertDiagBlocksLowerTriangular" | custom-call | tf_op jit(solution)/shard_map/triangular_solve | solution.py:24
  168.7 0.3 fusion.10
  169.1 0.3 convolution_bitcast_fusion
  169.4 3.0 %fusion.1 = f32[128,8,512]{2,0,1:T(8,128)S(1)} fusion(f32[128,128,1]{1,0,2:T(8,128)S(1)} %convolution_bitcast_fusion, f32[128,8,512]{2,1,0:T(8,128)S(1)} %copy-done), kind=kOutput, calls=%fused_computation.4 | convolution fusion | flops 805306368 | bytes 4259840 | tf_op jit(solution)/shard_map/jk,kry->jry/dot_general | solution.py:398
  172.4 2.8 %fusion.column_ref = f32[128,8,512]{2,1,0:T(8,128)} fusion(f32[128,8,512]{2,1,0:T(8,128)S(1)} %copy-done, f32[128,8,512]{2,0,1:T(8,128)S(1)} %fusion.1), kind=kLoop, calls=%fused_computation.3 | loop fusion | flops 1048576 | bytes 6291456 | tf_op jit(solution)/shard_map/add | solution.py:399
  175.2 40.7 %shard_map.115 = f32[8,128,512]{2,1,0:T(8,128)} custom-call(f32[128,8,512]{2,1,0:T(8,128)} %fusion.column_ref), custom_call_target="tpu_custom_call" | custom-call | tf_op jit(solution)/shard_map/pallas_call | solution.py:306
  216.0 3.3 %copy.44 = f32[8,2,64,512]{3,2,1,0:T(8,128)} copy(f32[8,2,64,512]{3,2,1,0:T(8,128)} %bitcast.4) | data formatting | bytes 4194304
  219.3 1.3 copy.45
  (36 shorter events, 0.4 us)
Async XLA Ops:
  0.6 1.6 copy-start.2
  0.6 1.6 copy-start.3
  3.0 9.8 %collective-permute-start = (f32[2,64,512]{2,1,0:T(8,128)S(1)}, f32[2,64,512]{2,1,0:T(8,128)S(1)}, u32[]{:S(2)}, u32[]{:S(2)}) collective-permute-start(f32[2,64,512]{2,1,0:T(8,128)S(1)} %get-tuple-element.34), channel_id=1, source_target_pairs={{0,32},{1,33},{2,34},{3,35},{4,36},{5,37},{6,38},{7,39},{8,40},{9,... | collective-permute-start | bytes 786440 | tf_op jit(solution)/shard_map/ppermute | solution.py:333
  4.6 23.3 %collective-permute-start.1 = (f32[2,64,512]{2,1,0:T(8,128)S(1)}, f32[2,64,512]{2,1,0:T(8,128)S(1)}, u32[]{:S(2)}, u32[]{:S(2)}) collective-permute-start(f32[2,64,512]{2,1,0:T(8,128)S(1)} %get-tuple-element.34), channel_id=1, source_target_pairs={{0,64},{1,65},{2,66},{3,67},{4,68},{5,69},{6,70},{7,71},{8,72},{9,... | collective-permute-start | bytes 786440 | tf_op jit(solution)/shard_map/ppermute | solution.py:333
  7.9 20.7 %collective-permute-start.2 = (f32[2,64,512]{2,1,0:T(8,128)S(1)}, f32[2,64,512]{2,1,0:T(8,128)S(1)}, u32[]{:S(2)}, u32[]{:S(2)}) collective-permute-start(f32[2,64,512]{2,1,0:T(8,128)S(1)} %get-tuple-element.34), channel_id=1, source_target_pairs={{0,96},{1,97},{2,98},{3,99},{4,100},{5,101},{6,102},{7,103},{8,104... | collective-permute-start | bytes 786440 | tf_op jit(solution)/shard_map/ppermute | solution.py:333
  8.7 20.7 %collective-permute-start.3 = (f32[2,64,512]{2,1,0:T(8,128)S(1)}, f32[2,64,512]{2,1,0:T(8,128)S(1)}, u32[]{:S(2)}, u32[]{:S(2)}) collective-permute-start(f32[2,64,512]{2,1,0:T(8,128)S(1)} %get-tuple-element.34), channel_id=1, source_target_pairs={{0,18},{1,19},{2,16},{3,17},{4,22},{5,23},{6,20},{7,21},{8,26},{9,... | collective-permute-start | bytes 786440 | tf_op jit(solution)/shard_map/ppermute | solution.py:333
  11.2 19.0 %collective-permute-start.4 = (f32[2,64,512]{2,1,0:T(8,128)S(1)}, f32[2,64,512]{2,1,0:T(8,128)S(1)}, u32[]{:S(2)}, u32[]{:S(2)}) collective-permute-start(f32[2,64,512]{2,1,0:T(8,128)S(1)} %get-tuple-element.34), channel_id=1, source_target_pairs={{0,50},{1,51},{2,48},{3,49},{4,54},{5,55},{6,52},{7,53},{8,58},{9,... | collective-permute-start | bytes 786440 | tf_op jit(solution)/shard_map/ppermute | solution.py:333
  12.8 18.1 %collective-permute-start.5 = (f32[2,64,512]{2,1,0:T(8,128)S(1)}, f32[2,64,512]{2,1,0:T(8,128)S(1)}, u32[]{:S(2)}, u32[]{:S(2)}) collective-permute-start(f32[2,64,512]{2,1,0:T(8,128)S(1)} %get-tuple-element.34), channel_id=1, source_target_pairs={{0,82},{1,83},{2,80},{3,81},{4,86},{5,87},{6,84},{7,85},{8,90},{9,... | collective-permute-start | bytes 786440 | tf_op jit(solution)/shard_map/ppermute | solution.py:333
  28.0 7.3 %collective-permute-start.6 = (f32[2,64,512]{2,1,0:T(8,128)S(1)}, f32[2,64,512]{2,1,0:T(8,128)S(1)}, u32[]{:S(2)}, u32[]{:S(2)}) collective-permute-start(f32[2,64,512]{2,1,0:T(8,128)S(1)} %get-tuple-element.34), channel_id=1, source_target_pairs={{0,114},{1,115},{2,112},{3,113},{4,118},{5,119},{6,116},{7,117},{8... | collective-permute-start | bytes 786440 | tf_op jit(solution)/shard_map/ppermute | solution.py:333
  36.0 10.2 %copy-start.8 = (s32[16]{0:T(128)S(1)}, s32[16]{0:T(128)}, u32[]{:S(2)}) copy-start(s32[16]{0:T(128)} %param.17) | copy-start | bytes 196
  36.0 17.1 %collective-permute-start.7 = (f32[16,64,512]{2,1,0:T(8,128)}, f32[16,64,512]{2,1,0:T(8,128)}, u32[]{:S(2)}, u32[]{:S(2)}) collective-permute-start(f32[16,64,512]{2,1,0:T(8,128)} %constant_dynamic-update-slice_fusion), channel_id=1, source_target_pairs={{0,1},{1,0},{2,3},{3,2},{4,5},{5,4},{6,7},{7,6},{8,9},{9,8},{10,11... | collective-permute-start | bytes 6291464 | tf_op jit(solution)/shard_map/ppermute | solution.py:365
  41.6 32.8 %all-to-all-start = ((f32[8,2,64,512]{3,2,1,0:T(8,128)}), f32[8,2,64,512]{3,2,1,0:T(8,128)}, u32[]{:S(2)}, u32[]{:S(2)}) async-start(f32[8,2,64,512]{3,2,1,0:T(8,128)} %param.14), calls=%async_computation | async-start | bytes 4194304 | tf_op jit(solution)/shard_map/all_to_all | solution.py:361
  48.4 3.6 %copy-start.9 = (s32[32]{0:T(128)S(1)}, s32[32]{0:T(128)}, u32[]{:S(2)}) copy-start(s32[32]{0:T(128)} %param.19) | copy-start | bytes 388
  48.4 4.2 %copy-start.10 = (f32[32]{0:T(128)S(1)}, f32[32]{0:T(128)}, u32[]{:S(2)}) copy-start(f32[32]{0:T(128)} %param.21) | copy-start | bytes 388
  132.1 3.0 %copy-start.7 = (f32[1,1,32]{2,1,0:T(1,128)S(1)}, f32[1,1,32]{2,1,0:T(1,128)}, u32[]{:S(2)}) copy-start(f32[1,1,32]{2,1,0:T(1,128)} %fusion.14) | copy-start | bytes 388
  132.1 22.2 %copy-start.6 = (f32[32]{0:T(128)S(1)}, f32[32]{0:T(128)}, u32[]{:S(2)}) copy-start(f32[32]{0:T(128)} %param.20) | copy-start | bytes 388
  135.4 0.6 copy-start.4
  157.2 4.7 %copy-start.5 = (f32[32]{0:T(128)S(1)}, f32[32]{0:T(128)}, u32[]{:S(2)}) copy-start(f32[32]{0:T(128)} %broadcast_divide_fusion) | copy-start | bytes 388
  157.2 12.2 %copy-start = (f32[128,8,512]{2,1,0:T(8,128)S(1)}, f32[128,8,512]{2,1,0:T(8,128)}, u32[]{:S(2)}) copy-start(f32[128,8,512]{2,1,0:T(8,128)} %get-tuple-element.29) | copy-start | bytes 6291460
  157.2 58.7 %all-to-all-start.1 = ((f32[1,16,64,512]{3,2,0,1:T(8,128)}), f32[1,16,64,512]{3,2,0,1:T(8,128)}, u32[]{:S(2)}, u32[]{:S(2)}) async-start(f32[1,16,64,512]{3,2,0,1:T(8,128)} %bitcast.39), calls=%async_computation.1 | async-start | bytes 4194304 | tf_op jit(solution)/shard_map/all_to_all | solution.py:381
  216.0 3.3 %copy-start.1 = (f32[8,128,512]{2,1,0:T(8,128)S(1)}, f32[8,128,512]{2,1,0:T(8,128)}, u32[]{:S(2)}) copy-start(f32[8,128,512]{2,1,0:T(8,128)} %shard_map.115) | copy-start | bytes 6291460

commit v16 on v15

--- a/solution.py
+++ b/solution.py
@@ -339,6 +339,79 @@
     return grid
 
 
+def grid_kernel(slab_ref, mine_ref, other_ref, send_sems, recv_sems, local_sem, pair_sems):
+    thick = slab_ref.shape[0]
+    rows = mine_ref.shape[0] // thick // 2
+    me_s = lax.axis_index("space")
+    me_e = lax.axis_index("ens")
+    z, half = me_s // 2, me_s % 2
+    across_x = me_e + 2 - 4 * ((me_e // 2) % 2)
+    partner = me_e + 1 - 2 * (me_e % 2)
+    mesh_id = pl.DeviceIdType.MESH
+    patterns = [(0, dz) for dz in range(1, rows)] + [(1, dz) for dz in range(rows)]
+
+    def place(flip, dz, sign):
+        s = ((z + sign * dz + rows) % rows) * 2 + (half + flip) % 2
+        return s, (across_x if flip else me_e)
+
+    barrier = pltpu.get_barrier_semaphore()
+    friends = [place(0, dz, 1) for dz in range(1, rows)] + [place(1, dz, 1) for dz in range(rows)]
+    for s, e in friends + [(me_s, partner)]:
+        pl.semaphore_signal(barrier, 1, device_id=(s, e), device_id_type=mesh_id)
+    pl.semaphore_wait(barrier, len(friends) + 1)
+
+    def push(k, flip, dz, sign):
+        s, e = place(flip, dz, sign)
+        where = me_s if sign > 0 else s
+        return pltpu.make_async_remote_copy(
+            src_ref=slab_ref,
+            dst_ref=mine_ref.at[pl.ds(where * thick, thick)],
+            send_sem=send_sems.at[k],
+            recv_sem=recv_sems.at[k],
+            device_id=(s, e),
+            device_id_type=mesh_id,
+        )
+
+    keep = pltpu.make_async_copy(slab_ref, mine_ref.at[pl.ds(me_s * thick, thick)], local_sem)
+    for k, (flip, dz) in enumerate(patterns):
+        push(k, flip, dz, 1).start()
+    keep.start()
+    keep.wait()
+    for k, (flip, dz) in enumerate(patterns):
+        push(k, flip, dz, 1).wait_send()
+        push(k, flip, dz, -1).wait_recv()
+    swap = pltpu.make_async_remote_copy(
+        src_ref=mine_ref,
+        dst_ref=other_ref,
+        send_sem=pair_sems.at[0],
+        recv_sem=pair_sems.at[1],
+        device_id=(me_s, partner),
+        device_id_type=mesh_id,
+    )
+    swap.start()
+    swap.wait_send()
+    swap.wait_recv()
+
+
+def gather_grids(slab, n_space):
+    thick, depth, across = slab.shape
+    anywhere = pl.BlockSpec(memory_space=pl.ANY)
+    grid = jax.ShapeDtypeStruct((n_space * thick, depth, across), jnp.float32)
+    return pl.pallas_call(
+        grid_kernel,
+        out_shape=(grid, grid),
+        in_specs=[anywhere],
+        out_specs=(anywhere, anywhere),
+        scratch_shapes=[
+            pltpu.SemaphoreType.DMA((n_space - 1,)),
+            pltpu.SemaphoreType.DMA((n_space - 1,)),
+            pltpu.SemaphoreType.DMA,
+            pltpu.SemaphoreType.DMA((2,)),
+        ],
+        compiler_params=pltpu.CompilerParams(collective_id=5, has_side_effects=True),
+    )(slab)
+
+
 def shards(
     log_perm,
     storage,
@@ -360,9 +433,7 @@
 
     whole_log = lax.all_to_all(log_perm, "space", 0, 1, tiled=True)
     core = lax.axis_index("ens") % 2
-    mine = gather_grid(jnp.where(core == 0, storage, head_init), n_space, n_ens)
-    pairs = [(e, e ^ 1) for e in range(n_ens)]
-    other = lax.ppermute(mine, "ens", pairs)
+    mine, other = gather_grids(jnp.where(core == 0, storage, head_init), n_space)
     whole_storage = jnp.where(core == 0, mine, other)
     whole_head = jnp.where(core == 0, other, mine)
     source = (

time: 222 us -> 224 us (level)
  Pallas kernels: 117 us -> 171 us
  waiting for transfers between devices: 31.1 us -> 0.01 us
  starting transfers between devices: 27.2 us -> 12.3 us
  local copies, waits for them, and re-layouts: 18.2 us -> 11.6 us
    pallas_call x0 -> x1, Pallas kernels: none -> 54.2 us  [gather_grids(): pl.pallas_call(grid_kernel, out_shape=(grid, grid), in_specs=[anywhere],...]
    ppermute x8 -> x0, starting transfers between devices: 18 us -> none  [the longest x7 12.4 us: gather_grid(): got = lax.ppermute(slab, ('space', 'ens'), pairs)]
    all_to_all x1, waiting for transfers between devices: 15.5 us -> 0.01 us  [shards(): whole_log = lax.all_to_all(log_perm, 'space', 0, 1, tiled=True)]
    ppermute x8 -> x0, waiting for transfers between devices: 15.5 us -> none  [the longest x7 15.5 us: gather_grid(): got = lax.ppermute(slab, ('space', 'ens'), pairs)]
    dynamic_update_slice x7 -> x0, local copies, waits for them, and re-layouts: 5.04 us -> none  [gather_grid(): grid = lax.dynamic_update_slice_in_dim(grid, got, source * thick, axis=0)]
    all_to_all x1, starting transfers between devices: 4.6 us -> 7.64 us  [shards(): whole_log = lax.all_to_all(log_perm, 'space', 0, 1, tiled=True)]
  transfers between devices with their start and end apart: 10 -> 2, of which waited for: 4 -> 0; matrix products, arithmetic and copies ran while one was open for 13% -> 12% of each run, Pallas kernels for 18% -> 43%
where the time goes in v16:
time: 224 us; the launch traced here: 223 us
  Pallas kernels  171 us (76%)
  other arithmetic  21.9 us (10%)
  starting transfers between devices  12.3 us (5%)
  local copies, waits for them, and re-layouts  11.6 us (5%)
  matrix products  3.99 us (2%)
    pallas_call x1, Pallas kernels, forward_pallas(): pl.pallas_call(forward_kernel, out_shape=(jax.ShapeDtypeStruct((planes, d...  57.7 us
    pallas_call x1, Pallas kernels, gather_grids(): pl.pallas_call(grid_kernel, out_shape=(grid, grid), in_specs=[anywhere],...  54.2 us
    pallas_call x1, Pallas kernels, send_back(): pl.pallas_call(return_kernel, out_shape=jax.ShapeDtypeStruct((members, sl...  40.8 us
    pallas_call x1, Pallas kernels, gather_rows(): pl.pallas_call(gather_kernel, out_shape=jax.ShapeDtypeStruct((total,) + r...  18.7 us
    all_to_all x1, starting transfers between devices, shards(): whole_log = lax.all_to_all(log_perm, 'space', 0, 1, tiled=True)  7.64 us
    unnamed x25, local copies, waits for them, and re-layouts  7.38 us
    add x1, other arithmetic, shards(): forcing = whole_storage * whole_head + source  5.7 us
    all_to_all x1, starting transfers between devices, shards(): head_field = lax.all_to_all(field[None], 'space', 1, 0, tiled=True)  4.66 us
  transfers between devices with their start and end apart: 2, of which 0 were waited for; matrix products, arithmetic and copies ran while one was open for 12% of the time, Pallas kernels for 43%

profile of v16, /device:TPU:25, one launch (start us, length us, event | category | flops | bytes accessed | tf_op | source)
XLA Modules:
  0.0 222.7 jit_solution(4051602857131051441)
XLA Ops:
  0.6 0.0 copy-start.2
  0.6 0.0 copy-start.3
  0.7 0.0 copy-start.8
  0.7 7.6 %all-to-all-start = ((f32[8,2,64,512]{3,2,1,0:T(8,128)}), f32[8,2,64,512]{3,2,1,0:T(8,128)}, u32[]{:S(2)}, u32[]{:S(2)}) async-start(f32[8,2,64,512]{3,2,1,0:T(8,128)} %param.14), calls=%async_computation | async-start | bytes 4194304 | tf_op jit(solution)/shard_map/all_to_all | solution.py:434
  8.3 0.0 copy-done.2
  8.3 0.0 copy-done.3
  8.3 0.7 broadcast_select_fusion.2.slab_ref
  9.1 54.2 %shard_map.113 = (f32[16,64,512]{2,1,0:T(8,128)}, f32[16,64,512]{2,1,0:T(8,128)}) custom-call(f32[2,64,512]{2,1,0:T(8,128)} %broadcast_select_fusion.2.slab_ref), custom_call_target="tpu_custom_call" | custom-call | tf_op jit(solution)/shard_map/pallas_call | solution.py:400
  63.3 0.0 copy-done.8
  63.3 2.2 scatter_custom_fusion
  65.5 1.8 reshape.124
  68.0 1.3 dynamic-slice_bitcast_fusion
  69.2 0.0 copy-done.9
  69.2 0.6 pad_clamp_fusion
  69.8 0.0 copy-done.10
  69.8 0.6 broadcast_divide_fusion
  70.4 5.7 %multiply_add_fusion = (f32[16,64,512]{2,1,0:T(8,128)}, f32[16,64,512]{2,1,0:T(8,128)}, f32[16,64,512]{2,1,0:T(8,128)}) fusion(f32[16,64,512]{2,1,0:T(8,128)S(1)} %reshape.124, f32[16,64,512]{2,1,0:T(8,128)} %get-tuple-element.31, f32[16,64,512]{2,1,0:T(8,128)} %get-tuple-element.30, pred[]{:T(512)S(6)} %eq.12), kind=kLoop, calls=%fused_computation.6 | loop fusion | flops 2097152 | bytes 12582913 | tf_op jit(solution)/shard_map/add | solution.py:445
  76.1 0.0 all-to-all-done
  76.1 57.7 %shard_map.114 = (f32[16,64,512]{2,1,0:T(8,128)}, f32[128,8,512]{2,1,0:T(8,128)}) custom-call(f32[16,64,512]{2,1,0:T(8,128)} %bitcast.log_ref, f32[16,64,512]{2,1,0:T(8,128)} %get-tuple-element.36.sto_ref, f32[16,64,512]{2,1,0:T(8,128)} %get-tuple-element.35.init_ref, f32[16,64,512]{2,1,0:T(8,128)} %get-tuple-element.34.forc_ref, f32[8,128,512]{2,1,0:T(8,128)} %bitcast.38), custom_call_target="tpu_custom_call" | custom-call | tf_op jit(solution)/shard_map/pallas_call | solution.py:166
  133.8 0.0 copy-start.7
  133.8 0.0 copy-start.6
  133.8 2.1 copy.26
  135.9 0.8 gather_fusion
  136.8 0.0 copy-done.7
  136.8 0.3 scatter.9.row_ref
  137.1 0.6 copy-done.4
  137.6 18.7 %shard_map.115 = f32[128,8,128]{2,1,0:T(8,128)} custom-call(f32[1,8,128]{2,1,0:T(8,128)} %copy-done.4), custom_call_target="tpu_custom_call" | custom-call | tf_op jit(solution)/shard_map/pallas_call | solution.py:244
  156.3 0.0 copy-done.6
  156.3 1.4 fusion.14
  157.8 1.1 broadcast_subtract_fusion
  158.9 0.3 convolution_multiply_fusion
  159.1 0.1 copy.22
  159.2 4.7 %all-to-all-start.1 = ((f32[1,16,64,512]{3,2,0,1:T(8,128)}), f32[1,16,64,512]{3,2,0,1:T(8,128)}, u32[]{:S(2)}, u32[]{:S(2)}) async-start(f32[1,16,64,512]{3,2,0,1:T(8,128)} %bitcast.40), calls=%async_computation.1 | async-start | bytes 4194304 | tf_op jit(solution)/shard_map/all_to_all | solution.py:452
  163.9 0.0 copy-done.5
  163.9 0.1 fusion.13
  164.0 2.9 %cholesky.16 = f32[32,32]{1,0:T(8,128)S(1)} custom-call(f32[32,32]{1,0:T(8,128)S(1)} %fusion.13), custom_call_target="Cholesky" | custom-call | tf_op jit(solution)/shard_map/jit(cholesky)/cholesky | solution.py:465
  166.9 0.6 compare_reduce_fusion
  167.5 0.7 fusion.7
  168.2 2.4 %custom-call.8 = f32[1,32,32]{1,2,0:T(8,128)S(1)} custom-call(f32[1,32,32]{2,1,0:T(8,128)S(1)} %fusion.7), custom_call_target="InvertDiagBlocksLowerTriangular" | custom-call | tf_op jit(solution)/shard_map/triangular_solve | solution.py:24
  170.6 0.3 fusion.10
  170.9 0.2 fusion.8
  171.1 0.3 convolution_bitcast_fusion
  171.4 3.0 %fusion.1 = f32[128,8,512]{2,0,1:T(8,128)S(1)} fusion(f32[128,128,1]{1,0,2:T(8,128)S(1)} %convolution_bitcast_fusion, f32[128,8,512]{2,1,0:T(8,128)S(1)} %copy-done), kind=kOutput, calls=%fused_computation.4 | convolution fusion | flops 805306368 | bytes 4259840 | tf_op jit(solution)/shard_map/jk,kry->jry/dot_general | solution.py:469
  174.4 2.8 %fusion.column_ref = f32[128,8,512]{2,1,0:T(8,128)} fusion(f32[128,8,512]{2,1,0:T(8,128)S(1)} %copy-done, f32[128,8,512]{2,0,1:T(8,128)S(1)} %fusion.1), kind=kLoop, calls=%fused_computation.3 | loop fusion | flops 1048576 | bytes 6291456 | tf_op jit(solution)/shard_map/add | solution.py:470
  177.2 40.8 %shard_map.116 = f32[8,128,512]{2,1,0:T(8,128)} custom-call(f32[128,8,512]{2,1,0:T(8,128)} %fusion.column_ref), custom_call_target="tpu_custom_call" | custom-call | tf_op jit(solution)/shard_map/pallas_call | solution.py:306
  218.0 0.0 all-to-all-done.1
  218.0 3.3 %copy.36 = f32[8,2,64,512]{3,2,1,0:T(8,128)} copy(f32[8,2,64,512]{3,2,1,0:T(8,128)} %bitcast.4) | data formatting | bytes 4194304
  221.3 1.3 copy.37
  (13 shorter events, 0.1 us)
Async XLA Ops:
  0.6 7.7 %copy-start.2 = (f32[2,64,512]{2,1,0:T(8,128)S(1)}, f32[2,64,512]{2,1,0:T(8,128)}, u32[]{:S(2)}) copy-start(f32[2,64,512]{2,1,0:T(8,128)} %param.15) | copy-start | bytes 786436
  0.6 7.7 %copy-start.3 = (f32[2,64,512]{2,1,0:T(8,128)S(1)}, f32[2,64,512]{2,1,0:T(8,128)}, u32[]{:S(2)}) copy-start(f32[2,64,512]{2,1,0:T(8,128)} %param.16) | copy-start | bytes 786436
  0.7 62.7 %copy-start.8 = (s32[16]{0:T(128)S(1)}, s32[16]{0:T(128)}, u32[]{:S(2)}) copy-start(s32[16]{0:T(128)} %param.17) | copy-start | bytes 196
  0.7 75.4 %all-to-all-start = ((f32[8,2,64,512]{3,2,1,0:T(8,128)}), f32[8,2,64,512]{3,2,1,0:T(8,128)}, u32[]{:S(2)}, u32[]{:S(2)}) async-start(f32[8,2,64,512]{3,2,1,0:T(8,128)} %param.14), calls=%async_computation | async-start | bytes 4194304 | tf_op jit(solution)/shard_map/all_to_all | solution.py:434
  65.5 3.7 %copy-start.9 = (s32[32]{0:T(128)S(1)}, s32[32]{0:T(128)}, u32[]{:S(2)}) copy-start(s32[32]{0:T(128)} %param.19) | copy-start | bytes 388
  65.5 4.3 %copy-start.10 = (f32[32]{0:T(128)S(1)}, f32[32]{0:T(128)}, u32[]{:S(2)}) copy-start(f32[32]{0:T(128)} %param.21) | copy-start | bytes 388
  133.8 3.0 %copy-start.7 = (f32[1,1,32]{2,1,0:T(1,128)S(1)}, f32[1,1,32]{2,1,0:T(1,128)}, u32[]{:S(2)}) copy-start(f32[1,1,32]{2,1,0:T(1,128)} %dynamic-slice_bitcast_fusion) | copy-start | bytes 388
  133.8 22.5 %copy-start.6 = (f32[32]{0:T(128)S(1)}, f32[32]{0:T(128)}, u32[]{:S(2)}) copy-start(f32[32]{0:T(128)} %param.20) | copy-start | bytes 388
  137.1 0.6 copy-start.4
  159.2 4.7 %copy-start.5 = (f32[32]{0:T(128)S(1)}, f32[32]{0:T(128)}, u32[]{:S(2)}) copy-start(f32[32]{0:T(128)} %broadcast_divide_fusion) | copy-start | bytes 388
  159.2 12.2 %copy-start = (f32[128,8,512]{2,1,0:T(8,128)S(1)}, f32[128,8,512]{2,1,0:T(8,128)}, u32[]{:S(2)}) copy-start(f32[128,8,512]{2,1,0:T(8,128)} %get-tuple-element.33) | copy-start | bytes 6291460
  159.2 58.8 %all-to-all-start.1 = ((f32[1,16,64,512]{3,2,0,1:T(8,128)}), f32[1,16,64,512]{3,2,0,1:T(8,128)}, u32[]{:S(2)}, u32[]{:S(2)}) async-start(f32[1,16,64,512]{3,2,0,1:T(8,128)} %bitcast.40), calls=%async_computation.1 | async-start | bytes 4194304 | tf_op jit(solution)/shard_map/all_to_all | solution.py:452
  218.0 3.3 %copy-start.1 = (f32[8,128,512]{2,1,0:T(8,128)S(1)}, f32[8,128,512]{2,1,0:T(8,128)}, u32[]{:S(2)}) copy-start(f32[8,128,512]{2,1,0:T(8,128)} %shard_map.116) | copy-start | bytes 6291460

commit v17 on v16

--- a/solution.py
+++ b/solution.py
@@ -372,25 +372,30 @@
             device_id_type=mesh_id,
         )
 
+    def hand(slab_index, source):
+        return pltpu.make_async_remote_copy(
+            src_ref=source,
+            dst_ref=other_ref.at[pl.ds(slab_index * thick, thick)],
+            send_sem=pair_sems.at[0, slab_index],
+            recv_sem=pair_sems.at[1, slab_index],
+            device_id=(me_s, partner),
+            device_id_type=mesh_id,
+        )
+
     keep = pltpu.make_async_copy(slab_ref, mine_ref.at[pl.ds(me_s * thick, thick)], local_sem)
     for k, (flip, dz) in enumerate(patterns):
         push(k, flip, dz, 1).start()
     keep.start()
+    hand(me_s, slab_ref).start()
     keep.wait()
     for k, (flip, dz) in enumerate(patterns):
         push(k, flip, dz, 1).wait_send()
         push(k, flip, dz, -1).wait_recv()
-    swap = pltpu.make_async_remote_copy(
-        src_ref=mine_ref,
-        dst_ref=other_ref,
-        send_sem=pair_sems.at[0],
-        recv_sem=pair_sems.at[1],
-        device_id=(me_s, partner),
-        device_id_type=mesh_id,
-    )
-    swap.start()
-    swap.wait_send()
-    swap.wait_recv()
+        landed, _ = place(flip, dz, -1)
+        hand(landed, mine_ref.at[pl.ds(landed * thick, thick)]).start()
+    for slab_index in range(2 * rows):
+        hand(slab_index, mine_ref.at[pl.ds(slab_index * thick, thick)]).wait_send()
+        hand(slab_index, mine_ref.at[pl.ds(slab_index * thick, thick)]).wait_recv()
 
 
 def gather_grids(slab, n_space):
@@ -406,7 +411,7 @@
             pltpu.SemaphoreType.DMA((n_space - 1,)),
             pltpu.SemaphoreType.DMA((n_space - 1,)),
             pltpu.SemaphoreType.DMA,
-            pltpu.SemaphoreType.DMA((2,)),
+            pltpu.SemaphoreType.DMA((2, n_space)),
         ],
         compiler_params=pltpu.CompilerParams(collective_id=5, has_side_effects=True),
     )(slab)

time: 224 us -> 222 us (level)
  transfers between devices with their start and end apart: 2 -> 2, of which waited for: 0 -> 0; matrix products, arithmetic and copies ran while one was open for 12% -> 12% of each run, Pallas kernels for 43% -> 42%
where the time goes in v17:
time: 222 us; the launch traced here: 221 us
  Pallas kernels  170 us (77%)
  other arithmetic  21.9 us (10%)
  starting transfers between devices  12.3 us (6%)
  local copies, waits for them, and re-layouts  11.6 us (5%)
  matrix products  4 us (2%)
    pallas_call x1, Pallas kernels, forward_pallas(): pl.pallas_call(forward_kernel, out_shape=(jax.ShapeDtypeStruct((planes, d...  57.7 us
    pallas_call x1, Pallas kernels, gather_grids(): pl.pallas_call(grid_kernel, out_shape=(grid, grid), in_specs=[anywhere],...  52.6 us
    pallas_call x1, Pallas kernels, send_back(): pl.pallas_call(return_kernel, out_shape=jax.ShapeDtypeStruct((members, sl...  40.7 us
    pallas_call x1, Pallas kernels, gather_rows(): pl.pallas_call(gather_kernel, out_shape=jax.ShapeDtypeStruct((total,) + r...  18.7 us
    all_to_all x1, starting transfers between devices, shards(): whole_log = lax.all_to_all(log_perm, 'space', 0, 1, tiled=True)  7.64 us
    unnamed x25, local copies, waits for them, and re-layouts  7.38 us
    add x1, other arithmetic, shards(): forcing = whole_storage * whole_head + source  5.7 us
    all_to_all x1, starting transfers between devices, shards(): head_field = lax.all_to_all(field[None], 'space', 1, 0, tiled=True)  4.66 us
  transfers between devices with their start and end apart: 2, of which 0 were waited for; matrix products, arithmetic and copies ran while one was open for 12% of the time, Pallas kernels for 42%

profile of v17, /device:TPU:25, one launch (start us, length us, event | category | flops | bytes accessed | tf_op | source)
XLA Modules:
  0.0 221.0 jit_solution(9716394104450680937)
XLA Ops:
  0.6 0.0 copy-start.2
  0.6 0.0 copy-start.3
  0.7 0.0 copy-start.8
  0.7 7.6 %all-to-all-start = ((f32[8,2,64,512]{3,2,1,0:T(8,128)}), f32[8,2,64,512]{3,2,1,0:T(8,128)}, u32[]{:S(2)}, u32[]{:S(2)}) async-start(f32[8,2,64,512]{3,2,1,0:T(8,128)} %param.14), calls=%async_computation | async-start | bytes 4194304 | tf_op jit(solution)/shard_map/all_to_all | solution.py:439
  8.3 0.0 copy-done.2
  8.3 0.0 copy-done.3
  8.3 0.7 broadcast_select_fusion.2.slab_ref
  9.1 52.6 %shard_map.113 = (f32[16,64,512]{2,1,0:T(8,128)}, f32[16,64,512]{2,1,0:T(8,128)}) custom-call(f32[2,64,512]{2,1,0:T(8,128)} %broadcast_select_fusion.2.slab_ref), custom_call_target="tpu_custom_call" | custom-call | tf_op jit(solution)/shard_map/pallas_call | solution.py:405
  61.7 0.0 copy-done.8
  61.7 2.2 scatter_custom_fusion
  63.9 1.8 reshape.124
  66.3 1.3 dynamic-slice_bitcast_fusion
  67.6 0.0 copy-done.9
  67.6 0.6 pad_clamp_fusion
  68.2 0.0 copy-done.10
  68.2 0.6 broadcast_divide_fusion
  68.8 5.7 %multiply_add_fusion = (f32[16,64,512]{2,1,0:T(8,128)}, f32[16,64,512]{2,1,0:T(8,128)}, f32[16,64,512]{2,1,0:T(8,128)}) fusion(f32[16,64,512]{2,1,0:T(8,128)S(1)} %reshape.124, f32[16,64,512]{2,1,0:T(8,128)} %get-tuple-element.31, f32[16,64,512]{2,1,0:T(8,128)} %get-tuple-element.30, pred[]{:T(512)S(6)} %eq.12), kind=kLoop, calls=%fused_computation.6 | loop fusion | flops 2097152 | bytes 12582913 | tf_op jit(solution)/shard_map/add | solution.py:450
  74.5 0.0 all-to-all-done
  74.5 57.7 %shard_map.114 = (f32[16,64,512]{2,1,0:T(8,128)}, f32[128,8,512]{2,1,0:T(8,128)}) custom-call(f32[16,64,512]{2,1,0:T(8,128)} %bitcast.log_ref, f32[16,64,512]{2,1,0:T(8,128)} %get-tuple-element.36.sto_ref, f32[16,64,512]{2,1,0:T(8,128)} %get-tuple-element.35.init_ref, f32[16,64,512]{2,1,0:T(8,128)} %get-tuple-element.34.forc_ref, f32[8,128,512]{2,1,0:T(8,128)} %bitcast.38), custom_call_target="tpu_custom_call" | custom-call | tf_op jit(solution)/shard_map/pallas_call | solution.py:166
  132.2 0.0 copy-start.7
  132.2 0.0 copy-start.6
  132.2 2.1 copy.26
  134.3 0.8 gather_fusion
  135.2 0.0 copy-done.7
  135.2 0.3 scatter.9.row_ref
  135.5 0.6 copy-done.4
  136.0 18.7 %shard_map.115 = f32[128,8,128]{2,1,0:T(8,128)} custom-call(f32[1,8,128]{2,1,0:T(8,128)} %copy-done.4), custom_call_target="tpu_custom_call" | custom-call | tf_op jit(solution)/shard_map/pallas_call | solution.py:244
  154.8 0.0 copy-done.6
  154.8 1.4 fusion.14
  156.2 1.1 broadcast_subtract_fusion
  157.3 0.3 convolution_multiply_fusion
  157.6 0.1 copy.22
  157.6 4.7 %all-to-all-start.1 = ((f32[1,16,64,512]{3,2,0,1:T(8,128)}), f32[1,16,64,512]{3,2,0,1:T(8,128)}, u32[]{:S(2)}, u32[]{:S(2)}) async-start(f32[1,16,64,512]{3,2,0,1:T(8,128)} %bitcast.40), calls=%async_computation.1 | async-start | bytes 4194304 | tf_op jit(solution)/shard_map/all_to_all | solution.py:457
  162.3 0.0 copy-done.5
  162.3 0.1 fusion.13
  162.4 2.9 %cholesky.16 = f32[32,32]{1,0:T(8,128)S(1)} custom-call(f32[32,32]{1,0:T(8,128)S(1)} %fusion.13), custom_call_target="Cholesky" | custom-call | tf_op jit(solution)/shard_map/jit(cholesky)/cholesky | solution.py:470
  165.3 0.6 compare_reduce_fusion
  166.0 0.7 fusion.7
  166.6 2.4 %custom-call.8 = f32[1,32,32]{1,2,0:T(8,128)S(1)} custom-call(f32[1,32,32]{2,1,0:T(8,128)S(1)} %fusion.7), custom_call_target="InvertDiagBlocksLowerTriangular" | custom-call | tf_op jit(solution)/shard_map/triangular_solve | solution.py:24
  169.1 0.3 fusion.10
  169.3 0.2 fusion.8
  169.5 0.3 convolution_bitcast_fusion
  169.8 3.0 %fusion.1 = f32[128,8,512]{2,0,1:T(8,128)S(1)} fusion(f32[128,128,1]{1,0,2:T(8,128)S(1)} %convolution_bitcast_fusion, f32[128,8,512]{2,1,0:T(8,128)S(1)} %copy-done), kind=kOutput, calls=%fused_computation.4 | convolution fusion | flops 805306368 | bytes 4259840 | tf_op jit(solution)/shard_map/jk,kry->jry/dot_general | solution.py:474
  172.9 2.8 %fusion.column_ref = f32[128,8,512]{2,1,0:T(8,128)} fusion(f32[128,8,512]{2,1,0:T(8,128)S(1)} %copy-done, f32[128,8,512]{2,0,1:T(8,128)S(1)} %fusion.1), kind=kLoop, calls=%fused_computation.3 | loop fusion | flops 1048576 | bytes 6291456 | tf_op jit(solution)/shard_map/add | solution.py:475
  175.7 40.7 %shard_map.116 = f32[8,128,512]{2,1,0:T(8,128)} custom-call(f32[128,8,512]{2,1,0:T(8,128)} %fusion.column_ref), custom_call_target="tpu_custom_call" | custom-call | tf_op jit(solution)/shard_map/pallas_call | solution.py:306
  216.3 0.0 all-to-all-done.1
  216.4 3.3 %copy.36 = f32[8,2,64,512]{3,2,1,0:T(8,128)} copy(f32[8,2,64,512]{3,2,1,0:T(8,128)} %bitcast.4) | data formatting | bytes 4194304
  219.6 1.3 copy.37
  (13 shorter events, 0.1 us)
Async XLA Ops:
  0.6 7.7 %copy-start.2 = (f32[2,64,512]{2,1,0:T(8,128)S(1)}, f32[2,64,512]{2,1,0:T(8,128)}, u32[]{:S(2)}) copy-start(f32[2,64,512]{2,1,0:T(8,128)} %param.15) | copy-start | bytes 786436
  0.6 7.7 %copy-start.3 = (f32[2,64,512]{2,1,0:T(8,128)S(1)}, f32[2,64,512]{2,1,0:T(8,128)}, u32[]{:S(2)}) copy-start(f32[2,64,512]{2,1,0:T(8,128)} %param.16) | copy-start | bytes 786436
  0.7 61.0 %copy-start.8 = (s32[16]{0:T(128)S(1)}, s32[16]{0:T(128)}, u32[]{:S(2)}) copy-start(s32[16]{0:T(128)} %param.17) | copy-start | bytes 196
  0.7 73.8 %all-to-all-start = ((f32[8,2,64,512]{3,2,1,0:T(8,128)}), f32[8,2,64,512]{3,2,1,0:T(8,128)}, u32[]{:S(2)}, u32[]{:S(2)}) async-start(f32[8,2,64,512]{3,2,1,0:T(8,128)} %param.14), calls=%async_computation | async-start | bytes 4194304 | tf_op jit(solution)/shard_map/all_to_all | solution.py:439
  63.9 3.7 %copy-start.9 = (s32[32]{0:T(128)S(1)}, s32[32]{0:T(128)}, u32[]{:S(2)}) copy-start(s32[32]{0:T(128)} %param.19) | copy-start | bytes 388
  63.9 4.3 %copy-start.10 = (f32[32]{0:T(128)S(1)}, f32[32]{0:T(128)}, u32[]{:S(2)}) copy-start(f32[32]{0:T(128)} %param.21) | copy-start | bytes 388
  132.2 3.0 %copy-start.7 = (f32[1,1,32]{2,1,0:T(1,128)S(1)}, f32[1,1,32]{2,1,0:T(1,128)}, u32[]{:S(2)}) copy-start(f32[1,1,32]{2,1,0:T(1,128)} %dynamic-slice_bitcast_fusion) | copy-start | bytes 388
  132.2 22.6 %copy-start.6 = (f32[32]{0:T(128)S(1)}, f32[32]{0:T(128)}, u32[]{:S(2)}) copy-start(f32[32]{0:T(128)} %param.20) | copy-start | bytes 388
  135.4 0.6 copy-start.4
  157.6 4.7 %copy-start.5 = (f32[32]{0:T(128)S(1)}, f32[32]{0:T(128)}, u32[]{:S(2)}) copy-start(f32[32]{0:T(128)} %broadcast_divide_fusion) | copy-start | bytes 388
  157.6 12.2 %copy-start = (f32[128,8,512]{2,1,0:T(8,128)S(1)}, f32[128,8,512]{2,1,0:T(8,128)}, u32[]{:S(2)}) copy-start(f32[128,8,512]{2,1,0:T(8,128)} %get-tuple-element.33) | copy-start | bytes 6291460
  157.6 58.7 %all-to-all-start.1 = ((f32[1,16,64,512]{3,2,0,1:T(8,128)}), f32[1,16,64,512]{3,2,0,1:T(8,128)}, u32[]{:S(2)}, u32[]{:S(2)}) async-start(f32[1,16,64,512]{3,2,0,1:T(8,128)} %bitcast.40), calls=%async_computation.1 | async-start | bytes 4194304 | tf_op jit(solution)/shard_map/all_to_all | solution.py:457
  216.3 3.3 %copy-start.1 = (f32[8,128,512]{2,1,0:T(8,128)S(1)}, f32[8,128,512]{2,1,0:T(8,128)}, u32[]{:S(2)}) copy-start(f32[8,128,512]{2,1,0:T(8,128)} %shard_map.116) | copy-start | bytes 6291460

commit v18 on v17

--- a/solution.py
+++ b/solution.py
@@ -339,7 +339,10 @@
     return grid
 
 
-def grid_kernel(slab_ref, mine_ref, other_ref, send_sems, recv_sems, local_sem, pair_sems):
+def grid_kernel(
+    slab_ref, log_ref, mine_ref, other_ref, whole_ref,
+    send_sems, recv_sems, local_sem, pair_sems, part_sems, part_local,
+):
     thick = slab_ref.shape[0]
     rows = mine_ref.shape[0] // thick // 2
     me_s = lax.axis_index("space")
@@ -356,9 +359,29 @@
 
     barrier = pltpu.get_barrier_semaphore()
     friends = [place(0, dz, 1) for dz in range(1, rows)] + [place(1, dz, 1) for dz in range(rows)]
-    for s, e in friends + [(me_s, partner)]:
+    crosswise = [(zz * 2 + 1 - half, me_e) for zz in range(rows)]
+    for s, e in friends + crosswise + [(me_s, partner)]:
         pl.semaphore_signal(barrier, 1, device_id=(s, e), device_id_type=mesh_id)
-    pl.semaphore_wait(barrier, len(friends) + 1)
+    pl.semaphore_wait(barrier, len(friends) + len(crosswise) + 1)
+
+    def particle(t, landing):
+        return pltpu.make_async_remote_copy(
+            src_ref=log_ref.at[t],
+            dst_ref=whole_ref.at[pl.ds(landing * thick, thick)],
+            send_sem=part_sems.at[0, t],
+            recv_sem=part_sems.at[1, landing],
+            device_id=(t, me_e),
+            device_id_type=mesh_id,
+        )
+
+    own_part = pltpu.make_async_copy(
+        log_ref.at[me_s], whole_ref.at[pl.ds(me_s * thick, thick)], part_local
+    )
+    for t in range(2 * rows):
+        @pl.when(me_s != t)
+        def _():
+            particle(t, me_s).start()
+    own_part.start()
 
     def push(k, flip, dz, sign):
         s, e = place(flip, dz, sign)
@@ -396,25 +419,33 @@
     for slab_index in range(2 * rows):
         hand(slab_index, mine_ref.at[pl.ds(slab_index * thick, thick)]).wait_send()
         hand(slab_index, mine_ref.at[pl.ds(slab_index * thick, thick)]).wait_recv()
-
-
-def gather_grids(slab, n_space):
+    own_part.wait()
+    for t in range(2 * rows):
+        @pl.when(me_s != t)
+        def _():
+            particle(t, me_s).wait_send()
+            particle(t, t).wait_recv()
+
+
+def gather_grids(slab, log_perm, n_space):
     thick, depth, across = slab.shape
     anywhere = pl.BlockSpec(memory_space=pl.ANY)
     grid = jax.ShapeDtypeStruct((n_space * thick, depth, across), jnp.float32)
     return pl.pallas_call(
         grid_kernel,
-        out_shape=(grid, grid),
-        in_specs=[anywhere],
-        out_specs=(anywhere, anywhere),
+        out_shape=(grid, grid, grid),
+        in_specs=[anywhere, anywhere],
+        out_specs=(anywhere, anywhere, anywhere),
         scratch_shapes=[
             pltpu.SemaphoreType.DMA((n_space - 1,)),
             pltpu.SemaphoreType.DMA((n_space - 1,)),
             pltpu.SemaphoreType.DMA,
             pltpu.SemaphoreType.DMA((2, n_space)),
+            pltpu.SemaphoreType.DMA((2, n_space)),
+            pltpu.SemaphoreType.DMA,
         ],
         compiler_params=pltpu.CompilerParams(collective_id=5, has_side_effects=True),
-    )(slab)
+    )(slab, log_perm)
 
 
 def shards(
@@ -436,9 +467,10 @@
     total_members = members * n_ens
     grid_planes = planes * n_space
 
-    whole_log = lax.all_to_all(log_perm, "space", 0, 1, tiled=True)
     core = lax.axis_index("ens") % 2
-    mine, other = gather_grids(jnp.where(core == 0, storage, head_init), n_space)
+    mine, other, whole_log = gather_grids(
+        jnp.where(core == 0, storage, head_init), log_perm, n_space
+    )
     whole_storage = jnp.where(core == 0, mine, other)
     whole_head = jnp.where(core == 0, other, mine)
     source = (
@@ -451,7 +483,7 @@
     slab_rows = planes * depth
     by_rows = log_perm.reshape(members, slab_rows, across)
     field, band = forward_pallas(
-        whole_log[0], whole_storage, whole_head, forcing, by_rows, n_ens
+        whole_log, whole_storage, whole_head, forcing, by_rows, n_ens
     )
     picked = field.reshape(-1)[obs_cells]
     head_field = lax.all_to_all(field[None], "space", 1, 0, tiled=True)

time: 222 us -> 233 us (1.050)
  Pallas kernels: 170 us -> 188 us
  starting transfers between devices: 12.3 us -> 4.53 us
    pallas_call x1, Pallas kernels: 18.7 us -> 30.6 us  [gather_rows(): pl.pallas_call(gather_kernel, out_shape=jax.ShapeDtypeStruct((total,) + r...]
    pallas_call x1, Pallas kernels: 52.6 us -> 63.2 us  [gather_grids(): pl.pallas_call(grid_kernel, out_shape=(grid, grid, grid), in_specs=[anywh...]
    all_to_all x1 -> x0, starting transfers between devices: 7.64 us -> none  [shards(): whole_log = lax.all_to_all(log_perm, 'space', 0, 1, tiled=True)]
    pallas_call x1, Pallas kernels: 40.7 us -> 36.9 us  [send_back(): pl.pallas_call(return_kernel, out_shape=jax.ShapeDtypeStruct((members, sl...]
    unnamed x25 -> x19, local copies, waits for them, and re-layouts: 7.38 us -> 8.83 us
  transfers between devices with their start and end apart: 2 -> 1, of which waited for: 0 -> 0; matrix products, arithmetic and copies ran while one was open for 12% -> 10% of each run, Pallas kernels for 42% -> 29%
where the time goes in v18:
time: 233 us
  Pallas kernels  188 us (81%)
  other arithmetic  21.4 us (9%)
  local copies, waits for them, and re-layouts  13.2 us (6%)
  starting transfers between devices  4.53 us (2%)
  matrix products  3.99 us (2%)
    pallas_call x1, Pallas kernels, gather_grids(): pl.pallas_call(grid_kernel, out_shape=(grid, grid, grid), in_specs=[anywh...  63.2 us
    pallas_call x1, Pallas kernels, forward_pallas(): pl.pallas_call(forward_kernel, out_shape=(jax.ShapeDtypeStruct((planes, d...  57.7 us
    pallas_call x1, Pallas kernels, send_back(): pl.pallas_call(return_kernel, out_shape=jax.ShapeDtypeStruct((members, sl...  36.9 us
    pallas_call x1, Pallas kernels, gather_rows(): pl.pallas_call(gather_kernel, out_shape=jax.ShapeDtypeStruct((total,) + r...  30.6 us
    unnamed x19, local copies, waits for them, and re-layouts  8.83 us
    add x1, other arithmetic, shards(): forcing = whole_storage * whole_head + source  5.7 us
  transfers between devices with their start and end apart: 1, of which 0 were waited for; matrix products, arithmetic and copies ran while one was open for 10% of the time, Pallas kernels for 29%

profile of v18, /device:TPU:25, one launch (start us, length us, event | category | flops | bytes accessed | tf_op | source)
XLA Modules:
  0.0 233.0 jit_solution(10525090736029229891)
XLA Ops:
  0.6 0.7 compare_select_fusion.1
  1.3 2.2 scatter_custom_fusion
  3.5 0.0 copy-start.2
  3.5 0.0 copy-start.3
  3.5 1.8 reshape.120
  5.3 0.0 copy-done.2
  5.3 0.0 copy-done.3
  5.3 0.7 broadcast_select_fusion.2.slab_ref
  6.1 63.2 %shard_map.113 = (f32[16,64,512]{2,1,0:T(8,128)}, f32[16,64,512]{2,1,0:T(8,128)}, f32[16,64,512]{2,1,0:T(8,128)}) custom-call(f32[2,64,512]{2,1,0:T(8,128)} %broadcast_select_fusion.2.slab_ref, f32[8,2,64,512]{3,2,1,0:T(8,128)} %log_ref.1), custom_call_target="tpu_custom_call" | custom-call | tf_op jit(solution)/shard_map/pallas_call | solution.py:434
  69.2 5.7 %multiply_add_fusion = (f32[16,64,512]{2,1,0:T(8,128)}, f32[16,64,512]{2,1,0:T(8,128)}, f32[16,64,512]{2,1,0:T(8,128)}) fusion(f32[16,64,512]{2,1,0:T(8,128)S(1)} %reshape.120, f32[16,64,512]{2,1,0:T(8,128)} %get-tuple-element.33, f32[16,64,512]{2,1,0:T(8,128)} %get-tuple-element.32, pred[]{:T(512)S(6)} %eq.12), kind=kLoop, calls=%fused_computation.6 | loop fusion | flops 2097152 | bytes 12582913 | tf_op jit(solution)/shard_map/add | solution.py:482
  74.9 57.7 %shard_map.114 = (f32[16,64,512]{2,1,0:T(8,128)}, f32[128,8,512]{2,1,0:T(8,128)}) custom-call(f32[16,64,512]{2,1,0:T(8,128)} %get-tuple-element.31.log_ref, f32[16,64,512]{2,1,0:T(8,128)} %get-tuple-element.38.sto_ref, f32[16,64,512]{2,1,0:T(8,128)} %get-tuple-element.37.init_ref, f32[16,64,512]{2,1,0:T(8,128)} %get-tuple-element.36.forc_ref, ...), custom_call_target="tpu_custom_call" | custom-call | tf_op jit(solution)/shard_map/pallas_call | solution.py:166
  132.7 4.5 %all-to-all-start = ((f32[1,16,64,512]{3,2,0,1:T(8,128)}), f32[1,16,64,512]{3,2,0,1:T(8,128)}, u32[]{:S(2)}, u32[]{:S(2)}) async-start(f32[1,16,64,512]{3,2,0,1:T(8,128)} %bitcast.38), calls=%async_computation | async-start | bytes 4194304 | tf_op jit(solution)/shard_map/all_to_all | solution.py:489
  137.2 0.0 copy-start.6
  137.2 0.0 copy-start.5
  137.2 0.0 copy-start.7
  137.2 0.0 copy-start
  137.2 3.6 %copy.26 = f32[128,4,8,128]{3,1,2,0:T(4,128)} copy(f32[128,4,8,128]{3,2,1,0:T(8,128)} %bitcast.39) | data formatting | bytes 4194304
  140.8 0.0 copy-done.6
  140.9 1.6 gather_fusion
  142.4 0.7 dynamic-slice_bitcast_fusion
  143.1 0.2 scatter.9.row_ref
  143.3 0.0 copy-start.4
  143.4 0.6 copy-done.4
  143.9 30.6 %shard_map.115 = f32[128,8,128]{2,1,0:T(8,128)} custom-call(f32[1,8,128]{2,1,0:T(8,128)} %copy-done.4), custom_call_target="tpu_custom_call" | custom-call | tf_op jit(solution)/shard_map/pallas_call | solution.py:244
  174.6 0.0 copy-done.5
  174.6 1.4 fusion.14
  176.0 1.1 broadcast_subtract_fusion
  177.1 0.3 convolution_multiply_fusion
  177.3 0.1 copy.22
  178.1 0.0 copy-done.7
  178.1 0.1 fusion.13
  178.2 2.9 %cholesky.16 = f32[32,32]{1,0:T(8,128)S(1)} custom-call(f32[32,32]{1,0:T(8,128)S(1)} %fusion.13), custom_call_target="Cholesky" | custom-call | tf_op jit(solution)/shard_map/jit(cholesky)/cholesky | solution.py:502
  181.1 0.6 compare_reduce_fusion
  181.8 0.7 fusion.7
  182.4 2.4 %custom-call.8 = f32[1,32,32]{1,2,0:T(8,128)S(1)} custom-call(f32[1,32,32]{2,1,0:T(8,128)S(1)} %fusion.7), custom_call_target="InvertDiagBlocksLowerTriangular" | custom-call | tf_op jit(solution)/shard_map/triangular_solve | solution.py:24
  184.9 0.3 fusion.10
  185.1 0.2 fusion.8
  185.3 0.3 convolution_bitcast_fusion
  185.6 0.0 copy-done
  185.6 3.0 %fusion.1 = f32[128,8,512]{2,0,1:T(8,128)S(1)} fusion(f32[128,128,1]{1,0,2:T(8,128)S(1)} %convolution_bitcast_fusion, f32[128,8,512]{2,1,0:T(8,128)S(1)} %copy-done), kind=kOutput, calls=%fused_computation.4 | convolution fusion | flops 805306368 | bytes 4259840 | tf_op jit(solution)/shard_map/jk,kry->jry/dot_general | solution.py:506
  188.6 2.8 %fusion.column_ref = f32[128,8,512]{2,1,0:T(8,128)} fusion(f32[128,8,512]{2,1,0:T(8,128)S(1)} %copy-done, f32[128,8,512]{2,0,1:T(8,128)S(1)} %fusion.1), kind=kLoop, calls=%fused_computation.3 | loop fusion | flops 1048576 | bytes 6291456 | tf_op jit(solution)/shard_map/add | solution.py:507
  191.4 36.9 %shard_map.116 = f32[8,128,512]{2,1,0:T(8,128)} custom-call(f32[128,8,512]{2,1,0:T(8,128)} %fusion.column_ref), custom_call_target="tpu_custom_call" | custom-call | tf_op jit(solution)/shard_map/pallas_call | solution.py:306
  228.3 0.0 all-to-all-done
  228.3 0.0 copy-start.1
  228.3 3.3 %copy.36 = f32[8,2,64,512]{3,2,1,0:T(8,128)} copy(f32[8,2,64,512]{3,2,1,0:T(8,128)} %bitcast.3) | data formatting | bytes 4194304
  231.6 0.0 copy-done.1
  231.6 1.3 copy.37
  (6 shorter events, 0.1 us)
Async XLA Ops:
  3.5 1.8 copy-start.2
  3.5 1.8 copy-start.3
  132.7 95.7 %all-to-all-start = ((f32[1,16,64,512]{3,2,0,1:T(8,128)}), f32[1,16,64,512]{3,2,0,1:T(8,128)}, u32[]{:S(2)}, u32[]{:S(2)}) async-start(f32[1,16,64,512]{3,2,0,1:T(8,128)} %bitcast.38), calls=%async_computation | async-start | bytes 4194304 | tf_op jit(solution)/shard_map/all_to_all | solution.py:489
  137.2 3.6 %copy-start.6 = (s32[32]{0:T(128)S(1)}, s32[32]{0:T(128)}, u32[]{:S(2)}) copy-start(s32[32]{0:T(128)} %param.19) | copy-start | bytes 388
  137.2 37.4 %copy-start.5 = (f32[32]{0:T(128)S(1)}, f32[32]{0:T(128)}, u32[]{:S(2)}) copy-start(f32[32]{0:T(128)} %param.20) | copy-start | bytes 388
  137.2 40.9 %copy-start.7 = (f32[32]{0:T(128)S(1)}, f32[32]{0:T(128)}, u32[]{:S(2)}) copy-start(f32[32]{0:T(128)} %param.21) | copy-start | bytes 388
  137.2 48.4 %copy-start = (f32[128,8,512]{2,1,0:T(8,128)S(1)}, f32[128,8,512]{2,1,0:T(8,128)}, u32[]{:S(2)}) copy-start(f32[128,8,512]{2,1,0:T(8,128)} %get-tuple-element.35) | copy-start | bytes 6291460
  143.3 0.6 copy-start.4
  228.3 3.3 %copy-start.1 = (f32[8,128,512]{2,1,0:T(8,128)S(1)}, f32[8,128,512]{2,1,0:T(8,128)}, u32[]{:S(2)}) copy-start(f32[8,128,512]{2,1,0:T(8,128)} %shard_map.116) | copy-start | bytes 6291460

commit v19 on v17

--- a/solution.py
+++ b/solution.py
@@ -471,8 +471,8 @@
     gain_rows = solve_pair(factor_lower, obs_values[None, :] + every_perturb - every_obs)
     mixing = jnp.dot(gain_rows, spread.T, precision=HIGHEST)
 
-    change = jnp.einsum("jk,kry->jry", mixing, band, precision=HIGHEST)
-    new_band = band + change / (total_members - 1)
+    step = jnp.eye(total_members, dtype=jnp.float32) + mixing / (total_members - 1)
+    new_band = jnp.einsum("jk,kry->jry", step, band, precision=HIGHEST)
     updated = send_back(new_band, slab_rows)
     updated = updated.reshape(log_perm.shape)
     return (head_field, updated)

time: 222 us -> 219 us (0.986)
  Pallas kernels: 170 us -> 167 us
  other arithmetic: 21.9 us -> 19.1 us
    pallas_call x1, Pallas kernels: 40.7 us -> 37.8 us  [send_back(): pl.pallas_call(return_kernel, out_shape=jax.ShapeDtypeStruct((members, sl...]
    add x1 -> x0, other arithmetic: 2.8 us -> none  [shards(): new_band = band + change / (total_members - 1)]
    dot_general x0 -> x1, local copies, waits for them, and re-layouts: none -> 2.54 us  [shards(): new_band = jnp.einsum('jk,kry->jry', step, band, precision=HIGHEST)]
    unnamed x25 -> x23, local copies, waits for them, and re-layouts: 7.38 us -> 6.42 us
  transfers between devices with their start and end apart: 2 -> 2, of which waited for: 0 -> 0; matrix products, arithmetic and copies ran while one was open for 12% -> 13% of each run, Pallas kernels for 42% -> 42%
where the time goes in v19:
time: 219 us; the launch traced here: 218 us
  Pallas kernels  167 us (76%)
  other arithmetic  19.1 us (9%)
  local copies, waits for them, and re-layouts  13.1 us (6%)
  starting transfers between devices  11.4 us (5%)
  matrix products  5.53 us (3%)
    pallas_call x1, Pallas kernels, forward_pallas(): pl.pallas_call(forward_kernel, out_shape=(jax.ShapeDtypeStruct((planes, d...  57.7 us
    pallas_call x1, Pallas kernels, gather_grids(): pl.pallas_call(grid_kernel, out_shape=(grid, grid), in_specs=[anywhere],...  52.6 us
    pallas_call x1, Pallas kernels, send_back(): pl.pallas_call(return_kernel, out_shape=jax.ShapeDtypeStruct((members, sl...  37.8 us
    pallas_call x1, Pallas kernels, gather_rows(): pl.pallas_call(gather_kernel, out_shape=jax.ShapeDtypeStruct((total,) + r...  18.7 us
    all_to_all x1, starting transfers between devices, shards(): whole_log = lax.all_to_all(log_perm, 'space', 0, 1, tiled=True)  7.64 us
    unnamed x23, local copies, waits for them, and re-layouts  6.42 us
    add x1, other arithmetic, shards(): forcing = whole_storage * whole_head + source  5.7 us
    dot_general x1, matrix products, shards(): new_band = jnp.einsum('jk,kry->jry', step, band, precision=HIGHEST)  4.54 us
  transfers between devices with their start and end apart: 2, of which 0 were waited for; matrix products, arithmetic and copies ran while one was open for 13% of the time, Pallas kernels for 42%

profile of v19, /device:TPU:25, one launch (start us, length us, event | category | flops | bytes accessed | tf_op | source)
XLA Modules:
  0.0 217.6 jit_solution(4175938566075642461)
XLA Ops:
  0.6 0.0 copy-start.1
  0.6 0.0 copy-start.2
  0.7 0.0 copy-start.7
  0.7 7.6 %all-to-all-start = ((f32[8,2,64,512]{3,2,1,0:T(8,128)}), f32[8,2,64,512]{3,2,1,0:T(8,128)}, u32[]{:S(2)}, u32[]{:S(2)}) async-start(f32[8,2,64,512]{3,2,1,0:T(8,128)} %param.14), calls=%async_computation | async-start | bytes 4194304 | tf_op jit(solution)/shard_map/all_to_all | solution.py:439
  8.3 0.0 copy-done.1
  8.3 0.0 copy-done.2
  8.3 0.7 broadcast_select_fusion.2.slab_ref
  9.1 52.6 %shard_map.113 = (f32[16,64,512]{2,1,0:T(8,128)}, f32[16,64,512]{2,1,0:T(8,128)}) custom-call(f32[2,64,512]{2,1,0:T(8,128)} %broadcast_select_fusion.2.slab_ref), custom_call_target="tpu_custom_call" | custom-call | tf_op jit(solution)/shard_map/pallas_call | solution.py:405
  61.7 0.0 copy-done.7
  61.7 2.2 %scatter_custom_fusion = f32[524288]{0:T(1024)} fusion(s32[16]{0:T(128)S(1)} %compare_select_fusion.1, f32[16]{0:T(128)} %param.18, f32[]{:T(128)} %constant.138.clone.1), kind=kCustom, calls=%fused_computation.9 | custom fusion | flops 16 | bytes 2097664 | tf_op jit(solution)/shard_map/scatter-add | solution.py:447
  63.9 1.8 reshape.124
  66.3 1.2 dynamic-slice_bitcast_fusion
  67.6 0.0 copy-done.8
  67.6 0.6 pad_clamp_fusion
  68.2 0.0 copy-done.9
  68.2 0.6 broadcast_divide_fusion
  68.8 5.7 %multiply_add_fusion = (f32[16,64,512]{2,1,0:T(8,128)}, f32[16,64,512]{2,1,0:T(8,128)}, f32[16,64,512]{2,1,0:T(8,128)}) fusion(f32[16,64,512]{2,1,0:T(8,128)S(1)} %reshape.124, f32[16,64,512]{2,1,0:T(8,128)} %get-tuple-element.31, f32[16,64,512]{2,1,0:T(8,128)} %get-tuple-element.30, pred[]{:T(512)S(6)} %eq.15), kind=kLoop, calls=%fused_computation.4 | loop fusion | flops 2097152 | bytes 12582913 | tf_op jit(solution)/shard_map/add | solution.py:450
  74.5 0.0 all-to-all-done
  74.5 57.7 %shard_map.114 = (f32[16,64,512]{2,1,0:T(8,128)}, f32[128,8,512]{2,1,0:T(8,128)}) custom-call(f32[16,64,512]{2,1,0:T(8,128)} %bitcast.log_ref, f32[16,64,512]{2,1,0:T(8,128)} %get-tuple-element.36.sto_ref, f32[16,64,512]{2,1,0:T(8,128)} %get-tuple-element.35.init_ref, f32[16,64,512]{2,1,0:T(8,128)} %get-tuple-element.34.forc_ref, f32[8,128,512]{2,1,0:T(8,128)} %bitcast.38), custom_call_target="tpu_custom_call" | custom-call | tf_op jit(solution)/shard_map/pallas_call | solution.py:166
  132.2 0.0 copy-start.6
  132.2 0.0 copy-start.5
  132.2 2.1 copy.26
  134.3 0.8 gather_fusion
  135.2 0.0 copy-done.6
  135.2 0.3 scatter.9.row_ref
  135.5 0.6 copy-done.3
  136.0 18.7 %shard_map.115 = f32[128,8,128]{2,1,0:T(8,128)} custom-call(f32[1,8,128]{2,1,0:T(8,128)} %copy-done.3), custom_call_target="tpu_custom_call" | custom-call | tf_op jit(solution)/shard_map/pallas_call | solution.py:244
  154.8 0.0 copy-done.5
  154.8 1.4 fusion.15
  156.2 3.8 %all-to-all-start.1 = ((f32[1,16,64,512]{3,2,0,1:T(8,128)}), f32[1,16,64,512]{3,2,0,1:T(8,128)S(1)}, u32[]{:S(2)}, u32[]{:S(2)}) async-start(f32[1,16,64,512]{3,2,0,1:T(8,128)} %bitcast.3), calls=%async_computation.1 | async-start | bytes 4194304 | tf_op jit(solution)/shard_map/all_to_all | solution.py:457
  160.0 1.1 broadcast_subtract_fusion
  161.1 0.3 convolution_multiply_fusion.1
  161.4 0.1 copy.22
  161.4 0.1 fusion.14
  161.5 2.9 %cholesky.16 = f32[32,32]{1,0:T(8,128)S(1)} custom-call(f32[32,32]{1,0:T(8,128)S(1)} %fusion.14), custom_call_target="Cholesky" | custom-call | tf_op jit(solution)/shard_map/jit(cholesky)/cholesky | solution.py:470
  164.5 0.6 compare_reduce_fusion
  165.1 0.7 fusion.8
  165.8 2.4 %custom-call.8 = f32[1,32,32]{1,2,0:T(8,128)S(1)} custom-call(f32[1,32,32]{2,1,0:T(8,128)S(1)} %fusion.8), custom_call_target="InvertDiagBlocksLowerTriangular" | custom-call | tf_op jit(solution)/shard_map/triangular_solve | solution.py:24
  168.2 0.3 fusion.11
  168.5 0.2 fusion.9
  168.6 0.3 fusion.3
  168.9 4.5 %fusion = f32[128,8,512]{2,0,1:T(8,128)S(1)} fusion(f32[128,128,1]{1,0,2:T(8,128)S(1)} %fusion.3, f32[128,8,512]{2,1,0:T(8,128)} %get-tuple-element.33), kind=kOutput, calls=%fused_computation.2 | convolution fusion | flops 805306368 | bytes 4259840 | tf_op jit(solution)/shard_map/jk,kry->jry/dot_general | solution.py:475
  173.5 2.5 %copy.24.column_ref = f32[128,8,512]{2,1,0:T(8,128)} copy(f32[128,8,512]{2,0,1:T(8,128)S(1)} %fusion) | data formatting | bytes 4194304 | tf_op jit(solution)/shard_map/jk,kry->jry/dot_general | solution.py:475
  176.0 37.8 %shard_map.116 = f32[8,128,512]{2,1,0:T(8,128)} custom-call(f32[128,8,512]{2,1,0:T(8,128)} %copy.24.column_ref), custom_call_target="tpu_custom_call" | custom-call | tf_op jit(solution)/shard_map/pallas_call | solution.py:306
  213.9 0.0 all-to-all-done.1
  213.9 1.3 copy.33
  215.2 1.0 copy-done
  216.2 1.3 copy.34
  (11 shorter events, 0.1 us)
Async XLA Ops:
  0.6 7.7 %copy-start.1 = (f32[2,64,512]{2,1,0:T(8,128)S(1)}, f32[2,64,512]{2,1,0:T(8,128)}, u32[]{:S(2)}) copy-start(f32[2,64,512]{2,1,0:T(8,128)} %param.15) | copy-start | bytes 786436
  0.6 7.7 %copy-start.2 = (f32[2,64,512]{2,1,0:T(8,128)S(1)}, f32[2,64,512]{2,1,0:T(8,128)}, u32[]{:S(2)}) copy-start(f32[2,64,512]{2,1,0:T(8,128)} %param.16) | copy-start | bytes 786436
  0.7 61.0 %copy-start.7 = (s32[16]{0:T(128)S(1)}, s32[16]{0:T(128)}, u32[]{:S(2)}) copy-start(s32[16]{0:T(128)} %param.17) | copy-start | bytes 196
  0.7 73.8 %all-to-all-start = ((f32[8,2,64,512]{3,2,1,0:T(8,128)}), f32[8,2,64,512]{3,2,1,0:T(8,128)}, u32[]{:S(2)}, u32[]{:S(2)}) async-start(f32[8,2,64,512]{3,2,1,0:T(8,128)} %param.14), calls=%async_computation | async-start | bytes 4194304 | tf_op jit(solution)/shard_map/all_to_all | solution.py:439
  63.9 3.7 %copy-start.8 = (s32[32]{0:T(128)S(1)}, s32[32]{0:T(128)}, u32[]{:S(2)}) copy-start(s32[32]{0:T(128)} %param.19) | copy-start | bytes 388
  63.9 4.3 %copy-start.9 = (f32[32]{0:T(128)S(1)}, f32[32]{0:T(128)}, u32[]{:S(2)}) copy-start(f32[32]{0:T(128)} %param.21) | copy-start | bytes 388
  132.2 3.0 %copy-start.6 = (f32[1,1,32]{2,1,0:T(1,128)S(1)}, f32[1,1,32]{2,1,0:T(1,128)}, u32[]{:S(2)}) copy-start(f32[1,1,32]{2,1,0:T(1,128)} %dynamic-slice_bitcast_fusion) | copy-start | bytes 388
  132.2 22.6 %copy-start.5 = (f32[32]{0:T(128)S(1)}, f32[32]{0:T(128)}, u32[]{:S(2)}) copy-start(f32[32]{0:T(128)} %param.20) | copy-start | bytes 388
  135.4 0.6 copy-start.3
  156.2 5.2 %copy-start.4 = (f32[32]{0:T(128)S(1)}, f32[32]{0:T(128)}, u32[]{:S(2)}) copy-start(f32[32]{0:T(128)} %broadcast_divide_fusion) | copy-start | bytes 388
  156.2 57.7 %all-to-all-start.1 = ((f32[1,16,64,512]{3,2,0,1:T(8,128)}), f32[1,16,64,512]{3,2,0,1:T(8,128)S(1)}, u32[]{:S(2)}, u32[]{:S(2)}) async-start(f32[1,16,64,512]{3,2,0,1:T(8,128)} %bitcast.3), calls=%async_computation.1 | async-start | bytes 4194304 | tf_op jit(solution)/shard_map/all_to_all | solution.py:457
  213.9 2.3 %copy-start = (f32[8,128,512]{2,1,0:T(8,128)S(1)}, f32[8,128,512]{2,1,0:T(8,128)}, u32[]{:S(2)}) copy-start(f32[8,128,512]{2,1,0:T(8,128)} %shard_map.116) | copy-start | bytes 6291460

commit v20 on v19

--- a/solution.py
+++ b/solution.py
@@ -57,8 +57,8 @@
 
 
 def forward_kernel(
-    log_ref, sto_ref, init_ref, forc_ref, rows_ref, out_ref, band_ref,
-    perm, trans, diag, head_a, head_b, band_send, band_recv, local_sem,
+    log_ref, mine_ref, other_ref, src_ref, rows_ref, out_ref, band_ref,
+    perm, trans, diag, head_a, head_b, band_send, band_recv, local_sem, forc_ref,
 ):
     planes, depth, across = log_ref.shape
     members, slab_rows, _ = rows_ref.shape
@@ -93,9 +93,14 @@
         buf[0] = zero
         buf[planes + 1] = zero
 
+    first_core = lax.axis_index("ens") % 2 == 0
+
     def fill(p, carry):
         perm[p + 1] = jnp.exp(log_ref[p])
-        head_a[p + 1] = init_ref[p]
+        storage = jnp.where(first_core, mine_ref[p], other_ref[p])
+        start = jnp.where(first_core, other_ref[p], mine_ref[p])
+        head_a[p + 1] = start
+        forc_ref[p] = storage * start + src_ref[p]
         return carry
 
     lax.fori_loop(0, planes, fill, 0)
@@ -118,7 +123,7 @@
     keep_band.start()
 
     def diagonal(p, carry):
-        total = sto_ref[p]
+        total = jnp.where(first_core, mine_ref[p], other_ref[p])
         for k, (a, b, c) in enumerate(HALF):
             back = p - a
             inside = (back >= 0) & (back < planes)
@@ -158,7 +163,7 @@
             band_copy(e, e).wait_recv()
 
 
-def forward_pallas(log_row, storage, head_init, forcing, by_rows, groups):
+def forward_pallas(log_row, mine, other, source, by_rows, groups):
     planes, depth, across = log_row.shape
     members, slab_rows, _ = by_rows.shape
     vmem = pl.BlockSpec(memory_space=pltpu.VMEM)
@@ -180,11 +185,12 @@
             pltpu.SemaphoreType.DMA((groups,)),
             pltpu.SemaphoreType.DMA((groups,)),
             pltpu.SemaphoreType.DMA,
+            pltpu.VMEM((planes, depth, across), jnp.float32),
         ],
         compiler_params=pltpu.CompilerParams(
             vmem_limit_bytes=66 * 1024 * 1024, collective_id=3, has_side_effects=True
         ),
-    )(log_row, storage, head_init, forcing, by_rows)
+    )(log_row, mine, other, source, by_rows)
 
 
 def gather_kernel(row_ref, out_ref, landing, send_sem, recv_sem):
@@ -439,19 +445,16 @@
     whole_log = lax.all_to_all(log_perm, "space", 0, 1, tiled=True)
     core = lax.axis_index("ens") % 2
     mine, other = gather_grids(jnp.where(core == 0, storage, head_init), n_space)
-    whole_storage = jnp.where(core == 0, mine, other)
-    whole_head = jnp.where(core == 0, other, mine)
     source = (
         jnp.zeros((grid_planes * depth * across,), jnp.float32)
         .at[well_cells]
         .add(well_rates)
         .reshape(grid_planes, depth, across)
     )
-    forcing = whole_storage * whole_head + source
     slab_rows = planes * depth
     by_rows = log_perm.reshape(members, slab_rows, across)
     field, band = forward_pallas(
-        whole_log[0], whole_storage, whole_head, forcing, by_rows, n_ens
+        whole_log[0], mine, other, source, by_rows, n_ens
     )
     picked = field.reshape(-1)[obs_cells]
     head_field = lax.all_to_all(field[None], "space", 1, 0, tiled=True)

time: 219 us -> 212 us (0.968)
  other arithmetic: 19.1 us -> 12.4 us
    add x1 -> x0, other arithmetic: 5.7 us -> none  [shards(): forcing = whole_storage * whole_head + source]
  transfers between devices with their start and end apart: 2 -> 2, of which waited for: 0 -> 0; matrix products, arithmetic and copies ran while one was open for 13% -> 10% of each run, Pallas kernels for 42% -> 43%
where the time goes in v20:
time: 212 us; the launch traced here: 211 us
  Pallas kernels  167 us (79%)
  local copies, waits for them, and re-layouts  12.8 us (6%)
  other arithmetic  12.4 us (6%)
  starting transfers between devices  11.4 us (5%)
  matrix products  5.53 us (3%)
    pallas_call x1, Pallas kernels, forward_pallas(): pl.pallas_call(forward_kernel, out_shape=(jax.ShapeDtypeStruct((planes, d...  58 us
    pallas_call x1, Pallas kernels, gather_grids(): pl.pallas_call(grid_kernel, out_shape=(grid, grid), in_specs=[anywhere],...  52.6 us
    pallas_call x1, Pallas kernels, send_back(): pl.pallas_call(return_kernel, out_shape=jax.ShapeDtypeStruct((members, sl...  37.8 us
    pallas_call x1, Pallas kernels, gather_rows(): pl.pallas_call(gather_kernel, out_shape=jax.ShapeDtypeStruct((total,) + r...  18.7 us
    all_to_all x1, starting transfers between devices, shards(): whole_log = lax.all_to_all(log_perm, 'space', 0, 1, tiled=True)  7.64 us
    unnamed x23, local copies, waits for them, and re-layouts  6.42 us
    dot_general x1, matrix products, shards(): new_band = jnp.einsum('jk,kry->jry', step, band, precision=HIGHEST)  4.54 us
  transfers between devices with their start and end apart: 2, of which 0 were waited for; matrix products, arithmetic and copies ran while one was open for 10% of the time, Pallas kernels for 43%

profile of v20, /device:TPU:25, one launch (start us, length us, event | category | flops | bytes accessed | tf_op | source)
XLA Modules:
  0.0 210.9 jit_solution(12498545312196695271)
XLA Ops:
  0.6 0.0 copy-start.1
  0.6 0.0 copy-start.2
  0.7 0.0 copy-start.7
  0.7 7.6 %all-to-all-start = ((f32[8,2,64,512]{3,2,1,0:T(8,128)}), f32[8,2,64,512]{3,2,1,0:T(8,128)}, u32[]{:S(2)}, u32[]{:S(2)}) async-start(f32[8,2,64,512]{3,2,1,0:T(8,128)} %param.14), calls=%async_computation | async-start | bytes 4194304 | tf_op jit(solution)/shard_map/all_to_all | solution.py:445
  8.3 0.0 copy-done.1
  8.3 0.0 copy-done.2
  8.3 0.7 broadcast_select_fusion.slab_ref
  9.1 52.6 %shard_map.113 = (f32[16,64,512]{2,1,0:T(8,128)}, f32[16,64,512]{2,1,0:T(8,128)}) custom-call(f32[2,64,512]{2,1,0:T(8,128)} %broadcast_select_fusion.slab_ref), custom_call_target="tpu_custom_call" | custom-call | tf_op jit(solution)/shard_map/pallas_call | solution.py:411
  61.7 0.0 copy-done.7
  61.7 1.3 scatter_custom_fusion
  63.0 0.0 copy-start.8
  63.0 0.0 copy-start.9
  63.1 1.5 reshape.124.src_ref
  65.2 1.2 dynamic-slice_bitcast_fusion
  66.4 0.0 copy-done.8
  66.4 0.6 pad_clamp_fusion
  67.0 0.0 copy-done.9
  67.0 0.5 broadcast_divide_fusion
  67.5 0.0 all-to-all-done
  67.5 58.0 %shard_map.114 = (f32[16,64,512]{2,1,0:T(8,128)}, f32[128,8,512]{2,1,0:T(8,128)}) custom-call(f32[16,64,512]{2,1,0:T(8,128)} %bitcast.log_ref, f32[16,64,512]{2,1,0:T(8,128)} %get-tuple-element.30.mine_ref, f32[16,64,512]{2,1,0:T(8,128)} %get-tuple-element.31.other_ref, f32[16,64,512]{2,1,0:T(8,128)} %reshape.124.src_ref, f32[8,128,512]{2,1,0:T(8,128)} %bitcast.38), custom_call_target="tpu_custom_call" | custom-call | tf_op jit(solution)/shard_map/pallas_call | solution.py:171
  125.6 0.0 copy-start.6
  125.6 0.0 copy-start.5
  125.6 2.1 %copy.26 = f32[128,4,8,128]{3,1,2,0:T(4,128)S(1)} copy(f32[128,4,8,128]{3,2,1,0:T(8,128)} %bitcast.17) | data formatting | bytes 4194304
  127.7 0.8 gather_fusion
  128.6 0.3 scatter.9.row_ref
  128.9 0.6 copy-done.3
  129.4 18.7 %shard_map.115 = f32[128,8,128]{2,1,0:T(8,128)} custom-call(f32[1,8,128]{2,1,0:T(8,128)} %copy-done.3), custom_call_target="tpu_custom_call" | custom-call | tf_op jit(solution)/shard_map/pallas_call | solution.py:250
  148.2 0.0 copy-done.5
  148.2 1.4 fusion.15
  149.6 3.8 %all-to-all-start.1 = ((f32[1,16,64,512]{3,2,0,1:T(8,128)}), f32[1,16,64,512]{3,2,0,1:T(8,128)S(1)}, u32[]{:S(2)}, u32[]{:S(2)}) async-start(f32[1,16,64,512]{3,2,0,1:T(8,128)} %bitcast.3), calls=%async_computation.1 | async-start | bytes 4194304 | tf_op jit(solution)/shard_map/all_to_all | solution.py:460
  153.4 1.1 broadcast_subtract_fusion
  154.5 0.3 convolution_multiply_fusion.1
  154.8 0.1 copy.22
  154.8 0.1 fusion.14
  154.9 2.9 %cholesky.16 = f32[32,32]{1,0:T(8,128)S(1)} custom-call(f32[32,32]{1,0:T(8,128)S(1)} %fusion.14), custom_call_target="Cholesky" | custom-call | tf_op jit(solution)/shard_map/jit(cholesky)/cholesky | solution.py:473
  157.9 0.6 compare_reduce_fusion
  158.5 0.7 fusion.8
  159.2 2.4 %custom-call.8 = f32[1,32,32]{1,2,0:T(8,128)S(1)} custom-call(f32[1,32,32]{2,1,0:T(8,128)S(1)} %fusion.8), custom_call_target="InvertDiagBlocksLowerTriangular" | custom-call | tf_op jit(solution)/shard_map/triangular_solve | solution.py:24
  161.6 0.3 fusion.11
  161.9 0.2 fusion.9
  162.0 0.3 fusion.3
  162.3 4.5 %fusion = f32[128,8,512]{2,0,1:T(8,128)S(1)} fusion(f32[128,128,1]{1,0,2:T(8,128)S(1)} %fusion.3, f32[128,8,512]{2,1,0:T(8,128)} %get-tuple-element.33), kind=kOutput, calls=%fused_computation.2 | convolution fusion | flops 805306368 | bytes 4259840 | tf_op jit(solution)/shard_map/jk,kry->jry/dot_general | solution.py:478
  166.9 2.5 %copy.24.column_ref = f32[128,8,512]{2,1,0:T(8,128)} copy(f32[128,8,512]{2,0,1:T(8,128)S(1)} %fusion) | data formatting | bytes 4194304 | tf_op jit(solution)/shard_map/jk,kry->jry/dot_general | solution.py:478
  169.4 37.8 %shard_map.116 = f32[8,128,512]{2,1,0:T(8,128)} custom-call(f32[128,8,512]{2,1,0:T(8,128)} %copy.24.column_ref), custom_call_target="tpu_custom_call" | custom-call | tf_op jit(solution)/shard_map/pallas_call | solution.py:312
  207.3 0.0 all-to-all-done.1
  207.3 1.3 copy.33
  208.6 1.0 copy-done
  209.6 1.3 copy.34
  (10 shorter events, 0.1 us)
Async XLA Ops:
  0.6 7.7 %copy-start.1 = (f32[2,64,512]{2,1,0:T(8,128)S(1)}, f32[2,64,512]{2,1,0:T(8,128)}, u32[]{:S(2)}) copy-start(f32[2,64,512]{2,1,0:T(8,128)} %param.15) | copy-start | bytes 786436
  0.6 7.7 %copy-start.2 = (f32[2,64,512]{2,1,0:T(8,128)S(1)}, f32[2,64,512]{2,1,0:T(8,128)}, u32[]{:S(2)}) copy-start(f32[2,64,512]{2,1,0:T(8,128)} %param.16) | copy-start | bytes 786436
  0.7 61.0 %copy-start.7 = (s32[16]{0:T(128)S(1)}, s32[16]{0:T(128)}, u32[]{:S(2)}) copy-start(s32[16]{0:T(128)} %param.17) | copy-start | bytes 196
  0.7 66.9 %all-to-all-start = ((f32[8,2,64,512]{3,2,1,0:T(8,128)}), f32[8,2,64,512]{3,2,1,0:T(8,128)}, u32[]{:S(2)}, u32[]{:S(2)}) async-start(f32[8,2,64,512]{3,2,1,0:T(8,128)} %param.14), calls=%async_computation | async-start | bytes 4194304 | tf_op jit(solution)/shard_map/all_to_all | solution.py:445
  63.0 3.4 %copy-start.8 = (s32[32]{0:T(128)S(1)}, s32[32]{0:T(128)}, u32[]{:S(2)}) copy-start(s32[32]{0:T(128)} %param.19) | copy-start | bytes 388
  63.0 4.0 %copy-start.9 = (f32[32]{0:T(128)S(1)}, f32[32]{0:T(128)}, u32[]{:S(2)}) copy-start(f32[32]{0:T(128)} %param.21) | copy-start | bytes 388
  125.6 3.0 %copy-start.6 = (f32[1,1,32]{2,1,0:T(1,128)S(1)}, f32[1,1,32]{2,1,0:T(1,128)}, u32[]{:S(2)}) copy-start(f32[1,1,32]{2,1,0:T(1,128)} %dynamic-slice_bitcast_fusion) | copy-start | bytes 388
  125.6 22.6 %copy-start.5 = (f32[32]{0:T(128)S(1)}, f32[32]{0:T(128)}, u32[]{:S(2)}) copy-start(f32[32]{0:T(128)} %param.20) | copy-start | bytes 388
  128.8 0.6 copy-start.3
  149.6 5.2 %copy-start.4 = (f32[32]{0:T(128)S(1)}, f32[32]{0:T(128)}, u32[]{:S(2)}) copy-start(f32[32]{0:T(128)} %broadcast_divide_fusion) | copy-start | bytes 388
  149.6 57.7 %all-to-all-start.1 = ((f32[1,16,64,512]{3,2,0,1:T(8,128)}), f32[1,16,64,512]{3,2,0,1:T(8,128)S(1)}, u32[]{:S(2)}, u32[]{:S(2)}) async-start(f32[1,16,64,512]{3,2,0,1:T(8,128)} %bitcast.3), calls=%async_computation.1 | async-start | bytes 4194304 | tf_op jit(solution)/shard_map/all_to_all | solution.py:460
  207.3 2.3 %copy-start = (f32[8,128,512]{2,1,0:T(8,128)S(1)}, f32[8,128,512]{2,1,0:T(8,128)}, u32[]{:S(2)}) copy-start(f32[8,128,512]{2,1,0:T(8,128)} %shard_map.116) | copy-start | bytes 6291460

commit v21 on v20

--- a/solution.py
+++ b/solution.py
@@ -445,11 +445,11 @@
     whole_log = lax.all_to_all(log_perm, "space", 0, 1, tiled=True)
     core = lax.axis_index("ens") % 2
     mine, other = gather_grids(jnp.where(core == 0, storage, head_init), n_space)
+    plane_cells = depth * across
     source = (
-        jnp.zeros((grid_planes * depth * across,), jnp.float32)
-        .at[well_cells]
+        jnp.zeros((grid_planes, depth, across), jnp.float32)
+        .at[well_cells // plane_cells, (well_cells % plane_cells) // across, well_cells % across]
         .add(well_rates)
-        .reshape(grid_planes, depth, across)
     )
     slab_rows = planes * depth
     by_rows = log_perm.reshape(members, slab_rows, across)

time: 212 us -> 214 us (level)
    unnamed x23 -> x25, local copies, waits for them, and re-layouts: 6.42 us -> 6.43 us
  transfers between devices with their start and end apart: 2 -> 2, of which waited for: 0 -> 0; matrix products, arithmetic and copies ran while one was open for 10% -> 11% of each run, Pallas kernels for 43% -> 43%
where the time goes in v21:
time: 214 us; the launch traced here: 213 us
  Pallas kernels  167 us (78%)
  other arithmetic  13.9 us (6%)
  local copies, waits for them, and re-layouts  13 us (6%)
  starting transfers between devices  11.4 us (5%)
  matrix products  5.54 us (3%)
    pallas_call x1, Pallas kernels, forward_pallas(): pl.pallas_call(forward_kernel, out_shape=(jax.ShapeDtypeStruct((planes, d...  58 us
    pallas_call x1, Pallas kernels, gather_grids(): pl.pallas_call(grid_kernel, out_shape=(grid, grid), in_specs=[anywhere],...  52.6 us
    pallas_call x1, Pallas kernels, send_back(): pl.pallas_call(return_kernel, out_shape=jax.ShapeDtypeStruct((members, sl...  37.8 us
    pallas_call x1, Pallas kernels, gather_rows(): pl.pallas_call(gather_kernel, out_shape=jax.ShapeDtypeStruct((total,) + r...  18.7 us
    all_to_all x1, starting transfers between devices, shards(): whole_log = lax.all_to_all(log_perm, 'space', 0, 1, tiled=True)  7.64 us
    unnamed x25, local copies, waits for them, and re-layouts  6.43 us
    dot_general x1, matrix products, shards(): new_band = jnp.einsum('jk,kry->jry', step, band, precision=HIGHEST)  4.55 us
  transfers between devices with their start and end apart: 2, of which 0 were waited for; matrix products, arithmetic and copies ran while one was open for 11% of the time, Pallas kernels for 43%

profile of v21, /device:TPU:25, one launch (start us, length us, event | category | flops | bytes accessed | tf_op | source)
XLA Modules:
  0.0 212.6 jit_solution(12796162604998458229)
XLA Ops:
  0.6 0.0 copy-start.1
  0.6 0.0 copy-start.2
  0.7 0.0 copy-start.8
  0.7 7.6 %all-to-all-start = ((f32[8,2,64,512]{3,2,1,0:T(8,128)}), f32[8,2,64,512]{3,2,1,0:T(8,128)}, u32[]{:S(2)}, u32[]{:S(2)}) async-start(f32[8,2,64,512]{3,2,1,0:T(8,128)} %param.14), calls=%async_computation | async-start | bytes 4194304 | tf_op jit(solution)/shard_map/all_to_all | solution.py:445
  8.3 0.0 copy-done.1
  8.3 0.0 copy-done.2
  8.3 0.0 copy-start.9
  8.3 0.0 copy-start.10
  8.4 0.7 broadcast_select_fusion.slab_ref
  9.1 52.6 %shard_map.113 = (f32[16,64,512]{2,1,0:T(8,128)}, f32[16,64,512]{2,1,0:T(8,128)}) custom-call(f32[2,64,512]{2,1,0:T(8,128)} %broadcast_select_fusion.slab_ref), custom_call_target="tpu_custom_call" | custom-call | tf_op jit(solution)/shard_map/pallas_call | solution.py:411
  62.3 0.0 copy-done.8
  62.4 1.6 broadcast_in_dim.43
  64.0 0.0 copy-done.5
  64.0 2.8 %scatter_fusion = f32[16,64,512]{2,1,0:T(8,128)} fusion(f32[16,64,512]{2,1,0:T(8,128)} %broadcast_in_dim.43, s32[16]{0:T(128)S(1)} %fusion.18, f32[16]{0:T(128)S(1)} %copy-done.5), kind=kCustom, calls=%fused_computation.1 | custom fusion | flops 16 | bytes 384 | tf_op jit(solution)/shard_map/scatter-add | solution.py:452
  66.8 1.3 dynamic-slice_bitcast_fusion
  68.0 0.0 copy-done.9
  68.0 0.6 pad_clamp_fusion
  68.6 0.0 copy-done.10
  68.6 0.5 broadcast_divide_fusion
  69.2 0.0 all-to-all-done
  69.2 58.0 %shard_map.114 = (f32[16,64,512]{2,1,0:T(8,128)}, f32[128,8,512]{2,1,0:T(8,128)}) custom-call(f32[16,64,512]{2,1,0:T(8,128)} %bitcast.log_ref, f32[16,64,512]{2,1,0:T(8,128)} %get-tuple-element.30.mine_ref, f32[16,64,512]{2,1,0:T(8,128)} %get-tuple-element.31.other_ref, f32[16,64,512]{2,1,0:T(8,128)} %scatter_fusion, f32[8,128,512]{2,1,0:T(8,128)} %bitcast.58), custom_call_target="tpu_custom_call" | custom-call | tf_op jit(solution)/shard_map/pallas_call | solution.py:171
  127.2 0.0 copy-start.7
  127.2 0.0 copy-start.6
  127.2 2.1 %copy.26 = f32[128,4,8,128]{3,1,2,0:T(4,128)S(1)} copy(f32[128,4,8,128]{3,2,1,0:T(8,128)} %bitcast.21) | data formatting | bytes 4194304
  129.4 0.8 gather_fusion
  130.2 0.3 scatter.9.row_ref
  130.5 0.6 copy-done.3
  131.1 18.7 %shard_map.115 = f32[128,8,128]{2,1,0:T(8,128)} custom-call(f32[1,8,128]{2,1,0:T(8,128)} %copy-done.3), custom_call_target="tpu_custom_call" | custom-call | tf_op jit(solution)/shard_map/pallas_call | solution.py:250
  149.8 1.4 fusion.19
  151.3 3.8 %all-to-all-start.1 = ((f32[1,16,64,512]{3,2,0,1:T(8,128)}), f32[1,16,64,512]{3,2,0,1:T(8,128)S(1)}, u32[]{:S(2)}, u32[]{:S(2)}) async-start(f32[1,16,64,512]{3,2,0,1:T(8,128)} %bitcast.7), calls=%async_computation.1 | async-start | bytes 4194304 | tf_op jit(solution)/shard_map/all_to_all | solution.py:460
  155.1 1.1 broadcast_subtract_fusion
  156.1 0.3 convolution_multiply_fusion.1
  156.4 0.1 copy.22
  156.5 0.1 fusion.12
  156.6 2.9 %cholesky.16 = f32[32,32]{1,0:T(8,128)S(1)} custom-call(f32[32,32]{1,0:T(8,128)S(1)} %fusion.12), custom_call_target="Cholesky" | custom-call | tf_op jit(solution)/shard_map/jit(cholesky)/cholesky | solution.py:473
  159.5 0.6 compare_reduce_fusion
  160.2 0.7 fusion.6
  160.8 2.4 %custom-call.8 = f32[1,32,32]{1,2,0:T(8,128)S(1)} custom-call(f32[1,32,32]{2,1,0:T(8,128)S(1)} %fusion.6), custom_call_target="InvertDiagBlocksLowerTriangular" | custom-call | tf_op jit(solution)/shard_map/triangular_solve | solution.py:24
  163.2 0.3 fusion.9
  163.5 0.2 fusion.7
  163.7 0.3 fusion.3
  164.0 4.6 %fusion = f32[128,8,512]{2,0,1:T(8,128)S(1)} fusion(f32[128,128,1]{1,0,2:T(8,128)S(1)} %fusion.3, f32[128,8,512]{2,1,0:T(8,128)} %get-tuple-element.33), kind=kOutput, calls=%fused_computation.2 | convolution fusion | flops 805306368 | bytes 4259840 | tf_op jit(solution)/shard_map/jk,kry->jry/dot_general | solution.py:478
  168.6 2.5 %copy.24.column_ref = f32[128,8,512]{2,1,0:T(8,128)} copy(f32[128,8,512]{2,0,1:T(8,128)S(1)} %fusion) | data formatting | bytes 4194304 | tf_op jit(solution)/shard_map/jk,kry->jry/dot_general | solution.py:478
  171.1 37.8 %shard_map.116 = f32[8,128,512]{2,1,0:T(8,128)} custom-call(f32[128,8,512]{2,1,0:T(8,128)} %copy.24.column_ref), custom_call_target="tpu_custom_call" | custom-call | tf_op jit(solution)/shard_map/pallas_call | solution.py:312
  208.9 0.0 all-to-all-done.1
  208.9 1.3 copy.34
  210.3 1.0 copy-done
  211.3 1.3 copy.35
  (12 shorter events, 0.1 us)
Async XLA Ops:
  0.6 7.7 %copy-start.1 = (f32[2,64,512]{2,1,0:T(8,128)S(1)}, f32[2,64,512]{2,1,0:T(8,128)}, u32[]{:S(2)}) copy-start(f32[2,64,512]{2,1,0:T(8,128)} %param.15) | copy-start | bytes 786436
  0.6 7.7 %copy-start.2 = (f32[2,64,512]{2,1,0:T(8,128)S(1)}, f32[2,64,512]{2,1,0:T(8,128)}, u32[]{:S(2)}) copy-start(f32[2,64,512]{2,1,0:T(8,128)} %param.16) | copy-start | bytes 786436
  0.7 61.7 %copy-start.8 = (s32[16]{0:T(128)S(1)}, s32[16]{0:T(128)}, u32[]{:S(2)}) copy-start(s32[16]{0:T(128)} %param.17) | copy-start | bytes 196
  0.7 68.5 %all-to-all-start = ((f32[8,2,64,512]{3,2,1,0:T(8,128)}), f32[8,2,64,512]{3,2,1,0:T(8,128)}, u32[]{:S(2)}, u32[]{:S(2)}) async-start(f32[8,2,64,512]{3,2,1,0:T(8,128)} %param.14), calls=%async_computation | async-start | bytes 4194304 | tf_op jit(solution)/shard_map/all_to_all | solution.py:445
  8.3 55.7 %copy-start.5 = (f32[16]{0:T(128)S(1)}, f32[16]{0:T(128)}, u32[]{:S(2)}) copy-start(f32[16]{0:T(128)} %param.18) | copy-start | bytes 196
  8.3 59.7 %copy-start.9 = (s32[32]{0:T(128)S(1)}, s32[32]{0:T(128)}, u32[]{:S(2)}) copy-start(s32[32]{0:T(128)} %param.19) | copy-start | bytes 388
  8.3 60.3 %copy-start.10 = (f32[32]{0:T(128)S(1)}, f32[32]{0:T(128)}, u32[]{:S(2)}) copy-start(f32[32]{0:T(128)} %param.21) | copy-start | bytes 388
  127.2 3.0 %copy-start.7 = (f32[1,1,32]{2,1,0:T(1,128)S(1)}, f32[1,1,32]{2,1,0:T(1,128)}, u32[]{:S(2)}) copy-start(f32[1,1,32]{2,1,0:T(1,128)} %dynamic-slice_bitcast_fusion) | copy-start | bytes 388
  127.2 22.6 %copy-start.6 = (f32[32]{0:T(128)S(1)}, f32[32]{0:T(128)}, u32[]{:S(2)}) copy-start(f32[32]{0:T(128)} %param.20) | copy-start | bytes 388
  130.5 0.6 copy-start.3
  151.2 5.2 %copy-start.4 = (f32[32]{0:T(128)S(1)}, f32[32]{0:T(128)}, u32[]{:S(2)}) copy-start(f32[32]{0:T(128)} %broadcast_divide_fusion) | copy-start | bytes 388
  151.3 57.7 %all-to-all-start.1 = ((f32[1,16,64,512]{3,2,0,1:T(8,128)}), f32[1,16,64,512]{3,2,0,1:T(8,128)S(1)}, u32[]{:S(2)}, u32[]{:S(2)}) async-start(f32[1,16,64,512]{3,2,0,1:T(8,128)} %bitcast.7), calls=%async_computation.1 | async-start | bytes 4194304 | tf_op jit(solution)/shard_map/all_to_all | solution.py:460
  208.9 2.3 %copy-start = (f32[8,128,512]{2,1,0:T(8,128)S(1)}, f32[8,128,512]{2,1,0:T(8,128)}, u32[]{:S(2)}) copy-start(f32[8,128,512]{2,1,0:T(8,128)} %shard_map.116) | copy-start | bytes 6291460
